TPU v7x, 32 devices: a whole 2x2x4 slice. The times are simulated.
32 devices in a mesh: dp: 8 (over y, x, core), tensor: 4 (over z).
Axes of the slice: x: 2, y: 2, z: 4, core: 2. Of those that a mesh axis runs over, the one named last changes fastest.
Arguments:
- activations: bfloat16 [8, 2048, 2048], P('dp', 'tensor'), may hold values from -6 to 6
- segment_ids: int32 [8, 2048], P('dp'), may hold values from 0 to 3, as said below
- attn_gain: float32 [2048], replicated, may hold values from 0.1 to 1.9
- w_query: bfloat16 [2048, 2048], P('dp', 'tensor'), may hold values from -0.125 to 0.125
- w_key: bfloat16 [2048, 512], P('dp', 'tensor'), may hold values from -0.125 to 0.125
- w_value: bfloat16 [2048, 512], P('dp', 'tensor'), may hold values from -0.125 to 0.125
- w_out: bfloat16 [2048, 2048], P('dp', 'tensor'), may hold values from -0.375 to 0.375
- mlp_gain: float32 [2048], replicated, may hold values from 0.1 to 1.9
- w_gate: bfloat16 [2048, 8192], P('dp', 'tensor'), may hold values from -0.125 to 0.125
- w_up: bfloat16 [2048, 8192], P('dp', 'tensor'), may hold values from -0.125 to 0.125
- w_down: bfloat16 [2048, 8192], P('dp', 'tensor'), may hold values from -0.09375 to 0.09375
- cotangent: bfloat16 [8, 2048, 2048], P('dp', 'tensor'), may hold values from -6 to 6
Outputs:
- output: bfloat16 [8, 2048, 2048], P('dp', 'tensor')
- input_grad: bfloat16 [8, 2048, 2048], P('dp', 'tensor')
- attn_gain_grad: float32 [2048], replicated
- w_query_grad: float32 [2048, 2048], P('dp', 'tensor')
- w_key_grad: float32 [2048, 512], P('dp', 'tensor')
- w_value_grad: float32 [2048, 512], P('dp', 'tensor')
- w_out_grad: float32 [2048, 2048], P('dp', 'tensor')
- mlp_gain_grad: float32 [2048], replicated
- w_gate_grad: float32 [2048, 8192], P('dp', 'tensor')
- w_up_grad: float32 [2048, 8192], P('dp', 'tensor')
- w_down_grad: float32 [2048, 8192], P('dp', 'tensor')
Inputs may be any that keep to these rules, and one draw needn't show every extreme that they name: `segment_ids`: along each sequence the ids never fall; each of the 4 documents has 204 to 1024 tokens, and exactly one document of each sequence has 1024.
All inputs are finite; a program needn't handle non-finite values.
Results may differ from a plain program's by a relative error of at most 0.018.
Values may be sent and summed in bfloat16 or wider, within the bound.
A program may use at most 320 MiB of HBM per device.

v0:
```python
import math

import jax
import jax.numpy as jnp
from jax import lax
from jax.sharding import PartitionSpec as P

HEAD_DIM = 64
DOCS = 4
QBLOCK = 512


NORM_EPS = 1e-05
ROPE_THETA = 500000.0


def matmul(left, right):
    return jnp.dot(left, right, preferred_element_type=jnp.float32)


def matmul_nt(left, right):
    return lax.dot_general(
        left, right, (((1,), (1,)), ((), ())), preferred_element_type=jnp.float32
    )


def matmul_tn(left, right):
    return lax.dot_general(
        left, right, (((0,), (0,)), ((), ())), preferred_element_type=jnp.float32
    )


def rope_tables(segments):
    length = segments.shape[-1]
    doc_ids = jnp.arange(DOCS, dtype=jnp.int32)
    member = (segments[..., :, None] == doc_ids).astype(jnp.int32)
    counts = jnp.sum(member, axis=-2)
    before = (doc_ids < segments[..., :, None]).astype(jnp.int32)
    first = jnp.sum(before * counts[..., None, :], axis=-1)
    position = (jnp.arange(length, dtype=jnp.int32) - first).astype(jnp.float32)
    frequency = jnp.exp(
        jnp.arange(HEAD_DIM // 2, dtype=jnp.float32) * (-2.0 * math.log(ROPE_THETA) / HEAD_DIM)
    )
    angles = position[..., None] * frequency
    return (jnp.cos(angles), jnp.sin(angles))


def rotate(values_in, cosine, sine_tab):
    half_dim = HEAD_DIM // 2
    first_half = values_in[..., :half_dim]
    second_half = values_in[..., half_dim:]
    cos_wide = cosine[..., None, :]
    sin_wide = sine_tab[..., None, :]
    return jnp.concatenate(
        [
            first_half * cos_wide - second_half * sin_wide,
            second_half * cos_wide + first_half * sin_wide,
        ],
        axis=-1,
    )


def rotate_back(grad_in, cosine, sine_tab):
    half_dim = HEAD_DIM // 2
    first_half = grad_in[..., :half_dim]
    second_half = grad_in[..., half_dim:]
    cos_wide = cosine[..., None, :]
    sin_wide = sine_tab[..., None, :]
    return jnp.concatenate(
        [
            first_half * cos_wide + second_half * sin_wide,
            second_half * cos_wide - first_half * sin_wide,
        ],
        axis=-1,
    )


def rms_scale(values_in):
    return lax.rsqrt(jnp.mean(values_in * values_in, axis=-1, keepdims=True) + NORM_EPS)


def norm_back(values_in, scaling, gain, grad_in):
    gained = grad_in * gain
    gain_part = jnp.sum(grad_in * values_in * scaling, axis=(0, 1))
    inner = jnp.mean(gained * values_in, axis=-1, keepdims=True)
    return (gain_part, scaling * gained - values_in * scaling * scaling * scaling * inner)


def gather_rows(local_rows):
    return lax.all_gather(local_rows, "tensor", axis=1, tiled=True)


def sum_rows(partial_rows):
    return lax.psum_scatter(partial_rows, "tensor", scatter_dimension=1, tiled=True)


def block_inputs(block_id, query_rot, key_rot, value_rows, segment_ids):
    length = segment_ids.shape[1]
    blocks = length // QBLOCK
    seq_id = block_id // blocks
    offset = block_id % blocks * QBLOCK
    query_seq = lax.dynamic_index_in_dim(query_rot, seq_id, 0, False)
    query_block = lax.dynamic_slice_in_dim(query_seq, offset, QBLOCK, 0)
    key_seq = lax.dynamic_index_in_dim(key_rot, seq_id, 0, False)
    value_seq = lax.dynamic_index_in_dim(value_rows, seq_id, 0, False)
    seg_seq = lax.dynamic_index_in_dim(segment_ids, seq_id, 0, False)
    query_seg = lax.dynamic_slice_in_dim(seg_seq, offset, QBLOCK, 0)
    query_pos = offset + jnp.arange(QBLOCK, dtype=jnp.int32)
    key_pos = jnp.arange(length, dtype=jnp.int32)
    allowed = (query_seg[:, None] == seg_seq[None, :]) & (key_pos[None, :] <= query_pos[:, None])
    score = jnp.einsum(
        "qkgd,skd->kgqs", query_block, key_seq, preferred_element_type=jnp.float32
    ) * HEAD_DIM ** (-0.5)
    score = jnp.where(allowed, score, -1e30)
    return (seq_id, offset, query_block, key_seq, value_seq, score)


def attend(query_rot, key_rot, value_rows, segment_ids):
    seq_count, length = segment_ids.shape

    def one_block(block_id):
        seq_id, offset, query_block, key_seq, value_seq, score = block_inputs(
            block_id, query_rot, key_rot, value_rows, segment_ids
        )
        row_max = jnp.max(score, axis=-1, keepdims=True)
        expd = jnp.exp(score - row_max)
        row_sum = jnp.sum(expd, axis=-1, keepdims=True)
        weights = (expd / row_sum).astype(jnp.bfloat16)
        result = jnp.einsum(
            "kgqs,skd->qkgd", weights, value_seq, preferred_element_type=jnp.float32
        ).astype(jnp.bfloat16)
        return (result, row_max[..., 0] + jnp.log(row_sum[..., 0]))

    count_blocks = seq_count * (length // QBLOCK)
    results, log_sums = lax.map(one_block, jnp.arange(count_blocks, dtype=jnp.int32))
    return (results.reshape(seq_count, length, *results.shape[2:]), log_sums)


def attend_back(query_rot, key_rot, value_rows, grad_att, log_sums, segment_ids):
    seq_count, length = segment_ids.shape
    blocks = length // QBLOCK

    def one_block(block_id):
        seq_id, offset, query_block, key_seq, value_seq, score = block_inputs(
            block_id, query_rot, key_rot, value_rows, segment_ids
        )
        grad_seq = lax.dynamic_index_in_dim(grad_att, seq_id, 0, False)
        grad_block = lax.dynamic_slice_in_dim(grad_seq, offset, QBLOCK, 0)
        lse_block = lax.dynamic_index_in_dim(log_sums, block_id, 0, False)
        prob_rows = jnp.exp(score - lse_block[..., None])
        weights = prob_rows.astype(jnp.bfloat16)
        grad_weights = jnp.einsum(
            "qkgd,skd->kgqs", grad_block, value_seq, preferred_element_type=jnp.float32
        )
        row_dot = jnp.sum(grad_weights * prob_rows, axis=-1, keepdims=True)
        grad_score = (prob_rows * (grad_weights - row_dot)).astype(jnp.bfloat16)
        scaling = HEAD_DIM ** (-0.5)
        grad_query = (
            jnp.einsum("kgqs,skd->qkgd", grad_score, key_seq, preferred_element_type=jnp.float32)
            * scaling
        )
        grad_key = (
            jnp.einsum(
                "kgqs,qkgd->skd", grad_score, query_block, preferred_element_type=jnp.float32
            )
            * scaling
        )
        grad_value = jnp.einsum(
            "kgqs,qkgd->skd", weights, grad_block, preferred_element_type=jnp.float32
        )
        return (grad_query, grad_key, grad_value)

    grad_query, grad_key, grad_value = lax.map(
        one_block, jnp.arange(seq_count * blocks, dtype=jnp.int32)
    )
    grad_query = grad_query.reshape(seq_count, length, *grad_query.shape[2:])
    grad_key = jnp.sum(grad_key.reshape(seq_count, blocks, length, *grad_key.shape[2:]), axis=1)
    grad_value = jnp.sum(
        grad_value.reshape(seq_count, blocks, length, *grad_value.shape[2:]), axis=1
    )
    return (grad_query, grad_key, grad_value)


def per_device(
    activations,
    segment_ids,
    attn_gain,
    w_query,
    w_key,
    w_value,
    w_out,
    mlp_gain,
    w_gate,
    w_up,
    w_down,
    cotangent,
):
    seq_count, row_count, model_width = activations.shape
    length = segment_ids.shape[1]
    tok_count = seq_count * length
    kv_local = w_key.shape[1] // HEAD_DIM
    head_local = w_query.shape[1] // HEAD_DIM
    group_size = head_local // kv_local
    cosine, sine_tab = rope_tables(segment_ids)
    attn_full = (
        lax.all_gather(w_query, "dp", axis=0, tiled=True),
        lax.all_gather(w_key, "dp", axis=0, tiled=True),
        lax.all_gather(w_value, "dp", axis=0, tiled=True),
        lax.all_gather(w_out, "dp", axis=0, tiled=True),
    )
    x_float = activations.astype(jnp.float32)
    scale_one = rms_scale(x_float)
    normed = gather_rows((x_float * scale_one * attn_gain).astype(jnp.bfloat16)).reshape(
        tok_count, model_width
    )
    query_rot = rotate(
        matmul(normed, attn_full[0]).reshape(seq_count, length, head_local, HEAD_DIM),
        cosine,
        sine_tab,
    )
    query_rot = query_rot.astype(jnp.bfloat16).reshape(
        seq_count, length, kv_local, group_size, HEAD_DIM
    )
    key_rot = rotate(
        matmul(normed, attn_full[1]).reshape(seq_count, length, kv_local, HEAD_DIM),
        cosine,
        sine_tab,
    ).astype(jnp.bfloat16)
    value_rows = (
        matmul(normed, attn_full[2])
        .astype(jnp.bfloat16)
        .reshape(seq_count, length, kv_local, HEAD_DIM)
    )
    attended, log_sums = attend(query_rot, key_rot, value_rows, segment_ids)
    attended_flat = attended.reshape(tok_count, head_local * HEAD_DIM)
    resid = x_float + sum_rows(
        matmul_nt(attended_flat, attn_full[3]).reshape(seq_count, length, model_width)
    )
    mlp_full = (
        lax.all_gather(w_gate, "dp", axis=0, tiled=True),
        lax.all_gather(w_up, "dp", axis=0, tiled=True),
        lax.all_gather(w_down, "dp", axis=0, tiled=True),
    )
    scale_two = rms_scale(resid)
    normed_mlp = gather_rows((resid * scale_two * mlp_gain).astype(jnp.bfloat16)).reshape(
        tok_count, model_width
    )
    gate_pre = matmul(normed_mlp, mlp_full[0])
    up_proj = matmul(normed_mlp, mlp_full[1])
    hidden = (jax.nn.silu(gate_pre) * up_proj).astype(jnp.bfloat16)
    output = (
        resid + sum_rows(matmul_nt(hidden, mlp_full[2]).reshape(seq_count, length, model_width))
    ).astype(jnp.bfloat16)
    mlp_back = (
        lax.all_gather(w_gate, "dp", axis=0, tiled=True),
        lax.all_gather(w_up, "dp", axis=0, tiled=True),
        lax.all_gather(w_down, "dp", axis=0, tiled=True),
    )
    grad_full = gather_rows(cotangent).reshape(tok_count, model_width)
    grad_down_w = matmul_tn(grad_full, hidden)
    grad_hidden = matmul(grad_full, mlp_back[2])
    sigma = jax.nn.sigmoid(gate_pre)
    grad_gate = (grad_hidden * up_proj * sigma * (1.0 + gate_pre * (1.0 - sigma))).astype(
        jnp.bfloat16
    )
    grad_up = (grad_hidden * gate_pre * sigma).astype(jnp.bfloat16)
    grad_gate_w = matmul_tn(normed_mlp, grad_gate)
    grad_up_w = matmul_tn(normed_mlp, grad_up)
    grad_normed_mlp = matmul_nt(grad_gate, mlp_back[0]) + matmul_nt(grad_up, mlp_back[1])
    grad_normed_mlp = sum_rows(grad_normed_mlp.reshape(seq_count, length, model_width))
    gain_two_part, grad_resid_norm = norm_back(resid, scale_two, mlp_gain, grad_normed_mlp)
    grad_resid = cotangent.astype(jnp.float32) + grad_resid_norm
    attn_back = (
        lax.all_gather(w_query, "dp", axis=0, tiled=True),
        lax.all_gather(w_key, "dp", axis=0, tiled=True),
        lax.all_gather(w_value, "dp", axis=0, tiled=True),
        lax.all_gather(w_out, "dp", axis=0, tiled=True),
    )
    grad_resid_full = gather_rows(grad_resid.astype(jnp.bfloat16)).reshape(tok_count, model_width)
    grad_out_w = matmul_tn(grad_resid_full, attended_flat)
    grad_att = matmul(grad_resid_full, attn_back[3]).astype(jnp.bfloat16)
    grad_att = grad_att.reshape(seq_count, length, kv_local, group_size, HEAD_DIM)
    grad_query_rot, grad_key_rot, grad_value_rows = attend_back(
        query_rot, key_rot, value_rows, grad_att, log_sums, segment_ids
    )
    grad_query = rotate_back(
        grad_query_rot.reshape(seq_count, length, head_local, HEAD_DIM), cosine, sine_tab
    )
    grad_query = grad_query.astype(jnp.bfloat16).reshape(tok_count, head_local * HEAD_DIM)
    grad_key = (
        rotate_back(grad_key_rot, cosine, sine_tab)
        .astype(jnp.bfloat16)
        .reshape(tok_count, kv_local * HEAD_DIM)
    )
    grad_value = grad_value_rows.astype(jnp.bfloat16).reshape(tok_count, kv_local * HEAD_DIM)
    grad_query_w = matmul_tn(normed, grad_query)
    grad_key_w = matmul_tn(normed, grad_key)
    grad_value_w = matmul_tn(normed, grad_value)
    grad_normed = (
        matmul_nt(grad_query, attn_back[0])
        + matmul_nt(grad_key, attn_back[1])
        + matmul_nt(grad_value, attn_back[2])
    )
    grad_normed = sum_rows(grad_normed.reshape(seq_count, length, model_width))
    gain_one_part, grad_x_norm = norm_back(x_float, scale_one, attn_gain, grad_normed)
    input_grad = (grad_resid + grad_x_norm).astype(jnp.bfloat16)
    gain_totals = lax.psum((gain_one_part, gain_two_part), ("dp", "tensor"))
    all_sums = (
        lax.psum_scatter(
            grad_query_w.astype(jnp.bfloat16), "dp", scatter_dimension=0, tiled=True
        ).astype(jnp.float32),
        lax.psum_scatter(
            grad_key_w.astype(jnp.bfloat16), "dp", scatter_dimension=0, tiled=True
        ).astype(jnp.float32),
        lax.psum_scatter(
            grad_value_w.astype(jnp.bfloat16), "dp", scatter_dimension=0, tiled=True
        ).astype(jnp.float32),
        lax.psum_scatter(
            grad_out_w.astype(jnp.bfloat16), "dp", scatter_dimension=0, tiled=True
        ).astype(jnp.float32),
        lax.psum_scatter(
            grad_gate_w.astype(jnp.bfloat16), "dp", scatter_dimension=0, tiled=True
        ).astype(jnp.float32),
        lax.psum_scatter(
            grad_up_w.astype(jnp.bfloat16), "dp", scatter_dimension=0, tiled=True
        ).astype(jnp.float32),
        lax.psum_scatter(
            grad_down_w.astype(jnp.bfloat16), "dp", scatter_dimension=0, tiled=True
        ).astype(jnp.float32),
    )
    attn_sums = all_sums[:4]
    mlp_sums = all_sums[4:]
    return (
        output,
        input_grad,
        gain_totals[0],
        attn_sums[0],
        attn_sums[1],
        attn_sums[2],
        attn_sums[3],
        gain_totals[1],
        mlp_sums[0],
        mlp_sums[1],
        mlp_sums[2],
    )


def solution(mesh):
    in_specs = (
        P("dp", "tensor", None),
        P("dp", None),
        P(),
        P("dp", "tensor"),
        P("dp", "tensor"),
        P("dp", "tensor"),
        P("dp", "tensor"),
        P(),
        P("dp", "tensor"),
        P("dp", "tensor"),
        P("dp", "tensor"),
        P("dp", "tensor", None),
    )
    out_specs = (
        P("dp", "tensor", None),
        P("dp", "tensor", None),
        P(),
        P("dp", "tensor"),
        P("dp", "tensor"),
        P("dp", "tensor"),
        P("dp", "tensor"),
        P(),
        P("dp", "tensor"),
        P("dp", "tensor"),
        P("dp", "tensor"),
    )
    return jax.shard_map(
        per_device, mesh=mesh, in_specs=in_specs, out_specs=out_specs, check_vma=False
    )
```

profile of v0, /device:TPU:0, one launch (start us, length us, event | category | flops | bytes accessed | tf_op | source)
XLA Modules:
  0.0 2988.1 jit_solution(1791326415638827385)
XLA Ops:
  14.7 12.7 all_gather.42
  27.4 10.7 all_gather.43
  45.6 149.2 %all-gather.10.cloned.1.call-done = bf16[1,2048,2048]{2,1,0:T(8,128)(2,1)} async-done(((bf16[1,512,2048]{2,1,0:T(8,128)(2,1)}), bf16[1,2048,2048]{2,1,0:T(8,128)(2,1)}) %all-gather.10.cloned.1.call-update) | async-done | bytes 8388624 | tf_op jit(solution)/shard_map/all_gather | solution.py:90
  211.1 199.4 %while.30 = (s32[]{:T(128)}, bf16[4,512,2,4,64]{1,4,3,2,0:T(8,128)(2,1)}, f32[4,2,4,512]{3,2,1,0:T(4,128)}, s32[4]{0:T(128)S(1)}, s32[1,2048]{1,0:T(1,128)S(1)},...) while((s32[]{:T(128)}, ...), condition=%wide.region_6.7_spmd, body=%wide.region_3.6_spmd.sunk | while | flops 2251551232 | bytes 107104584 | solution.py:135
  215.1 14.5 bitcast_reduce_fusion.2
  229.7 15.0 fusion.180
  244.7 15.8 fusion.181
  264.8 14.5 bitcast_reduce_fusion.2
  279.4 15.0 fusion.180
  294.4 15.8 fusion.181
  314.5 14.5 bitcast_reduce_fusion.2
  329.1 15.0 fusion.180
  344.1 15.8 fusion.181
  364.2 14.5 bitcast_reduce_fusion.2
  378.8 15.0 fusion.180
  393.7 15.8 fusion.181
  416.1 12.6 convolution_bitcast_fusion.2
  429.4 278.2 %reduce-scatter.12.cloned.1.call-done = f32[1,512,2048]{2,1,0:T(8,128)} async-done(((f32[1,2048,2048]{2,1,0:T(8,128)}), f32[1,512,2048]{2,1,0:T(8,128)}) %reduce-scatter.12.cloned.1.call-update) | async-done | bytes 4194320 | tf_op jit(solution)/shard_map/reduce_scatter | solution.py:94
  716.5 48.2 %all-gather.20.cloned.1.call-done = bf16[2048,2048]{1,0:T(8,128)(2,1)} async-done(((bf16[256,2048]{1,0:T(8,128)(2,1)}), bf16[2048,2048]{1,0:T(8,128)(2,1)}) %all-gather.20.cloned.1.call-update) | async-done | bytes 8388624 | tf_op jit(solution)/shard_map/all_gather | solution.py:241
  764.6 151.7 %all-gather.16.cloned.1.call-done = bf16[1,2048,2048]{2,1,0:T(8,128)(2,1)} async-done(((bf16[1,512,2048]{2,1,0:T(8,128)(2,1)}), bf16[1,2048,2048]{2,1,0:T(8,128)(2,1)}) %all-gather.16.cloned.1.call-update) | async-done | bytes 8388624 | tf_op jit(solution)/shard_map/all_gather | solution.py:90
  916.4 24.4 fusion.65
  940.7 30.3 %all-gather.18.cloned.1.call-done = bf16[2048,2048]{1,0:T(8,128)(2,1)} async-done(((bf16[256,2048]{1,0:T(8,128)(2,1)}), bf16[2048,2048]{1,0:T(8,128)(2,1)}) %all-gather.18.cloned.1.call-update) | async-done | bytes 8388624 | tf_op jit(solution)/shard_map/all_gather | solution.py:240
  971.1 24.2 fusion.67
  995.3 127.1 %all-gather.24.cloned.1.call-done = bf16[1,2048,2048]{2,1,0:T(8,128)(2,1)} async-done(((bf16[1,512,2048]{2,1,0:T(8,128)(2,1)}), bf16[1,2048,2048]{2,1,0:T(8,128)(2,1)}) %all-gather.24.cloned.1.call-update) | async-done | bytes 8388624 | tf_op jit(solution)/shard_map/all_gather | solution.py:90
  1122.4 54.7 %all-gather.22.cloned.1.call-done = bf16[2048,2048]{1,0:T(8,128)(2,1)} async-done(((bf16[256,2048]{1,0:T(8,128)(2,1)}), bf16[2048,2048]{1,0:T(8,128)(2,1)}) %all-gather.22.cloned.1.call-update) | async-done | bytes 8388624 | tf_op jit(solution)/shard_map/all_gather | solution.py:242
  1177.1 34.8 %multiply_convert_fusion = (bf16[2048,2048]{1,0:T(8,128)(2,1)}, bf16[2048,2048]{1,0:T(8,128)(2,1)}, bf16[2048,2048]{1,0:T(8,128)(2,1)}) fusion(f32[2048,2048]{1,0:T(8,128)} %fusion.67, f32[2048,2048]{1,0:T(8,128)} %fusion.65, bf16[2048,2048]{1,0:T(8,128)(2,1)} %all-gather.22.cloned.1.call-done, bf16[1,2048,2048]{2,1,0:T(8,128)(2,1)} %all-gather.24.cloned.1.call-done), kind=kOutput, calls=%fused_computation.67 | convolution fusion | flops 17246978048 | bytes 75497472 | tf_op jit(solution)/shard_map/dot_general | solution.py:18
  1211.9 24.3 fusion.126
  1236.2 26.7 add_bitcast_fusion.1
  1263.0 280.4 %reduce-scatter.16.cloned.1.call-done = f32[1,512,2048]{2,1,0:T(8,128)} async-done(((f32[1,2048,2048]{2,1,0:T(8,128)}), f32[1,512,2048]{2,1,0:T(8,128)}) %reduce-scatter.16.cloned.1.call-update) | async-done | bytes 4194320 | tf_op jit(solution)/shard_map/reduce_scatter | solution.py:94
  1552.2 23.7 convert_bitcast_fusion
  1576.1 24.0 fusion.84
  1600.1 23.8 fusion.81
  1624.0 78.7 %all-gather.26.cloned.1.call-done = bf16[1,2048,2048]{2,1,0:T(8,128)(2,1)} async-done(((bf16[1,512,2048]{2,1,0:T(8,128)(2,1)}), bf16[1,2048,2048]{2,1,0:T(8,128)(2,1)}) %all-gather.26.cloned.1.call-update) | async-done | bytes 8388624 | tf_op jit(solution)/shard_map/all_gather | solution.py:90
  1712.6 521.1 %while.31 = (s32[]{:T(128)}, f32[4,512,2,4,64]{1,0,4,3,2:T(4,128)}, f32[4,2048,2,64]{1,3,2,0:T(8,128)}, f32[4,2048,2,64]{1,3,2,0:T(8,128)}, s32[4]{0:T(128)S(1)}...) while((s32[]{:T(128)}, f32[4,512,2,4,64]{1,0,4,3,2:T(4,128)}, ...), condition=%wide.region_14.15_spmd, body=%wide.region_12.14_spmd.sunk | while | flops 5498204672 | bytes 367659456 | solution.py:173
  1718.9 14.9 fusion.190
  1733.8 16.2 fusion.196
  1750.0 26.5 fusion.192
  1776.5 31.1 %fusion.193 = bf16[2,4,512,2048]{3,2,1,0:T(8,128)(2,1)} fusion(f32[2,512,4,2048]{3,1,2,0:T(8,128)} %get-tuple-element.479, f32[2,512,4,2048]{3,1,2,0:T(8,128)} %fusion.190, f32[2,4,512]{2,1,0:T(4,128)S(1)} %get-tuple-element.480, f32[2,4,512]{2,1,0:T(4,128)S(1)} %dynamic-slice_bitcast_fusion.2, pred[512,2048]{1,0:T(8,128)(4,1)S(1)} %fusion.191), kind=kLoop, calls=%fused_computation.27.clone.1 | loop fusion | flops 50331648 | bytes 84967424 | tf_op jit(solution)/shard_map/while/body/eval_jaxpr/convert_element_type | solution.py:156
  1807.6 10.8 fusion.194
  1825.2 21.1 dynamic_update_slice.47
  1852.1 18.3 fusion.190
  1870.4 16.0 fusion.196
  1886.3 26.4 fusion.192
  1912.8 28.3 fusion.193
  1941.1 10.8 fusion.194
  1958.0 21.0 dynamic_update_slice.47
  1984.8 14.3 fusion.190
  1999.1 15.1 fusion.196
  2014.3 26.3 fusion.192
  2040.6 27.7 fusion.193
  2068.3 10.8 fusion.194
  2085.2 21.0 dynamic_update_slice.47
  2112.1 14.3 fusion.190
  2126.4 15.1 fusion.196
  2141.5 26.3 fusion.192
  2167.8 27.7 fusion.193
  2195.5 10.8 fusion.194
  2212.6 21.0 dynamic_update_slice.47
  2299.4 18.2 add_bitcast_fusion
  2317.6 24.6 convolution_bitcast_fusion.1
  2360.8 43.2 %reduce-scatter.20.cloned.1.call-done = bf16[256,512]{1,0:T(8,128)(2,1)} async-done(((bf16[2048,512]{1,0:T(8,128)(2,1)}), bf16[256,512]{1,0:T(8,128)(2,1)}) %reduce-scatter.20.cloned.1.call-update) | async-done | bytes 262160 | tf_op jit(solution)/shard_map/reduce_scatter | solution.py:309
  2405.8 281.0 %reduce-scatter.18.cloned.1.call-done = f32[1,512,2048]{2,1,0:T(8,128)} async-done(((f32[1,2048,2048]{2,1,0:T(8,128)}), f32[1,512,2048]{2,1,0:T(8,128)}) %reduce-scatter.18.cloned.1.call-update) | async-done | bytes 4194320 | tf_op jit(solution)/shard_map/reduce_scatter | solution.py:94
  2690.3 46.1 %all-reduce = (f32[2048]{0:T(1024)}, f32[2048]{0:T(1024)}) all-reduce(f32[2048]{0:T(1024)S(1)} %get-tuple-element.294, f32[2048]{0:T(1024)S(1)} %copy-done.38), channel_id=1, replica_groups=mesh['dp'=8,'tensor'=4] {'dp','tensor'}, use_global_device_ids=true, to_apply=%region_20.21 | all-reduce | flops 4096 | bytes 32768 | tf_op jit(solution)/shard_map/psum | solution.py:307
  2736.4 234.7 %reduce-scatter.14.cloned.1.call-done = f32[1,512,2048]{2,1,0:T(8,128)} async-done(((f32[1,2048,2048]{2,1,0:T(8,128)}), f32[1,512,2048]{2,1,0:T(8,128)}) %reduce-scatter.14.cloned.1.call-update) | async-done | bytes 4194320 | tf_op jit(solution)/shard_map/reduce_scatter | solution.py:94
  (252 shorter events, 209.0 us)
Async XLA Ops:
  7.2 35.5 %all-gather.12.cloned.1.call-start = ((), (), s32[]{:S(2)}) async-start(), calls=%async_computation.12 | async-start | bytes 2359296 | tf_op jit(solution)/shard_map/all_gather | solution.py:206
  7.9 6.5 copy-start.25
  7.9 6.7 copy-start.31
  7.9 19.4 copy-start.32
  7.9 186.9 %all-gather.10.cloned.1.call-start = ((), (), s32[]{:S(2)}) async-start(), calls=%async_computation.11 | async-start | bytes 10485760 | tf_op jit(solution)/shard_map/all_gather | solution.py:90
  10.1 4.6 copy-start.36
  13.6 402.6 %all-gather.14.cloned.1.call-start = ((), (), s32[]{:S(2)}) async-start(), calls=%async_computation.13 | async-start | bytes 2359296 | tf_op jit(solution)/shard_map/all_gather | solution.py:209
  14.3 693.3 %reduce-scatter.12.cloned.1.call-start = ((), (), s32[]{:S(2)}) async-start(), calls=%async_computation.14 | async-start | bytes 20971520 | tf_op jit(solution)/shard_map/reduce_scatter | solution.py:94
  27.4 10.7 copy-start.18
  38.1 170.1 %copy-start.16 = (bf16[2048,128]{1,0:T(8,128)(2,1)}, bf16[2048,128]{1,0:T(8,128)(2,1)S(1)}, u32[]{:S(2)}) copy-start(bf16[2048,128]{1,0:T(8,128)(2,1)S(1)} %all_gather.43) | copy-start | bytes 1572868
  40.1 165.9 %copy-start.12 = (f32[2048,32]{0,1:T(8,128)}, f32[2048,32]{0,1:T(8,128)S(1)}, u32[]{:S(2)}) copy-start(f32[2048,32]{0,1:T(8,128)S(1)} %get-tuple-element.355) | copy-start | bytes 786436
  40.1 165.9 %copy-start.14 = (f32[2048,32]{0,1:T(8,128)}, f32[2048,32]{0,1:T(8,128)S(1)}, u32[]{:S(2)}) copy-start(f32[2048,32]{0,1:T(8,128)S(1)} %get-tuple-element.356) | copy-start | bytes 786436
  194.9 6.6 copy-start.11
  410.5 5.6 copy-start.3
  410.6 5.6 copy-start.8
  428.7 278.9 %copy-start.5 = (bf16[1,512,2048]{2,1,0:T(8,128)(2,1)S(1)}, bf16[1,512,2048]{2,1,0:T(8,128)(2,1)}, u32[]{:S(2)}) copy-start(bf16[1,512,2048]{2,1,0:T(8,128)(2,1)} %param.16) | copy-start | bytes 6291460
  428.7 335.9 %all-gather.20.cloned.1.call-start = ((), (), s32[]{:S(2)}) async-start(), calls=%async_computation.17 | async-start | bytes 9437184 | tf_op jit(solution)/shard_map/all_gather | solution.py:241
  429.3 283.1 %copy-start.27 = (f32[2048]{0:T(1024)S(1)}, f32[2048]{0:T(1024)}, u32[]{:S(2)}) copy-start(f32[2048]{0:T(1024)} %param.23) | copy-start | bytes 24580
  429.3 487.0 %all-gather.16.cloned.1.call-start = ((), (), s32[]{:S(2)}) async-start(), calls=%async_computation.15 | async-start | bytes 10485760 | tf_op jit(solution)/shard_map/all_gather | solution.py:90
  714.2 256.9 %all-gather.18.cloned.1.call-start = ((), (), s32[]{:S(2)}) async-start(), calls=%async_computation.16 | async-start | bytes 9437184 | tf_op jit(solution)/shard_map/all_gather | solution.py:240
  714.9 407.5 %all-gather.24.cloned.1.call-start = ((), (), s32[]{:S(2)}) async-start(), calls=%async_computation.20 | async-start | bytes 10485760 | tf_op jit(solution)/shard_map/all_gather | solution.py:90
  715.7 461.4 %all-gather.22.cloned.1.call-start = ((), (), s32[]{:S(2)}) async-start(), calls=%async_computation.18 | async-start | bytes 9437184 | tf_op jit(solution)/shard_map/all_gather | solution.py:242
  716.4 827.0 %reduce-scatter.16.cloned.1.call-start = ((), (), s32[]{:S(2)}) async-start(), calls=%async_computation.21 | async-start | bytes 20971520 | tf_op jit(solution)/shard_map/reduce_scatter | solution.py:94
  1262.9 280.5 %copy-start.28 = (f32[2048]{0:T(1024)S(1)}, f32[2048]{0:T(1024)}, u32[]{:S(2)}) copy-start(f32[2048]{0:T(1024)} %param.23) | copy-start | bytes 24580
  1262.9 280.5 %copy-start.34 = (f32[512]{0:T(512)S(1)}, f32[512]{0:T(512)}, u32[]{:S(2)}) copy-start(f32[512]{0:T(512)} %copy-done.33) | copy-start | bytes 6148
  1262.9 286.3 %copy-start.10 = (bf16[1,512,2048]{2,1,0:T(8,128)(2,1)S(1)}, bf16[1,512,2048]{2,1,0:T(8,128)(2,1)}, u32[]{:S(2)}) copy-start(bf16[1,512,2048]{2,1,0:T(8,128)(2,1)} %param.27) | copy-start | bytes 6291460
  1262.9 439.8 %all-gather.26.cloned.1.call-start = ((), (), s32[]{:S(2)}) async-start(), calls=%async_computation.22 | async-start | bytes 10485760 | tf_op jit(solution)/shard_map/all_gather | solution.py:90
  1543.4 5.9 copy-start.2
  1543.4 5.9 copy-start.7
  1552.2 790.1 %reduce-scatter.32.cloned.1.call-start = ((), (), s32[]{:S(2)}) async-start(), calls=%async_computation.30 | async-start | bytes 9437184 | tf_op jit(solution)/shard_map/reduce_scatter | solution.py:327
  1576.0 768.8 %reduce-scatter.30.cloned.1.call-start = ((), (), s32[]{:S(2)}) async-start(), calls=%async_computation.29 | async-start | bytes 9437184 | tf_op jit(solution)/shard_map/reduce_scatter | solution.py:324
  1600.0 747.8 %reduce-scatter.28.cloned.1.call-start = ((), (), s32[]{:S(2)}) async-start(), calls=%async_computation.28 | async-start | bytes 9437184 | tf_op jit(solution)/shard_map/reduce_scatter | solution.py:321
  1623.9 88.7 %copy-start.4 = (bf16[1,2048,2,64]{1,3,2,0:T(8,128)(2,1)S(1)}, bf16[1,2048,2,64]{1,3,2,0:T(8,128)(2,1)}, u32[]{:S(2)}) copy-start(bf16[1,2048,2,64]{1,3,2,0:T(8,128)(2,1)} %copy-done.3) | copy-start | bytes 1572868
  1623.9 88.7 %copy-start.9 = (bf16[1,2048,2,64]{1,3,2,0:T(8,128)(2,1)S(1)}, bf16[1,2048,2,64]{1,3,2,0:T(8,128)(2,1)}, u32[]{:S(2)}) copy-start(bf16[1,2048,2,64]{1,3,2,0:T(8,128)(2,1)} %copy-done.8) | copy-start | bytes 1572868
  1623.9 88.7 %copy-start.26 = (s32[1,2048]{1,0:T(1,128)S(1)}, s32[1,2048]{1,0:T(1,128)}, u32[]{:S(2)}) copy-start(s32[1,2048]{1,0:T(1,128)} %param.17) | copy-start | bytes 24580
  1624.0 726.7 %reduce-scatter.22.cloned.1.call-start = ((), (), s32[]{:S(2)}) async-start(), calls=%async_computation.25 | async-start | bytes 589824 | tf_op jit(solution)/shard_map/reduce_scatter | solution.py:312
  1718.9 14.9 copy-start.20
  1750.0 26.5 copy-start.21
  1807.6 11.4 copy-start
  1852.1 18.3 copy-start.20
  1886.3 26.5 copy-start.21
  1941.1 10.8 copy-start
  1984.8 14.3 copy-start.20
  2014.3 26.3 copy-start.21
  2068.3 10.8 copy-start
  2112.0 14.3 copy-start.20
  2141.5 26.3 copy-start.21
  2195.5 10.8 copy-start
  2243.2 108.9 %reduce-scatter.24.cloned.1.call-start = ((), (), s32[]{:S(2)}) async-start(), calls=%async_computation.26 | async-start | bytes 589824 | tf_op jit(solution)/shard_map/reduce_scatter | solution.py:315
  2252.6 106.5 %reduce-scatter.26.cloned.1.call-start = ((), (), s32[]{:S(2)}) async-start(), calls=%async_computation.27 | async-start | bytes 2359296 | tf_op jit(solution)/shard_map/reduce_scatter | solution.py:318
  2262.6 141.4 %reduce-scatter.20.cloned.1.call-start = ((), (), s32[]{:S(2)}) async-start(), calls=%async_computation.24 | async-start | bytes 2359296 | tf_op jit(solution)/shard_map/reduce_scatter | solution.py:309
  2273.3 9.7 copy-start.19
  2282.9 404.0 %reduce-scatter.18.cloned.1.call-start = ((), (), s32[]{:S(2)}) async-start(), calls=%async_computation.23 | async-start | bytes 20971520 | tf_op jit(solution)/shard_map/reduce_scatter | solution.py:94
  2282.9 8.2 copy-start.22
  2282.9 8.2 copy-start.24
  2291.1 8.2 copy-start.17
  2317.5 653.5 %reduce-scatter.14.cloned.1.call-start = ((), (), s32[]{:S(2)}) async-start(), calls=%async_computation.19 | async-start | bytes 20971520 | tf_op jit(solution)/shard_map/reduce_scatter | solution.py:94
  2344.8 342.0 %copy-start.6 = (bf16[1,512,2048]{2,1,0:T(8,128)(2,1)S(1)}, bf16[1,512,2048]{2,1,0:T(8,128)(2,1)}, u32[]{:S(2)}) copy-start(bf16[1,512,2048]{2,1,0:T(8,128)(2,1)} %param.16) | copy-start | bytes 6291460
  2344.8 342.0 %copy-start.30 = (f32[2048]{0:T(1024)S(1)}, f32[2048]{0:T(1024)}, u32[]{:S(2)}) copy-start(f32[2048]{0:T(1024)} %param.18) | copy-start | bytes 24580
  2344.8 342.0 %copy-start.37 = (f32[512]{0:T(512)S(1)}, f32[512]{0:T(512)}, u32[]{:S(2)}) copy-start(f32[512]{0:T(512)} %copy-done.36) | copy-start | bytes 6148
  2350.6 339.7 %copy-start.38 = (f32[2048]{0:T(1024)S(1)}, f32[2048]{0:T(1024)}, u32[]{:S(2)}) copy-start(f32[2048]{0:T(1024)} %get-tuple-element.292) | copy-start | bytes 24580
  2350.6 620.5 %copy-start.29 = (f32[2048]{0:T(1024)S(1)}, f32[2048]{0:T(1024)}, u32[]{:S(2)}) copy-start(f32[2048]{0:T(1024)} %param.23) | copy-start | bytes 24580
  2350.6 620.5 %copy-start.35 = (f32[512]{0:T(512)S(1)}, f32[512]{0:T(512)}, u32[]{:S(2)}) copy-start(f32[512]{0:T(512)} %copy-done.33) | copy-start | bytes 6148
  2350.6 620.5 %copy-start.40 = (f32[512]{0:T(512)S(1)}, f32[512]{0:T(512)}, u32[]{:S(2)}) copy-start(f32[512]{0:T(512)} %copy-done.39) | copy-start | bytes 6148
  (6 other events, 11.3 us)
Sparse Core Ops, SparseCore 0:
  9.9 32.7 all-gather.11
  44.8 149.9 all-gather.9
  196.7 26.1 all-gather.13
  428.8 278.6 reduce-scatter.11
  709.5 55.1 all-gather.19
  766.7 149.6 all-gather.15
  918.4 52.6 all-gather.17
  972.7 149.6 all-gather.23
  1124.4 52.6 all-gather.21
  1263.1 280.2 reduce-scatter.15
  1552.3 150.3 all-gather.25
  1706.0 69.5 reduce-scatter.31
  1779.5 71.2 reduce-scatter.29
  1854.1 71.2 reduce-scatter.27
  2243.4 32.6 reduce-scatter.21
  2279.6 34.1 reduce-scatter.23
  2317.8 41.2 reduce-scatter.25
  2362.8 41.2 reduce-scatter.19
  2406.5 280.2 reduce-scatter.17
  2689.0 282.0 reduce-scatter.13
where the time goes:
time: 3000 us; the launch traced here: 2990 us
  waiting for transfers between devices  1770 us (59%)
  matrix products  749 us (25%)
  other arithmetic  242 us (8%)
  local copies, waits for them, and re-layouts  119 us (4%)
  blocking collectives  69.5 us (2%)
    reduce_scatter x4, waiting for transfers between devices, sum_rows(): lax.psum_scatter(partial_rows, 'tensor', scatter_dimension=1, tiled=True)  1070 us
    all_gather x4, waiting for transfers between devices, gather_rows(): return lax.all_gather(local_rows, 'tensor', axis=1, tiled=True)  507 us
    dot_general x7, matrix products, matmul_nt(): lax.dot_general(left, right, (((1,), (1,)), ((), ())), preferred_element_...  123 us
    dot_general x8, matrix products, block_inputs(): jnp.einsum('qkgd,skd->kgqs', query_block, key_seq, preferred_element_type...  120 us
    convert_element_type x4, other arithmetic, one_block(): grad_score = (prob_rows * (grad_weights - row_dot)).astype(jnp.bfloat16)  115 us
    dot_general x7, matrix products, matmul(): return jnp.dot(left, right, preferred_element_type=jnp.float32)  107 us
    dot_general x4, matrix products, one_block(): jnp.einsum('qkgd,skd->kgqs', grad_block, value_seq, preferred_element_typ...  105 us
    dot_general x7, matrix products, matmul_tn(): lax.dot_general(left, right, (((0,), (0,)), ((), ())), preferred_element_...  104 us
  transfers between devices with their start and end apart: 20, of which 14 were waited for; matrix products, arithmetic and copies ran while one was open for 33% of the time, Pallas kernels for 0%

commit v1 on v0

v1 whole, which is shorter than its diff:
```python
import functools
import math

import jax
import jax.numpy as jnp
from jax import lax
from jax.experimental import pallas as pl
from jax.experimental.pallas import tpu as pltpu
from jax.sharding import PartitionSpec as P

HEAD_DIM = 64
DOCS = 4
MOST_DOC = 1024
NORM_EPS = 1e-05
ROPE_THETA = 500000.0
GROUP = 8
LANES = 128
QTILE = 256
SCALE = HEAD_DIM ** (-0.5)
LOG2E = 1.4426950408889634
FAR = -1e30
NTILE = 512

F32 = jnp.float32
BF16 = jnp.bfloat16


def dot_nn(left, right):
    return lax.dot_general(left, right, (((1,), (0,)), ((), ())), preferred_element_type=F32)


def dot_nt(left, right):
    return lax.dot_general(left, right, (((1,), (1,)), ((), ())), preferred_element_type=F32)


def dot_tn(left, right):
    return lax.dot_general(left, right, (((0,), (0,)), ((), ())), preferred_element_type=F32)


def document_starts(segments):
    doc_ids = jnp.arange(DOCS, dtype=jnp.int32)
    counts = jnp.sum((segments[:, None] == doc_ids).astype(jnp.int32), axis=0)
    before = (doc_ids < segments[:, None]).astype(jnp.int32)
    return jnp.sum(before * counts[None, :], axis=-1)


def rope_tables(positions):
    half = HEAD_DIM // 2
    frequency = jnp.exp(
        jnp.arange(half, dtype=F32) * (-2.0 * math.log(ROPE_THETA) / HEAD_DIM)
    )
    angles = positions.astype(F32)[:, None] * frequency
    cosine, sine = jnp.cos(angles), jnp.sin(angles)
    wide_cos = jnp.concatenate([cosine] * 4, axis=1)
    wide_sin = jnp.concatenate([-sine, sine, -sine, sine], axis=1)
    return wide_cos, wide_sin


def swap_halves(values):
    lane = lax.broadcasted_iota(jnp.int32, values.shape, 1)
    ahead = pltpu.roll(values, LANES - 32, 1)
    behind = pltpu.roll(values, 32, 1)
    return jnp.where((lane % 64) < 32, ahead, behind)


def qkv_kernel(x_ref, wq_ref, wkv_ref, cos_ref, sin_ref, q_ref, kv_ref):
    x = x_ref[...]
    cosine, sine = cos_ref[...], sin_ref[...]
    for at in range(wq_ref.shape[1] // LANES):
        part = pl.ds(at * LANES, LANES)
        value = dot_nn(x, wq_ref[:, part])
        q_ref[:, part] = (value * cosine + swap_halves(value) * sine).astype(BF16)
    value = dot_nn(x, wkv_ref[...])
    key = value[:, :LANES]
    kv_ref[:, :LANES] = (key * cosine + swap_halves(key) * sine).astype(BF16)
    kv_ref[:, LANES:] = value[:, LANES:].astype(BF16)


def project_qkv(x, wq, wkv, cosine, sine):
    rows, width = x.shape
    blocks = wkv.shape[1] // (2 * LANES)
    qcols = wq.shape[1] // blocks
    return pl.pallas_call(
        qkv_kernel,
        grid=(blocks,),
        in_specs=[
            pl.BlockSpec((rows, width), lambda g: (0, 0)),
            pl.BlockSpec((width, qcols), lambda g: (0, g)),
            pl.BlockSpec((width, 2 * LANES), lambda g: (0, g)),
            pl.BlockSpec((rows, LANES), lambda g: (0, 0)),
            pl.BlockSpec((rows, LANES), lambda g: (0, 0)),
        ],
        out_specs=[
            pl.BlockSpec((rows, qcols), lambda g: (0, g)),
            pl.BlockSpec((rows, 2 * LANES), lambda g: (0, g)),
        ],
        out_shape=[
            jax.ShapeDtypeStruct((rows, wq.shape[1]), BF16),
            jax.ShapeDtypeStruct((rows, wkv.shape[1]), BF16),
        ],
        compiler_params=pltpu.CompilerParams(vmem_limit_bytes=40 << 20),
        cost_estimate=pl.CostEstimate(
            flops=2 * rows * width * (wq.shape[1] + wkv.shape[1]),
            bytes_accessed=2 * width * (wq.shape[1] + wkv.shape[1]),
            transcendentals=0,
        ),
    )(x, wq, wkv, cosine, sine)


def fill_bias(bias_ref, low_ref, reach):
    span = bias_ref.shape[1]
    for tile in range(bias_ref.shape[0]):
        row = lax.broadcasted_iota(jnp.int32, (span, QTILE), 0)
        col = lax.broadcasted_iota(jnp.int32, (span, QTILE), 1)
        low = low_ref[0:1, tile * QTILE : (tile + 1) * QTILE]
        allowed = (row <= reach + col) & (row + tile * QTILE >= low)
        bias_ref[tile] = jnp.where(allowed, 0.0, FAR)


def spread_pair(pair, half):
    wide = pair.astype(F32)
    turned = pltpu.roll(wide, 64, 1)
    lane = lax.broadcasted_iota(jnp.int32, wide.shape, 1)
    mine = (lane // 64) == half
    even = half == 0
    first = jnp.where(mine, jnp.where(even, wide, turned), 0.0)
    second = jnp.where(mine, jnp.where(even, turned, wide), 0.0)
    return jnp.concatenate([first, second], axis=0).astype(BF16)


def gather_pair(transposed, half):
    count = transposed.shape[1] // 2
    mine = jnp.where(half == 0, transposed[:64], transposed[64:])
    return jnp.concatenate([mine[:, :count], mine[:, count:]], axis=0).T


def attend_kernel(reach, q_ref, k_ref, v_ref, low_ref, att_ref, lse_ref, bias_ref):
    head, tile, pair = pl.program_id(0), pl.program_id(1), pl.program_id(2)
    half = head % 2

    @pl.when((head == 0) & (tile == 0) & (pair == 0))
    def _():
        fill_bias(bias_ref, low_ref, reach)

    keys = pl.ds(pl.multiple_of(tile * QTILE, QTILE), bias_ref.shape[1])
    queries = spread_pair(q_ref[...], half)
    bias = bias_ref[tile]
    score = dot_nt(k_ref[keys, :], queries)
    score = score + jnp.concatenate([bias, bias], axis=1)
    top = jnp.max(score, axis=0, keepdims=True) * (SCALE * LOG2E)
    weight = jnp.exp2(score * (SCALE * LOG2E) - top)
    total = jnp.sum(weight, axis=0, keepdims=True)
    result = dot_tn(v_ref[keys, :], weight.astype(BF16)) / total
    att_ref[...] = gather_pair(result, half).astype(BF16)
    lse_ref[0] = top + jnp.log2(total)


def attend(q, kv, low):
    rows, width = q.shape
    keys = kv.shape[0]
    reach = keys - rows
    tiles = rows // QTILE
    pairs = width // LANES
    heads = kv.shape[1] // LANES
    per_head = pairs // heads
    span = reach + QTILE
    return pl.pallas_call(
        functools.partial(attend_kernel, reach),
        grid=(heads, tiles, per_head),
        in_specs=[
            pl.BlockSpec((QTILE, LANES), lambda a, t, p: (t, a * per_head + p)),
            pl.BlockSpec((keys, LANES), lambda a, t, p: (0, 2 * (a // 2))),
            pl.BlockSpec((keys, LANES), lambda a, t, p: (0, 2 * (a // 2) + 1)),
            pl.BlockSpec((1, rows), lambda a, t, p: (0, 0)),
        ],
        out_specs=[
            pl.BlockSpec((QTILE, LANES), lambda a, t, p: (t, a * per_head + p)),
            pl.BlockSpec((1, 1, 2 * QTILE), lambda a, t, p: ((a * tiles + t) * per_head + p, 0, 0)),
        ],
        out_shape=[
            jax.ShapeDtypeStruct((rows, width), BF16),
            jax.ShapeDtypeStruct((pairs * tiles, 1, 2 * QTILE), F32),
        ],
        scratch_shapes=[pltpu.VMEM((tiles, span, QTILE), F32)],
        compiler_params=pltpu.CompilerParams(vmem_limit_bytes=48 << 20),
        cost_estimate=pl.CostEstimate(
            flops=16 * rows * span * LANES * pairs,
            bytes_accessed=4 * rows * width + 2 * keys * kv.shape[1],
            transcendentals=2 * rows * span * pairs,
        ),
    )(q, kv, kv, low)


def attend_back_kernel(
    reach, q_ref, do_ref, o_ref, k_ref, v_ref, lse_ref, low_ref, cos_ref, sin_ref,
    dq_ref, dkv_ref, bias_ref, dk_acc, dv_acc,
):
    block, half, tile, pair = (pl.program_id(at) for at in range(4))
    inner = (half * pl.num_programs(2) + tile) * pl.num_programs(3) + pair

    @pl.when((block == 0) & (inner == 0))
    def _():
        fill_bias(bias_ref, low_ref, reach)

    @pl.when(inner == 0)
    def _():
        dk_acc[...] = jnp.zeros_like(dk_acc)
        dv_acc[...] = jnp.zeros_like(dv_acc)

    keys = pl.ds(pl.multiple_of(tile * QTILE, QTILE), bias_ref.shape[1])
    queries = spread_pair(q_ref[...], half)
    grads = spread_pair(do_ref[...], half)
    product = (do_ref[...].astype(F32) * o_ref[...].astype(F32)).T
    row_dot = jnp.concatenate(
        [
            jnp.sum(product[:64], axis=0, keepdims=True),
            jnp.sum(product[64:], axis=0, keepdims=True),
        ],
        axis=1,
    )
    bias = bias_ref[tile]
    key, value = k_ref[keys, :], v_ref[keys, :]
    score = dot_nt(key, queries) + jnp.concatenate([bias, bias], axis=1)
    weight = jnp.exp2(score * (SCALE * LOG2E) - lse_ref[0])
    dv_acc[keys, :] += dot_nn(weight.astype(BF16), grads)
    dscore = (weight * (dot_nt(value, grads) - row_dot)).astype(BF16)
    dk_acc[keys, :] += dot_nn(dscore, queries)
    dq = gather_pair(dot_tn(key, dscore), half) * SCALE
    dq_ref[...] = (dq * cos_ref[...] - swap_halves(dq) * sin_ref[...]).astype(BF16)

    @pl.when(inner == pl.num_programs(1) * pl.num_programs(2) * pl.num_programs(3) - 1)
    def _():
        dkv_ref[:, :LANES] = (dk_acc[...] * SCALE).astype(BF16)
        dkv_ref[:, LANES:] = dv_acc[...].astype(BF16)


def attend_back(q, do, att, kv, lse, low, cosine, sine):
    rows, width = q.shape
    keys = kv.shape[0]
    reach = keys - rows
    tiles = rows // QTILE
    pairs = width // LANES
    heads = kv.shape[1] // LANES
    per_head = pairs // heads
    span = reach + QTILE

    def pair_at(g, h, t, p):
        return (t, (2 * g + h) * per_head + p)

    return pl.pallas_call(
        functools.partial(attend_back_kernel, reach),
        grid=(heads // 2, 2, tiles, per_head),
        in_specs=[
            pl.BlockSpec((QTILE, LANES), pair_at),
            pl.BlockSpec((QTILE, LANES), pair_at),
            pl.BlockSpec((QTILE, LANES), pair_at),
            pl.BlockSpec((keys, LANES), lambda g, h, t, p: (0, 2 * g)),
            pl.BlockSpec((keys, LANES), lambda g, h, t, p: (0, 2 * g + 1)),
            pl.BlockSpec(
                (1, 1, 2 * QTILE),
                lambda g, h, t, p: (((2 * g + h) * tiles + t) * per_head + p, 0, 0),
            ),
            pl.BlockSpec((1, rows), lambda g, h, t, p: (0, 0)),
            pl.BlockSpec((QTILE, LANES), lambda g, h, t, p: (t, 0)),
            pl.BlockSpec((QTILE, LANES), lambda g, h, t, p: (t, 0)),
        ],
        out_specs=[
            pl.BlockSpec((QTILE, LANES), pair_at),
            pl.BlockSpec((keys, 2 * LANES), lambda g, h, t, p: (0, g)),
        ],
        out_shape=[
            jax.ShapeDtypeStruct((rows, width), BF16),
            jax.ShapeDtypeStruct(kv.shape, BF16),
        ],
        scratch_shapes=[
            pltpu.VMEM((tiles, span, QTILE), F32),
            pltpu.VMEM((keys, LANES), F32),
            pltpu.VMEM((keys, LANES), F32),
        ],
        compiler_params=pltpu.CompilerParams(vmem_limit_bytes=56 << 20),
        cost_estimate=pl.CostEstimate(
            flops=40 * rows * span * LANES * pairs,
            bytes_accessed=8 * rows * width + 4 * keys * kv.shape[1],
            transcendentals=2 * rows * span * pairs,
        ),
    )(q, do, att, kv, kv, lse, low, cosine, sine)


def finish_dkv_kernel(own_ref, recv_ref, cos_ref, sin_ref, out_ref):
    total = own_ref[...].astype(F32) + recv_ref[...].astype(F32)
    key = total[:, :LANES]
    out_ref[:, :LANES] = (key * cos_ref[...] - swap_halves(key) * sin_ref[...]).astype(BF16)
    out_ref[:, LANES:] = total[:, LANES:].astype(BF16)


def finish_dkv(own, recv, cosine, sine):
    rows, width = own.shape
    spec = pl.BlockSpec((rows, 2 * LANES), lambda g: (0, g))
    table = pl.BlockSpec((rows, LANES), lambda g: (0, 0))
    return pl.pallas_call(
        finish_dkv_kernel,
        grid=(width // (2 * LANES),),
        in_specs=[spec, spec, table, table],
        out_specs=spec,
        out_shape=jax.ShapeDtypeStruct((rows, width), BF16),
    )(own, recv, cosine, sine)


MESH = pl.DeviceIdType.MESH


def neighbours(wide):
    dp = lax.axis_index("dp")
    core, col, row = dp % 2, (dp // 2) % 2, (dp // (2 * wide)) % 2
    sibling = dp + 1 - 2 * core
    beside = dp + 2 - 4 * col
    above = dp + 2 * wide - 4 * wide * row
    return (row, col, core), (sibling, beside, above)


def meet(peers):
    barrier = pltpu.get_barrier_semaphore()
    for peer in peers:
        pl.semaphore_signal(barrier, inc=1, device_id={"dp": peer}, device_id_type=MESH)
    pl.semaphore_wait(barrier, len(peers))


SIB, XN, YN = 0, 1, 2


def spread_kernel(wide, z_size, mlp_count, *refs):
    attn_count = (len(refs) - 3) // 2 - mlp_count
    count = mlp_count + attn_count
    ins, outs = refs[:count], refs[count : 2 * count]
    own_sem, send_sem, recv_sem = refs[2 * count :]
    (row, col, core), _ = neighbours(wide)
    dp, place = lax.axis_index("dp"), lax.axis_index("tensor")
    mine = 4 * row + 2 * col + core
    base = dp - (2 * wide * row + 2 * col + core)

    def peer(dy, dx, dc):
        y, x, c = (row + dy) % 2, (col + dx) % 2, (core + dc) % 2
        return base + 2 * wide * y + 2 * x + c, 4 * y + 2 * x + c

    flips = [(dy, dx, dc) for dy in range(2) for dx in range(2) for dc in range(2)][1:]
    barrier = pltpu.get_barrier_semaphore()
    for flip in flips:
        pl.semaphore_signal(
            barrier, inc=1, device_id={"dp": peer(*flip)[0]}, device_id_type=MESH
        )
    for step in range(1, z_size):
        pl.semaphore_signal(
            barrier, inc=1, device_id={"tensor": (place + step) % z_size}, device_id_type=MESH
        )
    pl.semaphore_wait(barrier, len(flips) + z_size - 1)

    copies, local = [], []
    slot = 0
    for at in range(mlp_count, count):
        src, dst = ins[at], outs[at]
        cols = src.shape[1]
        part = pl.ds(pl.multiple_of(place * cols, LANES), cols)
        for step in range(1, z_size):
            copies.append(
                pltpu.make_async_remote_copy(
                    src_ref=src, dst_ref=dst.at[:, part],
                    send_sem=send_sem.at[slot], recv_sem=recv_sem.at[slot],
                    device_id={"tensor": (place + step) % z_size}, device_id_type=MESH,
                )
            )
            slot += 1
        local.append(pltpu.make_async_copy(src, dst.at[:, part], own_sem.at[at]))
    for at in range(mlp_count):
        src, dst = ins[at], outs[at]
        rows, cols = src.shape[0], dst.shape[1]
        here = pl.ds(pl.multiple_of(mine * rows, rows), rows)
        for flip in flips:
            device, other = peer(*flip)
            copies.append(
                pltpu.make_async_remote_copy(
                    src_ref=src.at[:, pl.ds(pl.multiple_of(other * cols, LANES), cols)],
                    dst_ref=dst.at[here],
                    send_sem=send_sem.at[slot], recv_sem=recv_sem.at[slot],
                    device_id={"dp": device}, device_id_type=MESH,
                )
            )
            slot += 1
        own = src.at[:, pl.ds(pl.multiple_of(mine * cols, LANES), cols)]
        local.append(pltpu.make_async_copy(own, dst.at[here], own_sem.at[at]))
    for copy in copies:
        copy.start()
    for copy in local:
        copy.start()
    for copy in local:
        copy.wait()
    for copy in copies:
        copy.wait()


def spread_weights(mlp, attn, dp_size, z_size):
    count = len(mlp) + len(attn)
    slots = (z_size - 1) * len(attn) + (GROUP - 1) * len(mlp)
    spec = pl.BlockSpec(memory_space=pl.ANY)
    out = [jax.ShapeDtypeStruct((GROUP * w.shape[0], w.shape[1] // GROUP), BF16) for w in mlp]
    out += [jax.ShapeDtypeStruct((w.shape[0], z_size * w.shape[1]), BF16) for w in attn]
    return pl.pallas_call(
        functools.partial(spread_kernel, 2 * math.isqrt(dp_size // GROUP), z_size, len(mlp)),
        in_specs=[spec] * count,
        out_specs=[spec] * count,
        out_shape=out,
        scratch_shapes=[
            pltpu.SemaphoreType.DMA((count,)),
            pltpu.SemaphoreType.DMA((slots,)),
            pltpu.SemaphoreType.DMA((slots,)),
        ],
        compiler_params=pltpu.CompilerParams(collective_id=2, has_side_effects=True),
    )(*mlp, *attn)


class Ring:
    FLIP = {SIB: (0, 0, 1), XN: (0, 1, 0), YN: (1, 0, 0)}
    COPIES = 14

    def __init__(self, wide, ref, rows, send_sem, recv_sem):
        (self.row, self.col, self.core), self.peers = neighbours(wide)
        self.ref, self.rows, self.part = ref, rows, rows // 2
        self.send_sem, self.recv_sem = send_sem, recv_sem
        self.sends = {}
        for half in range(2):
            self.sends["own", XN, half] = (2 + half, 0, 0, 0, half)
            self.sends["own", YN, half] = (4 + half, 0, 0, 0, half)
            self.sends["own", SIB, half] = (0 + half, 0, 0, 0, half)
        for half in range(2):
            self.sends["x", SIB, half] = (6 + half, 0, 1, 0, half)
            self.sends["y", SIB, half] = (8 + half, 1, 0, 0, half)
            self.sends["d", SIB, half] = (10 + half, 1, 1, 0, half)
        self.sends["x", YN, 0] = (12, 0, 1, 0, 0)
        self.sends["y", XN, 1] = (13, 1, 0, 0, 1)

    def place(self, dy, dx, dc, half):
        p = 4 * ((self.row + dy) % 2) + 2 * ((self.col + dx) % 2) + (self.core + dc) % 2
        return pl.ds(pl.multiple_of(p * self.rows + half * self.part, self.part), self.part)

    def mine(self):
        p = 4 * self.row + 2 * self.col + self.core
        return pl.ds(pl.multiple_of(p * self.rows, self.rows), self.rows)

    def copy(self, slot, dy, dx, dc, half, peer):
        where = self.place(dy, dx, dc, half)
        return pltpu.make_async_remote_copy(
            src_ref=self.ref.at[where], dst_ref=self.ref.at[where],
            send_sem=self.send_sem.at[slot], recv_sem=self.recv_sem.at[slot],
            device_id={"dp": self.peers[peer]}, device_id_type=MESH,
        )

    def start(self, name, peer, half):
        self.copy(*self.sends[name, peer, half], peer).start()

    def arrived(self, name, peer, half):
        slot, dy, dx, dc, half = self.sends[name, peer, half]
        fy, fx, fc = self.FLIP[peer]
        self.copy(slot, (dy + fy) % 2, (dx + fx) % 2, (dc + fc) % 2, half, peer).wait_recv()

    def start_own(self):
        for half in range(2):
            for peer in (XN, YN, SIB):
                self.start("own", peer, half)

    def first_halves(self):
        self.arrived("own", XN, 0)
        self.start("x", YN, 0)
        self.start("x", SIB, 0)
        self.arrived("own", YN, 0)
        self.start("y", SIB, 0)

    def second_halves(self):
        self.arrived("own", YN, 1)
        self.start("y", XN, 1)
        self.start("y", SIB, 1)
        self.arrived("own", XN, 1)
        self.start("x", SIB, 1)

    def far_halves(self):
        self.arrived("x", YN, 0)
        self.start("d", SIB, 0)
        self.arrived("y", XN, 1)
        self.start("d", SIB, 1)

    def from_sibling(self, name, *halves):
        for half in halves:
            self.arrived(name, SIB, half)

    def sent(self):
        for (name, peer, half), entry in self.sends.items():
            self.copy(*entry, peer).wait_send()


def gather_kernel(wide, count, *refs):
    ins, outs = refs[:count], refs[count : 2 * count]
    own_sem, send_sem, recv_sem = refs[2 * count :]
    rings = [
        Ring(wide, outs[at], ins[at].shape[0], send_sem.at[at], recv_sem.at[at])
        for at in range(count)
    ]
    local = [
        pltpu.make_async_copy(ins[at], outs[at].at[rings[at].mine()], own_sem.at[at])
        for at in range(count)
    ]
    for copy in local:
        copy.start()
    meet(rings[0].peers)
    for copy, ring in zip(local, rings):
        copy.wait()
        ring.start_own()
    for ring in rings:
        ring.first_halves()
        ring.second_halves()
    for ring in rings:
        ring.far_halves()
        for name in ("own", "x", "y", "d"):
            ring.from_sibling(name, 0, 1)
    for ring in rings:
        ring.sent()


def gather_rows(arrays, dp_size):
    count = len(arrays)
    spec = pl.BlockSpec(memory_space=pl.ANY)
    return pl.pallas_call(
        functools.partial(gather_kernel, 2 * math.isqrt(dp_size // GROUP), count),
        in_specs=[spec] * count,
        out_specs=[spec] * count,
        out_shape=[jax.ShapeDtypeStruct((GROUP * a.shape[0], a.shape[1]), a.dtype) for a in arrays],
        scratch_shapes=[
            pltpu.SemaphoreType.DMA((count,)),
            pltpu.SemaphoreType.DMA((count, Ring.COPIES)),
            pltpu.SemaphoreType.DMA((count, Ring.COPIES)),
        ],
        compiler_params=pltpu.CompilerParams(collective_id=3, has_side_effects=True),
    )(*arrays)


def gate_up_kernel(
    wide, own_ref, wg_ref, wu_ref, all_ref, gate_ref, up_ref, hid_ref,
    full, stage, own_sem, send_sem, recv_sem, out_sem, all_sem,
):
    rows = own_ref.shape[0]
    cols = gate_ref.shape[1]
    ring = Ring(wide, full, rows, send_sem, recv_sem)
    local = pltpu.make_async_copy(own_ref, full.at[ring.mine()], own_sem)
    local.start()
    meet(ring.peers)
    local.wait()
    ring.start_own()

    def out_copies(slot, where):
        return [
            pltpu.make_async_copy(stage.at[slot, i], ref.at[where], out_sem.at[slot, i])
            for i, ref in enumerate((gate_ref, up_ref, hid_ref))
        ] + [pltpu.make_async_copy(full.at[where], all_ref.at[where], all_sem.at[slot])]

    def step_place(step):
        phase, i = step // 4, step % 4
        high, low = phase // 2, phase % 2
        first, last = (1 - high) * (1 - low), high * low
        middle = high + low - 2 * last
        half = (first + last) * (i % 2) + high * (1 - low)
        dx = middle * (1 - i % 2) + last
        dy = middle * (i % 2) + last
        return ring.place(dy, dx, i // 2, half)

    @pl.loop(0, 16)
    def _(step):
        pl.when(step == 2)(lambda: ring.from_sibling("own", 0, 1))
        pl.when(step == 4)(ring.first_halves)

        @pl.when(step == 6)
        def _():
            ring.from_sibling("x", 0)
            ring.from_sibling("y", 0)

        pl.when(step == 8)(ring.second_halves)

        @pl.when(step == 10)
        def _():
            ring.from_sibling("x", 1)
            ring.from_sibling("y", 1)

        pl.when(step == 12)(ring.far_halves)
        pl.when(step == 14)(lambda: ring.from_sibling("d", 0, 1))

        slot = step % 2
        where = step_place(step)

        @pl.when(step >= 2)
        def _():
            for copy in out_copies(slot, step_place(step - 2)):
                copy.wait()

        x = full[where, :]

        @pl.loop(0, cols // NTILE)
        def _(at):
            n = pl.ds(pl.multiple_of(at * NTILE, NTILE), NTILE)
            gate = dot_nn(x, wg_ref[:, n])
            up = dot_nn(x, wu_ref[:, n])
            stage[slot, 0, :, n] = gate.astype(BF16)
            stage[slot, 1, :, n] = up.astype(BF16)
            stage[slot, 2, :, n] = (gate * up / (1.0 + jnp.exp(-gate))).astype(BF16)

        for copy in out_copies(slot, where):
            copy.start()

    for step in (14, 15):
        for copy in out_copies(step % 2, step_place(step)):
            copy.wait()
    ring.sent()


def gate_up(hn, wg, wu, dp_size):
    rows, width = hn.shape
    cols = wg.shape[1]
    tokens = GROUP * rows
    far = pl.BlockSpec(memory_space=pl.ANY)
    near = pl.BlockSpec(memory_space=pltpu.VMEM)
    return pl.pallas_call(
        functools.partial(gate_up_kernel, 2 * math.isqrt(dp_size // GROUP)),
        in_specs=[far, near, near],
        out_specs=[far] * 4,
        out_shape=[jax.ShapeDtypeStruct((tokens, width), BF16)]
        + [jax.ShapeDtypeStruct((tokens, cols), BF16)] * 3,
        scratch_shapes=[
            pltpu.VMEM((tokens, width), BF16),
            pltpu.VMEM((2, 3, rows // 2, cols), BF16),
            pltpu.SemaphoreType.DMA,
            pltpu.SemaphoreType.DMA((Ring.COPIES,)),
            pltpu.SemaphoreType.DMA((Ring.COPIES,)),
            pltpu.SemaphoreType.DMA((2, 3)),
            pltpu.SemaphoreType.DMA((2,)),
        ],
        compiler_params=pltpu.CompilerParams(
            collective_id=1, has_side_effects=True, vmem_limit_bytes=56 << 20
        ),
        cost_estimate=pl.CostEstimate(
            flops=4 * tokens * width * cols,
            bytes_accessed=tokens * (2 * width + 6 * cols) + 4 * width * cols,
            transcendentals=tokens * cols,
        ),
    )(hn, wg, wu)


class Layout:
    def __init__(self, dp_size):
        self.blocks = dp_size // GROUP
        side = math.isqrt(self.blocks)
        self.rows, self.cols = side, self.blocks // side
        wide = 2 * self.cols

        def index(by, bx, y, x, core):
            return ((2 * by + y) * wide + 2 * bx + x) * 2 + core

        places = [(y, x, c) for y in range(2) for x in range(2) for c in range(2)]
        spots = [(by, bx) for by in range(self.rows) for bx in range(self.cols)]
        self.inner = [[index(*s, *p) for p in places] for s in spots]
        self.outer = [[index(*s, *p) for s in spots] for p in places]

    def groups(self):
        return None if self.blocks == 1 else self.inner

    def to_rows(self, array):
        if self.blocks == 1:
            return array
        rest = array.shape[1:]
        split = array.reshape(2, 2, 2, self.rows, self.cols, -1, *rest)
        order = (3, 0, 4, 1, 2, 5) + tuple(range(6, 6 + len(rest)))
        return split.transpose(order).reshape(array.shape)

    def from_rows(self, array):
        if self.blocks == 1:
            return array
        rest = array.shape[1:]
        split = array.reshape(self.rows, 2, self.cols, 2, 2, -1, *rest)
        order = (1, 3, 4, 0, 2, 5) + tuple(range(6, 6 + len(rest)))
        return split.transpose(order).reshape(array.shape)

    def gather_outer(self, array):
        if self.blocks == 1:
            return array
        return lax.all_gather(array, "dp", axis_index_groups=self.outer, axis=0, tiled=True)

    def scatter_outer(self, array):
        if self.blocks == 1:
            return array
        return lax.psum_scatter(
            array, "dp", scatter_dimension=0, axis_index_groups=self.outer, tiled=True
        )

    def gather(self, array):
        return lax.all_gather(array, "dp", axis_index_groups=self.groups(), axis=0, tiled=True)

    def scatter(self, array):
        return lax.psum_scatter(
            array, "dp", scatter_dimension=0, axis_index_groups=self.groups(), tiled=True
        )

    def spread(self, array):
        return lax.all_to_all(
            array, "dp", 1, 0, axis_index_groups=self.groups(), tiled=True
        )

    def unspread(self, array):
        return lax.all_to_all(
            array, "dp", 0, 1, axis_index_groups=self.groups(), tiled=True
        )


def rms_scale(values):
    return lax.rsqrt(jnp.mean(values * values, axis=-1, keepdims=True) + NORM_EPS)


def norm_back(values, scaling, gain, grad):
    gained = grad * gain
    gain_part = jnp.sum(grad * values * scaling, axis=0)
    inner = jnp.mean(gained * values, axis=-1, keepdims=True)
    return gain_part, scaling * gained - values * scaling * scaling * scaling * inner


def gather_all(array):
    return lax.all_gather(
        lax.all_gather(array, "tensor", axis=1, tiled=True), "dp", axis=0, tiled=True
    )


def scatter_all(array):
    part = lax.psum_scatter(array.astype(BF16), "dp", scatter_dimension=0, tiled=True)
    return lax.psum_scatter(part, "tensor", scatter_dimension=1, tiled=True).astype(F32)


def per_device(
    dp_size, z_size, activations, segment_ids, attn_gain, w_query, w_key, w_value, w_out,
    mlp_gain, w_gate, w_up, w_down, cotangent,
):
    layout = Layout(dp_size)
    rows, width = activations.shape[1:]
    x = activations[0].astype(F32)
    place = lax.axis_index("tensor")
    reach = -(-(MOST_DOC - 1) // rows) * rows

    def shift(array, step):
        pairs = [(at, at + step) for at in range(z_size) if 0 <= at + step < z_size]
        return lax.ppermute(array, "tensor", pairs)

    starts = document_starts(segment_ids[0])
    own_starts = lax.dynamic_slice_in_dim(starts, place * rows, rows)
    own_tokens = place * rows + jnp.arange(rows, dtype=jnp.int32)
    cosine, sine = rope_tables(own_tokens - own_starts)
    low = (own_starts - place * rows + reach)[None, :]

    shards = [
        layout.gather_outer(w)
        for w in (w_gate, w_up, w_down, jnp.concatenate([w_key, w_value], axis=1), w_query, w_out)
    ]
    spread = spread_weights(shards[:3], shards[3:], dp_size, z_size)
    wg, wu, wd = (
        layout.to_rows(lax.all_gather(w, "tensor", axis=1, tiled=True)) for w in spread[:3]
    )
    wkv, wq, wo = (layout.to_rows(w) for w in gather_rows(spread[3:], dp_size))

    r1 = rms_scale(x)
    xn = (x * r1 * attn_gain).astype(BF16)
    q, kv = project_qkv(xn, wq, wkv, cosine, sine)
    pieces, moved = [kv], kv
    for _ in range(reach // rows):
        moved = shift(moved, 1)
        pieces.insert(0, moved)
    kv_all = jnp.concatenate(pieces, axis=0)
    att, lse = attend(q, kv_all, low)
    h = x + dot_nt(att, wo)

    r2 = rms_scale(h)
    hn, gate, up, hidden = gate_up((h * r2 * mlp_gain).astype(BF16), wg, wu, dp_size)
    grad, wd = lax.optimization_barrier((cotangent[0], wd))
    dy = layout.gather(grad)
    gate, up = gate.astype(F32), up.astype(F32)
    sigma = jax.nn.sigmoid(gate)
    output = h + layout.scatter(dot_nt(hidden, wd).astype(BF16)).astype(F32)
    dhid = dot_nn(dy, wd)
    dgate = (dhid * up * sigma * (1.0 + gate * (1.0 - sigma))).astype(BF16)
    dup = (dhid * gate * sigma).astype(BF16)
    dhn = layout.scatter((dot_nt(dgate, wg) + dot_nt(dup, wu)).astype(BF16)).astype(F32)

    def mlp_grad(left, right):
        total = layout.from_rows(dot_tn(left, right).astype(BF16))
        part = lax.psum_scatter(total, "tensor", scatter_dimension=1, tiled=True)
        return layout.scatter_outer(layout.unspread(part)).astype(F32)

    wd_grad = mlp_grad(dy, hidden)
    wg_grad = mlp_grad(hn, dgate)
    wu_grad = mlp_grad(hn, dup)
    gain_two, dh_norm = norm_back(h, r2, mlp_gain, dhn)
    dh = cotangent[0].astype(F32) + dh_norm

    dhb = dh.astype(BF16)
    wo_grad = scatter_all(dot_tn(dhb, att))
    datt = dot_nn(dhb, wo).astype(BF16)
    dq, dkv_all = attend_back(q, datt, att, kv_all, lse, low, cosine, sine)
    count = reach // rows
    moved = dkv_all[:rows]
    for at in range(1, count + 1):
        moved = shift(moved, -1)
        if at < count:
            here = dkv_all[at * rows : (at + 1) * rows]
            moved = (moved.astype(F32) + here.astype(F32)).astype(BF16)
    dkv = finish_dkv(dkv_all[count * rows :], moved, cosine, sine)
    wq_grad = scatter_all(dot_tn(xn, dq))
    wkv_grad = scatter_all(dot_tn(xn, dkv))
    key_cols = w_key.shape[1]
    dxn = dot_nt(dq, wq) + dot_nt(dkv, wkv)
    gain_one, dx_norm = norm_back(x, r1, attn_gain, dxn)
    input_grad = (dh + dx_norm).astype(BF16)
    gain_one, gain_two = lax.psum((gain_one, gain_two), ("dp", "tensor"))
    return (
        output.astype(BF16)[None],
        input_grad[None],
        gain_one,
        wq_grad,
        wkv_grad[:, :key_cols],
        wkv_grad[:, key_cols:],
        wo_grad,
        gain_two,
        wg_grad,
        wu_grad,
        wd_grad,
    )


def solution(mesh):
    split = P("dp", "tensor")
    tokens = P("dp", "tensor", None)
    in_specs = (
        tokens, P("dp", None), P(), split, split, split, split, P(), split, split, split, tokens,
    )
    out_specs = (tokens, tokens, P(), split, split, split, split, P(), split, split, split)
    return jax.shard_map(
        functools.partial(per_device, mesh.shape["dp"], mesh.shape["tensor"]),
        mesh=mesh, in_specs=in_specs, out_specs=out_specs, check_vma=False,
    )
```

time: 3000 us -> 1450 us (0.48)
  waiting for transfers between devices: 1770 us -> 649 us
  matrix products: 749 us -> 242 us
  Pallas kernels: 0 us -> 428 us
  other arithmetic: 242 us -> 28.5 us
  local copies, waits for them, and re-layouts: 119 us -> 15.5 us
    reduce_scatter x11, waiting for transfers between devices: 1120 us -> 456 us  [the longest x2 182 us: scatter(): lax.psum_scatter(array, 'dp', scatter_dimension=0, axis_index_groups=self...]
    all_gather x9 -> x4, waiting for transfers between devices: 643 us -> 82.8 us  [the longest x3 82.7 us: per_device(): lax.all_gather(w, 'tensor', axis=1, tiled=True)]
    dot_general x49 -> x14, matrix products: 749 us -> 242 us  [the longest x6 100 us: dot_nt(): lax.dot_general(left, right, (((1,), (1,)), ((), ())), preferred_element_...]
    pallas_call x0 -> x7, Pallas kernels: none -> 428 us  [the longest x1 137 us: gather_rows(): pl.pallas_call(functools.partial(gather_kernel, 2 * math.isqrt(dp_size //...]
    convert_element_type x17 -> x5, other arithmetic: 145 us -> 7.5 us  [the longest x2 3.61 us: scatter_all(): lax.psum_scatter(part, 'tensor', scatter_dimension=1, tiled=True)]
    ppermute x0 -> x4, waiting for transfers between devices: none -> 95.6 us  [shift(): return lax.ppermute(array, 'tensor', pairs)]
    dynamic_update_slice x8 -> x0, local copies, waits for them, and re-layouts: 88.5 us -> none  [attend_back(): lax.map(one_block, jnp.arange(seq_count * blocks, dtype=jnp.int32))]
    reduce_sum x12 -> x4, other arithmetic: 79.1 us -> 5.47 us  [the longest x1 4.76 us: norm_back(): gain_part = jnp.sum(grad * values * scaling, axis=0)]
  transfers between devices with their start and end apart: 20 -> 22, of which waited for: 14 -> 13; matrix products, arithmetic and copies ran while one was open for 33% -> 13% of each run, Pallas kernels for 0% -> 26%
where the time goes in v1:
time: 1450 us; the launch traced here: 1440 us
  waiting for transfers between devices  649 us (45%)
  Pallas kernels  428 us (30%)
  matrix products  242 us (17%)
  blocking collectives  40.9 us (3%)
  other arithmetic  28.5 us (2%)
  starting transfers between devices  21 us (1%)
  local copies, waits for them, and re-layouts  15.5 us (1%)
  between operations  14.9 us (1%)
    reduce_scatter x2, waiting for transfers between devices, scatter(): lax.psum_scatter(array, 'dp', scatter_dimension=0, axis_index_groups=self...  182 us
    pallas_call x1, Pallas kernels, gather_rows(): pl.pallas_call(functools.partial(gather_kernel, 2 * math.isqrt(dp_size //...  137 us
    reduce_scatter x3, waiting for transfers between devices, mlp_grad(): part = lax.psum_scatter(total, 'tensor', scatter_dimension=1, tiled=True)  137 us
    reduce_scatter x3, waiting for transfers between devices, scatter_all(): lax.psum_scatter(array.astype(BF16), 'dp', scatter_dimension=0, tiled=True)  120 us
    dot_general x6, matrix products, dot_nt(): lax.dot_general(left, right, (((1,), (1,)), ((), ())), preferred_element_...  100 us
    dot_general x6, matrix products, dot_tn(): lax.dot_general(left, right, (((0,), (0,)), ((), ())), preferred_element_...  97.6 us
    ppermute x4, waiting for transfers between devices, shift(): return lax.ppermute(array, 'tensor', pairs)  95.6 us
    pallas_call x1, Pallas kernels, gate_up(): pl.pallas_call(functools.partial(gate_up_kernel, 2 * math.isqrt(dp_size /...  86 us
  transfers between devices with their start and end apart: 22, of which 13 were waited for; matrix products, arithmetic and copies ran while one was open for 13% of the time, Pallas kernels for 26%

profile of v1, /device:TPU:0, one launch (start us, length us, event | category | flops | bytes accessed | tf_op | source)
XLA Modules:
  0.0 1438.6 jit_solution(9985093438192549650)
XLA Ops:
  7.2 1.5 pad_maximum_fusion.2.refs_3_
  8.8 59.6 %shard_map.203 = (bf16[2048,256]{1,0:T(8,128)(2,1)}, bf16[2048,256]{1,0:T(8,128)(2,1)}, bf16[2048,256]{1,0:T(8,128)(2,1)}, bf16[256,1024]{1,0:T(8,128)(2,1)}, bf...) custom-call(bf16[256,2048]{1,0:T(8,128)(2,1)} %refs_0_.1, bf16[256,2048]{1,0:T(8,128)(2,1)} %refs_1_.1, ...), custom_call_target="tpu_custom_call" | custom-call | tf_op jit(solution)/shard_map/pallas_call | solution.py:406
  68.5 0.7 all-gather.5.cloned.1.call-update
  69.2 0.7 all-gather.7.cloned.1.call-update
  70.0 82.7 %all-gather.9.cloned.1.call-done = bf16[2048,1024]{1,0:T(8,128)(2,1)} async-done(((bf16[2048,256]{1,0:T(8,128)(2,1)}), bf16[2048,1024]{1,0:T(8,128)(2,1)}) %all-gather.9.cloned.1.call-update) | async-done | bytes 4194320 | tf_op jit(solution)/shard_map/all_gather | solution.py:765
  152.8 137.2 %shard_map.204 = (bf16[2048,1024]{1,0:T(8,128)(2,1)}, bf16[2048,2048]{1,0:T(8,128)(2,1)}, bf16[2048,2048]{1,0:T(8,128)(2,1)}) custom-call(bf16[256,1024]{1,0:T(8,128)(2,1)} %get-tuple-element.32.refs_0_, bf16[256,2048]{1,0:T(8,128)(2,1)} %get-tuple-element.33.refs_1_, bf16[256,2048]{1,0:T(8,128)(2,1)} %get-tuple-element.34.refs_2_), custom_call_target="tpu_custom_call" | custom-call | tf_op jit(solution)/shard_map/pallas_call | solution.py:529
  290.4 1.0 fusion.31
  292.4 0.5 fusion.12.x_ref
  293.0 15.2 %shard_map.205 = (bf16[512,2048]{1,0:T(8,128)(2,1)S(1)}, bf16[512,1024]{1,0:T(8,128)(2,1)S(1)}) custom-call(bf16[512,2048]{1,0:T(8,128)(2,1)S(1)} %fusion.12.x_ref, bf16[2048,2048]{1,0:T(8,128)(2,1)} %get-tuple-element.35.wq_ref, bf16[2048,1024]{1,0:T(8,128)(2,1)S(1)} %copy-done.5, f32[512,128]{1,0:T(8,128)S(1)} %get-tuple-element.75.cos_ref, ...), custom_call_target="tpu_custom_call" | custom-call | flops 6442450944 | bytes 12582912 | tf_op jit(solution)/shard_map/pallas_call | solution.py:83
  308.2 1.4 collective-permute-start
  309.6 23.2 %collective-permute-done = bf16[512,1024]{1,0:T(8,128)(2,1)S(1)} collective-permute-done((bf16[512,1024]{1,0:T(8,128)(2,1)S(1)}, bf16[512,1024]{1,0:T(8,128)(2,1)S(1)}, u32[]{:S(2)}, u32[]{:S(2)}) %collective-permute-start) | collective-permute-done | bytes 1048608 | tf_op jit(solution)/shard_map/ppermute | solution.py:751
  332.8 5.0 collective-permute-start.1
  337.8 22.0 %collective-permute-done.1 = bf16[512,1024]{1,0:T(8,128)(2,1)S(1)} collective-permute-done((bf16[512,1024]{1,0:T(8,128)(2,1)S(1)}, bf16[512,1024]{1,0:T(8,128)(2,1)S(1)}, u32[]{:S(2)}, u32[]{:S(2)}) %collective-permute-start.1) | collective-permute-done | bytes 1048608 | tf_op jit(solution)/shard_map/ppermute | solution.py:751
  360.0 1.6 copy-done.17
  361.6 51.7 %shard_map.206 = (bf16[512,2048]{1,0:T(8,128)(2,1)S(1)}, f32[32,1,512]{2,1,0:T(1,128)S(1)}) custom-call(bf16[512,2048]{1,0:T(8,128)(2,1)S(1)} %get-tuple-element.37.q_ref, bf16[1536,1024]{1,0:T(8,128)(2,1)} %copy-done.17, bf16[1536,1024]{1,0:T(8,128)(2,1)} %copy-done.17, s32[1,512]{1,0:T(1,128)S(1)} %bitcast.57), custom_call_target="tpu_custom_call" | custom-call | flops 21474836480 | bytes 7340032 | tf_op jit(solution)/shard_map/pallas_call | solution.py:167
  413.4 7.9 multiply_reduce_fusion
  421.4 1.9 copy-done.10
  423.3 1.7 multiply_convert_fusion.own_ref
  425.0 86.0 %shard_map.207 = (bf16[4096,2048]{1,0:T(8,128)(2,1)}, bf16[4096,1024]{1,0:T(8,128)(2,1)}, bf16[4096,1024]{1,0:T(8,128)(2,1)}, bf16[4096,1024]{1,0:T(8,128)(2,1)}) custom-call(bf16[512,2048]{1,0:T(8,128)(2,1)} %multiply_convert_fusion.own_ref, bf16[2048,1024]{1,0:T(8,128)(2,1)} %all-gather.5.cloned.1.call-done.wg_ref, ...), custom_call_target="tpu_custom_call" | custom-call | flops 34359738368 | bytes 50331648 | tf_op jit(solution)/shard_map/pallas_call | solution.py:626
  511.1 32.4 %fusion.7 = (bf16[4096,1024]{1,0:T(8,128)(2,1)}, bf16[4096,1024]{1,0:T(8,128)(2,1)}) fusion(bf16[4096,1024]{1,0:T(8,128)(2,1)} %get-tuple-element.48, bf16[4096,1024]{1,0:T(8,128)(2,1)} %get-tuple-element.47, bf16[4096,2048]{1,0:T(8,128)(2,1)} %all-gather.11.cloned.1.call-done, bf16[2048,1024]{1,0:T(8,128)(2,1)} %all-gather.9.cloned.1.call-done), kind=kOutput, calls=%fused_computation.11 | convolution fusion | flops 17242783744 | bytes 54525952 | tf_op jit(solution)/shard_map/dot_general | solution.py:29
  543.5 24.7 %fusion.34 = f32[4096,2048]{1,0:T(8,128)} fusion(bf16[4096,1024]{1,0:T(8,128)(2,1)} %get-tuple-element.60, bf16[2048,1024]{1,0:T(8,128)(2,1)S(1)} %copy-done.28), kind=kOutput, calls=%fused_computation.80 | convolution fusion | flops 17179869184 | bytes 46137344 | tf_op jit(solution)/shard_map/dot_general | solution.py:33
  568.2 26.6 %add_convert_fusion = bf16[4096,2048]{1,0:T(8,128)(2,1)} fusion(f32[4096,2048]{1,0:T(8,128)} %fusion.34, bf16[4096,1024]{1,0:T(8,128)(2,1)} %get-tuple-element.59, bf16[2048,1024]{1,0:T(8,128)(2,1)S(1)} %copy-done.29), kind=kOutput, calls=%fused_computation | convolution fusion | flops 17196646400 | bytes 62914560 | tf_op jit(solution)/shard_map/dot_general | solution.py:33
  594.9 24.6 %convolution_convert_fusion = bf16[4096,2048]{1,0:T(8,128)(2,1)} fusion(bf16[4096,1024]{1,0:T(8,128)(2,1)} %get-tuple-element.43, bf16[2048,1024]{1,0:T(8,128)(2,1)} %all-gather.9.cloned.1.call-done), kind=kOutput, calls=%fused_computation.12 | convolution fusion | flops 17188257792 | bytes 29360128 | tf_op jit(solution)/shard_map/dot_general | solution.py:33
  619.5 24.8 %convolution_convert_fusion.3 = bf16[2048,1024]{1,0:T(8,128)(2,1)} fusion(bf16[4096,2048]{1,0:T(8,128)(2,1)} %all-gather.11.cloned.1.call-done, bf16[4096,1024]{1,0:T(8,128)(2,1)} %get-tuple-element.43), kind=kOutput, calls=%fused_computation.44 | convolution fusion | flops 17181966336 | bytes 29360128 | tf_op jit(solution)/shard_map/dot_general | solution.py:37
  644.4 67.2 %reduce-scatter.14.cloned.1.call-done = bf16[512,2048]{1,0:T(8,128)(2,1)} async-done(((bf16[4096,2048]{1,0:T(8,128)(2,1)}), bf16[512,2048]{1,0:T(8,128)(2,1)}) %reduce-scatter.14.cloned.1.call-update) | async-done | bytes 2097168 | tf_op jit(solution)/shard_map/reduce_scatter | solution.py:702
  711.7 4.8 fusion.22
  716.4 114.7 %reduce-scatter.12.cloned.1.call-done = bf16[512,2048]{1,0:T(8,128)(2,1)} async-done(((bf16[4096,2048]{1,0:T(8,128)(2,1)}), bf16[512,2048]{1,0:T(8,128)(2,1)}) %reduce-scatter.12.cloned.1.call-update) | async-done | bytes 2097168 | tf_op jit(solution)/shard_map/reduce_scatter | solution.py:702
  831.1 5.6 fusion.19
  836.7 11.2 convolution_convert_fusion.7.do_ref
  847.9 73.9 %shard_map.208 = (bf16[512,2048]{1,0:T(8,128)(2,1)}, bf16[1536,1024]{1,0:T(8,128)(2,1)}) custom-call(bf16[512,2048]{1,0:T(8,128)(2,1)} %copy-done.7, bf16[512,2048]{1,0:T(8,128)(2,1)} %convolution_convert_fusion.7.do_ref, bf16[512,2048]{1,0:T(8,128)(2,1)} %copy-done.8, bf16[1536,1024]{1,0:T(8,128)(2,1)} %copy-done.17, bf16[1536,1024]{1,0:T(8,128)(2,1)} %copy-done.17, ...), custom_call_target="tpu_custom_call" | custom-call | flops 53687091200 | bytes 14680064 | tf_op jit(solution)/shard_map/pallas_call | solution.py:250
  921.8 2.7 fusion.32
  924.5 1.4 collective-permute-start.2
  925.9 25.6 %collective-permute-done.2 = bf16[512,1024]{1,0:T(8,128)(2,1)S(1)} collective-permute-done((bf16[512,1024]{1,0:T(8,128)(2,1)S(1)}, bf16[512,1024]{1,0:T(8,128)(2,1)S(1)}, u32[]{:S(2)}, u32[]{:S(2)}) %collective-permute-start.2) | collective-permute-done | bytes 1048608 | tf_op jit(solution)/shard_map/ppermute | solution.py:751
  951.5 1.6 add_convert_fusion.2
  953.2 1.3 collective-permute-start.3
  954.5 24.8 %collective-permute-done.3.recv_ref = bf16[512,1024]{1,0:T(8,128)(2,1)S(1)} collective-permute-done((bf16[512,1024]{1,0:T(8,128)(2,1)S(1)}, bf16[512,1024]{1,0:T(8,128)(2,1)S(1)}, u32[]{:S(2)}, u32[]{:S(2)}) %collective-permute-start.3) | collective-permute-done | bytes 1048608 | tf_op jit(solution)/shard_map/ppermute | solution.py:751
  979.2 1.0 copy-done.16
  980.2 4.1 shard_map.209
  984.4 5.6 convolution_convert_fusion.6
  990.1 24.0 %convolution_convert_fusion.5 = bf16[2048,1024]{1,0:T(8,128)(2,1)} fusion(bf16[4096,2048]{1,0:T(8,128)(2,1)} %get-tuple-element.52, bf16[4096,1024]{1,0:T(8,128)(2,1)} %get-tuple-element.60), kind=kOutput, calls=%fused_computation.46 | convolution fusion | flops 17181966336 | bytes 29360128 | tf_op jit(solution)/shard_map/dot_general | solution.py:37
  1014.4 10.8 convolution_convert_fusion.1
  1025.2 23.8 %convolution_convert_fusion.4 = bf16[2048,1024]{1,0:T(8,128)(2,1)} fusion(bf16[4096,2048]{1,0:T(8,128)(2,1)} %get-tuple-element.52, bf16[4096,1024]{1,0:T(8,128)(2,1)} %get-tuple-element.59), kind=kOutput, calls=%fused_computation.45 | convolution fusion | flops 17181966336 | bytes 29360128 | tf_op jit(solution)/shard_map/dot_general | solution.py:37
  1049.1 8.5 convolution_convert_fusion.2
  1057.7 3.6 all-to-all-start.2
  1061.3 0.7 reduce-scatter.22.cloned.1.call-update
  1062.0 57.5 %reduce-scatter.28.cloned.1.call-done = bf16[2048,256]{1,0:T(8,128)(2,1)} async-done(((bf16[2048,1024]{1,0:T(8,128)(2,1)}), bf16[2048,256]{1,0:T(8,128)(2,1)}) %reduce-scatter.28.cloned.1.call-update) | async-done | bytes 1048592 | tf_op jit(solution)/shard_map/reduce_scatter | solution.py:794
  1119.5 3.7 all-to-all-start
  1123.2 71.8 %reduce-scatter.24.cloned.1.call-done = bf16[256,2048]{1,0:T(8,128)(2,1)} async-done(((bf16[2048,2048]{1,0:T(8,128)(2,1)}), bf16[256,2048]{1,0:T(8,128)(2,1)}) %reduce-scatter.24.cloned.1.call-update) | async-done | bytes 1048592 | tf_op jit(solution)/shard_map/reduce_scatter | solution.py:735
  1195.1 79.1 %reduce-scatter.30.cloned.1.call-done = bf16[2048,256]{1,0:T(8,128)(2,1)} async-done(((bf16[2048,1024]{1,0:T(8,128)(2,1)}), bf16[2048,256]{1,0:T(8,128)(2,1)}) %reduce-scatter.30.cloned.1.call-update) | async-done | bytes 1048592 | tf_op jit(solution)/shard_map/reduce_scatter | solution.py:794
  1274.1 3.7 all-to-all-start.1
  1278.3 1.6 copy.35
  1280.0 1.6 copy.33
  1281.6 11.6 all-to-all-done.1
  1293.4 1.6 copy.34
  1295.0 1.4 copy-done.6
  1296.7 4.4 fusion.35
  1301.1 48.6 %reduce-scatter.16.cloned.1.call-done = bf16[256,2048]{1,0:T(8,128)(2,1)} async-done(((bf16[2048,2048]{1,0:T(8,128)(2,1)}), bf16[256,2048]{1,0:T(8,128)(2,1)}) %reduce-scatter.16.cloned.1.call-update) | async-done | bytes 1048592 | tf_op jit(solution)/shard_map/reduce_scatter | solution.py:735
  1349.7 12.2 fusion.26
  1361.9 40.9 %all-reduce = (f32[2048]{0:T(1024)}, f32[2048]{0:T(1024)}) all-reduce(f32[2048]{0:T(1024)S(1)} %get-tuple-element.55, f32[2048]{0:T(1024)S(1)} %copy-done.24), channel_id=1, replica_groups=mesh['dp'=8,'tensor'=4] {'dp','tensor'}, use_global_device_ids=true, to_apply=%region_9.0 | all-reduce | flops 4096 | bytes 32768 | tf_op jit(solution)/shard_map/psum | solution.py:821
  1402.8 6.3 fusion.28
  1409.1 1.6 fusion.33
  1410.7 1.8 convert_element_type.148
  1412.5 17.3 %reduce-scatter.18.cloned.1.call-done = bf16[256,512]{1,0:T(8,128)(2,1)} async-done(((bf16[256,2048]{1,0:T(8,128)(2,1)}), bf16[256,512]{1,0:T(8,128)(2,1)}) %reduce-scatter.18.cloned.1.call-update) | async-done | bytes 262160 | tf_op jit(solution)/shard_map/reduce_scatter | solution.py:736
  1429.8 1.8 convert_element_type.144
  (108 shorter events, 3.9 us)
Async XLA Ops:
  7.2 145.5 %all-gather.9.cloned.1.call-start = ((), (), s32[]{:S(2)}) async-start(), calls=%async_computation.16 | async-start | bytes 5242880 | tf_op jit(solution)/shard_map/all_gather | solution.py:765
  68.4 221.7 %copy-start.25 = (s32[1,2048]{1,0:T(1,128)S(1)}, s32[1,2048]{1,0:T(1,128)}, u32[]{:S(2)}) copy-start(s32[1,2048]{1,0:T(1,128)} %param.13) | copy-start | bytes 24580
  68.4 356.6 %all-gather.5.cloned.1.call-start = ((), (), s32[]{:S(2)}) async-start(), calls=%async_computation.14 | async-start | bytes 5242880 | tf_op jit(solution)/shard_map/all_gather | solution.py:765
  69.2 222.7 %copy-start.11 = (bf16[1,512,2048]{2,1,0:T(8,128)(2,1)S(1)}, bf16[1,512,2048]{2,1,0:T(8,128)(2,1)}, u32[]{:S(2)}) copy-start(bf16[1,512,2048]{2,1,0:T(8,128)(2,1)} %param.12) | copy-start | bytes 6291460
  69.2 355.9 %all-gather.7.cloned.1.call-start = ((), (), s32[]{:S(2)}) async-start(), calls=%async_computation.15 | async-start | bytes 5242880 | tf_op jit(solution)/shard_map/all_gather | solution.py:765
  69.9 441.2 %all-gather.11.cloned.1.call-start = ((), (), s32[]{:S(2)}) async-start(), calls=%async_computation.18 | async-start | bytes 18874368 | tf_op jit(solution)/shard_map/all_gather | solution.py:699
  152.7 139.7 %copy-start.20 = (f32[2048]{0:T(1024)S(1)}, f32[2048]{0:T(1024)}, u32[]{:S(2)}) copy-start(f32[2048]{0:T(1024)} %param.14) | copy-start | bytes 24580
  152.7 558.9 %reduce-scatter.14.cloned.1.call-start = ((), (), s32[]{:S(2)}) async-start(), calls=%async_computation.19 | async-start | bytes 18874368 | tf_op jit(solution)/shard_map/reduce_scatter | solution.py:702
  290.4 69.6 %copy-start.4 = (s32[512]{0:T(512)}, s32[512]{0:T(512)S(1)}, u32[]{:S(2)}) copy-start(s32[512]{0:T(512)S(1)} %get-tuple-element.67) | copy-start | bytes 6148
  290.4 2.6 copy-start.5
  291.9 16.3 %copy-start.2 = (f32[512,128]{1,0:T(8,128)}, f32[512,128]{1,0:T(8,128)S(1)}, u32[]{:S(2)}) copy-start(f32[512,128]{1,0:T(8,128)S(1)} %get-tuple-element.75.cos_ref) | copy-start | bytes 786436
  291.9 16.3 %copy-start.3 = (f32[512,128]{1,0:T(8,128)}, f32[512,128]{1,0:T(8,128)S(1)}, u32[]{:S(2)}) copy-start(f32[512,128]{1,0:T(8,128)S(1)} %get-tuple-element.76.sin_ref) | copy-start | bytes 786436
  292.4 15.8 %copy-start.26 = (f32[512]{0:T(512)}, f32[512]{0:T(512)S(1)}, u32[]{:S(2)}) copy-start(f32[512]{0:T(512)S(1)} %add_rsqrt_fusion.1) | copy-start | bytes 6148
  293.0 15.2 %copy-start = (bf16[512,2048]{1,0:T(8,128)(2,1)}, bf16[512,2048]{1,0:T(8,128)(2,1)S(1)}, u32[]{:S(2)}) copy-start(bf16[512,2048]{1,0:T(8,128)(2,1)S(1)} %fusion.12.x_ref) | copy-start | bytes 6291460
  308.2 105.1 %copy-start.7 = (bf16[512,2048]{1,0:T(8,128)(2,1)}, bf16[512,2048]{1,0:T(8,128)(2,1)S(1)}, u32[]{:S(2)}) copy-start(bf16[512,2048]{1,0:T(8,128)(2,1)S(1)} %get-tuple-element.37.q_ref) | copy-start | bytes 6291460
  308.2 24.6 %collective-permute-start = (bf16[512,1024]{1,0:T(8,128)(2,1)S(1)}, bf16[512,1024]{1,0:T(8,128)(2,1)S(1)}, u32[]{:S(2)}, u32[]{:S(2)}) collective-permute-start(bf16[512,1024]{1,0:T(8,128)(2,1)S(1)} %get-tuple-element.38), channel_id=1, source_target_pairs={{0,1},{1,2},{2,3},{4,5},{5,6},{6,7},{8,9},{9,10},{10,11},{12,13},{... | collective-permute-start | bytes 3145736 | tf_op jit(solution)/shard_map/ppermute | solution.py:751
  332.8 26.9 %collective-permute-start.1 = (bf16[512,1024]{1,0:T(8,128)(2,1)S(1)}, bf16[512,1024]{1,0:T(8,128)(2,1)S(1)}, u32[]{:S(2)}, u32[]{:S(2)}) collective-permute-start(bf16[512,1024]{1,0:T(8,128)(2,1)S(1)} %collective-permute-done), channel_id=1, source_target_pairs={{0,1},{1,2},{2,3},{4,5},{5,6},{6,7},{8,9},{9,10},{10,11},{12,13},{... | collective-permute-start | bytes 3145736 | tf_op jit(solution)/shard_map/ppermute | solution.py:751
  360.0 1.6 copy-start.17
  413.4 8.0 copy-start.8
  413.4 8.0 copy-start.9
  413.4 9.9 copy-start.18
  421.3 2.0 copy-start.10
  421.4 1.9 copy-start.22
  511.1 32.4 %copy-start.28 = (bf16[2048,1024]{1,0:T(8,128)(2,1)S(1)}, bf16[2048,1024]{1,0:T(8,128)(2,1)}, u32[]{:S(2)}) copy-start(bf16[2048,1024]{1,0:T(8,128)(2,1)} %all-gather.5.cloned.1.call-done.wg_ref) | copy-start | bytes 12582916
  543.5 24.7 %copy-start.29 = (bf16[2048,1024]{1,0:T(8,128)(2,1)S(1)}, bf16[2048,1024]{1,0:T(8,128)(2,1)}, u32[]{:S(2)}) copy-start(bf16[2048,1024]{1,0:T(8,128)(2,1)} %all-gather.7.cloned.1.call-done.wu_ref) | copy-start | bytes 12582916
  594.8 236.3 %reduce-scatter.12.cloned.1.call-start = ((), (), s32[]{:S(2)}) async-start(), calls=%async_computation.17 | async-start | bytes 18874368 | tf_op jit(solution)/shard_map/reduce_scatter | solution.py:702
  619.4 438.2 %reduce-scatter.32.cloned.1.call-start = ((), (), s32[]{:S(2)}) async-start(), calls=%async_computation.28 | async-start | bytes 5242880 | tf_op jit(solution)/shard_map/reduce_scatter | solution.py:794
  644.3 67.3 %copy-start.19 = (f32[2048]{0:T(1024)S(1)}, f32[2048]{0:T(1024)}, u32[]{:S(2)}) copy-start(f32[2048]{0:T(1024)} %param.19) | copy-start | bytes 24580
  644.3 67.3 %copy-start.23 = (f32[512]{0:T(512)S(1)}, f32[512]{0:T(512)}, u32[]{:S(2)}) copy-start(f32[512]{0:T(512)} %copy-done.22) | copy-start | bytes 6148
  644.3 186.8 %copy-start.14 = (bf16[1,512,2048]{2,1,0:T(8,128)(2,1)S(1)}, bf16[1,512,2048]{2,1,0:T(8,128)(2,1)}, u32[]{:S(2)}) copy-start(bf16[1,512,2048]{2,1,0:T(8,128)(2,1)} %param.23) | copy-start | bytes 6291460
  644.4 417.0 %reduce-scatter.20.cloned.1.call-start = ((), (), s32[]{:S(2)}) async-start(), calls=%async_computation.22 | async-start | bytes 4718592 | tf_op jit(solution)/shard_map/reduce_scatter | solution.py:735
  836.7 11.2 copy-start.13
  924.5 59.9 %copy-start.1 = (bf16[512,2048]{1,0:T(8,128)(2,1)S(1)}, bf16[512,2048]{1,0:T(8,128)(2,1)}, u32[]{:S(2)}) copy-start(bf16[512,2048]{1,0:T(8,128)(2,1)} %copy-done) | copy-start | bytes 6291460
  924.5 27.1 %collective-permute-start.2 = (bf16[512,1024]{1,0:T(8,128)(2,1)S(1)}, bf16[512,1024]{1,0:T(8,128)(2,1)S(1)}, u32[]{:S(2)}, u32[]{:S(2)}) collective-permute-start(bf16[512,1024]{1,0:T(8,128)(2,1)S(1)} %get-tuple-element.63), channel_id=1, source_target_pairs={{1,0},{2,1},{3,2},{5,4},{6,5},{7,6},{9,8},{10,9},{11,10},{13,12},{... | collective-permute-start | bytes 3145736 | tf_op jit(solution)/shard_map/ppermute | solution.py:751
  953.2 26.1 %collective-permute-start.3 = (bf16[512,1024]{1,0:T(8,128)(2,1)S(1)}, bf16[512,1024]{1,0:T(8,128)(2,1)S(1)}, u32[]{:S(2)}, u32[]{:S(2)}) collective-permute-start(bf16[512,1024]{1,0:T(8,128)(2,1)S(1)} %add_convert_fusion.2), channel_id=1, source_target_pairs={{1,0},{2,1},{3,2},{5,4},{6,5},{7,6},{9,8},{10,9},{11,10},{13,12},{... | collective-permute-start | bytes 3145736 | tf_op jit(solution)/shard_map/ppermute | solution.py:751
  979.2 1.0 copy-start.16
  990.0 129.5 %reduce-scatter.28.cloned.1.call-start = ((), (), s32[]{:S(2)}) async-start(), calls=%async_computation.26 | async-start | bytes 5242880 | tf_op jit(solution)/shard_map/reduce_scatter | solution.py:794
  1014.1 180.9 %reduce-scatter.24.cloned.1.call-start = ((), (), s32[]{:S(2)}) async-start(), calls=%async_computation.24 | async-start | bytes 9437184 | tf_op jit(solution)/shard_map/reduce_scatter | solution.py:735
  1025.2 249.0 %reduce-scatter.30.cloned.1.call-start = ((), (), s32[]{:S(2)}) async-start(), calls=%async_computation.27 | async-start | bytes 5242880 | tf_op jit(solution)/shard_map/reduce_scatter | solution.py:794
  1049.1 300.6 %reduce-scatter.16.cloned.1.call-start = ((), (), s32[]{:S(2)}) async-start(), calls=%async_computation.20 | async-start | bytes 9437184 | tf_op jit(solution)/shard_map/reduce_scatter | solution.py:735
  1057.7 61.8 %all-to-all-start.2 = ((bf16[8,256,256]{2,1,0:T(8,128)(2,1)}), bf16[8,256,256]{2,1,0:T(8,128)(2,1)S(1)}, u32[]{:S(2)}, u32[]{:S(2)}) async-start(bf16[8,256,256]{2,1,0:T(8,128)(2,1)} %bitcast.63), calls=%async_computation.13 | async-start | bytes 2097152 | tf_op jit(solution)/shard_map/all_to_all | solution.py:712
  1061.3 347.9 %reduce-scatter.22.cloned.1.call-start = ((), (), s32[]{:S(2)}) async-start(), calls=%async_computation.23 | async-start | bytes 655360 | tf_op jit(solution)/shard_map/reduce_scatter | solution.py:736
  1119.5 154.6 %all-to-all-start = ((bf16[8,256,256]{2,1,0:T(8,128)(2,1)}), bf16[8,256,256]{2,1,0:T(8,128)(2,1)S(1)}, u32[]{:S(2)}, u32[]{:S(2)}) async-start(bf16[8,256,256]{2,1,0:T(8,128)(2,1)} %bitcast.64), calls=%async_computation.9 | async-start | bytes 2097152 | tf_op jit(solution)/shard_map/all_to_all | solution.py:712
  1123.2 287.6 %reduce-scatter.26.cloned.1.call-start = ((), (), s32[]{:S(2)}) async-start(), calls=%async_computation.25 | async-start | bytes 1310720 | tf_op jit(solution)/shard_map/reduce_scatter | solution.py:736
  1274.1 19.1 %all-to-all-start.1 = ((bf16[8,256,256]{2,1,0:T(8,128)(2,1)}), bf16[8,256,256]{2,1,0:T(8,128)(2,1)S(1)}, u32[]{:S(2)}, u32[]{:S(2)}) async-start(bf16[8,256,256]{2,1,0:T(8,128)(2,1)} %bitcast.65), calls=%async_computation.11 | async-start | bytes 2097152 | tf_op jit(solution)/shard_map/all_to_all | solution.py:712
  1277.8 152.1 %reduce-scatter.18.cloned.1.call-start = ((), (), s32[]{:S(2)}) async-start(), calls=%async_computation.21 | async-start | bytes 1310720 | tf_op jit(solution)/shard_map/reduce_scatter | solution.py:736
  1293.2 3.1 copy-start.6
  1293.2 3.5 copy-start.15
  1296.7 53.0 %copy-start.12 = (bf16[1,512,2048]{2,1,0:T(8,128)(2,1)S(1)}, bf16[1,512,2048]{2,1,0:T(8,128)(2,1)}, u32[]{:S(2)}) copy-start(bf16[1,512,2048]{2,1,0:T(8,128)(2,1)} %param.12) | copy-start | bytes 6291460
  1296.7 53.0 %copy-start.21 = (f32[2048]{0:T(1024)S(1)}, f32[2048]{0:T(1024)}, u32[]{:S(2)}) copy-start(f32[2048]{0:T(1024)} %param.14) | copy-start | bytes 24580
  1296.7 53.0 %copy-start.27 = (f32[512]{0:T(512)S(1)}, f32[512]{0:T(512)}, u32[]{:S(2)}) copy-start(f32[512]{0:T(512)} %copy-done.26) | copy-start | bytes 6148
  1349.7 12.2 copy-start.24
Sparse Core Ops, SparseCore 0:
  68.5 84.1 all-gather.8
  154.3 78.7 all-gather.4
  234.6 78.7 all-gather.6
  315.1 88.0 all-gather.10
  594.9 116.6 reduce-scatter.13
  715.1 115.9 reduce-scatter.11
  833.4 76.7 reduce-scatter.31
  990.2 50.2 reduce-scatter.19
  1042.7 76.7 reduce-scatter.27
  1123.2 71.7 reduce-scatter.23
  1197.3 76.7 reduce-scatter.29
  1277.8 71.7 reduce-scatter.15
  1351.9 21.6 reduce-scatter.21
  1375.8 25.9 reduce-scatter.25
  1404.0 25.7 reduce-scatter.17

commit v2 on v1

--- a/solution.py
+++ b/solution.py
@@ -20,6 +20,8 @@
 LOG2E = 1.4426950408889634
 FAR = -1e30
 NTILE = 512
+STRIP = 16
+LONG = 60_000_000_000
 
 F32 = jnp.float32
 BF16 = jnp.bfloat16
@@ -414,6 +416,7 @@
             pltpu.SemaphoreType.DMA((slots,)),
         ],
         compiler_params=pltpu.CompilerParams(collective_id=2, has_side_effects=True),
+        cost_estimate=pl.CostEstimate(flops=LONG, bytes_accessed=0, transcendentals=0),
     )(*mlp, *attn)
 
 
@@ -537,6 +540,7 @@
             pltpu.SemaphoreType.DMA((count, Ring.COPIES)),
         ],
         compiler_params=pltpu.CompilerParams(collective_id=3, has_side_effects=True),
+        cost_estimate=pl.CostEstimate(flops=2 * LONG, bytes_accessed=0, transcendentals=0),
     )(*arrays)
 
 
@@ -649,6 +653,283 @@
     )(hn, wg, wu)
 
 
+FAR_CHUNK, X_CHUNK, Y_CHUNK, OWN_CHUNK = range(4)
+
+
+class Reduce:
+    COPIES = 10
+
+    def __init__(self, wide, parts, cores, far, near, send_sem, recv_sem):
+        self.at, self.peers = neighbours(wide)
+        self.parts, self.cores, self.far, self.near = parts, cores, far, near
+        self.send_sem, self.recv_sem = send_sem, recv_sem
+        self.half = parts.shape[2] // 2
+
+    @staticmethod
+    def scratch(rows, cols):
+        return [
+            pltpu.VMEM((2, 4, rows, cols), BF16),
+            pltpu.VMEM((4, rows, cols), BF16),
+            pltpu.VMEM((2, rows // 2, cols), BF16),
+            pltpu.VMEM((2, rows, cols), BF16),
+            pltpu.SemaphoreType.DMA((Reduce.COPIES,)),
+            pltpu.SemaphoreType.DMA((Reduce.COPIES,)),
+        ]
+
+    def chunk(self, step):
+        slot, other = step // 2, 1 - step % 2
+        row, col, core = self.at
+        dy, dx = 1 - slot % 2, 1 - slot // 2
+        place = 4 * ((row + dy) % 2) + 2 * ((col + dx) % 2) + (core + other) % 2
+        return place, self.parts.at[other, slot]
+
+    def copy(self, name):
+        upper, lower = pl.ds(0, self.half), pl.ds(self.half, self.half)
+        mine = self.parts.at[0]
+        table = {
+            "far0": (self.parts.at[1, FAR_CHUNK], self.cores.at[FAR_CHUNK], SIB),
+            "x": (self.parts.at[1, X_CHUNK], self.cores.at[X_CHUNK], SIB),
+            "y": (self.parts.at[1, Y_CHUNK], self.cores.at[Y_CHUNK], SIB),
+            "own": (self.parts.at[1, OWN_CHUNK], self.cores.at[OWN_CHUNK], SIB),
+            "far_x": (mine.at[FAR_CHUNK, lower], self.far.at[0], XN),
+            "far_y": (mine.at[FAR_CHUNK, upper], self.far.at[1], YN),
+            "x_upper": (mine.at[X_CHUNK, upper], self.near.at[0, upper], XN),
+            "x_lower": (mine.at[X_CHUNK, lower], self.near.at[0, lower], XN),
+            "y_upper": (mine.at[Y_CHUNK, upper], self.near.at[1, upper], YN),
+            "y_lower": (mine.at[Y_CHUNK, lower], self.near.at[1, lower], YN),
+        }
+        src, dst, peer = table[name]
+        at = list(table).index(name)
+        return pltpu.make_async_remote_copy(
+            src_ref=src, dst_ref=dst, send_sem=self.send_sem.at[at],
+            recv_sem=self.recv_sem.at[at], device_id={"dp": self.peers[peer]},
+            device_id_type=MESH,
+        )
+
+    def start(self, *names):
+        for name in names:
+            self.copy(name).start()
+
+    def add(self, slot, start, other):
+        count = other.shape[0] // STRIP
+
+        @pl.loop(0, count)
+        def _(at):
+            here = pl.ds(pl.multiple_of(start + at * STRIP, STRIP), STRIP)
+            there = pl.ds(pl.multiple_of(at * STRIP, STRIP), STRIP)
+            value = self.parts[0, slot, here, :].astype(F32) + other[there, :].astype(F32)
+            self.parts[0, slot, here, :] = value.astype(BF16)
+
+    def merge_core(self, slot, name):
+        self.copy(name).wait_recv()
+        self.add(slot, 0, self.cores.at[slot])
+
+    def after(self, step):
+        names = ("far0", "x", "y", "own")
+        for slot in range(4):
+            pl.when(step == 2 * slot)(functools.partial(self.start, names[slot]))
+
+        @pl.when(step == 1)
+        def _():
+            self.merge_core(FAR_CHUNK, "far0")
+            self.start("far_x", "far_y")
+
+        @pl.when(step == 3)
+        def _():
+            self.merge_core(X_CHUNK, "x")
+            self.start("x_lower")
+
+        @pl.when(step == 5)
+        def _():
+            self.merge_core(Y_CHUNK, "y")
+            self.start("y_upper")
+
+    def pass_on(self):
+        self.copy("far_y").wait_recv()
+        self.add(X_CHUNK, 0, self.far.at[1])
+        self.start("x_upper")
+        self.copy("far_x").wait_recv()
+        self.add(Y_CHUNK, self.half, self.far.at[0])
+        self.start("y_lower")
+
+    def finish(self, store):
+        for name in ("own", "x_upper", "x_lower", "y_upper", "y_lower"):
+            self.copy(name).wait_recv()
+
+        @pl.loop(0, 2 * self.half // STRIP)
+        def _(at):
+            here = pl.ds(pl.multiple_of(at * STRIP, STRIP), STRIP)
+            value = self.parts[0, OWN_CHUNK, here, :].astype(F32)
+            value += self.cores[OWN_CHUNK, here, :].astype(F32)
+            value += self.near[0, here, :].astype(F32)
+            value += self.near[1, here, :].astype(F32)
+            store(here, value)
+
+    def sent(self):
+        for name in (
+            "far0", "x", "y", "own", "far_x", "far_y", "x_upper", "x_lower", "y_upper", "y_lower",
+        ):
+            self.copy(name).wait_send()
+
+
+def tail_kernel(
+    wide, z_size, x_ref, h_ref, dq_ref, dkv_ref, att_ref, gain_ref,
+    wo_out, wq_out, wkv_out, gain_out,
+    *scratch,
+):
+    own_scratch, (sums, zrecv, gain_z, gain_p, z_send, z_recv, g_send, g_recv) = (
+        scratch[:18], scratch[18:],
+    )
+    rings = [Reduce(wide, *own_scratch[6 * at : 6 * at + 6]) for at in range(3)]
+    place = lax.axis_index("tensor")
+    dp = lax.axis_index("dp")
+    row, col, core = rings[0].at
+    mine = 4 * row + 2 * col + core
+    base = dp - (2 * wide * row + 2 * col + core)
+    flips = [(y, x, c) for y in range(2) for x in range(2) for c in range(2)][1:]
+
+    def device(flip):
+        y, x, c = (row + flip[0]) % 2, (col + flip[1]) % 2, (core + flip[2]) % 2
+        return {"dp": base + 2 * wide * y + 2 * x + c}
+
+    along = [{"tensor": (place + step) % z_size} for step in range(1, z_size)]
+    around = [device(flip) for flip in flips]
+    barrier = pltpu.get_barrier_semaphore()
+    for peer in along + around:
+        pl.semaphore_signal(barrier, inc=1, device_id=peer, device_id_type=MESH)
+    pl.semaphore_wait(barrier, len(along) + len(around))
+
+    gain_z[place] = gain_ref[...]
+    gain_copies = [
+        pltpu.make_async_remote_copy(
+            src_ref=gain_ref, dst_ref=gain_z.at[place], send_sem=g_send.at[at],
+            recv_sem=g_recv.at[at], device_id=peer, device_id_type=MESH,
+        )
+        for at, peer in enumerate(along)
+    ]
+    for copy in gain_copies:
+        copy.start()
+
+    lefts = (h_ref, x_ref, x_ref)
+    rights = (att_ref, dq_ref, dkv_ref)
+    rows = sums.shape[0]
+    outs = (wo_out, wq_out, wkv_out)
+    z_copies = []
+    for index, ring in enumerate(rings):
+        left, right = lefts[index], rights[index]
+        cols = right.shape[1]
+
+        @pl.loop(0, 8)
+        def _(step):
+            chunk, target = ring.chunk(step)
+            x = left[:, pl.ds(pl.multiple_of(chunk * rows, rows), rows)].T
+
+            @pl.loop(0, cols // NTILE)
+            def _(at):
+                n = pl.ds(pl.multiple_of(at * NTILE, NTILE), NTILE)
+                target[:, n] = dot_nn(x, right[:, n]).astype(BF16)
+
+            ring.after(step)
+
+        if index == 0:
+            for copy in gain_copies:
+                copy.wait_recv()
+            total = gain_z[0]
+            for at in range(1, z_size):
+                total = total + gain_z[at]
+            gain_p[mine] = total
+            for at, peer in enumerate(around):
+                copy = pltpu.make_async_remote_copy(
+                    src_ref=gain_p.at[mine], dst_ref=gain_p.at[mine],
+                    send_sem=g_send.at[z_size - 1 + at], recv_sem=g_recv.at[z_size - 1 + at],
+                    device_id=peer, device_id_type=MESH,
+                )
+                gain_copies.append(copy)
+                copy.start()
+
+    def send_along(index, ring, start):
+        cols = rights[index].shape[1]
+        part = cols // z_size
+
+        def store(here, value):
+            sums[here, pl.ds(start, cols)] = value.astype(BF16)
+
+        ring.finish(store)
+        for at, peer in enumerate(along):
+            other = (place + at + 1) % z_size
+            copy = pltpu.make_async_remote_copy(
+                src_ref=sums.at[:, pl.ds(pl.multiple_of(start + other * part, LANES), part)],
+                dst_ref=zrecv.at[at, :, pl.ds(start // z_size, part)],
+                send_sem=z_send.at[index, at], recv_sem=z_recv.at[index, at],
+                device_id=peer, device_id_type=MESH,
+            )
+            z_copies.append(copy)
+            copy.start()
+
+    starts = [0, rights[0].shape[1], rights[0].shape[1] + rights[1].shape[1]]
+    for index, ring in enumerate(rings):
+        ring.pass_on()
+        if index:
+            send_along(index - 1, rings[index - 1], starts[index - 1])
+    send_along(2, rings[2], starts[2])
+
+    for copy in gain_copies[z_size - 1 :]:
+        copy.wait_recv()
+    total = gain_p[0]
+    for at in range(1, GROUP):
+        total = total + gain_p[at]
+    gain_out[...] = total
+
+    for copy in z_copies:
+        copy.wait_recv()
+    for index in range(3):
+        part = rights[index].shape[1] // z_size
+        own = pl.ds(pl.multiple_of(starts[index] + place * part, LANES), part)
+        value = sums[:, own].astype(F32)
+        for at in range(z_size - 1):
+            value += zrecv[at, :, pl.ds(starts[index] // z_size, part)].astype(F32)
+        outs[index][...] = value
+    for copy in z_copies + gain_copies:
+        copy.wait_send()
+    for ring in rings:
+        ring.sent()
+
+
+def attention_grads(x, h, dq, dkv, att, gains, dp_size, z_size):
+    tokens, width = x.shape
+    rows = width // GROUP
+    near = pl.BlockSpec(memory_space=pltpu.VMEM)
+    sizes = [att.shape[1], dq.shape[1], dkv.shape[1]]
+    scratch = []
+    for cols in sizes:
+        scratch += Reduce.scratch(rows, cols)
+    total = sum(sizes)
+    return pl.pallas_call(
+        functools.partial(tail_kernel, 2 * math.isqrt(dp_size // GROUP), z_size),
+        in_specs=[near] * 6,
+        out_specs=[near] * 4,
+        out_shape=[jax.ShapeDtypeStruct((rows, cols // z_size), F32) for cols in sizes]
+        + [jax.ShapeDtypeStruct(gains.shape, F32)],
+        scratch_shapes=scratch
+        + [
+            pltpu.VMEM((rows, total), BF16),
+            pltpu.VMEM((z_size - 1, rows, total // z_size), BF16),
+            pltpu.VMEM((z_size, *gains.shape), F32),
+            pltpu.VMEM((GROUP, *gains.shape), F32),
+            pltpu.SemaphoreType.DMA((3, z_size - 1)),
+            pltpu.SemaphoreType.DMA((3, z_size - 1)),
+            pltpu.SemaphoreType.DMA((z_size - 1 + GROUP - 1,)),
+            pltpu.SemaphoreType.DMA((z_size - 1 + GROUP - 1,)),
+        ],
+        compiler_params=pltpu.CompilerParams(
+            collective_id=4, has_side_effects=True, vmem_limit_bytes=60 << 20
+        ),
+        cost_estimate=pl.CostEstimate(
+            flops=2 * LONG, bytes_accessed=4 * tokens * total, transcendentals=0
+        ),
+    )(x, h, dq, dkv, att, gains)
+
+
 class Layout:
     def __init__(self, dp_size):
         self.blocks = dp_size // GROUP
@@ -683,6 +964,9 @@
         order = (1, 3, 4, 0, 2, 5) + tuple(range(6, 6 + len(rest)))
         return split.transpose(order).reshape(array.shape)
 
+    def from_cols(self, array):
+        return array if self.blocks == 1 else self.from_rows(array.T).T
+
     def gather_outer(self, array):
         if self.blocks == 1:
             return array
@@ -695,6 +979,11 @@
             array, "dp", scatter_dimension=0, axis_index_groups=self.outer, tiled=True
         )
 
+    def sum_outer(self, array):
+        if self.blocks == 1:
+            return array
+        return lax.psum(array, "dp", axis_index_groups=self.outer)
+
     def gather(self, array):
         return lax.all_gather(array, "dp", axis_index_groups=self.groups(), axis=0, tiled=True)
 
@@ -723,17 +1012,6 @@
     gain_part = jnp.sum(grad * values * scaling, axis=0)
     inner = jnp.mean(gained * values, axis=-1, keepdims=True)
     return gain_part, scaling * gained - values * scaling * scaling * scaling * inner
-
-
-def gather_all(array):
-    return lax.all_gather(
-        lax.all_gather(array, "tensor", axis=1, tiled=True), "dp", axis=0, tiled=True
-    )
-
-
-def scatter_all(array):
-    part = lax.psum_scatter(array.astype(BF16), "dp", scatter_dimension=0, tiled=True)
-    return lax.psum_scatter(part, "tensor", scatter_dimension=1, tiled=True).astype(F32)
 
 
 def per_device(
@@ -765,6 +1043,11 @@
         layout.to_rows(lax.all_gather(w, "tensor", axis=1, tiled=True)) for w in spread[:3]
     )
     wkv, wq, wo = (layout.to_rows(w) for w in gather_rows(spread[3:], dp_size))
+
+    def along_z(total):
+        return lax.psum_scatter(
+            layout.from_rows(total), "tensor", scatter_dimension=1, tiled=True
+        )
 
     r1 = rms_scale(x)
     xn = (x * r1 * attn_gain).astype(BF16)
@@ -781,29 +1064,37 @@
     hn, gate, up, hidden = gate_up((h * r2 * mlp_gain).astype(BF16), wg, wu, dp_size)
     grad, wd = lax.optimization_barrier((cotangent[0], wd))
     dy = layout.gather(grad)
+    total_wd = dot_tn(dy, hidden).astype(BF16)
+    dy, total_wd = lax.optimization_barrier((dy, total_wd))
+    part_wd = along_z(total_wd)
     gate, up = gate.astype(F32), up.astype(F32)
     sigma = jax.nn.sigmoid(gate)
-    output = h + layout.scatter(dot_nt(hidden, wd).astype(BF16)).astype(F32)
     dhid = dot_nn(dy, wd)
     dgate = (dhid * up * sigma * (1.0 + gate * (1.0 - sigma))).astype(BF16)
     dup = (dhid * gate * sigma).astype(BF16)
-    dhn = layout.scatter((dot_nt(dgate, wg) + dot_nt(dup, wu)).astype(BF16)).astype(F32)
-
-    def mlp_grad(left, right):
-        total = layout.from_rows(dot_tn(left, right).astype(BF16))
-        part = lax.psum_scatter(total, "tensor", scatter_dimension=1, tiled=True)
-        return layout.scatter_outer(layout.unspread(part)).astype(F32)
-
-    wd_grad = mlp_grad(dy, hidden)
-    wg_grad = mlp_grad(hn, dgate)
-    wu_grad = mlp_grad(hn, dup)
+    half = width // 2
+    left_dhn = (dot_nt(dgate, wg[:half]) + dot_nt(dup, wu[:half])).astype(BF16)
+    dgate, dup, left_dhn, part_wd = lax.optimization_barrier((dgate, dup, left_dhn, part_wd))
+    dhn_left = layout.scatter(left_dhn)
+    right_dhn = (dot_nt(dgate, wg[half:]) + dot_nt(dup, wu[half:])).astype(BF16)
+    hn, hidden, right_dhn = lax.optimization_barrier((hn, hidden, right_dhn))
+    dhn_right = layout.scatter(right_dhn)
+    total_wg = dot_tn(hn, dgate).astype(BF16)
+    total_wu = dot_tn(hn, dup).astype(BF16)
+    partial_out = dot_nt(hidden, wd).astype(BF16)
+    dhn_left, dhn_right, total_wg, total_wu, partial_out = lax.optimization_barrier(
+        (dhn_left, dhn_right, total_wg, total_wu, partial_out)
+    )
+    dhn = jnp.concatenate([dhn_left, dhn_right], axis=1).astype(F32)
     gain_two, dh_norm = norm_back(h, r2, mlp_gain, dhn)
     dh = cotangent[0].astype(F32) + dh_norm
 
     dhb = dh.astype(BF16)
-    wo_grad = scatter_all(dot_tn(dhb, att))
     datt = dot_nn(dhb, wo).astype(BF16)
     dq, dkv_all = attend_back(q, datt, att, kv_all, lse, low, cosine, sine)
+    out_sum = layout.scatter(partial_out)
+    out_sum, dkv_all = lax.optimization_barrier((out_sum, dkv_all))
+    output = h + out_sum.astype(F32)
     count = reach // rows
     moved = dkv_all[:rows]
     for at in range(1, count + 1):
@@ -812,22 +1103,32 @@
             here = dkv_all[at * rows : (at + 1) * rows]
             moved = (moved.astype(F32) + here.astype(F32)).astype(BF16)
     dkv = finish_dkv(dkv_all[count * rows :], moved, cosine, sine)
-    wq_grad = scatter_all(dot_tn(xn, dq))
-    wkv_grad = scatter_all(dot_tn(xn, dkv))
-    key_cols = w_key.shape[1]
     dxn = dot_nt(dq, wq) + dot_nt(dkv, wkv)
     gain_one, dx_norm = norm_back(x, r1, attn_gain, dxn)
     input_grad = (dh + dx_norm).astype(BF16)
-    gain_one, gain_two = lax.psum((gain_one, gain_two), ("dp", "tensor"))
+    out_sum, total_wg, total_wu = lax.optimization_barrier((out_sum, total_wg, total_wu))
+    part_wg, part_wu = along_z(total_wg), along_z(total_wu)
+    gains = layout.sum_outer(jnp.stack([gain_one, gain_two]))
+    wo_grad, wq_grad, wkv_grad, gains = attention_grads(
+        layout.from_cols(xn), layout.from_cols(dhb), dq, dkv, att, gains, dp_size, z_size
+    )
+    wo_grad, wq_grad, wkv_grad = (
+        layout.scatter_outer(grad) for grad in (wo_grad, wq_grad, wkv_grad)
+    )
+    wd_grad, wg_grad, wu_grad = (
+        layout.scatter_outer(layout.unspread(part)).astype(F32)
+        for part in (part_wd, part_wg, part_wu)
+    )
+    key_cols = w_key.shape[1]
     return (
         output.astype(BF16)[None],
         input_grad[None],
-        gain_one,
+        gains[0],
         wq_grad,
         wkv_grad[:, :key_cols],
         wkv_grad[:, key_cols:],
         wo_grad,
-        gain_two,
+        gains[1],
         wg_grad,
         wu_grad,
         wd_grad,

time: 1450 us -> 1220 us (0.84)
  waiting for transfers between devices: 649 us -> 336 us
  Pallas kernels: 428 us -> 568 us
  blocking collectives: 40.9 us -> 0 us
    reduce_scatter x9 -> x3, waiting for transfers between devices: 274 us -> 11.1 us  [along_z(): lax.psum_scatter(layout.from_rows(total), 'tensor', scatter_dimension=1,...]
    pallas_call x0 -> x1, Pallas kernels: none -> 140 us  [attention_grads(): pl.pallas_call(functools.partial(tail_kernel, 2 * math.isqrt(dp_size // G...]
    reduce_scatter x2 -> x3, waiting for transfers between devices: 182 us -> 69.6 us  [scatter(): lax.psum_scatter(array, 'dp', scatter_dimension=0, axis_index_groups=self...]
    ppermute x4, waiting for transfers between devices: 95.6 us -> 153 us  [shift(): return lax.ppermute(array, 'tensor', pairs)]
    psum x1 -> x0, blocking collectives: 40.9 us -> none  [per_device(): gain_one, gain_two = lax.psum((gain_one, gain_two), ('dp', 'tensor'))]
    dot_general x6 -> x3, matrix products: 97.6 us -> 72.3 us  [dot_tn(): lax.dot_general(left, right, (((0,), (0,)), ((), ())), preferred_element_...]
    dot_general x6 -> x8, matrix products: 100 us -> 115 us  [dot_nt(): lax.dot_general(left, right, (((1,), (1,)), ((), ())), preferred_element_...]
  transfers between devices with their start and end apart: 22 -> 17, of which waited for: 13 -> 10; matrix products, arithmetic and copies ran while one was open for 13% -> 20% of each run, Pallas kernels for 26% -> 42%
where the time goes in v2:
time: 1220 us; the launch traced here: 1210 us
  Pallas kernels  568 us (47%)
  waiting for transfers between devices  336 us (28%)
  matrix products  231 us (19%)
  other arithmetic  24.7 us (2%)
  starting transfers between devices  20.8 us (2%)
  local copies, waits for them, and re-layouts  16.9 us (1%)
  between operations  15.1 us (1%)
    ppermute x4, waiting for transfers between devices, shift(): return lax.ppermute(array, 'tensor', pairs)  153 us
    pallas_call x1, Pallas kernels, attention_grads(): pl.pallas_call(functools.partial(tail_kernel, 2 * math.isqrt(dp_size // G...  140 us
    pallas_call x1, Pallas kernels, gather_rows(): pl.pallas_call(functools.partial(gather_kernel, 2 * math.isqrt(dp_size //...  137 us
    dot_general x8, matrix products, dot_nt(): lax.dot_general(left, right, (((1,), (1,)), ((), ())), preferred_element_...  115 us
    pallas_call x1, Pallas kernels, gate_up(): pl.pallas_call(functools.partial(gate_up_kernel, 2 * math.isqrt(dp_size /...  86 us
    all_gather x3, waiting for transfers between devices, per_device(): lax.all_gather(w, 'tensor', axis=1, tiled=True)  82.8 us
    pallas_call x1, Pallas kernels, attend_back(): pl.pallas_call(functools.partial(attend_back_kernel, reach), grid=(heads...  74.1 us
    dot_general x3, matrix products, dot_tn(): lax.dot_general(left, right, (((0,), (0,)), ((), ())), preferred_element_...  72.3 us
  transfers between devices with their start and end apart: 17, of which 10 were waited for; matrix products, arithmetic and copies ran while one was open for 20% of the time, Pallas kernels for 42%

profile of v2, /device:TPU:0, one launch (start us, length us, event | category | flops | bytes accessed | tf_op | source)
XLA Modules:
  0.0 1212.3 jit_solution(9769726787913389073)
XLA Ops:
  7.2 1.5 pad_maximum_fusion.3.refs_3_
  8.8 59.6 %shard_map.203 = (bf16[2048,256]{1,0:T(8,128)(2,1)}, bf16[2048,256]{1,0:T(8,128)(2,1)}, bf16[2048,256]{1,0:T(8,128)(2,1)}, bf16[256,1024]{1,0:T(8,128)(2,1)}, bf...) custom-call(bf16[256,2048]{1,0:T(8,128)(2,1)} %refs_0_.1, bf16[256,2048]{1,0:T(8,128)(2,1)} %refs_1_.1, ...), custom_call_target="tpu_custom_call" | custom-call | flops 60000002048 | tf_op jit(solution)/shard_map/pallas_call | solution.py:408
  68.5 0.7 all-gather.9.cloned.1.call-update
  69.2 0.7 all-gather.11.cloned.1.call-update
  70.0 82.8 %all-gather.5.cloned.1.call-done = bf16[2048,1024]{1,0:T(8,128)(2,1)} async-done(((bf16[2048,256]{1,0:T(8,128)(2,1)}), bf16[2048,1024]{1,0:T(8,128)(2,1)}) %all-gather.5.cloned.1.call-update) | async-done | bytes 4194320 | tf_op jit(solution)/shard_map/all_gather | solution.py:1043
  153.2 1.0 fusion.35
  154.7 0.5 fusion.23
  155.2 0.5 fusion.12.x_ref
  155.8 137.2 %shard_map.204 = (bf16[2048,1024]{1,0:T(8,128)(2,1)}, bf16[2048,2048]{1,0:T(8,128)(2,1)}, bf16[2048,2048]{1,0:T(8,128)(2,1)}) custom-call(bf16[256,1024]{1,0:T(8,128)(2,1)} %get-tuple-element.54.refs_0_, bf16[256,2048]{1,0:T(8,128)(2,1)} %get-tuple-element.55.refs_1_, bf16[256,2048]{1,0:T(8,128)(2,1)} %get-tuple-element.56.refs_2_), custom_call_target="tpu_custom_call" | custom-call | flops 120000004096 | tf_op jit(solution)/shard_map/pallas_call | solution.py:532
  293.1 2.2 copy-done.4
  295.3 14.5 %shard_map.205 = (bf16[512,2048]{1,0:T(8,128)(2,1)S(1)}, bf16[512,1024]{1,0:T(8,128)(2,1)S(1)}) custom-call(bf16[512,2048]{1,0:T(8,128)(2,1)S(1)} %fusion.12.x_ref, bf16[2048,2048]{1,0:T(8,128)(2,1)} %get-tuple-element.57.wq_ref, bf16[2048,1024]{1,0:T(8,128)(2,1)S(1)} %copy-done.4, f32[512,128]{1,0:T(8,128)S(1)} %get-tuple-element.119.cos_ref, ...), custom_call_target="tpu_custom_call" | custom-call | flops 6442450944 | bytes 12582912 | tf_op jit(solution)/shard_map/pallas_call | solution.py:85
  309.8 1.4 collective-permute-start
  311.2 23.2 %collective-permute-done = bf16[512,1024]{1,0:T(8,128)(2,1)S(1)} collective-permute-done((bf16[512,1024]{1,0:T(8,128)(2,1)S(1)}, bf16[512,1024]{1,0:T(8,128)(2,1)S(1)}, u32[]{:S(2)}, u32[]{:S(2)}) %collective-permute-start) | collective-permute-done | bytes 1048608 | tf_op jit(solution)/shard_map/ppermute | solution.py:1029
  334.4 4.7 collective-permute-start.1
  339.0 22.2 %collective-permute-done.1 = bf16[512,1024]{1,0:T(8,128)(2,1)S(1)} collective-permute-done((bf16[512,1024]{1,0:T(8,128)(2,1)S(1)}, bf16[512,1024]{1,0:T(8,128)(2,1)S(1)}, u32[]{:S(2)}, u32[]{:S(2)}) %collective-permute-start.1) | collective-permute-done | bytes 1048608 | tf_op jit(solution)/shard_map/ppermute | solution.py:1029
  361.5 1.6 copy-done.22
  363.2 51.9 %shard_map.206 = (bf16[512,2048]{1,0:T(8,128)(2,1)S(1)}, f32[32,1,512]{2,1,0:T(1,128)S(1)}) custom-call(bf16[512,2048]{1,0:T(8,128)(2,1)S(1)} %get-tuple-element.59.q_ref, bf16[1536,1024]{1,0:T(8,128)(2,1)} %copy-done.22, bf16[1536,1024]{1,0:T(8,128)(2,1)} %copy-done.22, s32[1,512]{1,0:T(1,128)S(1)} %bitcast.61), custom_call_target="tpu_custom_call" | custom-call | flops 21474836480 | bytes 7340032 | tf_op jit(solution)/shard_map/pallas_call | solution.py:169
  415.1 7.9 multiply_reduce_fusion
  423.0 2.1 copy-done.8
  425.1 1.7 multiply_convert_fusion.own_ref
  426.8 86.0 %shard_map.207 = (bf16[4096,2048]{1,0:T(8,128)(2,1)}, bf16[4096,1024]{1,0:T(8,128)(2,1)}, bf16[4096,1024]{1,0:T(8,128)(2,1)}, bf16[4096,1024]{1,0:T(8,128)(2,1)}) custom-call(bf16[512,2048]{1,0:T(8,128)(2,1)} %multiply_convert_fusion.own_ref, bf16[2048,1024]{1,0:T(8,128)(2,1)} %all-gather.9.cloned.1.call-done.wg_ref, ...), custom_call_target="tpu_custom_call" | custom-call | flops 34359738368 | bytes 50331648 | tf_op jit(solution)/shard_map/pallas_call | solution.py:630
  512.9 23.7 %convolution_convert_fusion.3 = bf16[2048,1024]{1,0:T(8,128)(2,1)} fusion(bf16[4096,2048]{1,0:T(8,128)(2,1)} %all-gather.7.cloned.1.call-done, bf16[4096,1024]{1,0:T(8,128)(2,1)} %get-tuple-element.79), kind=kOutput, calls=%fused_computation.45 | convolution fusion | flops 17181966336 | bytes 29360128 | tf_op jit(solution)/shard_map/dot_general | solution.py:39
  537.1 32.6 %fusion.7 = (bf16[4096,1024]{1,0:T(8,128)(2,1)}, bf16[4096,1024]{1,0:T(8,128)(2,1)}) fusion(bf16[4096,1024]{1,0:T(8,128)(2,1)} %get-tuple-element.71, bf16[4096,1024]{1,0:T(8,128)(2,1)} %get-tuple-element.70, bf16[4096,2048]{1,0:T(8,128)(2,1)} %all-gather.7.cloned.1.call-done, bf16[2048,1024]{1,0:T(8,128)(2,1)} %all-gather.5.cloned.1.call-done), kind=kOutput, calls=%fused_computation.10 | convolution fusion | flops 17242783744 | bytes 54525952 | tf_op jit(solution)/shard_map/dot_general | solution.py:31
  569.7 14.9 %fusion.33 = f32[4096,1024]{1,0:T(8,128)} fusion(bf16[4096,1024]{1,0:T(8,128)(2,1)} %get-tuple-element.75, bf16[2048,1024]{1,0:T(8,128)(2,1)S(1)} %copy-done.38), kind=kOutput, calls=%fused_computation.54 | convolution fusion | flops 8589934592 | bytes 27262976 | tf_op jit(solution)/shard_map/dot_general | solution.py:35
  584.7 17.4 %add_convert_fusion.1 = bf16[4096,1024]{1,0:T(8,128)(2,1)} fusion(f32[4096,1024]{1,0:T(8,128)} %fusion.33, bf16[4096,1024]{1,0:T(8,128)(2,1)} %get-tuple-element.76, bf16[2048,1024]{1,0:T(8,128)(2,1)S(1)} %copy-done.39), kind=kOutput, calls=%fused_computation.12 | convolution fusion | flops 8598323200 | bytes 35651584 | tf_op jit(solution)/shard_map/dot_general | solution.py:35
  602.0 11.1 reduce-scatter.7.cloned.1.call-done
  613.2 17.6 %fusion.30 = f32[4096,1024]{1,0:T(8,128)} fusion(bf16[4096,1024]{1,0:T(8,128)(2,1)} %get-tuple-element.75, bf16[2048,1024]{1,0:T(8,128)(2,1)} %all-gather.9.cloned.1.call-done.wg_ref), kind=kOutput, calls=%fused_computation.51 | convolution fusion | flops 8589934592 | bytes 27262976 | tf_op jit(solution)/shard_map/dot_general | solution.py:35
  630.8 18.0 %add_convert_fusion = bf16[4096,1024]{1,0:T(8,128)(2,1)} fusion(f32[4096,1024]{1,0:T(8,128)} %fusion.30, bf16[4096,1024]{1,0:T(8,128)(2,1)} %get-tuple-element.76, bf16[2048,1024]{1,0:T(8,128)(2,1)S(1)} %copy-done.40), kind=kOutput, calls=%fused_computation.11 | convolution fusion | flops 8598323200 | bytes 35651584 | tf_op jit(solution)/shard_map/dot_general | solution.py:35
  648.9 24.2 %convolution_convert_fusion.1 = bf16[2048,1024]{1,0:T(8,128)(2,1)} fusion(bf16[4096,2048]{1,0:T(8,128)(2,1)} %get-tuple-element.78, bf16[4096,1024]{1,0:T(8,128)(2,1)} %get-tuple-element.76), kind=kOutput, calls=%fused_computation.43 | convolution fusion | flops 17181966336 | bytes 29360128 | tf_op jit(solution)/shard_map/dot_general | solution.py:39
  673.1 24.4 %convolution_convert_fusion.2 = bf16[2048,1024]{1,0:T(8,128)(2,1)} fusion(bf16[4096,2048]{1,0:T(8,128)(2,1)} %get-tuple-element.78, bf16[4096,1024]{1,0:T(8,128)(2,1)} %get-tuple-element.75), kind=kOutput, calls=%fused_computation.44 | convolution fusion | flops 17181966336 | bytes 29360128 | tf_op jit(solution)/shard_map/dot_general | solution.py:39
  697.5 24.0 %convolution_convert_fusion = bf16[4096,2048]{1,0:T(8,128)(2,1)} fusion(bf16[4096,1024]{1,0:T(8,128)(2,1)} %get-tuple-element.79, bf16[2048,1024]{1,0:T(8,128)(2,1)} %all-gather.5.cloned.1.call-done), kind=kOutput, calls=%fused_computation.13 | convolution fusion | flops 17188257792 | bytes 29360128 | tf_op jit(solution)/shard_map/dot_general | solution.py:35
  721.5 42.0 %reduce-scatter.11.cloned.1.call-done = bf16[512,1024]{1,0:T(8,128)(2,1)} async-done(((bf16[4096,1024]{1,0:T(8,128)(2,1)}), bf16[512,1024]{1,0:T(8,128)(2,1)}) %reduce-scatter.11.cloned.1.call-update) | async-done | bytes 1048592 | tf_op jit(solution)/shard_map/reduce_scatter | solution.py:991
  763.6 3.8 fusion.22
  767.4 0.6 copy-done.35
  768.0 2.8 fusion.36.h_ref
  770.9 10.8 convolution_convert_fusion.4.do_ref
  781.7 74.1 %shard_map.208 = (bf16[512,2048]{1,0:T(8,128)(2,1)}, bf16[1536,1024]{1,0:T(8,128)(2,1)}) custom-call(bf16[512,2048]{1,0:T(8,128)(2,1)} %copy-done.5, bf16[512,2048]{1,0:T(8,128)(2,1)} %convolution_convert_fusion.4.do_ref, bf16[512,2048]{1,0:T(8,128)(2,1)} %copy-done.6, bf16[1536,1024]{1,0:T(8,128)(2,1)} %copy-done.22, bf16[1536,1024]{1,0:T(8,128)(2,1)} %copy-done.22, ...), custom_call_target="tpu_custom_call" | custom-call | flops 53687091200 | bytes 14680064 | tf_op jit(solution)/shard_map/pallas_call | solution.py:252
  855.8 27.6 %reduce-scatter.13.cloned.1.call-done = bf16[512,2048]{1,0:T(8,128)(2,1)} async-done(((bf16[4096,2048]{1,0:T(8,128)(2,1)}), bf16[512,2048]{1,0:T(8,128)(2,1)}) %reduce-scatter.13.cloned.1.call-update) | async-done | bytes 2097168 | tf_op jit(solution)/shard_map/reduce_scatter | solution.py:991
  883.5 1.5 fusion.37
  885.0 1.3 collective-permute-start.2
  886.3 3.6 all-to-all-start.2
  889.9 58.7 %collective-permute-done.2 = bf16[512,1024]{1,0:T(8,128)(2,1)S(1)} collective-permute-done((bf16[512,1024]{1,0:T(8,128)(2,1)}, bf16[512,1024]{1,0:T(8,128)(2,1)S(1)}, u32[]{:S(2)}, u32[]{:S(2)}) %collective-permute-start.2) | collective-permute-done | bytes 1048608 | tf_op jit(solution)/shard_map/ppermute | solution.py:1029
  948.6 1.6 add_convert_fusion.3
  950.3 1.3 collective-permute-start.3
  951.8 1.6 copy.35
  953.4 48.5 %collective-permute-done.3.recv_ref = bf16[512,1024]{1,0:T(8,128)(2,1)S(1)} collective-permute-done((bf16[512,1024]{1,0:T(8,128)(2,1)S(1)}, bf16[512,1024]{1,0:T(8,128)(2,1)S(1)}, u32[]{:S(2)}, u32[]{:S(2)}) %collective-permute-start.3) | collective-permute-done | bytes 1048608 | tf_op jit(solution)/shard_map/ppermute | solution.py:1029
  1001.8 1.0 copy-done.19
  1002.8 4.3 shard_map.209.dkv_ref
  1007.1 5.0 fusion.40
  1012.2 10.5 fusion.26
  1022.7 0.6 pad_maximum_fusion.4.gain_ref
  1023.3 140.0 %shard_map.210 = (f32[256,512]{1,0:T(8,128)}, f32[256,512]{1,0:T(8,128)}, f32[256,256]{1,0:T(8,128)}, f32[2,2048]{1,0:T(2,128)}) custom-call(bf16[512,2048]{1,0:T(8,128)(2,1)} %copy-done, bf16[512,2048]{1,0:T(8,128)(2,1)} %copy-done.18, bf16[512,2048]{1,0:T(8,128)(2,1)} %get-tuple-element.86.dq_ref, bf16[512,1024]{1,0:T(8,128)(2,1)} %shard_map.209.dkv_ref, ...), custom_call_target="tpu_custom_call" | custom-call | flops 120000004096 | bytes 10485760 | tf_op jit(solution)/shard_map/pallas_call | solution.py:907
  1163.4 4.3 all-to-all-start
  1167.7 8.0 fusion.28
  1175.7 7.4 all-to-all-done
  1183.1 3.6 all-to-all-start.1
  1186.6 0.7 fusion.38
  1187.4 0.6 fusion.39
  1188.0 1.4 convert_bitcast_fusion.2
  1189.4 1.6 copy.33
  1190.9 11.0 all-to-all-done.1
  1202.2 1.6 copy.34
  1203.7 0.8 copy.40
  1204.5 0.8 copy.41
  (118 shorter events, 2.6 us)
Async XLA Ops:
  7.2 145.5 %all-gather.5.cloned.1.call-start = ((), (), s32[]{:S(2)}) async-start(), calls=%async_computation.9 | async-start | bytes 5242880 | tf_op jit(solution)/shard_map/all_gather | solution.py:1043
  68.4 84.4 %copy-start.32 = (s32[1,2048]{1,0:T(1,128)S(1)}, s32[1,2048]{1,0:T(1,128)}, u32[]{:S(2)}) copy-start(s32[1,2048]{1,0:T(1,128)} %param.13) | copy-start | bytes 24580
  68.4 86.2 %copy-start.10 = (bf16[1,512,2048]{2,1,0:T(8,128)(2,1)S(1)}, bf16[1,512,2048]{2,1,0:T(8,128)(2,1)}, u32[]{:S(2)}) copy-start(bf16[1,512,2048]{2,1,0:T(8,128)(2,1)} %param.12) | copy-start | bytes 6291460
  68.4 358.4 %all-gather.9.cloned.1.call-start = ((), (), s32[]{:S(2)}) async-start(), calls=%async_computation.11 | async-start | bytes 5242880 | tf_op jit(solution)/shard_map/all_gather | solution.py:1043
  68.5 86.7 %copy-start.30 = (f32[2048]{0:T(1024)S(1)}, f32[2048]{0:T(1024)}, u32[]{:S(2)}) copy-start(f32[2048]{0:T(1024)} %param.14) | copy-start | bytes 24580
  69.2 357.6 %all-gather.11.cloned.1.call-start = ((), (), s32[]{:S(2)}) async-start(), calls=%async_computation.12 | async-start | bytes 5242880 | tf_op jit(solution)/shard_map/all_gather | solution.py:1043
  69.9 443.0 %all-gather.7.cloned.1.call-start = ((), (), s32[]{:S(2)}) async-start(), calls=%async_computation.10 | async-start | bytes 18874368 | tf_op jit(solution)/shard_map/all_gather | solution.py:988
  152.7 460.4 %reduce-scatter.7.cloned.1.call-start = ((), (), s32[]{:S(2)}) async-start(), calls=%async_computation.13 | async-start | bytes 5242880 | tf_op jit(solution)/shard_map/reduce_scatter | solution.py:1048
  152.8 2.4 copy-start.11
  153.2 208.4 %copy-start.3 = (s32[512]{0:T(512)}, s32[512]{0:T(512)S(1)}, u32[]{:S(2)}) copy-start(s32[512]{0:T(512)S(1)} %get-tuple-element.111) | copy-start | bytes 6148
  154.6 138.4 %copy-start.1 = (f32[512,128]{1,0:T(8,128)}, f32[512,128]{1,0:T(8,128)S(1)}, u32[]{:S(2)}) copy-start(f32[512,128]{1,0:T(8,128)S(1)} %get-tuple-element.119.cos_ref) | copy-start | bytes 786436
  154.6 138.4 %copy-start.2 = (f32[512,128]{1,0:T(8,128)}, f32[512,128]{1,0:T(8,128)S(1)}, u32[]{:S(2)}) copy-start(f32[512,128]{1,0:T(8,128)S(1)} %get-tuple-element.120.sin_ref) | copy-start | bytes 786436
  155.2 0.6 copy-start.33
  155.8 137.3 %copy-start = (bf16[512,2048]{1,0:T(8,128)(2,1)}, bf16[512,2048]{1,0:T(8,128)(2,1)S(1)}, u32[]{:S(2)}) copy-start(bf16[512,2048]{1,0:T(8,128)(2,1)S(1)} %fusion.12.x_ref) | copy-start | bytes 6291460
  293.0 2.2 copy-start.4
  309.8 105.2 %copy-start.5 = (bf16[512,2048]{1,0:T(8,128)(2,1)}, bf16[512,2048]{1,0:T(8,128)(2,1)S(1)}, u32[]{:S(2)}) copy-start(bf16[512,2048]{1,0:T(8,128)(2,1)S(1)} %get-tuple-element.59.q_ref) | copy-start | bytes 6291460
  309.8 24.6 %collective-permute-start = (bf16[512,1024]{1,0:T(8,128)(2,1)S(1)}, bf16[512,1024]{1,0:T(8,128)(2,1)S(1)}, u32[]{:S(2)}, u32[]{:S(2)}) collective-permute-start(bf16[512,1024]{1,0:T(8,128)(2,1)S(1)} %get-tuple-element.60), channel_id=1, source_target_pairs={{0,1},{1,2},{2,3},{4,5},{5,6},{6,7},{8,9},{9,10},{10,11},{12,13},{... | collective-permute-start | bytes 3145736 | tf_op jit(solution)/shard_map/ppermute | solution.py:1029
  334.4 26.9 %collective-permute-start.1 = (bf16[512,1024]{1,0:T(8,128)(2,1)S(1)}, bf16[512,1024]{1,0:T(8,128)(2,1)S(1)}, u32[]{:S(2)}, u32[]{:S(2)}) collective-permute-start(bf16[512,1024]{1,0:T(8,128)(2,1)S(1)} %collective-permute-done), channel_id=1, source_target_pairs={{0,1},{1,2},{2,3},{4,5},{5,6},{6,7},{8,9},{9,10},{10,11},{12,13},{... | collective-permute-start | bytes 3145736 | tf_op jit(solution)/shard_map/ppermute | solution.py:1029
  361.5 1.6 copy-start.22
  363.2 51.9 %copy-start.12 = (bf16[1,512,2048]{2,1,0:T(8,128)(2,1)S(1)}, bf16[1,512,2048]{2,1,0:T(8,128)(2,1)}, u32[]{:S(2)}) copy-start(bf16[1,512,2048]{2,1,0:T(8,128)(2,1)} %param.12) | copy-start | bytes 6291460
  415.0 8.0 copy-start.6
  415.0 8.0 copy-start.7
  415.1 10.0 copy-start.24
  423.0 2.1 copy-start.8
  423.0 2.1 copy-start.27
  536.7 184.8 %reduce-scatter.9.cloned.1.call-start = ((), (), s32[]{:S(2)}) async-start(), calls=%async_computation.14 | async-start | bytes 9437184 | tf_op jit(solution)/shard_map/reduce_scatter | solution.py:991
  537.1 32.6 %copy-start.38 = (bf16[2048,1024]{1,0:T(8,128)(2,1)S(1)}, bf16[2048,1024]{1,0:T(8,128)(2,1)}, u32[]{:S(2)}) copy-start(bf16[2048,1024]{1,0:T(8,128)(2,1)} %all-gather.9.cloned.1.call-done.wg_ref) | copy-start | bytes 12582916
  569.7 15.0 %copy-start.39 = (bf16[2048,1024]{1,0:T(8,128)(2,1)S(1)}, bf16[2048,1024]{1,0:T(8,128)(2,1)}, u32[]{:S(2)}) copy-start(bf16[2048,1024]{1,0:T(8,128)(2,1)} %all-gather.11.cloned.1.call-done.wu_ref) | copy-start | bytes 12582916
  613.2 150.3 %reduce-scatter.11.cloned.1.call-start = ((), (), s32[]{:S(2)}) async-start(), calls=%async_computation.15 | async-start | bytes 9437184 | tf_op jit(solution)/shard_map/reduce_scatter | solution.py:991
  613.2 17.6 %copy-start.40 = (bf16[2048,1024]{1,0:T(8,128)(2,1)S(1)}, bf16[2048,1024]{1,0:T(8,128)(2,1)}, u32[]{:S(2)}) copy-start(bf16[2048,1024]{1,0:T(8,128)(2,1)} %all-gather.11.cloned.1.call-done.wu_ref) | copy-start | bytes 12582916
  648.8 234.7 %reduce-scatter.13.cloned.1.call-start = ((), (), s32[]{:S(2)}) async-start(), calls=%async_computation.16 | async-start | bytes 18874368 | tf_op jit(solution)/shard_map/reduce_scatter | solution.py:991
  721.5 42.1 %copy-start.25 = (f32[2048]{0:T(1024)S(1)}, f32[2048]{0:T(1024)}, u32[]{:S(2)}) copy-start(f32[2048]{0:T(1024)} %param.19) | copy-start | bytes 24580
  721.5 42.1 %copy-start.28 = (f32[512]{0:T(512)S(1)}, f32[512]{0:T(512)}, u32[]{:S(2)}) copy-start(f32[512]{0:T(512)} %copy-done.27) | copy-start | bytes 6148
  721.5 42.1 %copy-start.15 = (bf16[512,1024]{1,0:T(8,128)(2,1)S(1)}, bf16[512,1024]{1,0:T(8,128)(2,1)}, u32[]{:S(2)}) copy-start(bf16[512,1024]{1,0:T(8,128)(2,1)} %reduce-scatter.9.cloned.1.call-done) | copy-start | bytes 3145732
  763.5 4.5 copy-start.14
  763.5 399.8 %reduce-scatter.15.cloned.1.call-start = ((), (), s32[]{:S(2)}) async-start(), calls=%async_computation.17 | async-start | bytes 5242880 | tf_op jit(solution)/shard_map/reduce_scatter | solution.py:1048
  763.6 4.4 copy-start.9
  767.4 0.6 copy-start.35
  770.9 10.9 copy-start.18
  855.8 27.7 %copy-start.17 = (bf16[1536,1024]{1,0:T(8,128)(2,1)S(1)}, bf16[1536,1024]{1,0:T(8,128)(2,1)}, u32[]{:S(2)}) copy-start(bf16[1536,1024]{1,0:T(8,128)(2,1)} %get-tuple-element.87) | copy-start | bytes 9437188
  885.0 63.7 %collective-permute-start.2 = (bf16[512,1024]{1,0:T(8,128)(2,1)}, bf16[512,1024]{1,0:T(8,128)(2,1)S(1)}, u32[]{:S(2)}, u32[]{:S(2)}) collective-permute-start(bf16[512,1024]{1,0:T(8,128)(2,1)} %get-tuple-element.105), channel_id=1, source_target_pairs={{1,0},{2,1},{3,2},{5,4},{6,5},{7,6},{9,8},{10,9},{11,10},{13,12},{... | collective-permute-start | bytes 3145736 | tf_op jit(solution)/shard_map/ppermute | solution.py:1029
  886.3 65.3 %all-to-all-start.2 = ((bf16[8,256,256]{2,1,0:T(8,128)(2,1)}), bf16[8,256,256]{2,1,0:T(8,128)(2,1)S(1)}, u32[]{:S(2)}, u32[]{:S(2)}) async-start(bf16[8,256,256]{2,1,0:T(8,128)(2,1)} %bitcast.67), calls=%async_computation.8 | async-start | bytes 2097152 | tf_op jit(solution)/shard_map/all_to_all | solution.py:1001
  889.9 285.8 %reduce-scatter.17.cloned.1.call-start = ((), (), s32[]{:S(2)}) async-start(), calls=%async_computation.18 | async-start | bytes 5242880 | tf_op jit(solution)/shard_map/reduce_scatter | solution.py:1048
  950.3 51.5 %collective-permute-start.3 = (bf16[512,1024]{1,0:T(8,128)(2,1)S(1)}, bf16[512,1024]{1,0:T(8,128)(2,1)S(1)}, u32[]{:S(2)}, u32[]{:S(2)}) collective-permute-start(bf16[512,1024]{1,0:T(8,128)(2,1)S(1)} %add_convert_fusion.3), channel_id=1, source_target_pairs={{1,0},{2,1},{3,2},{5,4},{6,5},{7,6},{9,8},{10,9},{11,10},{13,12},{... | collective-permute-start | bytes 3145736 | tf_op jit(solution)/shard_map/ppermute | solution.py:1029
  1001.8 1.0 copy-start.19
  1007.1 5.1 copy-start.13
  1007.1 5.1 copy-start.31
  1007.1 5.1 copy-start.34
  1007.1 5.1 copy-start.41
  1023.3 144.3 %copy-start.16 = (bf16[512,1024]{1,0:T(8,128)(2,1)S(1)}, bf16[512,1024]{1,0:T(8,128)(2,1)}, u32[]{:S(2)}) copy-start(bf16[512,1024]{1,0:T(8,128)(2,1)} %reduce-scatter.9.cloned.1.call-done) | copy-start | bytes 3145732
  1023.3 144.3 %copy-start.26 = (f32[2048]{0:T(1024)S(1)}, f32[2048]{0:T(1024)}, u32[]{:S(2)}) copy-start(f32[2048]{0:T(1024)} %param.19) | copy-start | bytes 24580
  1023.3 144.3 %copy-start.29 = (f32[512]{0:T(512)S(1)}, f32[512]{0:T(512)}, u32[]{:S(2)}) copy-start(f32[512]{0:T(512)} %copy-done.27) | copy-start | bytes 6148
  1023.3 144.3 %copy-start.36 = (f32[512]{0:T(512)S(1)}, f32[512]{0:T(512)}, u32[]{:S(2)}) copy-start(f32[512]{0:T(512)} %copy-done.35) | copy-start | bytes 6148
  1163.4 19.7 %all-to-all-start = ((bf16[8,256,256]{2,1,0:T(8,128)(2,1)}), bf16[8,256,256]{2,1,0:T(8,128)(2,1)}, u32[]{:S(2)}, u32[]{:S(2)}) async-start(bf16[8,256,256]{2,1,0:T(8,128)(2,1)} %bitcast.68), calls=%async_computation.5 | async-start | bytes 2097152 | tf_op jit(solution)/shard_map/all_to_all | solution.py:1001
  1167.7 18.9 %copy-start.23 = (f32[256,256]{1,0:T(8,128)S(1)}, f32[256,256]{1,0:T(8,128)}, u32[]{:S(2)}) copy-start(f32[256,256]{1,0:T(8,128)} %get-tuple-element.90) | copy-start | bytes 786436
  1167.7 19.7 %copy-start.37 = (f32[2,2048]{1,0:T(2,128)S(1)}, f32[2,2048]{1,0:T(2,128)}, u32[]{:S(2)}) copy-start(f32[2,2048]{1,0:T(2,128)} %get-tuple-element.88) | copy-start | bytes 49156
  1183.1 18.9 %all-to-all-start.1 = ((bf16[8,256,256]{2,1,0:T(8,128)(2,1)}), bf16[8,256,256]{2,1,0:T(8,128)(2,1)S(1)}, u32[]{:S(2)}, u32[]{:S(2)}) async-start(bf16[8,256,256]{2,1,0:T(8,128)(2,1)} %bitcast.69), calls=%async_computation.7 | async-start | bytes 2097152 | tf_op jit(solution)/shard_map/all_to_all | solution.py:1001
  1190.9 12.8 %copy-start.21 = (f32[256,512]{1,0:T(8,128)S(1)}, f32[256,512]{1,0:T(8,128)}, u32[]{:S(2)}) copy-start(f32[256,512]{1,0:T(8,128)} %get-tuple-element.135) | copy-start | bytes 1572868
  1190.9 13.6 %copy-start.20 = (f32[256,512]{1,0:T(8,128)S(1)}, f32[256,512]{1,0:T(8,128)}, u32[]{:S(2)}) copy-start(f32[256,512]{1,0:T(8,128)} %get-tuple-element.138) | copy-start | bytes 1572868
Sparse Core Ops, SparseCore 0:
  68.6 84.1 all-gather.4
  154.3 78.7 all-gather.8
  234.6 78.7 all-gather.10
  315.2 88.0 all-gather.6
  536.8 76.3 reduce-scatter.6
  616.9 71.8 reduce-scatter.8
  692.2 71.2 reduce-scatter.10
  767.5 115.9 reduce-scatter.12
  885.9 116.5 reduce-scatter.14
  1004.6 77.7 reduce-scatter.16

commit v3 on v2

--- a/solution.py
+++ b/solution.py
@@ -194,15 +194,80 @@
 
 
 def attend_back_kernel(
-    reach, q_ref, do_ref, o_ref, k_ref, v_ref, lse_ref, low_ref, cos_ref, sin_ref,
-    dq_ref, dkv_ref, bias_ref, dk_acc, dv_acc,
+    reach, wide, z_size,
+    q_ref, do_ref, o_ref, k_ref, v_ref, lse_ref, low_ref, cos_ref, sin_ref, cos_all, sin_all,
+    h_ref, att_ref,
+    dq_ref, dkv_ref, wo_out,
+    bias_ref, dk_acc, dv_acc, own_part, send_part, recv_part, kv_send, kv_recv,
+    *scratch,
 ):
+    ring = Reduce(wide, *scratch[:6])
+    sums, zrecv, z_send, z_recv = scratch[6:]
     block, half, tile, pair = (pl.program_id(at) for at in range(4))
+    steps = pl.num_programs(1) * pl.num_programs(2) * pl.num_programs(3)
     inner = (half * pl.num_programs(2) + tile) * pl.num_programs(3) + pair
-
-    @pl.when((block == 0) & (inner == 0))
+    step = block * steps + inner
+    blocks = own_part.shape[0]
+    rows = own_part.shape[1]
+    count = reach // rows
+    place = lax.axis_index("tensor")
+
+    def exchange(at, distance):
+        return pltpu.make_async_remote_copy(
+            src_ref=send_part.at[at, pl.ds((count - distance) * rows, rows)],
+            dst_ref=recv_part.at[at, distance - 1],
+            send_sem=kv_send.at[at, distance - 1], recv_sem=kv_recv.at[at, distance - 1],
+            device_id={"tensor": (place + z_size - distance) % z_size}, device_id_type=MESH,
+        )
+
+    def each_exchange(at, condition, action):
+        for distance in range(1, count + 1):
+            pl.when(condition(distance))(
+                functools.partial(action, exchange(at, distance), at, distance)
+            )
+
+    def along(at):
+        cols = wo_out.shape[1]
+        other = (place + at + 1) % z_size
+        return pltpu.make_async_remote_copy(
+            src_ref=sums.at[:, pl.ds(pl.multiple_of(other * cols, LANES), cols)],
+            dst_ref=zrecv.at[at], send_sem=z_send.at[at], recv_sem=z_recv.at[at],
+            device_id={"tensor": other}, device_id_type=MESH,
+        )
+
+    @pl.when(step == 0)
     def _():
+        barrier = pltpu.get_barrier_semaphore()
+        peers = [{"dp": peer} for peer in ring.peers]
+        peers += [{"tensor": (place + at) % z_size} for at in range(1, z_size)]
+        for peer in peers:
+            pl.semaphore_signal(barrier, inc=1, device_id=peer, device_id_type=MESH)
+        pl.semaphore_wait(barrier, len(peers))
         fill_bias(bias_ref, low_ref, reach)
+
+    @pl.when((step % 2 == 0) & (step < 16))
+    def _():
+        chunk, target = ring.chunk(step // 2)
+        part = target.shape[0]
+        x = h_ref[:, pl.ds(pl.multiple_of(chunk * part, part), part)].T
+
+        @pl.loop(0, att_ref.shape[1] // NTILE)
+        def _(at):
+            n = pl.ds(pl.multiple_of(at * NTILE, NTILE), NTILE)
+            target[:, n] = dot_nn(x, att_ref[:, n]).astype(BF16)
+
+        ring.after(step // 2)
+
+    pl.when(step == 19)(ring.pass_on)
+
+    @pl.when(step == 27)
+    def _():
+        def store(here, value):
+            sums[here, :] = value.astype(BF16)
+
+        ring.finish(store)
+        for at in range(z_size - 1):
+            along(at).start()
 
     @pl.when(inner == 0)
     def _():
@@ -230,13 +295,44 @@
     dq = gather_pair(dot_tn(key, dscore), half) * SCALE
     dq_ref[...] = (dq * cos_ref[...] - swap_halves(dq) * sin_ref[...]).astype(BF16)
 
-    @pl.when(inner == pl.num_programs(1) * pl.num_programs(2) * pl.num_programs(3) - 1)
+    @pl.when(inner == steps - 1)
     def _():
-        dkv_ref[:, :LANES] = (dk_acc[...] * SCALE).astype(BF16)
-        dkv_ref[:, LANES:] = dv_acc[...].astype(BF16)
-
-
-def attend_back(q, do, att, kv, lse, low, cosine, sine):
+        send_part[block, :, :LANES] = (dk_acc[:reach] * SCALE).astype(BF16)
+        send_part[block, :, LANES:] = dv_acc[:reach].astype(BF16)
+        own_part[block, :, :LANES] = dk_acc[reach:] * SCALE
+        own_part[block, :, LANES:] = dv_acc[reach:]
+        each_exchange(block, lambda distance: place >= distance, lambda copy, *_: copy.start())
+
+    @pl.when(step == blocks * steps - 1)
+    def _():
+        def collect(copy, at, distance):
+            copy.wait_recv()
+            own_part[at] += recv_part[at, distance - 1].astype(F32)
+
+        for at in range(blocks):
+            each_exchange(at, lambda distance: place + distance < z_size, collect)
+            dkey = own_part[at, :, :LANES]
+            dkey = dkey * cos_all[...] - swap_halves(dkey) * sin_all[...]
+            dkv_ref[:, 2 * at * LANES : (2 * at + 1) * LANES] = dkey.astype(BF16)
+            dkv_ref[:, (2 * at + 1) * LANES : (2 * at + 2) * LANES] = own_part[
+                at, :, LANES:
+            ].astype(BF16)
+        total = sums[:, pl.ds(pl.multiple_of(place * wo_out.shape[1], LANES), wo_out.shape[1])]
+        total = total.astype(F32)
+        for at in range(z_size - 1):
+            along(at).wait_recv()
+            total += zrecv[at].astype(F32)
+        wo_out[...] = total
+        for at in range(z_size - 1):
+            along(at).wait_send()
+        for at in range(blocks):
+            each_exchange(
+                at, lambda distance: place >= distance, lambda copy, *_: copy.wait_send()
+            )
+        ring.sent()
+
+
+def attend_back(q, do, att, kv, lse, low, cosine, sine, h, dp_size, z_size):
     rows, width = q.shape
     keys = kv.shape[0]
     reach = keys - rows
@@ -245,13 +341,22 @@
     heads = kv.shape[1] // LANES
     per_head = pairs // heads
     span = reach + QTILE
+    blocks = heads // 2
+    part = h.shape[1] // GROUP
+    cols = width // z_size
 
     def pair_at(g, h, t, p):
         return (t, (2 * g + h) * per_head + p)
 
+    def whole(shape):
+        return pl.BlockSpec(shape, lambda g, h, t, p: (0, 0), pipeline_mode=pl.Buffered(1))
+
+    table = pl.BlockSpec((QTILE, LANES), lambda g, h, t, p: (t, 0))
     return pl.pallas_call(
-        functools.partial(attend_back_kernel, reach),
-        grid=(heads // 2, 2, tiles, per_head),
+        functools.partial(
+            attend_back_kernel, reach, 2 * math.isqrt(dp_size // GROUP), z_size
+        ),
+        grid=(blocks, 2, tiles, per_head),
         in_specs=[
             pl.BlockSpec((QTILE, LANES), pair_at),
             pl.BlockSpec((QTILE, LANES), pair_at),
@@ -262,50 +367,50 @@
                 (1, 1, 2 * QTILE),
                 lambda g, h, t, p: (((2 * g + h) * tiles + t) * per_head + p, 0, 0),
             ),
-            pl.BlockSpec((1, rows), lambda g, h, t, p: (0, 0)),
-            pl.BlockSpec((QTILE, LANES), lambda g, h, t, p: (t, 0)),
-            pl.BlockSpec((QTILE, LANES), lambda g, h, t, p: (t, 0)),
+            whole((1, rows)),
+            table,
+            table,
+            whole((rows, LANES)),
+            whole((rows, LANES)),
+            whole(h.shape),
+            whole(att.shape),
         ],
         out_specs=[
             pl.BlockSpec((QTILE, LANES), pair_at),
-            pl.BlockSpec((keys, 2 * LANES), lambda g, h, t, p: (0, g)),
+            pl.BlockSpec((rows, kv.shape[1]), lambda g, h, t, p: (0, 0)),
+            pl.BlockSpec((part, cols), lambda g, h, t, p: (0, 0)),
         ],
         out_shape=[
             jax.ShapeDtypeStruct((rows, width), BF16),
-            jax.ShapeDtypeStruct(kv.shape, BF16),
+            jax.ShapeDtypeStruct((rows, kv.shape[1]), BF16),
+            jax.ShapeDtypeStruct((part, cols), F32),
         ],
         scratch_shapes=[
             pltpu.VMEM((tiles, span, QTILE), F32),
             pltpu.VMEM((keys, LANES), F32),
             pltpu.VMEM((keys, LANES), F32),
-        ],
-        compiler_params=pltpu.CompilerParams(vmem_limit_bytes=56 << 20),
+            pltpu.VMEM((blocks, rows, 2 * LANES), F32),
+            pltpu.VMEM((blocks, reach, 2 * LANES), BF16),
+            pltpu.VMEM((blocks, reach // rows, rows, 2 * LANES), BF16),
+            pltpu.SemaphoreType.DMA((blocks, reach // rows)),
+            pltpu.SemaphoreType.DMA((blocks, reach // rows)),
+        ]
+        + Reduce.scratch(part, width)
+        + [
+            pltpu.VMEM((part, width), BF16),
+            pltpu.VMEM((z_size - 1, part, cols), BF16),
+            pltpu.SemaphoreType.DMA((z_size - 1,)),
+            pltpu.SemaphoreType.DMA((z_size - 1,)),
+        ],
+        compiler_params=pltpu.CompilerParams(
+            collective_id=5, has_side_effects=True, vmem_limit_bytes=60 << 20
+        ),
         cost_estimate=pl.CostEstimate(
             flops=40 * rows * span * LANES * pairs,
             bytes_accessed=8 * rows * width + 4 * keys * kv.shape[1],
             transcendentals=2 * rows * span * pairs,
         ),
-    )(q, do, att, kv, kv, lse, low, cosine, sine)
-
-
-def finish_dkv_kernel(own_ref, recv_ref, cos_ref, sin_ref, out_ref):
-    total = own_ref[...].astype(F32) + recv_ref[...].astype(F32)
-    key = total[:, :LANES]
-    out_ref[:, :LANES] = (key * cos_ref[...] - swap_halves(key) * sin_ref[...]).astype(BF16)
-    out_ref[:, LANES:] = total[:, LANES:].astype(BF16)
-
-
-def finish_dkv(own, recv, cosine, sine):
-    rows, width = own.shape
-    spec = pl.BlockSpec((rows, 2 * LANES), lambda g: (0, g))
-    table = pl.BlockSpec((rows, LANES), lambda g: (0, 0))
-    return pl.pallas_call(
-        finish_dkv_kernel,
-        grid=(width // (2 * LANES),),
-        in_specs=[spec, spec, table, table],
-        out_specs=spec,
-        out_shape=jax.ShapeDtypeStruct((rows, width), BF16),
-    )(own, recv, cosine, sine)
+    )(q, do, att, kv, kv, lse, low, cosine, sine, cosine, sine, h, att)
 
 
 MESH = pl.DeviceIdType.MESH
@@ -772,15 +877,89 @@
             self.copy(name).wait_send()
 
 
-def tail_kernel(
-    wide, z_size, x_ref, h_ref, dq_ref, dkv_ref, att_ref, gain_ref,
-    wo_out, wq_out, wkv_out, gain_out,
-    *scratch,
+def hidden_back_kernel(
+    wide, dgate_ref, dup_ref, wg_ref, wu_ref, out_ref, loaded, load_sem, *scratch
 ):
-    own_scratch, (sums, zrecv, gain_z, gain_p, z_send, z_recv, g_send, g_recv) = (
-        scratch[:18], scratch[18:],
-    )
-    rings = [Reduce(wide, *own_scratch[6 * at : 6 * at + 6]) for at in range(3)]
+    ring = Reduce(wide, *scratch)
+    rows = out_ref.shape[0]
+
+    def loads(step):
+        chunk, _ = ring.chunk(step)
+        here = pl.ds(pl.multiple_of(chunk * rows, rows), rows)
+        return [
+            pltpu.make_async_copy(
+                ref.at[here], loaded.at[step % 2, at], load_sem.at[step % 2, at]
+            )
+            for at, ref in enumerate((dgate_ref, dup_ref))
+        ]
+
+    for copy in loads(0):
+        copy.start()
+    meet(ring.peers)
+
+    @pl.loop(0, 8)
+    def _(step):
+        @pl.when(step < 7)
+        def _():
+            for copy in loads(step + 1):
+                copy.start()
+
+        for copy in loads(step):
+            copy.wait()
+        _, target = ring.chunk(step)
+        dgate, dup = loaded[step % 2, 0], loaded[step % 2, 1]
+
+        @pl.loop(0, out_ref.shape[1] // NTILE)
+        def _(at):
+            n = pl.ds(pl.multiple_of(at * NTILE, NTILE), NTILE)
+            value = dot_nt(dgate, wg_ref[n, :]) + dot_nt(dup, wu_ref[n, :])
+            target[:, n] = value.astype(BF16)
+
+        ring.after(step)
+
+    ring.pass_on()
+
+    def store(here, value):
+        out_ref[here, :] = value
+
+    ring.finish(store)
+    ring.sent()
+
+
+def hidden_back(dgate, dup, wg, wu, dp_size):
+    tokens, cols = dgate.shape
+    width = wg.shape[0]
+    rows = tokens // GROUP
+    far = pl.BlockSpec(memory_space=pl.ANY)
+    near = pl.BlockSpec(memory_space=pltpu.VMEM)
+    return pl.pallas_call(
+        functools.partial(hidden_back_kernel, 2 * math.isqrt(dp_size // GROUP)),
+        in_specs=[far, far, near, near],
+        out_specs=near,
+        out_shape=jax.ShapeDtypeStruct((rows, width), F32),
+        scratch_shapes=[
+            pltpu.VMEM((2, 2, rows, cols), BF16),
+            pltpu.SemaphoreType.DMA((2, 2)),
+        ]
+        + Reduce.scratch(rows, width),
+        compiler_params=pltpu.CompilerParams(
+            collective_id=6, has_side_effects=True, vmem_limit_bytes=60 << 20
+        ),
+        cost_estimate=pl.CostEstimate(
+            flops=4 * tokens * width * cols,
+            bytes_accessed=4 * tokens * cols + 4 * width * cols + 4 * rows * width,
+            transcendentals=0,
+        ),
+    )(dgate, dup, wg, wu)
+
+
+def tail_kernel(wide, z_size, mlp_count, x_ref, dq_ref, dkv_ref, gain_ref, *refs):
+    mlp_ins, refs = refs[:mlp_count], refs[mlp_count:]
+    wq_out, wkv_out, gain_out = refs[:3]
+    mlp_outs, scratch = refs[3 : 3 + mlp_count], refs[3 + mlp_count :]
+    own_scratch = scratch[:12]
+    sums, zrecv, gain_z, gain_p, z_send, z_recv, g_send, g_recv, m_own, m_send, m_recv = scratch[12:]
+    rings = [Reduce(wide, *own_scratch[6 * at : 6 * at + 6]) for at in range(2)]
     place = lax.axis_index("tensor")
     dp = lax.axis_index("dp")
     row, col, core = rings[0].at
@@ -798,6 +977,31 @@
     for peer in along + around:
         pl.semaphore_signal(barrier, inc=1, device_id=peer, device_id_type=MESH)
     pl.semaphore_wait(barrier, len(along) + len(around))
+
+    mlp_copies = []
+    for at in range(mlp_count):
+        src, dst = mlp_ins[at], mlp_outs[at]
+        part, cols = dst.shape[0], src.shape[1]
+        here = pl.ds(pl.multiple_of(mine * cols, LANES), cols)
+        for index, flip in enumerate(flips):
+            y, x, c = (row + flip[0]) % 2, (col + flip[1]) % 2, (core + flip[2]) % 2
+            other = 4 * y + 2 * x + c
+            mlp_copies.append(
+                pltpu.make_async_remote_copy(
+                    src_ref=src.at[pl.ds(pl.multiple_of(other * part, part), part)],
+                    dst_ref=dst.at[:, here],
+                    send_sem=m_send.at[at, index], recv_sem=m_recv.at[at, index],
+                    device_id=device(flip), device_id_type=MESH,
+                )
+            )
+        mlp_copies.append(
+            pltpu.make_async_copy(
+                src.at[pl.ds(pl.multiple_of(mine * part, part), part)],
+                dst.at[:, here], m_own.at[at],
+            )
+        )
+    for copy in mlp_copies:
+        copy.start()
 
     gain_z[place] = gain_ref[...]
     gain_copies = [
@@ -810,19 +1014,18 @@
     for copy in gain_copies:
         copy.start()
 
-    lefts = (h_ref, x_ref, x_ref)
-    rights = (att_ref, dq_ref, dkv_ref)
+    rights = (dkv_ref, dq_ref)
     rows = sums.shape[0]
-    outs = (wo_out, wq_out, wkv_out)
+    outs = (wkv_out, wq_out)
     z_copies = []
     for index, ring in enumerate(rings):
-        left, right = lefts[index], rights[index]
+        right = rights[index]
         cols = right.shape[1]
 
         @pl.loop(0, 8)
         def _(step):
             chunk, target = ring.chunk(step)
-            x = left[:, pl.ds(pl.multiple_of(chunk * rows, rows), rows)].T
+            x = x_ref[:, pl.ds(pl.multiple_of(chunk * rows, rows), rows)].T
 
             @pl.loop(0, cols // NTILE)
             def _(at):
@@ -866,12 +1069,12 @@
             z_copies.append(copy)
             copy.start()
 
-    starts = [0, rights[0].shape[1], rights[0].shape[1] + rights[1].shape[1]]
+    starts = [0, rights[0].shape[1]]
     for index, ring in enumerate(rings):
         ring.pass_on()
         if index:
             send_along(index - 1, rings[index - 1], starts[index - 1])
-    send_along(2, rings[2], starts[2])
+    send_along(1, rings[1], starts[1])
 
     for copy in gain_copies[z_size - 1 :]:
         copy.wait_recv()
@@ -882,7 +1085,7 @@
 
     for copy in z_copies:
         copy.wait_recv()
-    for index in range(3):
+    for index in range(2):
         part = rights[index].shape[1] // z_size
         own = pl.ds(pl.multiple_of(starts[index] + place * part, LANES), part)
         value = sums[:, own].astype(F32)
@@ -893,33 +1096,42 @@
         copy.wait_send()
     for ring in rings:
         ring.sent()
-
-
-def attention_grads(x, h, dq, dkv, att, gains, dp_size, z_size):
+    for copy in mlp_copies:
+        copy.wait()
+
+
+def last_grads(x, dq, dkv, gains, mlp, dp_size, z_size):
     tokens, width = x.shape
     rows = width // GROUP
     near = pl.BlockSpec(memory_space=pltpu.VMEM)
-    sizes = [att.shape[1], dq.shape[1], dkv.shape[1]]
+    far = pl.BlockSpec(memory_space=pl.ANY)
+    sizes = [dkv.shape[1], dq.shape[1]]
     scratch = []
     for cols in sizes:
         scratch += Reduce.scratch(rows, cols)
     total = sum(sizes)
     return pl.pallas_call(
-        functools.partial(tail_kernel, 2 * math.isqrt(dp_size // GROUP), z_size),
-        in_specs=[near] * 6,
-        out_specs=[near] * 4,
-        out_shape=[jax.ShapeDtypeStruct((rows, cols // z_size), F32) for cols in sizes]
-        + [jax.ShapeDtypeStruct(gains.shape, F32)],
+        functools.partial(tail_kernel, 2 * math.isqrt(dp_size // GROUP), z_size, len(mlp)),
+        in_specs=[near] * 4 + [far] * len(mlp),
+        out_specs=[near] * 3 + [far] * len(mlp),
+        out_shape=[jax.ShapeDtypeStruct((rows, cols // z_size), F32) for cols in sizes[::-1]]
+        + [jax.ShapeDtypeStruct(gains.shape, F32)]
+        + [
+            jax.ShapeDtypeStruct((m.shape[0] // GROUP, GROUP * m.shape[1]), BF16) for m in mlp
+        ],
         scratch_shapes=scratch
         + [
             pltpu.VMEM((rows, total), BF16),
             pltpu.VMEM((z_size - 1, rows, total // z_size), BF16),
             pltpu.VMEM((z_size, *gains.shape), F32),
             pltpu.VMEM((GROUP, *gains.shape), F32),
-            pltpu.SemaphoreType.DMA((3, z_size - 1)),
-            pltpu.SemaphoreType.DMA((3, z_size - 1)),
+            pltpu.SemaphoreType.DMA((2, z_size - 1)),
+            pltpu.SemaphoreType.DMA((2, z_size - 1)),
             pltpu.SemaphoreType.DMA((z_size - 1 + GROUP - 1,)),
             pltpu.SemaphoreType.DMA((z_size - 1 + GROUP - 1,)),
+            pltpu.SemaphoreType.DMA((len(mlp),)),
+            pltpu.SemaphoreType.DMA((len(mlp), GROUP - 1)),
+            pltpu.SemaphoreType.DMA((len(mlp), GROUP - 1)),
         ],
         compiler_params=pltpu.CompilerParams(
             collective_id=4, has_side_effects=True, vmem_limit_bytes=60 << 20
@@ -927,7 +1139,7 @@
         cost_estimate=pl.CostEstimate(
             flops=2 * LONG, bytes_accessed=4 * tokens * total, transcendentals=0
         ),
-    )(x, h, dq, dkv, att, gains)
+    )(x, dq, dkv, gains, *mlp)
 
 
 class Layout:
@@ -990,16 +1202,6 @@
     def scatter(self, array):
         return lax.psum_scatter(
             array, "dp", scatter_dimension=0, axis_index_groups=self.groups(), tiled=True
-        )
-
-    def spread(self, array):
-        return lax.all_to_all(
-            array, "dp", 1, 0, axis_index_groups=self.groups(), tiled=True
-        )
-
-    def unspread(self, array):
-        return lax.all_to_all(
-            array, "dp", 0, 1, axis_index_groups=self.groups(), tiled=True
         )
 
 
@@ -1052,6 +1254,7 @@
     r1 = rms_scale(x)
     xn = (x * r1 * attn_gain).astype(BF16)
     q, kv = project_qkv(xn, wq, wkv, cosine, sine)
+    grad, kv = lax.optimization_barrier((cotangent[0], kv))
     pieces, moved = [kv], kv
     for _ in range(reach // rows):
         moved = shift(moved, 1)
@@ -1062,7 +1265,6 @@
 
     r2 = rms_scale(h)
     hn, gate, up, hidden = gate_up((h * r2 * mlp_gain).astype(BF16), wg, wu, dp_size)
-    grad, wd = lax.optimization_barrier((cotangent[0], wd))
     dy = layout.gather(grad)
     total_wd = dot_tn(dy, hidden).astype(BF16)
     dy, total_wd = lax.optimization_barrier((dy, total_wd))
@@ -1072,53 +1274,41 @@
     dhid = dot_nn(dy, wd)
     dgate = (dhid * up * sigma * (1.0 + gate * (1.0 - sigma))).astype(BF16)
     dup = (dhid * gate * sigma).astype(BF16)
-    half = width // 2
-    left_dhn = (dot_nt(dgate, wg[:half]) + dot_nt(dup, wu[:half])).astype(BF16)
-    dgate, dup, left_dhn, part_wd = lax.optimization_barrier((dgate, dup, left_dhn, part_wd))
-    dhn_left = layout.scatter(left_dhn)
-    right_dhn = (dot_nt(dgate, wg[half:]) + dot_nt(dup, wu[half:])).astype(BF16)
-    hn, hidden, right_dhn = lax.optimization_barrier((hn, hidden, right_dhn))
-    dhn_right = layout.scatter(right_dhn)
     total_wg = dot_tn(hn, dgate).astype(BF16)
+    dgate, total_wg = lax.optimization_barrier((dgate, total_wg))
+    part_wg = along_z(total_wg)
+    dhn = hidden_back(dgate, dup, wg, wu, dp_size)
+    hn, hidden, dhn, part_wd = lax.optimization_barrier((hn, hidden, dhn, part_wd))
     total_wu = dot_tn(hn, dup).astype(BF16)
     partial_out = dot_nt(hidden, wd).astype(BF16)
-    dhn_left, dhn_right, total_wg, total_wu, partial_out = lax.optimization_barrier(
-        (dhn_left, dhn_right, total_wg, total_wu, partial_out)
+    dhn, total_wu, partial_out, part_wg = lax.optimization_barrier(
+        (dhn, total_wu, partial_out, part_wg)
     )
-    dhn = jnp.concatenate([dhn_left, dhn_right], axis=1).astype(F32)
+    part_wu = along_z(total_wu)
     gain_two, dh_norm = norm_back(h, r2, mlp_gain, dhn)
     dh = cotangent[0].astype(F32) + dh_norm
 
     dhb = dh.astype(BF16)
     datt = dot_nn(dhb, wo).astype(BF16)
-    dq, dkv_all = attend_back(q, datt, att, kv_all, lse, low, cosine, sine)
+    datt, partial_out = lax.optimization_barrier((datt, partial_out))
     out_sum = layout.scatter(partial_out)
-    out_sum, dkv_all = lax.optimization_barrier((out_sum, dkv_all))
-    output = h + out_sum.astype(F32)
-    count = reach // rows
-    moved = dkv_all[:rows]
-    for at in range(1, count + 1):
-        moved = shift(moved, -1)
-        if at < count:
-            here = dkv_all[at * rows : (at + 1) * rows]
-            moved = (moved.astype(F32) + here.astype(F32)).astype(BF16)
-    dkv = finish_dkv(dkv_all[count * rows :], moved, cosine, sine)
+    dq, dkv, wo_grad = attend_back(
+        q, datt, att, kv_all, lse, low, cosine, sine, layout.from_cols(dhb), dp_size, z_size
+    )
+    dq, part_wu = lax.optimization_barrier((dq, part_wu))
     dxn = dot_nt(dq, wq) + dot_nt(dkv, wkv)
     gain_one, dx_norm = norm_back(x, r1, attn_gain, dxn)
     input_grad = (dh + dx_norm).astype(BF16)
-    out_sum, total_wg, total_wu = lax.optimization_barrier((out_sum, total_wg, total_wu))
-    part_wg, part_wu = along_z(total_wg), along_z(total_wu)
     gains = layout.sum_outer(jnp.stack([gain_one, gain_two]))
-    wo_grad, wq_grad, wkv_grad, gains = attention_grads(
-        layout.from_cols(xn), layout.from_cols(dhb), dq, dkv, att, gains, dp_size, z_size
+    wq_grad, wkv_grad, gains, wd_grad, wg_grad, wu_grad = last_grads(
+        layout.from_cols(xn), dq, dkv, gains, (part_wd, part_wg, part_wu), dp_size, z_size
     )
-    wo_grad, wq_grad, wkv_grad = (
-        layout.scatter_outer(grad) for grad in (wo_grad, wq_grad, wkv_grad)
+    wo_grad, wq_grad, wkv_grad, wd_grad, wg_grad, wu_grad = (
+        layout.scatter_outer(grad).astype(F32)
+        for grad in (wo_grad, wq_grad, wkv_grad, wd_grad, wg_grad, wu_grad)
     )
-    wd_grad, wg_grad, wu_grad = (
-        layout.scatter_outer(layout.unspread(part)).astype(F32)
-        for part in (part_wd, part_wg, part_wu)
-    )
+    gains, out_sum = lax.optimization_barrier((gains, out_sum))
+    output = h + out_sum.astype(F32)
     key_cols = w_key.shape[1]
     return (
         output.astype(BF16)[None],

time: 1220 us -> 1010 us (0.83)
  waiting for transfers between devices: 336 us -> 43.9 us
  Pallas kernels: 568 us -> 723 us
  matrix products: 231 us -> 154 us
    pallas_call x3, Pallas kernels: 218 us -> 375 us  [the longest x1 149 us: attend_back(): pl.pallas_call(functools.partial(attend_back_kernel, reach, 2 * math.isqr...]
    ppermute x4 -> x2, waiting for transfers between devices: 153 us -> 43 us  [shift(): return lax.ppermute(array, 'tensor', pairs)]
    all_gather x3, waiting for transfers between devices: 82.8 us -> 0.02 us  [per_device(): lax.all_gather(w, 'tensor', axis=1, tiled=True)]
    dot_general x8 -> x4, matrix products: 115 us -> 44.6 us  [dot_nt(): lax.dot_general(left, right, (((1,), (1,)), ((), ())), preferred_element_...]
    reduce_scatter x3 -> x1, waiting for transfers between devices: 69.6 us -> 0.01 us  [scatter(): lax.psum_scatter(array, 'dp', scatter_dimension=0, axis_index_groups=self...]
    all_to_all x3 -> x0, waiting for transfers between devices: 18.4 us -> none  [unspread(): lax.all_to_all(array, 'dp', 0, 1, axis_index_groups=self.groups(), tiled=...]
  transfers between devices with their start and end apart: 17 -> 10, of which waited for: 10 -> 2; matrix products, arithmetic and copies ran while one was open for 20% -> 18% of each run, Pallas kernels for 42% -> 67%
where the time goes in v3:
time: 1010 us; the launch traced here: 997 us
  Pallas kernels  723 us (72%)
  matrix products  154 us (15%)
  waiting for transfers between devices  43.9 us (4%)
  other arithmetic  29 us (3%)
  local copies, waits for them, and re-layouts  16.3 us (2%)
  starting transfers between devices  15.8 us (2%)
  between operations  14.9 us (1%)
    pallas_call x1, Pallas kernels, attend_back(): pl.pallas_call(functools.partial(attend_back_kernel, reach, 2 * math.isqr...  149 us
    pallas_call x1, Pallas kernels, last_grads(): pl.pallas_call(functools.partial(tail_kernel, 2 * math.isqrt(dp_size // G...  138 us
    pallas_call x1, Pallas kernels, gather_rows(): pl.pallas_call(functools.partial(gather_kernel, 2 * math.isqrt(dp_size //...  135 us
    pallas_call x1, Pallas kernels, hidden_back(): pl.pallas_call(functools.partial(hidden_back_kernel, 2 * math.isqrt(dp_si...  88 us
    pallas_call x1, Pallas kernels, gate_up(): pl.pallas_call(functools.partial(gate_up_kernel, 2 * math.isqrt(dp_size /...  85.9 us
    dot_general x3, matrix products, dot_tn(): lax.dot_general(left, right, (((0,), (0,)), ((), ())), preferred_element_...  69.1 us
    pallas_call x1, Pallas kernels, spread_weights(): pl.pallas_call(functools.partial(spread_kernel, 2 * math.isqrt(dp_size //...  59.6 us
    pallas_call x1, Pallas kernels, attend(): pl.pallas_call(functools.partial(attend_kernel, reach), grid=(heads, tile...  51.9 us
  transfers between devices with their start and end apart: 10, of which 2 were waited for; matrix products, arithmetic and copies ran while one was open for 18% of the time, Pallas kernels for 67%

profile of v3, /device:TPU:0, one launch (start us, length us, event | category | flops | bytes accessed | tf_op | source)
XLA Modules:
  0.0 997.4 jit_solution(7585418756153754331)
XLA Ops:
  7.2 0.0 all-gather.5.cloned.1.call-start
  7.2 1.5 pad_maximum_fusion.2.refs_3_
  8.8 59.6 %shard_map.203 = (bf16[2048,256]{1,0:T(8,128)(2,1)}, bf16[2048,256]{1,0:T(8,128)(2,1)}, bf16[2048,256]{1,0:T(8,128)(2,1)}, bf16[256,1024]{1,0:T(8,128)(2,1)}, bf...) custom-call(bf16[256,2048]{1,0:T(8,128)(2,1)} %refs_0_.1, bf16[256,2048]{1,0:T(8,128)(2,1)} %refs_1_.1, ...), custom_call_target="tpu_custom_call" | custom-call | flops 60000002048 | tf_op jit(solution)/shard_map/pallas_call | solution.py:513
  68.4 0.0 all-gather.7.cloned.1.call-start
  68.5 0.7 all-gather.7.cloned.1.call-update
  69.2 0.0 all-gather.9.cloned.1.call-start
  69.2 135.4 %shard_map.204 = (bf16[2048,1024]{1,0:T(8,128)(2,1)}, bf16[2048,2048]{1,0:T(8,128)(2,1)}, bf16[2048,2048]{1,0:T(8,128)(2,1)}) custom-call(bf16[256,1024]{1,0:T(8,128)(2,1)} %get-tuple-element.57.refs_0_, bf16[256,2048]{1,0:T(8,128)(2,1)} %get-tuple-element.58.refs_1_, bf16[256,2048]{1,0:T(8,128)(2,1)} %get-tuple-element.59.refs_2_), custom_call_target="tpu_custom_call" | custom-call | flops 120000004096 | tf_op jit(solution)/shard_map/pallas_call | solution.py:637
  204.6 0.1 convert_reduce_fusion
  204.8 0.1 select_reduce_fusion
  204.9 0.1 subtract_add_fusion.1
  205.0 1.0 fusion.22
  206.0 0.5 pad_maximum_fusion
  206.5 0.5 fusion.16
  207.0 0.5 fusion.10.x_ref
  207.6 15.2 %shard_map.205 = (bf16[512,2048]{1,0:T(8,128)(2,1)S(1)}, bf16[512,1024]{1,0:T(8,128)(2,1)S(1)}) custom-call(bf16[512,2048]{1,0:T(8,128)(2,1)S(1)} %fusion.10.x_ref, bf16[2048,2048]{1,0:T(8,128)(2,1)} %get-tuple-element.60.wq_ref, bf16[2048,1024]{1,0:T(8,128)(2,1)S(1)} %copy-done.4, f32[512,128]{1,0:T(8,128)S(1)} %get-tuple-element.123.cos_ref.cos_all, ...), custom_call_target="tpu_custom_call" | custom-call | flops 6442450944 | bytes 12582912 | tf_op jit(solution)/shard_map/pallas_call | solution.py:85
  222.8 0.0 all-gather.11.cloned.1.call-start
  222.9 9.1 collective-permute-start
  231.9 22.0 %collective-permute-done = bf16[512,1024]{1,0:T(8,128)(2,1)} collective-permute-done((bf16[512,1024]{1,0:T(8,128)(2,1)S(1)}, bf16[512,1024]{1,0:T(8,128)(2,1)}, u32[]{:S(2)}, u32[]{:S(2)}) %collective-permute-start) | collective-permute-done | bytes 1048608 | tf_op jit(solution)/shard_map/ppermute | solution.py:1231
  254.0 5.5 collective-permute-start.1
  259.5 0.6 reduce-scatter.5.cloned.1.call-start
  260.0 21.0 %collective-permute-done.1 = bf16[512,1024]{1,0:T(8,128)(2,1)} collective-permute-done((bf16[512,1024]{1,0:T(8,128)(2,1)}, bf16[512,1024]{1,0:T(8,128)(2,1)}, u32[]{:S(2)}, u32[]{:S(2)}) %collective-permute-start.1) | collective-permute-done | bytes 1048608 | tf_op jit(solution)/shard_map/ppermute | solution.py:1231
  281.0 1.3 constant_dynamic-update-slice_fusion.2
  282.3 1.3 constant_dynamic-update-slice_fusion.1
  283.6 0.1 constant_dynamic-update-slice_fusion.k_ref.v_ref
  283.7 1.6 copy-done.21
  285.3 51.9 %shard_map.206 = (bf16[512,2048]{1,0:T(8,128)(2,1)S(1)}, f32[32,1,512]{2,1,0:T(1,128)S(1)}) custom-call(bf16[512,2048]{1,0:T(8,128)(2,1)S(1)} %get-tuple-element.62.q_ref, bf16[1536,1024]{1,0:T(8,128)(2,1)} %copy-done.21, bf16[1536,1024]{1,0:T(8,128)(2,1)} %copy-done.21, s32[1,512]{1,0:T(1,128)S(1)} %bitcast.42), custom_call_target="tpu_custom_call" | custom-call | flops 21474836480 | bytes 7340032 | tf_op jit(solution)/shard_map/pallas_call | solution.py:169
  337.2 7.9 multiply_reduce_fusion.2
  345.2 1.9 copy-done.9
  347.1 1.7 multiply_convert_fusion.own_ref
  348.9 85.9 %shard_map.207 = (bf16[4096,2048]{1,0:T(8,128)(2,1)}, bf16[4096,1024]{1,0:T(8,128)(2,1)}, bf16[4096,1024]{1,0:T(8,128)(2,1)}, bf16[4096,1024]{1,0:T(8,128)(2,1)}) custom-call(bf16[512,2048]{1,0:T(8,128)(2,1)} %multiply_convert_fusion.own_ref, bf16[2048,1024]{1,0:T(8,128)(2,1)} %all-gather.5.cloned.1.call-done.wg_ref, ...), custom_call_target="tpu_custom_call" | custom-call | flops 34359738368 | bytes 50331648 | tf_op jit(solution)/shard_map/pallas_call | solution.py:735
  434.8 0.0 all-gather.9.cloned.1.call-done
  434.8 23.7 %convolution_convert_fusion.3 = bf16[2048,1024]{1,0:T(8,128)(2,1)} fusion(bf16[4096,2048]{1,0:T(8,128)(2,1)} %all-gather.9.cloned.1.call-done, bf16[4096,1024]{1,0:T(8,128)(2,1)} %get-tuple-element.80), kind=kOutput, calls=%fused_computation.37 | convolution fusion | flops 17181966336 | bytes 29360128 | tf_op jit(solution)/shard_map/dot_general | solution.py:39
  458.6 0.2 reduce-scatter.7.cloned.1.call-start
  458.8 0.0 all-gather.11.cloned.1.call-done
  458.8 31.2 %fusion.7 = (bf16[4096,1024]{1,0:T(8,128)(2,1)}, bf16[4096,1024]{1,0:T(8,128)(2,1)S(1)}) fusion(bf16[4096,1024]{1,0:T(8,128)(2,1)} %get-tuple-element.75, bf16[4096,1024]{1,0:T(8,128)(2,1)} %get-tuple-element.74, bf16[4096,2048]{1,0:T(8,128)(2,1)} %all-gather.9.cloned.1.call-done, bf16[2048,1024]{1,0:T(8,128)(2,1)} %all-gather.11.cloned.1.call-done), kind=kOutput, calls=%fused_computation.10 | convolution fusion | flops 17242783744 | bytes 54525952 | tf_op jit(solution)/shard_map/dot_general | solution.py:31
  490.0 3.3 copy-done.38
  493.3 21.5 %convolution_convert_fusion.2 = bf16[2048,1024]{1,0:T(8,128)(2,1)} fusion(bf16[4096,2048]{1,0:T(8,128)(2,1)} %get-tuple-element.79, bf16[4096,1024]{1,0:T(8,128)(2,1)S(1)} %get-tuple-element.76.dgate_ref), kind=kOutput, calls=%fused_computation.36 | convolution fusion | flops 17181966336 | bytes 29360128 | tf_op jit(solution)/shard_map/dot_general | solution.py:39
  514.9 0.3 reduce-scatter.9.cloned.1.call-start
  515.1 88.0 %shard_map.208 = f32[512,2048]{1,0:T(8,128)} custom-call(bf16[4096,1024]{1,0:T(8,128)(2,1)} %copy-done.38, bf16[4096,1024]{1,0:T(8,128)(2,1)} %get-tuple-element.107.dup_ref, bf16[2048,1024]{1,0:T(8,128)(2,1)} %all-gather.5.cloned.1.call-done.wg_ref, bf16[2048,1024]{1,0:T(8,128)(2,1)} %all-gather.7.cloned.1.call-done.wu_ref), custom_call_target="tpu_custom_call" | custom-call | flops 34359738368 | bytes 29360128 | tf_op jit(solution)/shard_map/pallas_call | solution.py:935
  603.2 0.0 reduce-scatter.5.cloned.1.call-done.refs_0_
  603.2 23.8 %convolution_convert_fusion.1 = bf16[2048,1024]{1,0:T(8,128)(2,1)} fusion(bf16[4096,2048]{1,0:T(8,128)(2,1)} %get-tuple-element.79, bf16[4096,1024]{1,0:T(8,128)(2,1)} %get-tuple-element.107.dup_ref), kind=kOutput, calls=%fused_computation.35 | convolution fusion | flops 17181966336 | bytes 29360128 | tf_op jit(solution)/shard_map/dot_general | solution.py:39
  627.0 23.5 %convolution_convert_fusion = bf16[4096,2048]{1,0:T(8,128)(2,1)} fusion(bf16[4096,1024]{1,0:T(8,128)(2,1)} %get-tuple-element.80, bf16[2048,1024]{1,0:T(8,128)(2,1)} %all-gather.11.cloned.1.call-done), kind=kOutput, calls=%fused_computation.11 | convolution fusion | flops 17188257792 | bytes 29360128 | tf_op jit(solution)/shard_map/dot_general | solution.py:35
  650.5 0.0 reduce-scatter.11.cloned.1.call-start
  650.6 0.6 copy-done.24
  651.2 4.6 multiply_reduce_fusion
  655.9 0.1 copy-done.10
  656.0 1.7 copy-done.11
  657.7 1.5 fusion.23.h_ref
  659.3 1.3 copy-done.17
  660.6 9.4 convolution_convert_fusion.4.do_ref
  670.0 148.9 %shard_map.209 = (bf16[512,2048]{1,0:T(8,128)(2,1)}, bf16[512,1024]{1,0:T(8,128)(2,1)}, f32[256,512]{1,0:T(8,128)}) custom-call(bf16[512,2048]{1,0:T(8,128)(2,1)} %copy-done.6, bf16[512,2048]{1,0:T(8,128)(2,1)} %convolution_convert_fusion.4.do_ref, bf16[512,2048]{1,0:T(8,128)(2,1)} %copy-done.7, bf16[1536,1024]{1,0:T(8,128)(2,1)} %copy-done.21, ...), custom_call_target="tpu_custom_call" | custom-call | flops 53687091200 | bytes 14680064 | tf_op jit(solution)/shard_map/pallas_call | solution.py:355
  818.9 0.0 reduce-scatter.9.cloned.1.call-done.refs_2_
  819.0 8.0 fusion.26
  827.1 5.1 fusion.19
  832.2 0.6 pad_maximum_fusion.3.gain_ref
  832.8 138.3 %shard_map.210 = (f32[256,512]{1,0:T(8,128)}, f32[256,256]{1,0:T(8,128)}, f32[2,2048]{1,0:T(2,128)}, bf16[256,2048]{1,0:T(8,128)(2,1)}, bf16[256,2048]{1,0:T(8,128)(2,1)}, /*index=5*/bf16[256,2048]{1,0:T(8,128)(2,1)}) custom-call(bf16[512,2048]{1,0:T(8,128)(2,1)} %copy-done, bf16[512,2048]{1,0:T(8,128)(2,1)} %get-tuple-element.88.dq_ref, ...), custom_call_target="tpu_custom_call" | custom-call | flops 120000004096 | bytes 6291456 | tf_op jit(solution)/shard_map/pallas_call | solution.py:1113
  971.2 2.9 convert_element_type.90
  974.1 2.9 convert_element_type.91
  977.1 1.6 convert_element_type.92
  978.6 0.7 fusion.24
  979.3 0.6 fusion.25
  980.0 8.7 fusion.21
  988.7 0.8 copy.28
  989.5 0.8 copy.29
  (87 shorter events, 0.3 us)
Async XLA Ops:
  7.2 341.7 %all-gather.5.cloned.1.call-start = ((), (), s32[]{:S(2)}) async-start(), calls=%async_computation.4 | async-start | bytes 5242880 | tf_op jit(solution)/shard_map/all_gather | solution.py:1245
  68.4 280.5 %all-gather.7.cloned.1.call-start = ((), (), s32[]{:S(2)}) async-start(), calls=%async_computation.5 | async-start | bytes 5242880 | tf_op jit(solution)/shard_map/all_gather | solution.py:1245
  69.2 365.7 %all-gather.9.cloned.1.call-start = ((), (), s32[]{:S(2)}) async-start(), calls=%async_computation.6 | async-start | bytes 18874368 | tf_op jit(solution)/shard_map/all_gather | solution.py:1200
  69.2 135.4 %copy-start.31 = (s32[1,2048]{1,0:T(1,128)S(1)}, s32[1,2048]{1,0:T(1,128)}, u32[]{:S(2)}) copy-start(s32[1,2048]{1,0:T(1,128)} %param.13) | copy-start | bytes 24580
  69.2 137.2 %copy-start.14 = (bf16[1,512,2048]{2,1,0:T(8,128)(2,1)S(1)}, bf16[1,512,2048]{2,1,0:T(8,128)(2,1)}, u32[]{:S(2)}) copy-start(bf16[1,512,2048]{2,1,0:T(8,128)(2,1)} %param.12) | copy-start | bytes 6291460
  204.6 2.4 copy-start.29
  205.0 78.7 %copy-start.3 = (s32[512]{0:T(512)}, s32[512]{0:T(512)S(1)}, u32[]{:S(2)}) copy-start(s32[512]{0:T(512)S(1)} %get-tuple-element.115) | copy-start | bytes 6148
  205.0 2.6 copy-start.4
  206.4 16.3 %copy-start.1 = (f32[512,128]{1,0:T(8,128)}, f32[512,128]{1,0:T(8,128)S(1)}, u32[]{:S(2)}) copy-start(f32[512,128]{1,0:T(8,128)S(1)} %get-tuple-element.123.cos_ref.cos_all) | copy-start | bytes 786436
  206.5 16.3 %copy-start.2 = (f32[512,128]{1,0:T(8,128)}, f32[512,128]{1,0:T(8,128)S(1)}, u32[]{:S(2)}) copy-start(f32[512,128]{1,0:T(8,128)S(1)} %get-tuple-element.124.sin_ref.sin_all) | copy-start | bytes 786436
  207.0 15.8 %copy-start.32 = (f32[512]{0:T(512)}, f32[512]{0:T(512)S(1)}, u32[]{:S(2)}) copy-start(f32[512]{0:T(512)S(1)} %add_rsqrt_fusion.1) | copy-start | bytes 6148
  207.5 15.2 %copy-start = (bf16[512,2048]{1,0:T(8,128)(2,1)}, bf16[512,2048]{1,0:T(8,128)(2,1)S(1)}, u32[]{:S(2)}) copy-start(bf16[512,2048]{1,0:T(8,128)(2,1)S(1)} %fusion.10.x_ref) | copy-start | bytes 6291460
  222.8 60.9 %copy-start.6 = (bf16[512,2048]{1,0:T(8,128)(2,1)}, bf16[512,2048]{1,0:T(8,128)(2,1)S(1)}, u32[]{:S(2)}) copy-start(bf16[512,2048]{1,0:T(8,128)(2,1)S(1)} %get-tuple-element.62.q_ref) | copy-start | bytes 6291460
  222.8 236.0 %all-gather.11.cloned.1.call-start = ((), (), s32[]{:S(2)}) async-start(), calls=%async_computation.7 | async-start | bytes 5242880 | tf_op jit(solution)/shard_map/all_gather | solution.py:1245
  222.9 31.1 %collective-permute-start = (bf16[512,1024]{1,0:T(8,128)(2,1)S(1)}, bf16[512,1024]{1,0:T(8,128)(2,1)}, u32[]{:S(2)}, u32[]{:S(2)}) collective-permute-start(bf16[512,1024]{1,0:T(8,128)(2,1)S(1)} %get-tuple-element.64), channel_id=1, source_target_pairs={{0,1},{1,2},{2,3},{4,5},{5,6},{6,7},{8,9},{9,10},{10,11},{12,13},{... | collective-permute-start | bytes 3145736 | tf_op jit(solution)/shard_map/ppermute | solution.py:1231
  254.0 27.0 %collective-permute-start.1 = (bf16[512,1024]{1,0:T(8,128)(2,1)}, bf16[512,1024]{1,0:T(8,128)(2,1)}, u32[]{:S(2)}, u32[]{:S(2)}) collective-permute-start(bf16[512,1024]{1,0:T(8,128)(2,1)} %collective-permute-done), channel_id=1, source_target_pairs={{0,1},{1,2},{2,3},{4,5},{5,6},{6,7},{8,9},{9,10},{10,11},{12,13},{... | collective-permute-start | bytes 3145736 | tf_op jit(solution)/shard_map/ppermute | solution.py:1231
  259.5 343.7 %reduce-scatter.5.cloned.1.call-start = ((), (), s32[]{:S(2)}) async-start(), calls=%async_computation.8 | async-start | bytes 5242880 | tf_op jit(solution)/shard_map/reduce_scatter | solution.py:1250
  283.7 1.6 copy-start.21
  285.3 51.9 %copy-start.15 = (bf16[1,512,2048]{2,1,0:T(8,128)(2,1)S(1)}, bf16[1,512,2048]{2,1,0:T(8,128)(2,1)}, u32[]{:S(2)}) copy-start(bf16[1,512,2048]{2,1,0:T(8,128)(2,1)} %param.12) | copy-start | bytes 6291460
  337.2 8.0 copy-start.7
  337.2 8.0 copy-start.8
  337.2 9.9 copy-start.23
  345.2 2.0 copy-start.9
  345.2 2.0 copy-start.26
  458.6 191.9 %reduce-scatter.7.cloned.1.call-start = ((), (), s32[]{:S(2)}) async-start(), calls=%async_computation.9 | async-start | bytes 5242880 | tf_op jit(solution)/shard_map/reduce_scatter | solution.py:1250
  490.0 3.3 copy-start.38
  514.9 304.1 %reduce-scatter.9.cloned.1.call-start = ((), (), s32[]{:S(2)}) async-start(), calls=%async_computation.10 | async-start | bytes 5242880 | tf_op jit(solution)/shard_map/reduce_scatter | solution.py:1250
  650.5 0.7 copy-start.24
  650.5 0.7 copy-start.27
  650.5 5.4 copy-start.12
  650.5 328.8 %reduce-scatter.11.cloned.1.call-start = ((), (), s32[]{:S(2)}) async-start(), calls=%async_computation.11 | async-start | bytes 18874368 | tf_op jit(solution)/shard_map/reduce_scatter | solution.py:1203
  651.2 4.8 copy-start.10
  651.2 6.5 copy-start.11
  657.7 1.5 copy-start.34
  659.3 1.3 copy-start.17
  818.9 8.1 copy-start.5
  819.0 8.1 copy-start.16
  819.0 8.1 copy-start.30
  819.0 8.1 copy-start.33
  819.0 8.1 copy-start.37
  971.2 5.9 copy-start.18
  971.2 7.4 copy-start.22
  974.1 5.2 copy-start.36
  974.1 5.9 copy-start.13
  974.1 5.9 copy-start.25
  974.1 5.9 copy-start.28
  974.1 5.9 copy-start.35
  980.0 8.8 copy-start.20
  980.0 9.6 copy-start.19
Sparse Core Ops, SparseCore 0:
  68.5 84.1 all-gather.4
  154.3 78.7 all-gather.6
  234.9 88.0 all-gather.8
  324.4 80.5 all-gather.10
  458.7 76.5 reduce-scatter.4
  537.6 77.2 reduce-scatter.6
  650.7 97.1 reduce-scatter.8
  751.9 157.3 reduce-scatter.10

commit v4 on v3

--- a/solution.py
+++ b/solution.py
@@ -194,15 +194,17 @@
 
 
 def attend_back_kernel(
-    reach, wide, z_size,
+    reach, wide, z_size, mlp_count,
     q_ref, do_ref, o_ref, k_ref, v_ref, lse_ref, low_ref, cos_ref, sin_ref, cos_all, sin_all,
-    h_ref, att_ref,
-    dq_ref, dkv_ref, wo_out,
-    bias_ref, dk_acc, dv_acc, own_part, send_part, recv_part, kv_send, kv_recv,
-    *scratch,
+    h_ref, att_ref, *refs,
 ):
-    ring = Reduce(wide, *scratch[:6])
-    sums, zrecv, z_send, z_recv = scratch[6:]
+    mlp_ins, refs = refs[:mlp_count], refs[mlp_count:]
+    dq_ref, dkv_ref, wo_out = refs[:3]
+    mlp_outs, refs = refs[3 : 3 + mlp_count], refs[3 + mlp_count :]
+    bias_ref, dk_acc, dv_acc, own_part, send_part, recv_part, kv_send, kv_recv = refs[:8]
+    ring = Reduce(wide, *refs[8:14])
+    sums, zrecv, z_send, z_recv = refs[14:18]
+    home = refs[18:]
     block, half, tile, pair = (pl.program_id(at) for at in range(4))
     steps = pl.num_programs(1) * pl.num_programs(2) * pl.num_programs(3)
     inner = (half * pl.num_programs(2) + tile) * pl.num_programs(3) + pair
@@ -237,12 +239,9 @@
 
     @pl.when(step == 0)
     def _():
-        barrier = pltpu.get_barrier_semaphore()
-        peers = [{"dp": peer} for peer in ring.peers]
-        peers += [{"tensor": (place + at) % z_size} for at in range(1, z_size)]
-        for peer in peers:
-            pl.semaphore_signal(barrier, inc=1, device_id=peer, device_id_type=MESH)
-        pl.semaphore_wait(barrier, len(peers))
+        greet(along_peers(place, z_size) + [device for _, device in others(wide)[1]])
+        for copy in send_home(wide, mlp_ins, mlp_outs, *home):
+            copy.start()
         fill_bias(bias_ref, low_ref, reach)
 
     @pl.when((step % 2 == 0) & (step < 16))
@@ -330,9 +329,11 @@
                 at, lambda distance: place >= distance, lambda copy, *_: copy.wait_send()
             )
         ring.sent()
-
-
-def attend_back(q, do, att, kv, lse, low, cosine, sine, h, dp_size, z_size):
+        for copy in send_home(wide, mlp_ins, mlp_outs, *home):
+            copy.wait()
+
+
+def attend_back(q, do, att, kv, lse, low, cosine, sine, h, mlp, dp_size, z_size):
     rows, width = q.shape
     keys = kv.shape[0]
     reach = keys - rows
@@ -354,7 +355,7 @@
     table = pl.BlockSpec((QTILE, LANES), lambda g, h, t, p: (t, 0))
     return pl.pallas_call(
         functools.partial(
-            attend_back_kernel, reach, 2 * math.isqrt(dp_size // GROUP), z_size
+            attend_back_kernel, reach, 2 * math.isqrt(dp_size // GROUP), z_size, len(mlp)
         ),
         grid=(blocks, 2, tiles, per_head),
         in_specs=[
@@ -374,17 +375,20 @@
             whole((rows, LANES)),
             whole(h.shape),
             whole(att.shape),
-        ],
+        ]
+        + [pl.BlockSpec(memory_space=pl.ANY)] * len(mlp),
         out_specs=[
             pl.BlockSpec((QTILE, LANES), pair_at),
             pl.BlockSpec((rows, kv.shape[1]), lambda g, h, t, p: (0, 0)),
             pl.BlockSpec((part, cols), lambda g, h, t, p: (0, 0)),
-        ],
+        ]
+        + [pl.BlockSpec(memory_space=pl.ANY)] * len(mlp),
         out_shape=[
             jax.ShapeDtypeStruct((rows, width), BF16),
             jax.ShapeDtypeStruct((rows, kv.shape[1]), BF16),
             jax.ShapeDtypeStruct((part, cols), F32),
-        ],
+        ]
+        + home_shapes(mlp),
         scratch_shapes=[
             pltpu.VMEM((tiles, span, QTILE), F32),
             pltpu.VMEM((keys, LANES), F32),
@@ -401,7 +405,8 @@
             pltpu.VMEM((z_size - 1, part, cols), BF16),
             pltpu.SemaphoreType.DMA((z_size - 1,)),
             pltpu.SemaphoreType.DMA((z_size - 1,)),
-        ],
+        ]
+        + home_scratch(mlp),
         compiler_params=pltpu.CompilerParams(
             collective_id=5, has_side_effects=True, vmem_limit_bytes=60 << 20
         ),
@@ -410,7 +415,7 @@
             bytes_accessed=8 * rows * width + 4 * keys * kv.shape[1],
             transcendentals=2 * rows * span * pairs,
         ),
-    )(q, do, att, kv, kv, lse, low, cosine, sine, cosine, sine, h, att)
+    )(q, do, att, kv, kv, lse, low, cosine, sine, cosine, sine, h, att, *mlp)
 
 
 MESH = pl.DeviceIdType.MESH
@@ -430,6 +435,60 @@
     for peer in peers:
         pl.semaphore_signal(barrier, inc=1, device_id={"dp": peer}, device_id_type=MESH)
     pl.semaphore_wait(barrier, len(peers))
+
+
+def others(wide):
+    (row, col, core), _ = neighbours(wide)
+    base = lax.axis_index("dp") - (2 * wide * row + 2 * col + core)
+    found = []
+    for flip in range(1, GROUP):
+        y, x, c = (row + flip // 4) % 2, (col + flip // 2) % 2, (core + flip) % 2
+        found.append((4 * y + 2 * x + c, {"dp": base + 2 * wide * y + 2 * x + c}))
+    return 4 * row + 2 * col + core, found
+
+
+def along_peers(place, z_size):
+    return [{"tensor": (place + step) % z_size} for step in range(1, z_size)]
+
+
+def greet(peers):
+    barrier = pltpu.get_barrier_semaphore()
+    for peer in peers:
+        pl.semaphore_signal(barrier, inc=1, device_id=peer, device_id_type=MESH)
+    pl.semaphore_wait(barrier, len(peers))
+
+
+def send_home(wide, ins, outs, own_sem, send_sem, recv_sem):
+    mine, found = others(wide)
+    copies = []
+    for at, (src, dst) in enumerate(zip(ins, outs)):
+        part, cols = dst.shape[0], src.shape[1]
+        here = pl.ds(pl.multiple_of(mine * cols, LANES), cols)
+        for index, (other, device) in enumerate(found):
+            copies.append(
+                pltpu.make_async_remote_copy(
+                    src_ref=src.at[pl.ds(pl.multiple_of(other * part, part), part)],
+                    dst_ref=dst.at[:, here],
+                    send_sem=send_sem.at[at, index], recv_sem=recv_sem.at[at, index],
+                    device_id=device, device_id_type=MESH,
+                )
+            )
+        own = src.at[pl.ds(pl.multiple_of(mine * part, part), part)]
+        copies.append(pltpu.make_async_copy(own, dst.at[:, here], own_sem.at[at]))
+    return copies
+
+
+def home_shapes(arrays):
+    return [jax.ShapeDtypeStruct((a.shape[0] // GROUP, GROUP * a.shape[1]), BF16) for a in arrays]
+
+
+def home_scratch(arrays):
+    count = len(arrays)
+    return [
+        pltpu.SemaphoreType.DMA((count,)),
+        pltpu.SemaphoreType.DMA((count, GROUP - 1)),
+        pltpu.SemaphoreType.DMA((count, GROUP - 1)),
+    ]
 
 
 SIB, XN, YN = 0, 1, 2
@@ -961,45 +1020,12 @@
     sums, zrecv, gain_z, gain_p, z_send, z_recv, g_send, g_recv, m_own, m_send, m_recv = scratch[12:]
     rings = [Reduce(wide, *own_scratch[6 * at : 6 * at + 6]) for at in range(2)]
     place = lax.axis_index("tensor")
-    dp = lax.axis_index("dp")
-    row, col, core = rings[0].at
-    mine = 4 * row + 2 * col + core
-    base = dp - (2 * wide * row + 2 * col + core)
-    flips = [(y, x, c) for y in range(2) for x in range(2) for c in range(2)][1:]
-
-    def device(flip):
-        y, x, c = (row + flip[0]) % 2, (col + flip[1]) % 2, (core + flip[2]) % 2
-        return {"dp": base + 2 * wide * y + 2 * x + c}
-
-    along = [{"tensor": (place + step) % z_size} for step in range(1, z_size)]
-    around = [device(flip) for flip in flips]
-    barrier = pltpu.get_barrier_semaphore()
-    for peer in along + around:
-        pl.semaphore_signal(barrier, inc=1, device_id=peer, device_id_type=MESH)
-    pl.semaphore_wait(barrier, len(along) + len(around))
-
-    mlp_copies = []
-    for at in range(mlp_count):
-        src, dst = mlp_ins[at], mlp_outs[at]
-        part, cols = dst.shape[0], src.shape[1]
-        here = pl.ds(pl.multiple_of(mine * cols, LANES), cols)
-        for index, flip in enumerate(flips):
-            y, x, c = (row + flip[0]) % 2, (col + flip[1]) % 2, (core + flip[2]) % 2
-            other = 4 * y + 2 * x + c
-            mlp_copies.append(
-                pltpu.make_async_remote_copy(
-                    src_ref=src.at[pl.ds(pl.multiple_of(other * part, part), part)],
-                    dst_ref=dst.at[:, here],
-                    send_sem=m_send.at[at, index], recv_sem=m_recv.at[at, index],
-                    device_id=device(flip), device_id_type=MESH,
-                )
-            )
-        mlp_copies.append(
-            pltpu.make_async_copy(
-                src.at[pl.ds(pl.multiple_of(mine * part, part), part)],
-                dst.at[:, here], m_own.at[at],
-            )
-        )
+    mine, found = others(wide)
+    along = along_peers(place, z_size)
+    around = [device for _, device in found]
+    greet(along + around)
+
+    mlp_copies = send_home(wide, mlp_ins, mlp_outs, m_own, m_send, m_recv)
     for copy in mlp_copies:
         copy.start()
 
@@ -1116,9 +1142,7 @@
         out_specs=[near] * 3 + [far] * len(mlp),
         out_shape=[jax.ShapeDtypeStruct((rows, cols // z_size), F32) for cols in sizes[::-1]]
         + [jax.ShapeDtypeStruct(gains.shape, F32)]
-        + [
-            jax.ShapeDtypeStruct((m.shape[0] // GROUP, GROUP * m.shape[1]), BF16) for m in mlp
-        ],
+        + home_shapes(mlp),
         scratch_shapes=scratch
         + [
             pltpu.VMEM((rows, total), BF16),
@@ -1129,10 +1153,8 @@
             pltpu.SemaphoreType.DMA((2, z_size - 1)),
             pltpu.SemaphoreType.DMA((z_size - 1 + GROUP - 1,)),
             pltpu.SemaphoreType.DMA((z_size - 1 + GROUP - 1,)),
-            pltpu.SemaphoreType.DMA((len(mlp),)),
-            pltpu.SemaphoreType.DMA((len(mlp), GROUP - 1)),
-            pltpu.SemaphoreType.DMA((len(mlp), GROUP - 1)),
-        ],
+        ]
+        + home_scratch(mlp),
         compiler_params=pltpu.CompilerParams(
             collective_id=4, has_side_effects=True, vmem_limit_bytes=60 << 20
         ),
@@ -1190,6 +1212,12 @@
         return lax.psum_scatter(
             array, "dp", scatter_dimension=0, axis_index_groups=self.outer, tiled=True
         )
+
+    def swap(self, array, flip):
+        pairs = [
+            (block[at], block[at ^ flip]) for block in self.inner for at in range(GROUP)
+        ]
+        return lax.ppermute(array, "dp", pairs)
 
     def sum_outer(self, array):
         if self.blocks == 1:
@@ -1266,49 +1294,73 @@
     r2 = rms_scale(h)
     hn, gate, up, hidden = gate_up((h * r2 * mlp_gain).astype(BF16), wg, wu, dp_size)
     dy = layout.gather(grad)
+    row, col, core = neighbours(2 * layout.cols)[0]
+    by_core = hidden.reshape(GROUP // 2, 2, rows, -1)
+
+    def out_part(of_core):
+        some = lax.dynamic_index_in_dim(by_core, of_core, 1, False)
+        return dot_nt(some.reshape(GROUP * rows // 2, -1), wd)
+
+    def chunk(array, y, x):
+        return lax.dynamic_index_in_dim(array, 2 * y + x, 0, False)
+
+    away = out_part(1 - core).astype(BF16)
+    dy, away = lax.optimization_barrier((dy, away))
     total_wd = dot_tn(dy, hidden).astype(BF16)
-    dy, total_wd = lax.optimization_barrier((dy, total_wd))
+    near_sum = out_part(core) + layout.swap(away, 1).astype(F32)
+    near_sum = near_sum.astype(BF16)
+    dy, total_wd, near_sum = lax.optimization_barrier((dy, total_wd, near_sum))
     part_wd = along_z(total_wd)
+    near_sum = near_sum.reshape(GROUP // 2, rows, width)
+    far_chunk = chunk(near_sum, 1 - row, 1 - col)
+    from_x = layout.swap(far_chunk[rows // 2 :], 2)
+    from_y = layout.swap(far_chunk[: rows // 2], 4)
     gate, up = gate.astype(F32), up.astype(F32)
     sigma = jax.nn.sigmoid(gate)
     dhid = dot_nn(dy, wd)
     dgate = (dhid * up * sigma * (1.0 + gate * (1.0 - sigma))).astype(BF16)
     dup = (dhid * gate * sigma).astype(BF16)
+    x_chunk = chunk(near_sum, row, 1 - col)
+    y_chunk = chunk(near_sum, 1 - row, col)
+    x_upper = (x_chunk[: rows // 2].astype(F32) + from_y.astype(F32)).astype(BF16)
+    y_lower = (y_chunk[rows // 2 :].astype(F32) + from_x.astype(F32)).astype(BF16)
+    x_chunk = jnp.concatenate([x_upper, x_chunk[rows // 2 :]], axis=0)
+    y_chunk = jnp.concatenate([y_chunk[: rows // 2], y_lower], axis=0)
+    dgate, dup, x_chunk, y_chunk = lax.optimization_barrier((dgate, dup, x_chunk, y_chunk))
+    from_x, from_y = layout.swap(x_chunk, 2), layout.swap(y_chunk, 4)
     total_wg = dot_tn(hn, dgate).astype(BF16)
-    dgate, total_wg = lax.optimization_barrier((dgate, total_wg))
+    dup, total_wg = lax.optimization_barrier((dup, total_wg))
     part_wg = along_z(total_wg)
+    total_wu = dot_tn(hn, dup).astype(BF16)
+    dup, total_wu = lax.optimization_barrier((dup, total_wu))
+    part_wu = along_z(total_wu)
+    dup, from_x, from_y = lax.optimization_barrier((dup, from_x, from_y))
     dhn = hidden_back(dgate, dup, wg, wu, dp_size)
-    hn, hidden, dhn, part_wd = lax.optimization_barrier((hn, hidden, dhn, part_wd))
-    total_wu = dot_tn(hn, dup).astype(BF16)
-    partial_out = dot_nt(hidden, wd).astype(BF16)
-    dhn, total_wu, partial_out, part_wg = lax.optimization_barrier(
-        (dhn, total_wu, partial_out, part_wg)
-    )
-    part_wu = along_z(total_wu)
+    dhn, part_wd = lax.optimization_barrier((dhn, part_wd))
     gain_two, dh_norm = norm_back(h, r2, mlp_gain, dhn)
     dh = cotangent[0].astype(F32) + dh_norm
+    output = h + chunk(near_sum, row, col).astype(F32)
+    output = output + from_x.astype(F32) + from_y.astype(F32)
 
     dhb = dh.astype(BF16)
     datt = dot_nn(dhb, wo).astype(BF16)
-    datt, partial_out = lax.optimization_barrier((datt, partial_out))
-    out_sum = layout.scatter(partial_out)
-    dq, dkv, wo_grad = attend_back(
-        q, datt, att, kv_all, lse, low, cosine, sine, layout.from_cols(dhb), dp_size, z_size
+    datt, part_wg = lax.optimization_barrier((datt, part_wg))
+    dq, dkv, wo_grad, wd_grad, wg_grad = attend_back(
+        q, datt, att, kv_all, lse, low, cosine, sine, layout.from_cols(dhb),
+        (part_wd, part_wg), dp_size, z_size,
     )
     dq, part_wu = lax.optimization_barrier((dq, part_wu))
     dxn = dot_nt(dq, wq) + dot_nt(dkv, wkv)
     gain_one, dx_norm = norm_back(x, r1, attn_gain, dxn)
     input_grad = (dh + dx_norm).astype(BF16)
     gains = layout.sum_outer(jnp.stack([gain_one, gain_two]))
-    wq_grad, wkv_grad, gains, wd_grad, wg_grad, wu_grad = last_grads(
-        layout.from_cols(xn), dq, dkv, gains, (part_wd, part_wg, part_wu), dp_size, z_size
+    wq_grad, wkv_grad, gains, wu_grad = last_grads(
+        layout.from_cols(xn), dq, dkv, gains, (part_wu,), dp_size, z_size
     )
     wo_grad, wq_grad, wkv_grad, wd_grad, wg_grad, wu_grad = (
         layout.scatter_outer(grad).astype(F32)
         for grad in (wo_grad, wq_grad, wkv_grad, wd_grad, wg_grad, wu_grad)
     )
-    gains, out_sum = lax.optimization_barrier((gains, out_sum))
-    output = h + out_sum.astype(F32)
     key_cols = w_key.shape[1]
     return (
         output.astype(BF16)[None],

time: 1010 us -> 1070 us (1.059)
  waiting for transfers between devices: 43.9 us -> 102 us
  Pallas kernels: 723 us -> 699 us
  local copies, waits for them, and re-layouts: 16.3 us -> 28.3 us
    pallas_call x1, Pallas kernels: 138 us -> 90.1 us  [last_grads(): pl.pallas_call(functools.partial(tail_kernel, 2 * math.isqrt(dp_size // G...]
    pallas_call x1, Pallas kernels: 85.9 us -> 123 us  [gate_up(): pl.pallas_call(functools.partial(gate_up_kernel, 2 * math.isqrt(dp_size /...]
    ppermute x2, waiting for transfers between devices: 43 us -> 80.1 us  [shift(): return lax.ppermute(array, 'tensor', pairs)]
    ppermute x0 -> x5, waiting for transfers between devices: none -> 20.7 us  [swap(): return lax.ppermute(array, 'dp', pairs)]
    pallas_call x1, Pallas kernels: 149 us -> 135 us  [attend_back(): pl.pallas_call(functools.partial(attend_back_kernel, reach, 2 * math.isqr...]
    dot_general x4 -> x5, matrix products: 44.6 us -> 48.1 us  [dot_nt(): lax.dot_general(left, right, (((1,), (1,)), ((), ())), preferred_element_...]
  transfers between devices with their start and end apart: 10 -> 14, of which waited for: 2 -> 4; matrix products, arithmetic and copies ran while one was open for 18% -> 15% of each run, Pallas kernels for 67% -> 52%
where the time goes in v4:
time: 1070 us; the launch traced here: 1060 us
  Pallas kernels  699 us (65%)
  matrix products  159 us (15%)
  waiting for transfers between devices  102 us (10%)
  other arithmetic  34.5 us (3%)
  local copies, waits for them, and re-layouts  28.3 us (3%)
  starting transfers between devices  25.8 us (2%)
  between operations  15.3 us (1%)
    pallas_call x1, Pallas kernels, gather_rows(): pl.pallas_call(functools.partial(gather_kernel, 2 * math.isqrt(dp_size //...  135 us
    pallas_call x1, Pallas kernels, attend_back(): pl.pallas_call(functools.partial(attend_back_kernel, reach, 2 * math.isqr...  135 us
    pallas_call x1, Pallas kernels, gate_up(): pl.pallas_call(functools.partial(gate_up_kernel, 2 * math.isqrt(dp_size /...  123 us
    pallas_call x1, Pallas kernels, last_grads(): pl.pallas_call(functools.partial(tail_kernel, 2 * math.isqrt(dp_size // G...  90.1 us
    pallas_call x1, Pallas kernels, hidden_back(): pl.pallas_call(functools.partial(hidden_back_kernel, 2 * math.isqrt(dp_si...  88.7 us
    ppermute x2, waiting for transfers between devices, shift(): return lax.ppermute(array, 'tensor', pairs)  80.1 us
    dot_general x3, matrix products, dot_tn(): lax.dot_general(left, right, (((0,), (0,)), ((), ())), preferred_element_...  69.3 us
    pallas_call x1, Pallas kernels, spread_weights(): pl.pallas_call(functools.partial(spread_kernel, 2 * math.isqrt(dp_size //...  59.6 us
  transfers between devices with their start and end apart: 14, of which 4 were waited for; matrix products, arithmetic and copies ran while one was open for 15% of the time, Pallas kernels for 52%

profile of v4, /device:TPU:0, one launch (start us, length us, event | category | flops | bytes accessed | tf_op | source)
XLA Modules:
  0.0 1063.6 jit_solution(11164592443297096306)
XLA Ops:
  7.2 1.5 pad_maximum_fusion.4.refs_3_
  8.8 59.6 %shard_map.203 = (bf16[2048,256]{1,0:T(8,128)(2,1)}, bf16[2048,256]{1,0:T(8,128)(2,1)}, bf16[2048,256]{1,0:T(8,128)(2,1)}, bf16[256,1024]{1,0:T(8,128)(2,1)}, bf...) custom-call(bf16[256,2048]{1,0:T(8,128)(2,1)} %refs_0_.1, bf16[256,2048]{1,0:T(8,128)(2,1)} %refs_1_.1, ...), custom_call_target="tpu_custom_call" | custom-call | flops 60000002048 | tf_op jit(solution)/shard_map/pallas_call | solution.py:572
  68.5 0.7 all-gather.9.cloned.1.call-update
  69.2 0.7 all-gather.11.cloned.1.call-update
  70.0 135.4 %shard_map.204 = (bf16[2048,1024]{1,0:T(8,128)(2,1)}, bf16[2048,2048]{1,0:T(8,128)(2,1)}, bf16[2048,2048]{1,0:T(8,128)(2,1)}) custom-call(bf16[256,1024]{1,0:T(8,128)(2,1)} %get-tuple-element.61.refs_0_, bf16[256,2048]{1,0:T(8,128)(2,1)} %get-tuple-element.62.refs_1_, bf16[256,2048]{1,0:T(8,128)(2,1)} %get-tuple-element.63.refs_2_), custom_call_target="tpu_custom_call" | custom-call | flops 120000004096 | tf_op jit(solution)/shard_map/pallas_call | solution.py:696
  205.4 0.1 convert_reduce_fusion
  205.5 0.1 select_reduce_fusion
  205.6 0.1 subtract_add_fusion.1
  205.7 1.0 fusion.27
  206.7 0.5 pad_maximum_fusion.2
  207.2 0.5 fusion.16
  207.7 0.5 fusion.10.x_ref
  208.3 15.2 %shard_map.205 = (bf16[512,2048]{1,0:T(8,128)(2,1)S(1)}, bf16[512,1024]{1,0:T(8,128)(2,1)S(1)}) custom-call(bf16[512,2048]{1,0:T(8,128)(2,1)S(1)} %fusion.10.x_ref, bf16[2048,2048]{1,0:T(8,128)(2,1)} %get-tuple-element.64.wq_ref, bf16[2048,1024]{1,0:T(8,128)(2,1)S(1)} %copy-done.4, f32[512,128]{1,0:T(8,128)S(1)} %get-tuple-element.139.cos_ref.cos_all, ...), custom_call_target="tpu_custom_call" | custom-call | flops 6442450944 | bytes 12582912 | tf_op jit(solution)/shard_map/pallas_call | solution.py:85
  223.6 9.1 collective-permute-start
  232.7 35.4 %collective-permute-done = bf16[512,1024]{1,0:T(8,128)(2,1)} collective-permute-done((bf16[512,1024]{1,0:T(8,128)(2,1)S(1)}, bf16[512,1024]{1,0:T(8,128)(2,1)}, u32[]{:S(2)}, u32[]{:S(2)}) %collective-permute-start) | collective-permute-done | bytes 1048608 | tf_op jit(solution)/shard_map/ppermute | solution.py:1259
  268.1 12.4 %collective-permute-start.1 = (bf16[512,1024]{1,0:T(8,128)(2,1)}, bf16[512,1024]{1,0:T(8,128)(2,1)}, u32[]{:S(2)}, u32[]{:S(2)}) collective-permute-start(bf16[512,1024]{1,0:T(8,128)(2,1)} %collective-permute-done), channel_id=1, source_target_pairs={{0,1},{1,2},{2,3},{4,5},{5,6},{6,7},{8,9},{9,10},{10,11},{12,13},{... | collective-permute-start | bytes 3145736 | tf_op jit(solution)/shard_map/ppermute | solution.py:1259
  280.5 44.6 %collective-permute-done.1 = bf16[512,1024]{1,0:T(8,128)(2,1)} collective-permute-done((bf16[512,1024]{1,0:T(8,128)(2,1)}, bf16[512,1024]{1,0:T(8,128)(2,1)}, u32[]{:S(2)}, u32[]{:S(2)}) %collective-permute-start.1) | collective-permute-done | bytes 1048608 | tf_op jit(solution)/shard_map/ppermute | solution.py:1259
  325.2 1.3 constant_dynamic-update-slice_fusion.2
  326.5 1.3 constant_dynamic-update-slice_fusion.1
  327.8 0.1 constant_dynamic-update-slice_fusion.k_ref.v_ref
  327.9 1.7 copy-done.26
  329.6 51.8 %shard_map.206 = (bf16[512,2048]{1,0:T(8,128)(2,1)S(1)}, f32[32,1,512]{2,1,0:T(1,128)S(1)}) custom-call(bf16[512,2048]{1,0:T(8,128)(2,1)S(1)} %get-tuple-element.66.q_ref, bf16[1536,1024]{1,0:T(8,128)(2,1)} %copy-done.26, bf16[1536,1024]{1,0:T(8,128)(2,1)} %copy-done.26, s32[1,512]{1,0:T(1,128)S(1)} %bitcast.69), custom_call_target="tpu_custom_call" | custom-call | flops 21474836480 | bytes 7340032 | tf_op jit(solution)/shard_map/pallas_call | solution.py:169
  381.5 7.9 multiply_reduce_fusion.2
  389.4 2.1 copy-done.9
  391.6 1.7 multiply_convert_fusion.own_ref
  393.3 123.2 %shard_map.207 = (bf16[4096,2048]{1,0:T(8,128)(2,1)}, bf16[4096,1024]{1,0:T(8,128)(2,1)}, bf16[4096,1024]{1,0:T(8,128)(2,1)}, bf16[4096,1024]{1,0:T(8,128)(2,1)}) custom-call(bf16[512,2048]{1,0:T(8,128)(2,1)} %multiply_convert_fusion.own_ref, bf16[2048,1024]{1,0:T(8,128)(2,1)} %all-gather.7.cloned.1.call-done.wg_ref, ...), custom_call_target="tpu_custom_call" | custom-call | flops 34359738368 | bytes 50331648 | tf_op jit(solution)/shard_map/pallas_call | solution.py:794
  516.5 7.7 constant_dynamic-slice_fusion
  524.2 14.0 %convolution_convert_fusion = bf16[2048,2048]{1,0:T(8,128)(2,1)} fusion(bf16[2048,1024]{1,0:T(8,128)(2,1)} %bitcast.77, bf16[2048,1024]{1,0:T(8,128)(2,1)} %all-gather.11.cloned.1.call-done), kind=kOutput, calls=%fused_computation.17 | convolution fusion | flops 8594128896 | bytes 16777216 | tf_op jit(solution)/shard_map/dot_general | solution.py:35
  538.2 24.1 %convolution_convert_fusion.3 = bf16[2048,1024]{1,0:T(8,128)(2,1)} fusion(bf16[4096,2048]{1,0:T(8,128)(2,1)} %all-gather.5.cloned.1.call-done, bf16[4096,1024]{1,0:T(8,128)(2,1)} %get-tuple-element.74), kind=kOutput, calls=%fused_computation.41 | convolution fusion | flops 17181966336 | bytes 29360128 | tf_op jit(solution)/shard_map/dot_general | solution.py:39
  562.3 13.2 %add_convert_fusion = bf16[2048,2048]{1,0:T(8,128)(2,1)S(1)} fusion(bf16[2048,2048]{1,0:T(8,128)(2,1)} %collective-permute-done.2, bf16[2048,1024]{1,0:T(8,128)(2,1)} %bitcast.76, bf16[2048,1024]{1,0:T(8,128)(2,1)} %all-gather.11.cloned.1.call-done), kind=kOutput, calls=%fused_computation.11 | convolution fusion | flops 8602517504 | bytes 25165824 | tf_op jit(solution)/shard_map/dot_general | solution.py:35
  575.6 1.7 dynamic-slice_bitcast_fusion.2
  577.3 1.8 copy-done.19
  579.1 0.7 collective-permute-start.4
  579.8 0.3 collective-permute-start.3
  580.2 32.2 %fusion.7 = (bf16[4096,1024]{1,0:T(8,128)(2,1)}, bf16[4096,1024]{1,0:T(8,128)(2,1)}) fusion(bf16[4096,1024]{1,0:T(8,128)(2,1)} %get-tuple-element.81, bf16[4096,1024]{1,0:T(8,128)(2,1)} %get-tuple-element.80, bf16[4096,2048]{1,0:T(8,128)(2,1)} %all-gather.5.cloned.1.call-done, bf16[2048,1024]{1,0:T(8,128)(2,1)} %all-gather.11.cloned.1.call-done), kind=kOutput, calls=%fused_computation.10 | convolution fusion | flops 17242783744 | bytes 54525952 | tf_op jit(solution)/shard_map/dot_general | solution.py:31
  612.5 3.1 fusion.25
  615.6 1.5 pad_maximum_fusion
  617.1 1.5 pad_maximum_fusion.1
  618.6 1.9 copy-done.41
  620.5 21.3 %convolution_convert_fusion.2 = bf16[2048,1024]{1,0:T(8,128)(2,1)} fusion(bf16[4096,2048]{1,0:T(8,128)(2,1)} %get-tuple-element.83, bf16[4096,1024]{1,0:T(8,128)(2,1)S(1)} %copy-done.41), kind=kOutput, calls=%fused_computation.40 | convolution fusion | flops 17181966336 | bytes 29360128 | tf_op jit(solution)/shard_map/dot_general | solution.py:39
  641.8 1.6 collective-permute-start.5
  643.4 1.5 collective-permute-start.6
  644.9 24.0 %convolution_convert_fusion.1 = bf16[2048,1024]{1,0:T(8,128)(2,1)} fusion(bf16[4096,2048]{1,0:T(8,128)(2,1)} %get-tuple-element.83, bf16[4096,1024]{1,0:T(8,128)(2,1)} %get-tuple-element.91.dup_ref), kind=kOutput, calls=%fused_computation.39 | convolution fusion | flops 17181966336 | bytes 29360128 | tf_op jit(solution)/shard_map/dot_general | solution.py:39
  668.9 20.6 %collective-permute-done.5 = bf16[512,2048]{1,0:T(8,128)(2,1)S(1)} collective-permute-done((bf16[512,2048]{1,0:T(8,128)(2,1)}, bf16[512,2048]{1,0:T(8,128)(2,1)S(1)}, u32[]{:S(2)}, u32[]{:S(2)}) %collective-permute-start.5) | collective-permute-done | bytes 2097184 | tf_op jit(solution)/shard_map/ppermute | solution.py:1220
  689.5 1.3 copy-done.20
  690.9 88.7 %shard_map.208 = f32[512,2048]{1,0:T(8,128)} custom-call(bf16[4096,1024]{1,0:T(8,128)(2,1)} %get-tuple-element.84.dgate_ref, bf16[4096,1024]{1,0:T(8,128)(2,1)} %get-tuple-element.91.dup_ref, bf16[2048,1024]{1,0:T(8,128)(2,1)} %all-gather.7.cloned.1.call-done.wg_ref, bf16[2048,1024]{1,0:T(8,128)(2,1)} %all-gather.9.cloned.1.call-done.wu_ref), custom_call_target="tpu_custom_call" | custom-call | flops 34359738368 | bytes 29360128 | tf_op jit(solution)/shard_map/pallas_call | solution.py:994
  779.7 4.7 multiply_reduce_fusion
  784.5 1.2 copy-done.12
  785.7 1.5 fusion.28.h_ref
  787.2 1.3 copy-done.21
  788.5 9.0 convolution_convert_fusion.4.do_ref
  797.6 134.8 %shard_map.209 = (bf16[512,2048]{1,0:T(8,128)(2,1)}, bf16[512,1024]{1,0:T(8,128)(2,1)}, f32[256,512]{1,0:T(8,128)}, bf16[256,2048]{1,0:T(8,128)(2,1)}, bf16[256,2048]{1,0:T(8,128)(2,1)}) custom-call(bf16[512,2048]{1,0:T(8,128)(2,1)} %copy-done.6, bf16[512,2048]{1,0:T(8,128)(2,1)} %convolution_convert_fusion.4.do_ref, bf16[512,2048]{1,0:T(8,128)(2,1)} %copy-done.7, ...), custom_call_target="tpu_custom_call" | custom-call | flops 53687091200 | bytes 14680064 | tf_op jit(solution)/shard_map/pallas_call | solution.py:356
  932.4 7.8 fusion.31
  940.3 5.1 fusion.19
  945.4 0.6 pad_maximum_fusion.5.gain_ref
  946.0 90.1 %shard_map.210 = (f32[256,512]{1,0:T(8,128)}, f32[256,256]{1,0:T(8,128)}, f32[2,2048]{1,0:T(2,128)}, bf16[256,2048]{1,0:T(8,128)(2,1)}) custom-call(bf16[512,2048]{1,0:T(8,128)(2,1)} %copy-done, bf16[512,2048]{1,0:T(8,128)(2,1)} %get-tuple-element.101.dq_ref, bf16[512,1024]{1,0:T(8,128)(2,1)} %get-tuple-element.102.dkv_ref, ...), custom_call_target="tpu_custom_call" | custom-call | flops 120000004096 | bytes 6291456 | tf_op jit(solution)/shard_map/pallas_call | solution.py:1139
  1036.1 1.4 fusion.30
  1037.5 1.7 fusion.29
  1039.3 1.6 convert_element_type.142
  1040.8 3.6 convert_element_type.143
  1044.4 1.6 convert_element_type.144
  1046.0 8.6 fusion.24
  1054.7 0.8 copy.28
  1055.5 0.8 copy.29
  (106 shorter events, 0.7 us)
Async XLA Ops:
  7.2 386.1 %all-gather.7.cloned.1.call-start = ((), (), s32[]{:S(2)}) async-start(), calls=%async_computation.4 | async-start | bytes 5242880 | tf_op jit(solution)/shard_map/all_gather | solution.py:1273
  68.4 324.9 %all-gather.9.cloned.1.call-start = ((), (), s32[]{:S(2)}) async-start(), calls=%async_computation.5 | async-start | bytes 5242880 | tf_op jit(solution)/shard_map/all_gather | solution.py:1273
  69.2 455.0 %all-gather.11.cloned.1.call-start = ((), (), s32[]{:S(2)}) async-start(), calls=%async_computation.6 | async-start | bytes 5242880 | tf_op jit(solution)/shard_map/all_gather | solution.py:1273
  69.9 468.3 %all-gather.5.cloned.1.call-start = ((), (), s32[]{:S(2)}) async-start(), calls=%async_computation.3 | async-start | bytes 18874368 | tf_op jit(solution)/shard_map/all_gather | solution.py:1228
  69.9 135.4 %copy-start.35 = (s32[1,2048]{1,0:T(1,128)S(1)}, s32[1,2048]{1,0:T(1,128)}, u32[]{:S(2)}) copy-start(s32[1,2048]{1,0:T(1,128)} %param.13) | copy-start | bytes 24580
  70.0 137.2 %copy-start.16 = (bf16[1,512,2048]{2,1,0:T(8,128)(2,1)S(1)}, bf16[1,512,2048]{2,1,0:T(8,128)(2,1)}, u32[]{:S(2)}) copy-start(bf16[1,512,2048]{2,1,0:T(8,128)(2,1)} %param.12) | copy-start | bytes 6291460
  205.3 2.4 copy-start.33
  205.7 122.2 %copy-start.3 = (s32[512]{0:T(512)}, s32[512]{0:T(512)S(1)}, u32[]{:S(2)}) copy-start(s32[512]{0:T(512)S(1)} %get-tuple-element.131) | copy-start | bytes 6148
  205.7 2.6 copy-start.4
  207.2 16.3 %copy-start.1 = (f32[512,128]{1,0:T(8,128)}, f32[512,128]{1,0:T(8,128)S(1)}, u32[]{:S(2)}) copy-start(f32[512,128]{1,0:T(8,128)S(1)} %get-tuple-element.139.cos_ref.cos_all) | copy-start | bytes 786436
  207.2 16.3 %copy-start.2 = (f32[512,128]{1,0:T(8,128)}, f32[512,128]{1,0:T(8,128)S(1)}, u32[]{:S(2)}) copy-start(f32[512,128]{1,0:T(8,128)S(1)} %get-tuple-element.140.sin_ref.sin_all) | copy-start | bytes 786436
  207.7 15.8 %copy-start.36 = (f32[512]{0:T(512)}, f32[512]{0:T(512)S(1)}, u32[]{:S(2)}) copy-start(f32[512]{0:T(512)S(1)} %add_rsqrt_fusion.1) | copy-start | bytes 6148
  208.3 15.2 %copy-start = (bf16[512,2048]{1,0:T(8,128)(2,1)}, bf16[512,2048]{1,0:T(8,128)(2,1)S(1)}, u32[]{:S(2)}) copy-start(bf16[512,2048]{1,0:T(8,128)(2,1)S(1)} %fusion.10.x_ref) | copy-start | bytes 6291460
  223.5 104.4 %copy-start.6 = (bf16[512,2048]{1,0:T(8,128)(2,1)}, bf16[512,2048]{1,0:T(8,128)(2,1)S(1)}, u32[]{:S(2)}) copy-start(bf16[512,2048]{1,0:T(8,128)(2,1)S(1)} %get-tuple-element.66.q_ref) | copy-start | bytes 6291460
  223.5 556.1 %reduce-scatter.4.cloned.1.call-start = ((), (), s32[]{:S(2)}) async-start(), calls=%async_computation.7 | async-start | bytes 5242880 | tf_op jit(solution)/shard_map/reduce_scatter | solution.py:1278
  223.6 44.5 %collective-permute-start = (bf16[512,1024]{1,0:T(8,128)(2,1)S(1)}, bf16[512,1024]{1,0:T(8,128)(2,1)}, u32[]{:S(2)}, u32[]{:S(2)}) collective-permute-start(bf16[512,1024]{1,0:T(8,128)(2,1)S(1)} %get-tuple-element.68), channel_id=1, source_target_pairs={{0,1},{1,2},{2,3},{4,5},{5,6},{6,7},{8,9},{9,10},{10,11},{12,13},{... | collective-permute-start | bytes 3145736 | tf_op jit(solution)/shard_map/ppermute | solution.py:1259
  268.1 57.1 %collective-permute-start.1 = (bf16[512,1024]{1,0:T(8,128)(2,1)}, bf16[512,1024]{1,0:T(8,128)(2,1)}, u32[]{:S(2)}, u32[]{:S(2)}) collective-permute-start(bf16[512,1024]{1,0:T(8,128)(2,1)} %collective-permute-done), channel_id=1, source_target_pairs={{0,1},{1,2},{2,3},{4,5},{5,6},{6,7},{8,9},{9,10},{10,11},{12,13},{... | collective-permute-start | bytes 3145736 | tf_op jit(solution)/shard_map/ppermute | solution.py:1259
  327.9 1.7 copy-start.26
  329.6 51.9 %copy-start.17 = (bf16[1,512,2048]{2,1,0:T(8,128)(2,1)S(1)}, bf16[1,512,2048]{2,1,0:T(8,128)(2,1)}, u32[]{:S(2)}) copy-start(bf16[1,512,2048]{2,1,0:T(8,128)(2,1)} %param.12) | copy-start | bytes 6291460
  381.4 8.0 copy-start.7
  381.4 8.0 copy-start.8
  381.5 10.1 copy-start.27
  389.4 2.2 copy-start.9
  389.4 2.1 copy-start.30
  538.2 24.1 %collective-permute-start.2 = (bf16[2048,2048]{1,0:T(8,128)(2,1)}, bf16[2048,2048]{1,0:T(8,128)(2,1)}, u32[]{:S(2)}, u32[]{:S(2)}) collective-permute-start(bf16[2048,2048]{1,0:T(8,128)(2,1)} %convolution_convert_fusion), channel_id=1, source_target_pairs={{0,4},{4,0},{8,12},{12,8},{16,20},{20,16},{24,28},{28,24},{1,5},{5... | collective-permute-start | bytes 25165832 | tf_op jit(solution)/shard_map/ppermute | solution.py:1220
  575.6 3.6 copy-start.19
  579.1 33.3 %collective-permute-start.4 = (bf16[256,2048]{1,0:T(8,128)(2,1)}, bf16[256,2048]{1,0:T(8,128)(2,1)}, u32[]{:S(2)}, u32[]{:S(2)}) collective-permute-start(bf16[256,2048]{1,0:T(8,128)(2,1)} %get-tuple-element.119), channel_id=1, source_target_pairs={{0,8},{4,12},{8,0},{12,4},{16,24},{20,28},{24,16},{28,20},{1,9},{5... | collective-permute-start | bytes 3145736 | tf_op jit(solution)/shard_map/ppermute | solution.py:1220
  579.8 32.7 %collective-permute-start.3 = (bf16[256,2048]{1,0:T(8,128)(2,1)S(1)}, bf16[256,2048]{1,0:T(8,128)(2,1)}, u32[]{:S(2)}, u32[]{:S(2)}) collective-permute-start(bf16[256,2048]{1,0:T(8,128)(2,1)S(1)} %get-tuple-element.118), channel_id=1, source_target_pairs={{0,16},{4,20},{8,24},{12,28},{16,0},{20,4},{24,8},{28,12},{1,17},{... | collective-permute-start | bytes 3145736 | tf_op jit(solution)/shard_map/ppermute | solution.py:1220
  580.2 217.4 %reduce-scatter.6.cloned.1.call-start = ((), (), s32[]{:S(2)}) async-start(), calls=%async_computation.8 | async-start | bytes 5242880 | tf_op jit(solution)/shard_map/reduce_scatter | solution.py:1278
  615.6 4.9 copy-start.41
  641.8 290.6 %reduce-scatter.8.cloned.1.call-start = ((), (), s32[]{:S(2)}) async-start(), calls=%async_computation.9 | async-start | bytes 5242880 | tf_op jit(solution)/shard_map/reduce_scatter | solution.py:1278
  641.8 47.7 %collective-permute-start.5 = (bf16[512,2048]{1,0:T(8,128)(2,1)}, bf16[512,2048]{1,0:T(8,128)(2,1)S(1)}, u32[]{:S(2)}, u32[]{:S(2)}) collective-permute-start(bf16[512,2048]{1,0:T(8,128)(2,1)} %pad_maximum_fusion), channel_id=1, source_target_pairs={{0,8},{4,12},{8,0},{12,4},{16,24},{20,28},{24,16},{28,20},{1,9},{5... | collective-permute-start | bytes 6291464 | tf_op jit(solution)/shard_map/ppermute | solution.py:1220
  643.4 47.5 %collective-permute-start.6 = (bf16[512,2048]{1,0:T(8,128)(2,1)}, bf16[512,2048]{1,0:T(8,128)(2,1)}, u32[]{:S(2)}, u32[]{:S(2)}) collective-permute-start(bf16[512,2048]{1,0:T(8,128)(2,1)} %pad_maximum_fusion.1), channel_id=1, source_target_pairs={{0,16},{4,20},{8,24},{12,28},{16,0},{20,4},{24,8},{28,12},{1,17},{... | collective-permute-start | bytes 6291464 | tf_op jit(solution)/shard_map/ppermute | solution.py:1220
  668.9 110.7 %copy-start.28 = (f32[2048]{0:T(1024)S(1)}, f32[2048]{0:T(1024)}, u32[]{:S(2)}) copy-start(f32[2048]{0:T(1024)} %param.19) | copy-start | bytes 24580
  668.9 110.7 %copy-start.31 = (f32[512]{0:T(512)S(1)}, f32[512]{0:T(512)}, u32[]{:S(2)}) copy-start(f32[512]{0:T(512)} %copy-done.30) | copy-start | bytes 6148
  689.5 1.3 copy-start.20
  690.9 93.5 %copy-start.14 = (bf16[1,512,2048]{2,1,0:T(8,128)(2,1)S(1)}, bf16[1,512,2048]{2,1,0:T(8,128)(2,1)}, u32[]{:S(2)}) copy-start(bf16[1,512,2048]{2,1,0:T(8,128)(2,1)} %param.23) | copy-start | bytes 6291460
  779.7 4.8 copy-start.10
  779.7 6.0 copy-start.12
  785.7 1.5 copy-start.38
  787.2 1.3 copy-start.21
  932.4 7.8 copy-start.5
  932.4 7.8 copy-start.18
  932.4 7.8 copy-start.34
  932.4 7.8 copy-start.37
  932.4 7.8 copy-start.40
  946.0 93.2 %copy-start.23 = (bf16[256,2048]{1,0:T(8,128)(2,1)S(1)}, bf16[256,2048]{1,0:T(8,128)(2,1)}, u32[]{:S(2)}) copy-start(bf16[256,2048]{1,0:T(8,128)(2,1)} %get-tuple-element.108) | copy-start | bytes 3145732
  946.0 99.9 %copy-start.15 = (bf16[1,512,2048]{2,1,0:T(8,128)(2,1)S(1)}, bf16[1,512,2048]{2,1,0:T(8,128)(2,1)}, u32[]{:S(2)}) copy-start(bf16[1,512,2048]{2,1,0:T(8,128)(2,1)} %param.23) | copy-start | bytes 6291460
  1036.1 8.3 copy-start.22
  1039.2 6.8 copy-start.11
  1039.2 6.8 copy-start.13
  1039.2 6.8 copy-start.29
  1039.3 6.7 copy-start.32
  1039.3 6.7 copy-start.39
  1046.0 8.7 copy-start.25
  1046.0 9.5 copy-start.24
Sparse Core Ops, SparseCore 0:
  68.5 84.1 all-gather.6
  154.3 78.7 all-gather.8
  234.6 110.0 all-gather.10
  346.4 126.1 all-gather.4
  580.3 78.0 reduce-scatter.3
  660.6 77.2 reduce-scatter.5
  740.2 77.2 reduce-scatter.7

commit v5 on v4

--- a/solution.py
+++ b/solution.py
@@ -22,6 +22,7 @@
 NTILE = 512
 STRIP = 16
 LONG = 60_000_000_000
+SHORT = 1_000_000
 
 F32 = jnp.float32
 BF16 = jnp.bfloat16
@@ -63,50 +64,6 @@
     ahead = pltpu.roll(values, LANES - 32, 1)
     behind = pltpu.roll(values, 32, 1)
     return jnp.where((lane % 64) < 32, ahead, behind)
-
-
-def qkv_kernel(x_ref, wq_ref, wkv_ref, cos_ref, sin_ref, q_ref, kv_ref):
-    x = x_ref[...]
-    cosine, sine = cos_ref[...], sin_ref[...]
-    for at in range(wq_ref.shape[1] // LANES):
-        part = pl.ds(at * LANES, LANES)
-        value = dot_nn(x, wq_ref[:, part])
-        q_ref[:, part] = (value * cosine + swap_halves(value) * sine).astype(BF16)
-    value = dot_nn(x, wkv_ref[...])
-    key = value[:, :LANES]
-    kv_ref[:, :LANES] = (key * cosine + swap_halves(key) * sine).astype(BF16)
-    kv_ref[:, LANES:] = value[:, LANES:].astype(BF16)
-
-
-def project_qkv(x, wq, wkv, cosine, sine):
-    rows, width = x.shape
-    blocks = wkv.shape[1] // (2 * LANES)
-    qcols = wq.shape[1] // blocks
-    return pl.pallas_call(
-        qkv_kernel,
-        grid=(blocks,),
-        in_specs=[
-            pl.BlockSpec((rows, width), lambda g: (0, 0)),
-            pl.BlockSpec((width, qcols), lambda g: (0, g)),
-            pl.BlockSpec((width, 2 * LANES), lambda g: (0, g)),
-            pl.BlockSpec((rows, LANES), lambda g: (0, 0)),
-            pl.BlockSpec((rows, LANES), lambda g: (0, 0)),
-        ],
-        out_specs=[
-            pl.BlockSpec((rows, qcols), lambda g: (0, g)),
-            pl.BlockSpec((rows, 2 * LANES), lambda g: (0, g)),
-        ],
-        out_shape=[
-            jax.ShapeDtypeStruct((rows, wq.shape[1]), BF16),
-            jax.ShapeDtypeStruct((rows, wkv.shape[1]), BF16),
-        ],
-        compiler_params=pltpu.CompilerParams(vmem_limit_bytes=40 << 20),
-        cost_estimate=pl.CostEstimate(
-            flops=2 * rows * width * (wq.shape[1] + wkv.shape[1]),
-            bytes_accessed=2 * width * (wq.shape[1] + wkv.shape[1]),
-            transcendentals=0,
-        ),
-    )(x, wq, wkv, cosine, sine)
 
 
 def fill_bias(bias_ref, low_ref, reach):
@@ -495,77 +452,80 @@
 
 
 def spread_kernel(wide, z_size, mlp_count, *refs):
-    attn_count = (len(refs) - 3) // 2 - mlp_count
+    attn_count = (len(refs) - 5) // 2 - mlp_count
     count = mlp_count + attn_count
     ins, outs = refs[:count], refs[count : 2 * count]
-    own_sem, send_sem, recv_sem = refs[2 * count :]
-    (row, col, core), _ = neighbours(wide)
-    dp, place = lax.axis_index("dp"), lax.axis_index("tensor")
-    mine = 4 * row + 2 * col + core
-    base = dp - (2 * wide * row + 2 * col + core)
-
-    def peer(dy, dx, dc):
-        y, x, c = (row + dy) % 2, (col + dx) % 2, (core + dc) % 2
-        return base + 2 * wide * y + 2 * x + c, 4 * y + 2 * x + c
-
-    flips = [(dy, dx, dc) for dy in range(2) for dx in range(2) for dc in range(2)][1:]
-    barrier = pltpu.get_barrier_semaphore()
-    for flip in flips:
-        pl.semaphore_signal(
-            barrier, inc=1, device_id={"dp": peer(*flip)[0]}, device_id_type=MESH
-        )
-    for step in range(1, z_size):
-        pl.semaphore_signal(
-            barrier, inc=1, device_id={"tensor": (place + step) % z_size}, device_id_type=MESH
-        )
-    pl.semaphore_wait(barrier, len(flips) + z_size - 1)
-
-    copies, local = [], []
-    slot = 0
-    for at in range(mlp_count, count):
-        src, dst = ins[at], outs[at]
-        cols = src.shape[1]
-        part = pl.ds(pl.multiple_of(place * cols, LANES), cols)
-        for step in range(1, z_size):
-            copies.append(
-                pltpu.make_async_remote_copy(
-                    src_ref=src, dst_ref=dst.at[:, part],
-                    send_sem=send_sem.at[slot], recv_sem=recv_sem.at[slot],
-                    device_id={"tensor": (place + step) % z_size}, device_id_type=MESH,
-                )
-            )
-            slot += 1
-        local.append(pltpu.make_async_copy(src, dst.at[:, part], own_sem.at[at]))
+    own_sem, send_sem, recv_sem, z_send, z_recv = refs[2 * count :]
+    place = lax.axis_index("tensor")
+    mine, found = others(wide)
+    greet(along_peers(place, z_size) + [device for _, device in found])
+
+    local, copies = [], []
     for at in range(mlp_count):
         src, dst = ins[at], outs[at]
         rows, cols = src.shape[0], dst.shape[1]
         here = pl.ds(pl.multiple_of(mine * rows, rows), rows)
-        for flip in flips:
-            device, other = peer(*flip)
+        for index, (other, device) in enumerate(found):
             copies.append(
                 pltpu.make_async_remote_copy(
                     src_ref=src.at[:, pl.ds(pl.multiple_of(other * cols, LANES), cols)],
                     dst_ref=dst.at[here],
-                    send_sem=send_sem.at[slot], recv_sem=recv_sem.at[slot],
-                    device_id={"dp": device}, device_id_type=MESH,
+                    send_sem=send_sem.at[at, index], recv_sem=recv_sem.at[at, index],
+                    device_id=device, device_id_type=MESH,
                 )
             )
-            slot += 1
         own = src.at[:, pl.ds(pl.multiple_of(mine * cols, LANES), cols)]
         local.append(pltpu.make_async_copy(own, dst.at[here], own_sem.at[at]))
-    for copy in copies:
+
+    def block(at, origin):
+        cols = ins[at].shape[1]
+        return outs[at].at[:, pl.ds(pl.multiple_of(origin * cols, LANES), cols)]
+
+    def hop(at, way, step, receive=False):
+        sign = 1 - 2 * way
+        origin = place - sign * (step if receive else step - 1)
+        slot = 2 * (step - 1) + way
+        src = block(at, origin) if receive or step > 1 else ins[at]
+        return pltpu.make_async_remote_copy(
+            src_ref=src, dst_ref=block(at, origin),
+            send_sem=z_send.at[at - mlp_count, slot], recv_sem=z_recv.at[at - mlp_count, slot],
+            device_id={"tensor": (place + z_size + sign) % z_size}, device_id_type=MESH,
+        )
+
+    def sends(way, step):
+        if way == 0:
+            return (place + 1 < z_size) & (place >= step - 1)
+        return (place >= 1) & (place + step - 1 < z_size)
+
+    def receives(way, step):
+        return place >= step if way == 0 else place + step < z_size
+
+    for at in range(mlp_count, count):
+        local.append(pltpu.make_async_copy(ins[at], block(at, place), own_sem.at[at]))
+        for way in range(2):
+            pl.when(sends(way, 1))(lambda: hop(at, way, 1).start())
+    for copy in copies + local:
         copy.start()
-    for copy in local:
-        copy.start()
-    for copy in local:
-        copy.wait()
-    for copy in copies:
+    for step in range(1, z_size):
+        for at in range(mlp_count, count):
+            for way in range(2):
+
+                @pl.when(receives(way, step))
+                def _():
+                    hop(at, way, step, True).wait_recv()
+
+                if step + 1 < z_size:
+                    pl.when(sends(way, step + 1))(lambda: hop(at, way, step + 1).start())
+    for step in range(1, z_size):
+        for at in range(mlp_count, count):
+            for way in range(2):
+                pl.when(sends(way, step))(lambda: hop(at, way, step).wait_send())
+    for copy in local + copies:
         copy.wait()
 
 
 def spread_weights(mlp, attn, dp_size, z_size):
     count = len(mlp) + len(attn)
-    slots = (z_size - 1) * len(attn) + (GROUP - 1) * len(mlp)
     spec = pl.BlockSpec(memory_space=pl.ANY)
     out = [jax.ShapeDtypeStruct((GROUP * w.shape[0], w.shape[1] // GROUP), BF16) for w in mlp]
     out += [jax.ShapeDtypeStruct((w.shape[0], z_size * w.shape[1]), BF16) for w in attn]
@@ -576,8 +536,10 @@
         out_shape=out,
         scratch_shapes=[
             pltpu.SemaphoreType.DMA((count,)),
-            pltpu.SemaphoreType.DMA((slots,)),
-            pltpu.SemaphoreType.DMA((slots,)),
+            pltpu.SemaphoreType.DMA((len(mlp), GROUP - 1)),
+            pltpu.SemaphoreType.DMA((len(mlp), GROUP - 1)),
+            pltpu.SemaphoreType.DMA((len(attn), 2 * (z_size - 1))),
+            pltpu.SemaphoreType.DMA((len(attn), 2 * (z_size - 1))),
         ],
         compiler_params=pltpu.CompilerParams(collective_id=2, has_side_effects=True),
         cost_estimate=pl.CostEstimate(flops=LONG, bytes_accessed=0, transcendentals=0),
@@ -662,54 +624,136 @@
             self.copy(*entry, peer).wait_send()
 
 
-def gather_kernel(wide, count, *refs):
-    ins, outs = refs[:count], refs[count : 2 * count]
-    own_sem, send_sem, recv_sem = refs[2 * count :]
+def project_kernel(
+    wide, z_size, x_ref, cos_ref, sin_ref, wkv_ref, wq_ref, wo_ref,
+    q_ref, kv_ref, wkv_out, wq_out, wo_out,
+    wkv_all, wq_all, wo_all, keys, own_sem, send_sem, recv_sem, kv_send, kv_recv, out_sem,
+):
+    place = lax.axis_index("tensor")
+    rows = x_ref.shape[0]
+    count = keys.shape[0] // rows - 1
+    parts = ((wkv_ref, wkv_all, wkv_out), (wq_ref, wq_all, wq_out), (wo_ref, wo_all, wo_out))
     rings = [
-        Ring(wide, outs[at], ins[at].shape[0], send_sem.at[at], recv_sem.at[at])
-        for at in range(count)
+        Ring(wide, full, part.shape[0], send_sem.at[at], recv_sem.at[at])
+        for at, (part, full, _) in enumerate(parts)
     ]
     local = [
-        pltpu.make_async_copy(ins[at], outs[at].at[rings[at].mine()], own_sem.at[at])
-        for at in range(count)
+        pltpu.make_async_copy(part, full.at[ring.mine()], own_sem.at[at])
+        for at, ((part, full, _), ring) in enumerate(zip(parts, rings))
+    ]
+    outward = [
+        pltpu.make_async_copy(full, out, out_sem.at[at])
+        for at, (_, full, out) in enumerate(parts)
     ]
     for copy in local:
         copy.start()
-    meet(rings[0].peers)
-    for copy, ring in zip(local, rings):
+    keys[: count * rows, :] = jnp.zeros((count * rows, keys.shape[1]), BF16)
+    greet([{"dp": peer} for peer in rings[0].peers] + along_peers(place, z_size))
+    for copy in local:
         copy.wait()
-        ring.start_own()
-    for ring in rings:
-        ring.first_halves()
-        ring.second_halves()
-    for ring in rings:
+
+    def rotated(value):
+        return (value * cos_ref[...] + swap_halves(value) * sin_ref[...]).astype(BF16)
+
+    def hop(step):
+        return pltpu.make_async_remote_copy(
+            src_ref=keys.at[pl.ds((count - step + 1) * rows, rows)],
+            dst_ref=keys.at[pl.ds((count - step) * rows, rows)],
+            send_sem=kv_send.at[step - 1], recv_sem=kv_recv.at[step - 1],
+            device_id={"tensor": (place + 1) % z_size}, device_id_type=MESH,
+        )
+
+    def pass_keys(step):
+        if step > 1:
+            pl.when(place >= step - 1)(lambda: hop(step - 1).wait_recv())
+        if step <= count:
+            sends = (place + 1 < z_size) & (place >= step - 1)
+            pl.when(sends)(lambda: hop(step).start())
+
+    def finish(ring):
         ring.far_halves()
         for name in ("own", "x", "y", "d"):
             ring.from_sibling(name, 0, 1)
+
+    rings[0].start_own()
+    rings[0].first_halves()
+    rings[0].second_halves()
+    rings[1].start_own()
+    finish(rings[0])
+    outward[0].start()
+
+    @pl.loop(0, wkv_all.shape[1] // (2 * LANES))
+    def _(at):
+        n = pl.ds(pl.multiple_of(at * 2 * LANES, LANES), 2 * LANES)
+        value = dot_nn(x_ref[...], wkv_all[:, n])
+        both = jnp.concatenate([rotated(value[:, :LANES]), value[:, LANES:].astype(BF16)], axis=1)
+        keys[pl.ds(count * rows, rows), n] = both
+
+    pass_keys(1)
+    rings[1].first_halves()
+    rings[1].second_halves()
+    rings[2].start_own()
+    finish(rings[1])
+    outward[1].start()
+
+    @pl.loop(0, wq_all.shape[1] // (2 * LANES))
+    def _(at):
+        n = pl.ds(pl.multiple_of(at * 2 * LANES, LANES), 2 * LANES)
+        value = dot_nn(x_ref[...], wq_all[:, n])
+        both = [rotated(value[:, :LANES]), rotated(value[:, LANES:])]
+        q_ref[:, n] = jnp.concatenate(both, axis=1)
+
+    rings[2].first_halves()
+    rings[2].second_halves()
+    for step in range(2, count + 2):
+        pass_keys(step)
+    keys_out = pltpu.make_async_copy(keys, kv_ref, out_sem.at[3])
+    keys_out.start()
+    finish(rings[2])
+    outward[2].start()
+    for step in range(1, count + 1):
+        sends = (place + 1 < z_size) & (place >= step - 1)
+        pl.when(sends)(lambda: hop(step).wait_send())
     for ring in rings:
         ring.sent()
-
-
-def gather_rows(arrays, dp_size):
-    count = len(arrays)
-    spec = pl.BlockSpec(memory_space=pl.ANY)
+    for copy in outward + [keys_out]:
+        copy.wait()
+
+
+def project(x, cosine, sine, wkv, wq, wo, reach, dp_size, z_size):
+    rows, width = x.shape
+    far = pl.BlockSpec(memory_space=pl.ANY)
+    near = pl.BlockSpec(memory_space=pltpu.VMEM)
+    weights = (wkv, wq, wo)
+    whole = [(GROUP * w.shape[0], w.shape[1]) for w in weights]
+    keys = (reach + rows, wkv.shape[1])
     return pl.pallas_call(
-        functools.partial(gather_kernel, 2 * math.isqrt(dp_size // GROUP), count),
-        in_specs=[spec] * count,
-        out_specs=[spec] * count,
-        out_shape=[jax.ShapeDtypeStruct((GROUP * a.shape[0], a.shape[1]), a.dtype) for a in arrays],
-        scratch_shapes=[
-            pltpu.SemaphoreType.DMA((count,)),
-            pltpu.SemaphoreType.DMA((count, Ring.COPIES)),
-            pltpu.SemaphoreType.DMA((count, Ring.COPIES)),
+        functools.partial(project_kernel, 2 * math.isqrt(dp_size // GROUP), z_size),
+        in_specs=[near] * 3 + [far] * 3,
+        out_specs=[near] + [far] * 4,
+        out_shape=[jax.ShapeDtypeStruct((rows, wq.shape[1]), BF16)]
+        + [jax.ShapeDtypeStruct(shape, BF16) for shape in [keys] + whole],
+        scratch_shapes=[pltpu.VMEM(shape, BF16) for shape in whole + [keys]]
+        + [
+            pltpu.SemaphoreType.DMA((3,)),
+            pltpu.SemaphoreType.DMA((3, Ring.COPIES)),
+            pltpu.SemaphoreType.DMA((3, Ring.COPIES)),
+            pltpu.SemaphoreType.DMA((reach // rows,)),
+            pltpu.SemaphoreType.DMA((reach // rows,)),
+            pltpu.SemaphoreType.DMA((4,)),
         ],
-        compiler_params=pltpu.CompilerParams(collective_id=3, has_side_effects=True),
-        cost_estimate=pl.CostEstimate(flops=2 * LONG, bytes_accessed=0, transcendentals=0),
-    )(*arrays)
+        compiler_params=pltpu.CompilerParams(
+            collective_id=3, has_side_effects=True, vmem_limit_bytes=56 << 20
+        ),
+        cost_estimate=pl.CostEstimate(
+            flops=2 * LONG, bytes_accessed=4 * width * sum(w.shape[1] for w in weights),
+            transcendentals=0,
+        ),
+    )(x, cosine, sine, wkv, wq, wo)
 
 
 def gate_up_kernel(
-    wide, own_ref, wg_ref, wu_ref, all_ref, gate_ref, up_ref, hid_ref,
+    wide, own_ref, wg_ref, wu_ref, all_ref, gate_ref, up_ref, hid_ref, core_ref,
     full, stage, own_sem, send_sem, recv_sem, out_sem, all_sem,
 ):
     rows = own_ref.shape[0]
@@ -721,11 +765,15 @@
     local.wait()
     ring.start_own()
 
-    def out_copies(slot, where):
+    def out_copies(slot, places):
+        where, core, chip = places
         return [
             pltpu.make_async_copy(stage.at[slot, i], ref.at[where], out_sem.at[slot, i])
             for i, ref in enumerate((gate_ref, up_ref, hid_ref))
-        ] + [pltpu.make_async_copy(full.at[where], all_ref.at[where], all_sem.at[slot])]
+        ] + [
+            pltpu.make_async_copy(stage.at[slot, 2], core_ref.at[core, chip], out_sem.at[slot, 3]),
+            pltpu.make_async_copy(full.at[where], all_ref.at[where], all_sem.at[slot]),
+        ]
 
     def step_place(step):
         phase, i = step // 4, step % 4
@@ -735,7 +783,10 @@
         half = (first + last) * (i % 2) + high * (1 - low)
         dx = middle * (1 - i % 2) + last
         dy = middle * (i % 2) + last
-        return ring.place(dy, dx, i // 2, half)
+        chip = 2 * ((ring.row + dy) % 2) + (ring.col + dx) % 2
+        part = rows // 2
+        chip_rows = pl.ds(pl.multiple_of(chip * rows + half * part, part), part)
+        return ring.place(dy, dx, i // 2, half), i // 2, chip_rows
 
     @pl.loop(0, 16)
     def _(step):
@@ -758,14 +809,14 @@
         pl.when(step == 14)(lambda: ring.from_sibling("d", 0, 1))
 
         slot = step % 2
-        where = step_place(step)
+        places = step_place(step)
 
         @pl.when(step >= 2)
         def _():
             for copy in out_copies(slot, step_place(step - 2)):
                 copy.wait()
 
-        x = full[where, :]
+        x = full[places[0], :]
 
         @pl.loop(0, cols // NTILE)
         def _(at):
@@ -776,7 +827,7 @@
             stage[slot, 1, :, n] = up.astype(BF16)
             stage[slot, 2, :, n] = (gate * up / (1.0 + jnp.exp(-gate))).astype(BF16)
 
-        for copy in out_copies(slot, where):
+        for copy in out_copies(slot, places):
             copy.start()
 
     for step in (14, 15):
@@ -794,25 +845,24 @@
     return pl.pallas_call(
         functools.partial(gate_up_kernel, 2 * math.isqrt(dp_size // GROUP)),
         in_specs=[far, near, near],
-        out_specs=[far] * 4,
+        out_specs=[far] * 5,
         out_shape=[jax.ShapeDtypeStruct((tokens, width), BF16)]
-        + [jax.ShapeDtypeStruct((tokens, cols), BF16)] * 3,
+        + [jax.ShapeDtypeStruct((tokens, cols), BF16)] * 3
+        + [jax.ShapeDtypeStruct((2, tokens // 2, cols), BF16)],
         scratch_shapes=[
             pltpu.VMEM((tokens, width), BF16),
             pltpu.VMEM((2, 3, rows // 2, cols), BF16),
             pltpu.SemaphoreType.DMA,
             pltpu.SemaphoreType.DMA((Ring.COPIES,)),
             pltpu.SemaphoreType.DMA((Ring.COPIES,)),
-            pltpu.SemaphoreType.DMA((2, 3)),
+            pltpu.SemaphoreType.DMA((2, 4)),
             pltpu.SemaphoreType.DMA((2,)),
         ],
         compiler_params=pltpu.CompilerParams(
             collective_id=1, has_side_effects=True, vmem_limit_bytes=56 << 20
         ),
         cost_estimate=pl.CostEstimate(
-            flops=4 * tokens * width * cols,
-            bytes_accessed=tokens * (2 * width + 6 * cols) + 4 * width * cols,
-            transcendentals=tokens * cols,
+            flops=SHORT, bytes_accessed=0, transcendentals=0
         ),
     )(hn, wg, wu)
 
@@ -1269,10 +1319,10 @@
         for w in (w_gate, w_up, w_down, jnp.concatenate([w_key, w_value], axis=1), w_query, w_out)
     ]
     spread = spread_weights(shards[:3], shards[3:], dp_size, z_size)
-    wg, wu, wd = (
-        layout.to_rows(lax.all_gather(w, "tensor", axis=1, tiled=True)) for w in spread[:3]
-    )
-    wkv, wq, wo = (layout.to_rows(w) for w in gather_rows(spread[3:], dp_size))
+    def gather_z(array):
+        return layout.to_rows(lax.all_gather(array, "tensor", axis=1, tiled=True))
+
+    wg, wu = gather_z(spread[0]), gather_z(spread[1])
 
     def along_z(total):
         return lax.psum_scatter(
@@ -1281,33 +1331,27 @@
 
     r1 = rms_scale(x)
     xn = (x * r1 * attn_gain).astype(BF16)
-    q, kv = project_qkv(xn, wq, wkv, cosine, sine)
-    grad, kv = lax.optimization_barrier((cotangent[0], kv))
-    pieces, moved = [kv], kv
-    for _ in range(reach // rows):
-        moved = shift(moved, 1)
-        pieces.insert(0, moved)
-    kv_all = jnp.concatenate(pieces, axis=0)
+    q, kv_all, wkv, wq, wo = project(
+        layout.from_cols(xn), cosine, sine, *spread[3:], reach, dp_size, z_size
+    )
+    grad, q, spread_wd = lax.optimization_barrier((cotangent[0], q, spread[2]))
+    wkv, wq, wo = layout.to_rows(wkv), layout.to_rows(wq), layout.to_rows(wo)
+    dy = layout.gather(grad)
     att, lse = attend(q, kv_all, low)
+    wd = gather_z(spread_wd)
     h = x + dot_nt(att, wo)
 
     r2 = rms_scale(h)
-    hn, gate, up, hidden = gate_up((h * r2 * mlp_gain).astype(BF16), wg, wu, dp_size)
-    dy = layout.gather(grad)
+    hn, gate, up, hidden, by_core = gate_up((h * r2 * mlp_gain).astype(BF16), wg, wu, dp_size)
     row, col, core = neighbours(2 * layout.cols)[0]
-    by_core = hidden.reshape(GROUP // 2, 2, rows, -1)
-
-    def out_part(of_core):
-        some = lax.dynamic_index_in_dim(by_core, of_core, 1, False)
-        return dot_nt(some.reshape(GROUP * rows // 2, -1), wd)
-
     def chunk(array, y, x):
         return lax.dynamic_index_in_dim(array, 2 * y + x, 0, False)
 
-    away = out_part(1 - core).astype(BF16)
+    by_core, dy = lax.optimization_barrier((by_core, dy))
+    away = dot_nt(by_core[1], wd).astype(BF16)
     dy, away = lax.optimization_barrier((dy, away))
     total_wd = dot_tn(dy, hidden).astype(BF16)
-    near_sum = out_part(core) + layout.swap(away, 1).astype(F32)
+    near_sum = dot_nt(by_core[0], wd) + layout.swap(away, 1).astype(F32)
     near_sum = near_sum.astype(BF16)
     dy, total_wd, near_sum = lax.optimization_barrier((dy, total_wd, near_sum))
     part_wd = along_z(total_wd)

time: 1070 us -> 1030 us (0.963)
  Pallas kernels: 699 us -> 652 us
  waiting for transfers between devices: 102 us -> 139 us
  starting transfers between devices: 25.8 us -> 4.56 us
    all_gather x3, waiting for transfers between devices: 0.01 us -> 115 us  [gather_z(): return layout.to_rows(lax.all_gather(array, 'tensor', axis=1, tiled=True))]
    ppermute x2 -> x0, waiting for transfers between devices: 80.1 us -> none  [shift(): return lax.ppermute(array, 'tensor', pairs)]
    pallas_call x2 -> x1, Pallas kernels: 151 us -> 95.4 us  [project(): pl.pallas_call(functools.partial(project_kernel, 2 * math.isqrt(dp_size /...]
    pallas_call x1, Pallas kernels: 123 us -> 146 us  [gate_up(): pl.pallas_call(functools.partial(gate_up_kernel, 2 * math.isqrt(dp_size /...]
    ppermute x2 -> x0, starting transfers between devices: 21.5 us -> none  [shift(): return lax.ppermute(array, 'tensor', pairs)]
  transfers between devices with their start and end apart: 14 -> 12, of which waited for: 4 -> 3; matrix products, arithmetic and copies ran while one was open for 15% -> 13% of each run, Pallas kernels for 52% -> 50%
where the time goes in v5:
time: 1030 us; the launch traced here: 1020 us
  Pallas kernels  652 us (63%)
  matrix products  159 us (15%)
  waiting for transfers between devices  139 us (13%)
  other arithmetic  36.6 us (4%)
  local copies, waits for them, and re-layouts  17.7 us (2%)
  between operations  15.1 us (1%)
    pallas_call x1, Pallas kernels, gate_up(): pl.pallas_call(functools.partial(gate_up_kernel, 2 * math.isqrt(dp_size /...  146 us
    pallas_call x1, Pallas kernels, attend_back(): pl.pallas_call(functools.partial(attend_back_kernel, reach, 2 * math.isqr...  133 us
    all_gather x3, waiting for transfers between devices, gather_z(): return layout.to_rows(lax.all_gather(array, 'tensor', axis=1, tiled=True))  115 us
    pallas_call x1, Pallas kernels, project(): pl.pallas_call(functools.partial(project_kernel, 2 * math.isqrt(dp_size /...  95.4 us
    pallas_call x1, Pallas kernels, last_grads(): pl.pallas_call(functools.partial(tail_kernel, 2 * math.isqrt(dp_size // G...  89.3 us
    pallas_call x1, Pallas kernels, hidden_back(): pl.pallas_call(functools.partial(hidden_back_kernel, 2 * math.isqrt(dp_si...  87.7 us
    dot_general x3, matrix products, dot_tn(): lax.dot_general(left, right, (((0,), (0,)), ((), ())), preferred_element_...  69.4 us
    pallas_call x1, Pallas kernels, attend(): pl.pallas_call(functools.partial(attend_kernel, reach), grid=(heads, tile...  51.9 us
  transfers between devices with their start and end apart: 12, of which 3 were waited for; matrix products, arithmetic and copies ran while one was open for 13% of the time, Pallas kernels for 50%

profile of v5, /device:TPU:0, one launch (start us, length us, event | category | flops | bytes accessed | tf_op | source)
XLA Modules:
  0.0 1024.0 jit_solution(1498928960098149546)
XLA Ops:
  7.2 0.0 all-gather.5.cloned.1.call-start
  7.2 1.5 pad_maximum_fusion.4.refs_3_
  8.8 49.8 %shard_map.203 = (bf16[2048,256]{1,0:T(8,128)(2,1)}, bf16[2048,256]{1,0:T(8,128)(2,1)}, bf16[2048,256]{1,0:T(8,128)(2,1)}, bf16[256,1024]{1,0:T(8,128)(2,1)}, bf...) custom-call(bf16[256,2048]{1,0:T(8,128)(2,1)} %refs_0_.1, bf16[256,2048]{1,0:T(8,128)(2,1)} %refs_1_.1, ...), custom_call_target="tpu_custom_call" | custom-call | flops 60000002048 | tf_op jit(solution)/shard_map/pallas_call | solution.py:532
  58.6 0.0 all-gather.7.cloned.1.call-start
  58.7 0.7 all-gather.7.cloned.1.call-update
  59.4 0.0 all-gather.9.cloned.1.call-start
  59.4 0.5 fusion.16
  60.0 0.1 convert_reduce_fusion
  60.1 0.1 select_reduce_fusion
  60.2 1.9 fusion.10.x_ref
  62.1 0.1 subtract_add_fusion.1
  62.1 1.0 fusion.34
  63.1 1.3 pad_maximum_fusion.2
  64.4 95.4 %shard_map.204 = (bf16[512,2048]{1,0:T(8,128)(2,1)}, bf16[1536,1024]{1,0:T(8,128)(2,1)}, bf16[2048,1024]{1,0:T(8,128)(2,1)}, bf16[2048,2048]{1,0:T(8,128)(2,1)}, bf16[2048,2048]{1,0:T(8,128)(2,1)}) custom-call(bf16[512,2048]{1,0:T(8,128)(2,1)} %fusion.10.x_ref, f32[512,128]{1,0:T(8,128)} %get-tuple-element.145.cos_ref.cos_all, ...), custom_call_target="tpu_custom_call" | custom-call | flops 120000004096 | bytes 41943040 | tf_op jit(solution)/shard_map/pallas_call | solution.py:730
  159.9 0.0 all-gather.11.cloned.1.call-start
  159.9 0.5 all-gather.11.cloned.1.call-update
  160.4 0.3 reduce-scatter.4.cloned.1.call-start
  160.7 1.6 copy-done.2
  162.3 51.9 %shard_map.205 = (bf16[512,2048]{1,0:T(8,128)(2,1)S(1)}, f32[32,1,512]{2,1,0:T(1,128)S(1)}) custom-call(bf16[512,2048]{1,0:T(8,128)(2,1)S(1)} %copy-done.2, bf16[1536,1024]{1,0:T(8,128)(2,1)} %get-tuple-element.71.k_ref.v_ref, bf16[1536,1024]{1,0:T(8,128)(2,1)} %get-tuple-element.71.k_ref.v_ref, s32[1,512]{1,0:T(1,128)S(1)} %bitcast.72), custom_call_target="tpu_custom_call" | custom-call | flops 21474836480 | bytes 7340032 | tf_op jit(solution)/shard_map/pallas_call | solution.py:126
  214.2 4.7 multiply_reduce_fusion.2
  218.9 1.9 copy-done.4
  220.9 1.7 multiply_convert_fusion.own_ref
  222.6 29.3 %all-gather.7.cloned.1.call-done.wu_ref = bf16[2048,1024]{1,0:T(8,128)(2,1)} async-done(((bf16[2048,256]{1,0:T(8,128)(2,1)}), bf16[2048,1024]{1,0:T(8,128)(2,1)}) %all-gather.7.cloned.1.call-update) | async-done | bytes 4194320 | tf_op jit(solution)/shard_map/all_gather | solution.py:1323
  252.0 145.5 %shard_map.206 = (bf16[4096,2048]{1,0:T(8,128)(2,1)}, bf16[4096,1024]{1,0:T(8,128)(2,1)}, bf16[4096,1024]{1,0:T(8,128)(2,1)}, bf16[4096,1024]{1,0:T(8,128)(2,1)}, bf16[2,2048,1024]{2,1,0:T(8,128)(2,1)}) custom-call(bf16[512,2048]{1,0:T(8,128)(2,1)} %multiply_convert_fusion.own_ref, bf16[2048,1024]{1,0:T(8,128)(2,1)} %all-gather.5.cloned.1.call-done.wg_ref, ...), custom_call_target="tpu_custom_call" | custom-call | flops 1000000 | tf_op jit(solution)/shard_map/pallas_call | solution.py:845
  397.5 85.5 %all-gather.11.cloned.1.call-done = bf16[2048,1024]{1,0:T(8,128)(2,1)} async-done(((bf16[2048,256]{1,0:T(8,128)(2,1)}), bf16[2048,1024]{1,0:T(8,128)(2,1)}) %all-gather.11.cloned.1.call-update) | async-done | bytes 4194320 | tf_op jit(solution)/shard_map/all_gather | solution.py:1323
  483.0 14.0 %convolution_convert_fusion = bf16[2048,2048]{1,0:T(8,128)(2,1)} fusion(bf16[2048,1024]{1,0:T(8,128)(2,1)} %all-gather.11.cloned.1.call-done, bf16[2,2048,1024]{2,1,0:T(8,128)(2,1)} %get-tuple-element.79), kind=kOutput, calls=%fused_computation.17 | convolution fusion | flops 8594128896 | bytes 16777216 | tf_op jit(solution)/shard_map/dot_general | solution.py:36
  497.0 24.1 %convolution_convert_fusion.3 = bf16[2048,1024]{1,0:T(8,128)(2,1)} fusion(bf16[4096,2048]{1,0:T(8,128)(2,1)} %all-gather.9.cloned.1.call-done, bf16[4096,1024]{1,0:T(8,128)(2,1)} %get-tuple-element.82), kind=kOutput, calls=%fused_computation.46 | convolution fusion | flops 17181966336 | bytes 29360128 | tf_op jit(solution)/shard_map/dot_general | solution.py:40
  521.2 13.2 %add_convert_fusion = bf16[2048,2048]{1,0:T(8,128)(2,1)S(1)} fusion(bf16[2048,2048]{1,0:T(8,128)(2,1)} %collective-permute-done, bf16[2048,1024]{1,0:T(8,128)(2,1)} %all-gather.11.cloned.1.call-done, bf16[2,2048,1024]{2,1,0:T(8,128)(2,1)} %get-tuple-element.79), kind=kOutput, calls=%fused_computation.11 | convolution fusion | flops 8602517504 | bytes 25165824 | tf_op jit(solution)/shard_map/dot_general | solution.py:36
  534.4 1.8 dynamic-slice_bitcast_fusion.2
  536.2 1.7 copy-done.13
  538.0 1.5 collective-permute-start.2
  539.5 1.5 collective-permute-start.1
  541.0 0.0 reduce-scatter.6.cloned.1.call-start
  541.0 33.1 %fusion.7 = (bf16[4096,1024]{1,0:T(8,128)(2,1)}, bf16[4096,1024]{1,0:T(8,128)(2,1)}) fusion(bf16[4096,1024]{1,0:T(8,128)(2,1)} %get-tuple-element.87, bf16[4096,1024]{1,0:T(8,128)(2,1)} %get-tuple-element.86, bf16[4096,2048]{1,0:T(8,128)(2,1)} %all-gather.9.cloned.1.call-done, bf16[2048,1024]{1,0:T(8,128)(2,1)} %all-gather.11.cloned.1.call-done), kind=kOutput, calls=%fused_computation.10 | convolution fusion | flops 17242783744 | bytes 54525952 | tf_op jit(solution)/shard_map/dot_general | solution.py:32
  574.1 3.1 fusion.32
  577.2 1.5 pad_maximum_fusion
  578.7 1.5 pad_maximum_fusion.1
  580.2 1.9 copy-done.35
  582.1 21.3 %convolution_convert_fusion.2 = bf16[2048,1024]{1,0:T(8,128)(2,1)} fusion(bf16[4096,2048]{1,0:T(8,128)(2,1)} %get-tuple-element.89, bf16[4096,1024]{1,0:T(8,128)(2,1)S(1)} %copy-done.35), kind=kOutput, calls=%fused_computation.45 | convolution fusion | flops 17181966336 | bytes 29360128 | tf_op jit(solution)/shard_map/dot_general | solution.py:40
  603.4 0.0 reduce-scatter.8.cloned.1.call-start
  603.5 0.6 collective-permute-start.3
  604.1 0.5 collective-permute-start.4
  604.6 24.0 %convolution_convert_fusion.1 = bf16[2048,1024]{1,0:T(8,128)(2,1)} fusion(bf16[4096,2048]{1,0:T(8,128)(2,1)} %get-tuple-element.89, bf16[4096,1024]{1,0:T(8,128)(2,1)} %get-tuple-element.97.dup_ref), kind=kOutput, calls=%fused_computation.44 | convolution fusion | flops 17181966336 | bytes 29360128 | tf_op jit(solution)/shard_map/dot_general | solution.py:40
  628.6 22.6 %collective-permute-done.3 = bf16[512,2048]{1,0:T(8,128)(2,1)S(1)} collective-permute-done((bf16[512,2048]{1,0:T(8,128)(2,1)}, bf16[512,2048]{1,0:T(8,128)(2,1)S(1)}, u32[]{:S(2)}, u32[]{:S(2)}) %collective-permute-start.3) | collective-permute-done | bytes 2097184 | tf_op jit(solution)/shard_map/ppermute | solution.py:1270
  651.2 1.3 copy-done.14
  652.5 87.7 %shard_map.207 = f32[512,2048]{1,0:T(8,128)} custom-call(bf16[4096,1024]{1,0:T(8,128)(2,1)} %get-tuple-element.90.dgate_ref, bf16[4096,1024]{1,0:T(8,128)(2,1)} %get-tuple-element.97.dup_ref, bf16[2048,1024]{1,0:T(8,128)(2,1)} %all-gather.5.cloned.1.call-done.wg_ref, bf16[2048,1024]{1,0:T(8,128)(2,1)} %all-gather.7.cloned.1.call-done.wu_ref), custom_call_target="tpu_custom_call" | custom-call | flops 34359738368 | bytes 29360128 | tf_op jit(solution)/shard_map/pallas_call | solution.py:1044
  740.2 4.7 multiply_reduce_fusion
  745.0 1.2 copy-done.7
  746.2 1.5 fusion.35.h_ref
  747.8 1.3 copy-done.15
  749.1 9.0 convolution_convert_fusion.4.do_ref
  758.1 132.8 %shard_map.208 = (bf16[512,2048]{1,0:T(8,128)(2,1)}, bf16[512,1024]{1,0:T(8,128)(2,1)}, f32[256,512]{1,0:T(8,128)}, bf16[256,2048]{1,0:T(8,128)(2,1)}, bf16[256,2048]{1,0:T(8,128)(2,1)}) custom-call(bf16[512,2048]{1,0:T(8,128)(2,1)} %get-tuple-element.70.q_ref, bf16[512,2048]{1,0:T(8,128)(2,1)} %convolution_convert_fusion.4.do_ref, ...), custom_call_target="tpu_custom_call" | custom-call | flops 53687091200 | bytes 14680064 | tf_op jit(solution)/shard_map/pallas_call | solution.py:313
  891.0 5.0 fusion.38
  896.1 10.5 %fusion.19 = (f32[2048]{0:T(1024)S(1)}, f32[512]{0:T(512)S(1)}, f32[512,2048]{1,0:T(8,128)}) fusion(bf16[1,512,2048]{2,1,0:T(8,128)(2,1)S(1)} %copy-done.12, f32[512]{0:T(512)S(1)} %copy-done.30, f32[2048]{0:T(1024)S(1)} %copy-done.27, f32[512,2048]{1,0:T(8,128)S(1)} %fusion.38, bf16[512,2048]{1,0:T(8,128)(2,1)S(1)} %copy-done.33, ...), kind=kOutput, calls=%fused_computation.29 | convolution fusion | flops 4303353344 | bytes 20992000 | tf_op jit(solution)/shard_map/dot_general | solution.py:36
  906.6 0.6 pad_maximum_fusion.5.gain_ref
  907.3 89.3 %shard_map.209 = (f32[256,512]{1,0:T(8,128)}, f32[256,256]{1,0:T(8,128)}, f32[2,2048]{1,0:T(2,128)}, bf16[256,2048]{1,0:T(8,128)(2,1)}) custom-call(bf16[512,2048]{1,0:T(8,128)(2,1)} %fusion.10.x_ref, bf16[512,2048]{1,0:T(8,128)(2,1)} %get-tuple-element.107.dq_ref, bf16[512,1024]{1,0:T(8,128)(2,1)} %get-tuple-element.109.dkv_ref, ...), custom_call_target="tpu_custom_call" | custom-call | flops 120000004096 | bytes 6291456 | tf_op jit(solution)/shard_map/pallas_call | solution.py:1189
  996.6 1.4 fusion.37
  998.0 1.7 fusion.36
  999.7 1.6 convert_element_type.142
  1001.3 3.6 convert_element_type.143
  1004.9 1.6 convert_element_type.144
  1006.5 8.6 fusion.31
  1015.1 0.8 copy.26
  1015.9 0.8 copy.27
  (85 shorter events, 0.4 us)
Async XLA Ops:
  7.2 215.4 %all-gather.5.cloned.1.call-start = ((), (), s32[]{:S(2)}) async-start(), calls=%async_computation.3 | async-start | bytes 5242880 | tf_op jit(solution)/shard_map/all_gather | solution.py:1323
  8.8 50.7 %copy-start.11 = (bf16[1,512,2048]{2,1,0:T(8,128)(2,1)S(1)}, bf16[1,512,2048]{2,1,0:T(8,128)(2,1)}, u32[]{:S(2)}) copy-start(bf16[1,512,2048]{2,1,0:T(8,128)(2,1)} %param.12) | copy-start | bytes 6291460
  58.6 1.4 copy-start.28
  58.6 1.6 copy-start.26
  58.6 193.3 %all-gather.7.cloned.1.call-start = ((), (), s32[]{:S(2)}) async-start(), calls=%async_computation.4 | async-start | bytes 5242880 | tf_op jit(solution)/shard_map/all_gather | solution.py:1323
  59.4 338.1 %all-gather.9.cloned.1.call-start = ((), (), s32[]{:S(2)}) async-start(), calls=%async_computation.5 | async-start | bytes 18874368 | tf_op jit(solution)/shard_map/all_gather | solution.py:1278
  59.9 99.9 %copy-start.29 = (f32[512]{0:T(512)}, f32[512]{0:T(512)S(1)}, u32[]{:S(2)}) copy-start(f32[512]{0:T(512)S(1)} %add_rsqrt_fusion.1) | copy-start | bytes 6148
  62.1 98.6 %copy-start = (s32[512]{0:T(512)}, s32[512]{0:T(512)S(1)}, u32[]{:S(2)}) copy-start(s32[512]{0:T(512)S(1)} %get-tuple-element.137) | copy-start | bytes 6148
  159.9 323.1 %all-gather.11.cloned.1.call-start = ((), (), s32[]{:S(2)}) async-start(), calls=%async_computation.6 | async-start | bytes 5242880 | tf_op jit(solution)/shard_map/all_gather | solution.py:1323
  160.4 579.8 %reduce-scatter.4.cloned.1.call-start = ((), (), s32[]{:S(2)}) async-start(), calls=%async_computation.7 | async-start | bytes 5242880 | tf_op jit(solution)/shard_map/reduce_scatter | solution.py:1328
  160.7 1.6 copy-start.2
  162.3 51.9 %copy-start.34 = (bf16[2048,2048]{1,0:T(8,128)(2,1)S(1)}, bf16[2048,2048]{1,0:T(8,128)(2,1)}, u32[]{:S(2)}) copy-start(bf16[2048,2048]{1,0:T(8,128)(2,1)} %get-tuple-element.73) | copy-start | bytes 25165828
  214.2 4.7 copy-start.1
  214.2 4.7 copy-start.3
  214.2 6.7 copy-start.20
  218.9 2.0 copy-start.4
  218.9 1.9 copy-start.23
  497.0 24.1 %collective-permute-start = (bf16[2048,2048]{1,0:T(8,128)(2,1)}, bf16[2048,2048]{1,0:T(8,128)(2,1)}, u32[]{:S(2)}, u32[]{:S(2)}) collective-permute-start(bf16[2048,2048]{1,0:T(8,128)(2,1)} %convolution_convert_fusion), channel_id=1, source_target_pairs={{0,4},{4,0},{8,12},{12,8},{16,20},{20,16},{24,28},{28,24},{1,5},{5... | collective-permute-start | bytes 25165832 | tf_op jit(solution)/shard_map/ppermute | solution.py:1270
  534.4 3.6 copy-start.13
  538.0 36.1 %collective-permute-start.2 = (bf16[256,2048]{1,0:T(8,128)(2,1)}, bf16[256,2048]{1,0:T(8,128)(2,1)}, u32[]{:S(2)}, u32[]{:S(2)}) collective-permute-start(bf16[256,2048]{1,0:T(8,128)(2,1)} %get-tuple-element.127), channel_id=1, source_target_pairs={{0,8},{4,12},{8,0},{12,4},{16,24},{20,28},{24,16},{28,20},{1,9},{5... | collective-permute-start | bytes 3145736 | tf_op jit(solution)/shard_map/ppermute | solution.py:1270
  539.5 34.6 %collective-permute-start.1 = (bf16[256,2048]{1,0:T(8,128)(2,1)S(1)}, bf16[256,2048]{1,0:T(8,128)(2,1)}, u32[]{:S(2)}, u32[]{:S(2)}) collective-permute-start(bf16[256,2048]{1,0:T(8,128)(2,1)S(1)} %get-tuple-element.126), channel_id=1, source_target_pairs={{0,16},{4,20},{8,24},{12,28},{16,0},{20,4},{24,8},{28,12},{1,17},{... | collective-permute-start | bytes 3145736 | tf_op jit(solution)/shard_map/ppermute | solution.py:1270
  541.0 217.2 %reduce-scatter.6.cloned.1.call-start = ((), (), s32[]{:S(2)}) async-start(), calls=%async_computation.8 | async-start | bytes 5242880 | tf_op jit(solution)/shard_map/reduce_scatter | solution.py:1328
  577.2 4.9 copy-start.35
  603.4 287.5 %reduce-scatter.8.cloned.1.call-start = ((), (), s32[]{:S(2)}) async-start(), calls=%async_computation.9 | async-start | bytes 5242880 | tf_op jit(solution)/shard_map/reduce_scatter | solution.py:1328
  603.5 47.7 %collective-permute-start.3 = (bf16[512,2048]{1,0:T(8,128)(2,1)}, bf16[512,2048]{1,0:T(8,128)(2,1)S(1)}, u32[]{:S(2)}, u32[]{:S(2)}) collective-permute-start(bf16[512,2048]{1,0:T(8,128)(2,1)} %pad_maximum_fusion), channel_id=1, source_target_pairs={{0,8},{4,12},{8,0},{12,4},{16,24},{20,28},{24,16},{28,20},{1,9},{5... | collective-permute-start | bytes 6291464 | tf_op jit(solution)/shard_map/ppermute | solution.py:1270
  604.1 48.5 %collective-permute-start.4 = (bf16[512,2048]{1,0:T(8,128)(2,1)}, bf16[512,2048]{1,0:T(8,128)(2,1)}, u32[]{:S(2)}, u32[]{:S(2)}) collective-permute-start(bf16[512,2048]{1,0:T(8,128)(2,1)} %pad_maximum_fusion.1), channel_id=1, source_target_pairs={{0,16},{4,20},{8,24},{12,28},{16,0},{20,4},{24,8},{28,12},{1,17},{... | collective-permute-start | bytes 6291464 | tf_op jit(solution)/shard_map/ppermute | solution.py:1270
  628.6 111.6 %copy-start.21 = (f32[2048]{0:T(1024)S(1)}, f32[2048]{0:T(1024)}, u32[]{:S(2)}) copy-start(f32[2048]{0:T(1024)} %param.19) | copy-start | bytes 24580
  628.6 111.6 %copy-start.24 = (f32[512]{0:T(512)S(1)}, f32[512]{0:T(512)}, u32[]{:S(2)}) copy-start(f32[512]{0:T(512)} %copy-done.23) | copy-start | bytes 6148
  651.2 1.3 copy-start.14
  652.5 92.5 %copy-start.9 = (bf16[1,512,2048]{2,1,0:T(8,128)(2,1)S(1)}, bf16[1,512,2048]{2,1,0:T(8,128)(2,1)}, u32[]{:S(2)}) copy-start(bf16[1,512,2048]{2,1,0:T(8,128)(2,1)} %param.23) | copy-start | bytes 6291460
  740.2 4.8 copy-start.5
  740.2 6.0 copy-start.7
  746.2 1.5 copy-start.31
  747.8 1.3 copy-start.15
  891.0 5.1 copy-start.12
  891.0 5.1 copy-start.27
  891.0 5.1 copy-start.30
  891.0 5.1 copy-start.33
  907.3 92.4 %copy-start.17 = (bf16[256,2048]{1,0:T(8,128)(2,1)S(1)}, bf16[256,2048]{1,0:T(8,128)(2,1)}, u32[]{:S(2)}) copy-start(bf16[256,2048]{1,0:T(8,128)(2,1)} %get-tuple-element.116) | copy-start | bytes 3145732
  907.3 99.2 %copy-start.10 = (bf16[1,512,2048]{2,1,0:T(8,128)(2,1)S(1)}, bf16[1,512,2048]{2,1,0:T(8,128)(2,1)}, u32[]{:S(2)}) copy-start(bf16[1,512,2048]{2,1,0:T(8,128)(2,1)} %param.23) | copy-start | bytes 6291460
  996.5 8.3 copy-start.16
  999.7 6.8 copy-start.6
  999.7 6.8 copy-start.8
  999.7 6.8 copy-start.22
  999.7 6.7 copy-start.25
  999.7 6.7 copy-start.32
  1006.5 8.7 copy-start.19
  1006.5 9.5 copy-start.18
Sparse Core Ops, SparseCore 0:
  58.7 97.5 all-gather.4
  157.9 94.0 all-gather.6
  253.8 143.0 all-gather.8
  398.4 84.5 all-gather.10
  541.1 73.1 reduce-scatter.3
  616.5 77.2 reduce-scatter.5
  696.1 77.2 reduce-scatter.7

commit v6 on v5

--- a/solution.py
+++ b/solution.py
@@ -93,13 +93,33 @@
     return jnp.concatenate([mine[:, :count], mine[:, count:]], axis=0).T
 
 
-def attend_kernel(reach, q_ref, k_ref, v_ref, low_ref, att_ref, lse_ref, bias_ref):
+def attend_kernel(
+    reach, wide, q_ref, k_ref, v_ref, low_ref, own_ref, att_ref, lse_ref, all_ref,
+    bias_ref, full, own_sem, send_sem, recv_sem, out_sem,
+):
     head, tile, pair = pl.program_id(0), pl.program_id(1), pl.program_id(2)
     half = head % 2
-
-    @pl.when((head == 0) & (tile == 0) & (pair == 0))
+    inner = pl.num_programs(1) * pl.num_programs(2)
+    step = head * inner + tile * pl.num_programs(2) + pair
+    ring = Ring(wide, full, own_ref.shape[0], send_sem, recv_sem)
+
+    def outward(slot, *flips):
+        where = ring.whole(*flips)
+        return pltpu.make_async_copy(full.at[where], all_ref.at[where], out_sem.at[slot])
+
+    near = [(0, 0, 0), (0, 0, 1), (0, 1, 0), (1, 0, 0)]
+    rest = [(0, 1, 1), (1, 0, 1), (1, 1, 0), (1, 1, 1)]
+
+    @pl.when(step == 0)
     def _():
+        local = pltpu.make_async_copy(own_ref, full.at[ring.mine()], own_sem)
+        local.start()
+        meet(ring.peers)
+        local.wait()
+        ring.start_own()
         fill_bias(bias_ref, low_ref, reach)
+
+    pl.when(step == 4 * inner)(ring.first_halves)
 
     keys = pl.ds(pl.multiple_of(tile * QTILE, QTILE), bias_ref.shape[1])
     queries = spread_pair(q_ref[...], half)
@@ -113,8 +133,23 @@
     att_ref[...] = gather_pair(result, half).astype(BF16)
     lse_ref[0] = top + jnp.log2(total)
 
-
-def attend(q, kv, low):
+    @pl.when(step == pl.num_programs(0) * inner - 1)
+    def _():
+        ring.second_halves()
+        ring.from_sibling("own", 0, 1)
+        for slot, flips in enumerate(near):
+            outward(slot, *flips).start()
+        ring.far_halves()
+        for name in ("x", "y", "d"):
+            ring.from_sibling(name, 0, 1)
+        for slot, flips in enumerate(rest):
+            outward(4 + slot, *flips).start()
+        for slot, flips in enumerate(near + rest):
+            outward(slot, *flips).wait()
+        ring.sent()
+
+
+def attend(q, kv, low, grad, dp_size):
     rows, width = q.shape
     keys = kv.shape[0]
     reach = keys - rows
@@ -123,45 +158,57 @@
     heads = kv.shape[1] // LANES
     per_head = pairs // heads
     span = reach + QTILE
+    whole = (GROUP * grad.shape[0], grad.shape[1])
+    far = pl.BlockSpec(memory_space=pl.ANY)
     return pl.pallas_call(
-        functools.partial(attend_kernel, reach),
+        functools.partial(attend_kernel, reach, 2 * math.isqrt(dp_size // GROUP)),
         grid=(heads, tiles, per_head),
         in_specs=[
             pl.BlockSpec((QTILE, LANES), lambda a, t, p: (t, a * per_head + p)),
             pl.BlockSpec((keys, LANES), lambda a, t, p: (0, 2 * (a // 2))),
             pl.BlockSpec((keys, LANES), lambda a, t, p: (0, 2 * (a // 2) + 1)),
             pl.BlockSpec((1, rows), lambda a, t, p: (0, 0)),
+            far,
         ],
         out_specs=[
             pl.BlockSpec((QTILE, LANES), lambda a, t, p: (t, a * per_head + p)),
             pl.BlockSpec((1, 1, 2 * QTILE), lambda a, t, p: ((a * tiles + t) * per_head + p, 0, 0)),
+            far,
         ],
         out_shape=[
             jax.ShapeDtypeStruct((rows, width), BF16),
             jax.ShapeDtypeStruct((pairs * tiles, 1, 2 * QTILE), F32),
+            jax.ShapeDtypeStruct(whole, BF16),
         ],
-        scratch_shapes=[pltpu.VMEM((tiles, span, QTILE), F32)],
-        compiler_params=pltpu.CompilerParams(vmem_limit_bytes=48 << 20),
+        scratch_shapes=[
+            pltpu.VMEM((tiles, span, QTILE), F32),
+            pltpu.VMEM(whole, BF16),
+            pltpu.SemaphoreType.DMA,
+            pltpu.SemaphoreType.DMA((Ring.COPIES,)),
+            pltpu.SemaphoreType.DMA((Ring.COPIES,)),
+            pltpu.SemaphoreType.DMA((8,)),
+        ],
+        compiler_params=pltpu.CompilerParams(
+            collective_id=7, has_side_effects=True, vmem_limit_bytes=56 << 20
+        ),
         cost_estimate=pl.CostEstimate(
             flops=16 * rows * span * LANES * pairs,
             bytes_accessed=4 * rows * width + 2 * keys * kv.shape[1],
             transcendentals=2 * rows * span * pairs,
         ),
-    )(q, kv, kv, low)
+    )(q, kv, kv, low, grad)
 
 
 def attend_back_kernel(
     reach, wide, z_size, mlp_count,
     q_ref, do_ref, o_ref, k_ref, v_ref, lse_ref, low_ref, cos_ref, sin_ref, cos_all, sin_all,
-    h_ref, att_ref, *refs,
+    *refs,
 ):
     mlp_ins, refs = refs[:mlp_count], refs[mlp_count:]
-    dq_ref, dkv_ref, wo_out = refs[:3]
-    mlp_outs, refs = refs[3 : 3 + mlp_count], refs[3 + mlp_count :]
+    dq_ref, dkv_ref = refs[:2]
+    mlp_outs, refs = refs[2 : 2 + mlp_count], refs[2 + mlp_count :]
     bias_ref, dk_acc, dv_acc, own_part, send_part, recv_part, kv_send, kv_recv = refs[:8]
-    ring = Reduce(wide, *refs[8:14])
-    sums, zrecv, z_send, z_recv = refs[14:18]
-    home = refs[18:]
+    home = refs[8:]
     block, half, tile, pair = (pl.program_id(at) for at in range(4))
     steps = pl.num_programs(1) * pl.num_programs(2) * pl.num_programs(3)
     inner = (half * pl.num_programs(2) + tile) * pl.num_programs(3) + pair
@@ -185,45 +232,12 @@
                 functools.partial(action, exchange(at, distance), at, distance)
             )
 
-    def along(at):
-        cols = wo_out.shape[1]
-        other = (place + at + 1) % z_size
-        return pltpu.make_async_remote_copy(
-            src_ref=sums.at[:, pl.ds(pl.multiple_of(other * cols, LANES), cols)],
-            dst_ref=zrecv.at[at], send_sem=z_send.at[at], recv_sem=z_recv.at[at],
-            device_id={"tensor": other}, device_id_type=MESH,
-        )
-
     @pl.when(step == 0)
     def _():
         greet(along_peers(place, z_size) + [device for _, device in others(wide)[1]])
         for copy in send_home(wide, mlp_ins, mlp_outs, *home):
             copy.start()
         fill_bias(bias_ref, low_ref, reach)
-
-    @pl.when((step % 2 == 0) & (step < 16))
-    def _():
-        chunk, target = ring.chunk(step // 2)
-        part = target.shape[0]
-        x = h_ref[:, pl.ds(pl.multiple_of(chunk * part, part), part)].T
-
-        @pl.loop(0, att_ref.shape[1] // NTILE)
-        def _(at):
-            n = pl.ds(pl.multiple_of(at * NTILE, NTILE), NTILE)
-            target[:, n] = dot_nn(x, att_ref[:, n]).astype(BF16)
-
-        ring.after(step // 2)
-
-    pl.when(step == 19)(ring.pass_on)
-
-    @pl.when(step == 27)
-    def _():
-        def store(here, value):
-            sums[here, :] = value.astype(BF16)
-
-        ring.finish(store)
-        for at in range(z_size - 1):
-            along(at).start()
 
     @pl.when(inner == 0)
     def _():
@@ -273,24 +287,15 @@
             dkv_ref[:, (2 * at + 1) * LANES : (2 * at + 2) * LANES] = own_part[
                 at, :, LANES:
             ].astype(BF16)
-        total = sums[:, pl.ds(pl.multiple_of(place * wo_out.shape[1], LANES), wo_out.shape[1])]
-        total = total.astype(F32)
-        for at in range(z_size - 1):
-            along(at).wait_recv()
-            total += zrecv[at].astype(F32)
-        wo_out[...] = total
-        for at in range(z_size - 1):
-            along(at).wait_send()
         for at in range(blocks):
             each_exchange(
                 at, lambda distance: place >= distance, lambda copy, *_: copy.wait_send()
             )
-        ring.sent()
         for copy in send_home(wide, mlp_ins, mlp_outs, *home):
             copy.wait()
 
 
-def attend_back(q, do, att, kv, lse, low, cosine, sine, h, mlp, dp_size, z_size):
+def attend_back(q, do, att, kv, lse, low, cosine, sine, mlp, dp_size, z_size):
     rows, width = q.shape
     keys = kv.shape[0]
     reach = keys - rows
@@ -300,8 +305,6 @@
     per_head = pairs // heads
     span = reach + QTILE
     blocks = heads // 2
-    part = h.shape[1] // GROUP
-    cols = width // z_size
 
     def pair_at(g, h, t, p):
         return (t, (2 * g + h) * per_head + p)
@@ -330,20 +333,16 @@
             table,
             whole((rows, LANES)),
             whole((rows, LANES)),
-            whole(h.shape),
-            whole(att.shape),
         ]
         + [pl.BlockSpec(memory_space=pl.ANY)] * len(mlp),
         out_specs=[
             pl.BlockSpec((QTILE, LANES), pair_at),
             pl.BlockSpec((rows, kv.shape[1]), lambda g, h, t, p: (0, 0)),
-            pl.BlockSpec((part, cols), lambda g, h, t, p: (0, 0)),
         ]
         + [pl.BlockSpec(memory_space=pl.ANY)] * len(mlp),
         out_shape=[
             jax.ShapeDtypeStruct((rows, width), BF16),
             jax.ShapeDtypeStruct((rows, kv.shape[1]), BF16),
-            jax.ShapeDtypeStruct((part, cols), F32),
         ]
         + home_shapes(mlp),
         scratch_shapes=[
@@ -356,13 +355,6 @@
             pltpu.SemaphoreType.DMA((blocks, reach // rows)),
             pltpu.SemaphoreType.DMA((blocks, reach // rows)),
         ]
-        + Reduce.scratch(part, width)
-        + [
-            pltpu.VMEM((part, width), BF16),
-            pltpu.VMEM((z_size - 1, part, cols), BF16),
-            pltpu.SemaphoreType.DMA((z_size - 1,)),
-            pltpu.SemaphoreType.DMA((z_size - 1,)),
-        ]
         + home_scratch(mlp),
         compiler_params=pltpu.CompilerParams(
             collective_id=5, has_side_effects=True, vmem_limit_bytes=60 << 20
@@ -372,7 +364,7 @@
             bytes_accessed=8 * rows * width + 4 * keys * kv.shape[1],
             transcendentals=2 * rows * span * pairs,
         ),
-    )(q, do, att, kv, kv, lse, low, cosine, sine, cosine, sine, h, att, *mlp)
+    )(q, do, att, kv, kv, lse, low, cosine, sine, cosine, sine, *mlp)
 
 
 MESH = pl.DeviceIdType.MESH
@@ -572,6 +564,10 @@
 
     def mine(self):
         p = 4 * self.row + 2 * self.col + self.core
+        return pl.ds(pl.multiple_of(p * self.rows, self.rows), self.rows)
+
+    def whole(self, dy, dx, dc):
+        p = 4 * ((self.row + dy) % 2) + 2 * ((self.col + dx) % 2) + (self.core + dc) % 2
         return pl.ds(pl.multiple_of(p * self.rows, self.rows), self.rows)
 
     def copy(self, slot, dy, dx, dc, half, peer):
@@ -1062,12 +1058,15 @@
     )(dgate, dup, wg, wu)
 
 
-def tail_kernel(wide, z_size, mlp_count, x_ref, dq_ref, dkv_ref, gain_ref, *refs):
+def tail_kernel(
+    wide, z_size, mlp_count, x_ref, dq_ref, dkv_ref, wo_ref, gain_ref, *refs
+):
     mlp_ins, refs = refs[:mlp_count], refs[mlp_count:]
-    wq_out, wkv_out, gain_out = refs[:3]
-    mlp_outs, scratch = refs[3 : 3 + mlp_count], refs[3 + mlp_count :]
+    wq_out, wkv_out, wo_out, gain_out = refs[:4]
+    mlp_outs, scratch = refs[4 : 4 + mlp_count], refs[4 + mlp_count :]
     own_scratch = scratch[:12]
-    sums, zrecv, gain_z, gain_p, z_send, z_recv, g_send, g_recv, m_own, m_send, m_recv = scratch[12:]
+    sums, zrecv, gain_z, gain_p, z_send, z_recv, g_send, g_recv = scratch[12:20]
+    wo_recv, w_send, w_recv, m_own, m_send, m_recv = scratch[20:]
     rings = [Reduce(wide, *own_scratch[6 * at : 6 * at + 6]) for at in range(2)]
     place = lax.axis_index("tensor")
     mine, found = others(wide)
@@ -1076,7 +1075,19 @@
     greet(along + around)
 
     mlp_copies = send_home(wide, mlp_ins, mlp_outs, m_own, m_send, m_recv)
-    for copy in mlp_copies:
+    wo_part = wo_out.shape[1]
+    wo_copies = [
+        pltpu.make_async_remote_copy(
+            src_ref=wo_ref.at[
+                :,
+                pl.ds(pl.multiple_of((place + at + 1) % z_size * wo_part, LANES), wo_part),
+            ],
+            dst_ref=wo_recv.at[at], send_sem=w_send.at[at], recv_sem=w_recv.at[at],
+            device_id=peer, device_id_type=MESH,
+        )
+        for at, peer in enumerate(along)
+    ]
+    for copy in wo_copies:
         copy.start()
 
     gain_z[place] = gain_ref[...]
@@ -1090,9 +1101,9 @@
     for copy in gain_copies:
         copy.start()
 
-    rights = (dkv_ref, dq_ref)
+    rights = (dq_ref, dkv_ref)
     rows = sums.shape[0]
-    outs = (wkv_out, wq_out)
+    outs = (wq_out, wkv_out)
     z_copies = []
     for index, ring in enumerate(rings):
         right = rights[index]
@@ -1111,6 +1122,8 @@
             ring.after(step)
 
         if index == 0:
+            for copy in mlp_copies:
+                copy.start()
             for copy in gain_copies:
                 copy.wait_recv()
             total = gain_z[0]
@@ -1158,6 +1171,13 @@
     for at in range(1, GROUP):
         total = total + gain_p[at]
     gain_out[...] = total
+
+    for copy in wo_copies:
+        copy.wait()
+    total = wo_ref[:, pl.ds(pl.multiple_of(place * wo_part, LANES), wo_part)].astype(F32)
+    for at in range(z_size - 1):
+        total += wo_recv[at].astype(F32)
+    wo_out[...] = total
 
     for copy in z_copies:
         copy.wait_recv()
@@ -1176,21 +1196,22 @@
         copy.wait()
 
 
-def last_grads(x, dq, dkv, gains, mlp, dp_size, z_size):
+def last_grads(x, dq, dkv, wo_sum, gains, mlp, dp_size, z_size):
     tokens, width = x.shape
     rows = width // GROUP
     near = pl.BlockSpec(memory_space=pltpu.VMEM)
     far = pl.BlockSpec(memory_space=pl.ANY)
-    sizes = [dkv.shape[1], dq.shape[1]]
+    sizes = [dq.shape[1], dkv.shape[1]]
     scratch = []
     for cols in sizes:
         scratch += Reduce.scratch(rows, cols)
     total = sum(sizes)
     return pl.pallas_call(
         functools.partial(tail_kernel, 2 * math.isqrt(dp_size // GROUP), z_size, len(mlp)),
-        in_specs=[near] * 4 + [far] * len(mlp),
-        out_specs=[near] * 3 + [far] * len(mlp),
-        out_shape=[jax.ShapeDtypeStruct((rows, cols // z_size), F32) for cols in sizes[::-1]]
+        in_specs=[near] * 5 + [far] * len(mlp),
+        out_specs=[near] * 4 + [far] * len(mlp),
+        out_shape=[jax.ShapeDtypeStruct((rows, cols // z_size), F32) for cols in sizes]
+        + [jax.ShapeDtypeStruct((rows, wo_sum.shape[1] // z_size), F32)]
         + [jax.ShapeDtypeStruct(gains.shape, F32)]
         + home_shapes(mlp),
         scratch_shapes=scratch
@@ -1203,6 +1224,9 @@
             pltpu.SemaphoreType.DMA((2, z_size - 1)),
             pltpu.SemaphoreType.DMA((z_size - 1 + GROUP - 1,)),
             pltpu.SemaphoreType.DMA((z_size - 1 + GROUP - 1,)),
+            pltpu.VMEM((z_size - 1, rows, wo_sum.shape[1] // z_size), BF16),
+            pltpu.SemaphoreType.DMA((z_size - 1,)),
+            pltpu.SemaphoreType.DMA((z_size - 1,)),
         ]
         + home_scratch(mlp),
         compiler_params=pltpu.CompilerParams(
@@ -1211,7 +1235,7 @@
         cost_estimate=pl.CostEstimate(
             flops=2 * LONG, bytes_accessed=4 * tokens * total, transcendentals=0
         ),
-    )(x, dq, dkv, gains, *mlp)
+    )(x, dq, dkv, wo_sum, gains, *mlp)
 
 
 class Layout:
@@ -1334,11 +1358,9 @@
     q, kv_all, wkv, wq, wo = project(
         layout.from_cols(xn), cosine, sine, *spread[3:], reach, dp_size, z_size
     )
-    grad, q, spread_wd = lax.optimization_barrier((cotangent[0], q, spread[2]))
+    wd = gather_z(spread[2])
     wkv, wq, wo = layout.to_rows(wkv), layout.to_rows(wq), layout.to_rows(wo)
-    dy = layout.gather(grad)
-    att, lse = attend(q, kv_all, low)
-    wd = gather_z(spread_wd)
+    att, lse, dy = attend(q, kv_all, low, cotangent[0], dp_size)
     h = x + dot_nt(att, wo)
 
     r2 = rms_scale(h)
@@ -1347,7 +1369,6 @@
     def chunk(array, y, x):
         return lax.dynamic_index_in_dim(array, 2 * y + x, 0, False)
 
-    by_core, dy = lax.optimization_barrier((by_core, dy))
     away = dot_nt(by_core[1], wd).astype(BF16)
     dy, away = lax.optimization_barrier((dy, away))
     total_wd = dot_tn(dy, hidden).astype(BF16)
@@ -1370,36 +1391,37 @@
     y_lower = (y_chunk[rows // 2 :].astype(F32) + from_x.astype(F32)).astype(BF16)
     x_chunk = jnp.concatenate([x_upper, x_chunk[rows // 2 :]], axis=0)
     y_chunk = jnp.concatenate([y_chunk[: rows // 2], y_lower], axis=0)
-    dgate, dup, x_chunk, y_chunk = lax.optimization_barrier((dgate, dup, x_chunk, y_chunk))
-    from_x, from_y = layout.swap(x_chunk, 2), layout.swap(y_chunk, 4)
     total_wg = dot_tn(hn, dgate).astype(BF16)
     dup, total_wg = lax.optimization_barrier((dup, total_wg))
     part_wg = along_z(total_wg)
     total_wu = dot_tn(hn, dup).astype(BF16)
     dup, total_wu = lax.optimization_barrier((dup, total_wu))
     part_wu = along_z(total_wu)
-    dup, from_x, from_y = lax.optimization_barrier((dup, from_x, from_y))
+    dup, x_chunk, y_chunk = lax.optimization_barrier((dup, x_chunk, y_chunk))
     dhn = hidden_back(dgate, dup, wg, wu, dp_size)
-    dhn, part_wd = lax.optimization_barrier((dhn, part_wd))
+    dhn, part_wd, x_chunk, y_chunk = lax.optimization_barrier((dhn, part_wd, x_chunk, y_chunk))
+    from_x, from_y = layout.swap(x_chunk, 2), layout.swap(y_chunk, 4)
     gain_two, dh_norm = norm_back(h, r2, mlp_gain, dhn)
     dh = cotangent[0].astype(F32) + dh_norm
-    output = h + chunk(near_sum, row, col).astype(F32)
-    output = output + from_x.astype(F32) + from_y.astype(F32)
-
     dhb = dh.astype(BF16)
     datt = dot_nn(dhb, wo).astype(BF16)
-    datt, part_wg = lax.optimization_barrier((datt, part_wg))
-    dq, dkv, wo_grad, wd_grad, wg_grad = attend_back(
-        q, datt, att, kv_all, lse, low, cosine, sine, layout.from_cols(dhb),
-        (part_wd, part_wg), dp_size, z_size,
+    total_wo = layout.from_rows(dot_tn(dhb, att).astype(BF16))
+    datt, part_wg, total_wo = lax.optimization_barrier((datt, part_wg, total_wo))
+    part_wo = layout.scatter(total_wo)
+    dq, dkv, wd_grad, wg_grad = attend_back(
+        q, datt, att, kv_all, lse, low, cosine, sine, (part_wd, part_wg), dp_size, z_size
     )
     dq, part_wu = lax.optimization_barrier((dq, part_wu))
+    dq, part_wo = lax.optimization_barrier((dq, part_wo))
     dxn = dot_nt(dq, wq) + dot_nt(dkv, wkv)
     gain_one, dx_norm = norm_back(x, r1, attn_gain, dxn)
     input_grad = (dh + dx_norm).astype(BF16)
     gains = layout.sum_outer(jnp.stack([gain_one, gain_two]))
-    wq_grad, wkv_grad, gains, wu_grad = last_grads(
-        layout.from_cols(xn), dq, dkv, gains, (part_wu,), dp_size, z_size
+    gains, from_x, from_y = lax.optimization_barrier((gains, from_x, from_y))
+    output = h + chunk(near_sum, row, col).astype(F32)
+    output = output + from_x.astype(F32) + from_y.astype(F32)
+    wq_grad, wkv_grad, wo_grad, gains, wu_grad = last_grads(
+        layout.from_cols(xn), dq, dkv, part_wo, gains, (part_wu,), dp_size, z_size
     )
     wo_grad, wq_grad, wkv_grad, wd_grad, wg_grad, wu_grad = (
         layout.scatter_outer(grad).astype(F32)

time: 1030 us -> 926 us (0.90)
  waiting for transfers between devices: 139 us -> 7.13 us
  matrix products: 159 us -> 184 us
    all_gather x3, waiting for transfers between devices: 115 us -> 0.02 us  [gather_z(): return layout.to_rows(lax.all_gather(array, 'tensor', axis=1, tiled=True))]
    pallas_call x1, Pallas kernels: 146 us -> 88.6 us  [gate_up(): pl.pallas_call(functools.partial(gate_up_kernel, 2 * math.isqrt(dp_size /...]
    pallas_call x1, Pallas kernels: 51.9 us -> 87.3 us  [attend(): pl.pallas_call(functools.partial(attend_kernel, reach, 2 * math.isqrt(dp_...]
    ppermute x5, waiting for transfers between devices: 22.6 us -> 3.22 us  [swap(): return lax.ppermute(array, 'dp', pairs)]
    pallas_call x1, Pallas kernels: 89.3 us -> 106 us  [last_grads(): pl.pallas_call(functools.partial(tail_kernel, 2 * math.isqrt(dp_size // G...]
    dot_general x3 -> x4, matrix products: 69.4 us -> 86.3 us  [dot_tn(): lax.dot_general(left, right, (((0,), (0,)), ((), ())), preferred_element_...]
  transfers between devices with their start and end apart: 12 -> 12, of which waited for: 3 -> 3; matrix products, arithmetic and copies ran while one was open for 13% -> 20% of each run, Pallas kernels for 50% -> 54%
where the time goes in v6:
time: 926 us; the launch traced here: 922 us
  Pallas kernels  656 us (71%)
  matrix products  184 us (20%)
  other arithmetic  41.2 us (4%)
  local copies, waits for them, and re-layouts  15.4 us (2%)
  between operations  14.7 us (2%)
    pallas_call x1, Pallas kernels, attend_back(): pl.pallas_call(functools.partial(attend_back_kernel, reach, 2 * math.isqr...  140 us
    pallas_call x1, Pallas kernels, last_grads(): pl.pallas_call(functools.partial(tail_kernel, 2 * math.isqrt(dp_size // G...  106 us
    pallas_call x1, Pallas kernels, project(): pl.pallas_call(functools.partial(project_kernel, 2 * math.isqrt(dp_size /...  95.7 us
    pallas_call x1, Pallas kernels, gate_up(): pl.pallas_call(functools.partial(gate_up_kernel, 2 * math.isqrt(dp_size /...  88.6 us
    pallas_call x1, Pallas kernels, hidden_back(): pl.pallas_call(functools.partial(hidden_back_kernel, 2 * math.isqrt(dp_si...  88.4 us
    pallas_call x1, Pallas kernels, attend(): pl.pallas_call(functools.partial(attend_kernel, reach, 2 * math.isqrt(dp_...  87.3 us
    dot_general x4, matrix products, dot_tn(): lax.dot_general(left, right, (((0,), (0,)), ((), ())), preferred_element_...  86.3 us
    dot_general x5, matrix products, dot_nt(): lax.dot_general(left, right, (((1,), (1,)), ((), ())), preferred_element_...  56.3 us
  transfers between devices with their start and end apart: 12, of which 3 were waited for; matrix products, arithmetic and copies ran while one was open for 20% of the time, Pallas kernels for 54%

profile of v6, /device:TPU:0, one launch (start us, length us, event | category | flops | bytes accessed | tf_op | source)
XLA Modules:
  0.0 922.4 jit_solution(14465215969116523617)
XLA Ops:
  7.2 0.0 all-gather.4.cloned.1.call-start
  7.2 1.5 pad_maximum_fusion.4.refs_3_
  8.8 49.8 %shard_map.203 = (bf16[2048,256]{1,0:T(8,128)(2,1)}, bf16[2048,256]{1,0:T(8,128)(2,1)}, bf16[2048,256]{1,0:T(8,128)(2,1)}, bf16[256,1024]{1,0:T(8,128)(2,1)}, bf...) custom-call(bf16[256,2048]{1,0:T(8,128)(2,1)} %refs_0_.1, bf16[256,2048]{1,0:T(8,128)(2,1)} %refs_1_.1, ...), custom_call_target="tpu_custom_call" | custom-call | flops 60000002048 | tf_op jit(solution)/shard_map/pallas_call | solution.py:524
  58.6 0.0 all-gather.6.cloned.1.call-start
  58.7 0.7 all-gather.6.cloned.1.call-update
  59.4 0.0 all-gather.8.cloned.1.call-start
  59.4 0.7 all-gather.8.cloned.1.call-update
  60.1 0.0 reduce-scatter.5.cloned.1.call-start
  60.2 0.5 fusion.16
  60.7 0.1 convert_reduce_fusion
  60.8 0.1 select_reduce_fusion
  60.9 1.9 fusion.10.x_ref
  62.8 0.7 subtract_add_fusion.1
  63.5 1.0 fusion.36
  64.5 1.3 pad_maximum_fusion.2
  65.7 95.7 %shard_map.204 = (bf16[512,2048]{1,0:T(8,128)(2,1)}, bf16[1536,1024]{1,0:T(8,128)(2,1)}, bf16[2048,1024]{1,0:T(8,128)(2,1)}, bf16[2048,2048]{1,0:T(8,128)(2,1)}, bf16[2048,2048]{1,0:T(8,128)(2,1)}) custom-call(bf16[512,2048]{1,0:T(8,128)(2,1)} %fusion.10.x_ref, f32[512,128]{1,0:T(8,128)} %get-tuple-element.143.cos_ref.cos_all, ...), custom_call_target="tpu_custom_call" | custom-call | flops 120000004096 | bytes 41943040 | tf_op jit(solution)/shard_map/pallas_call | solution.py:726
  161.4 87.3 %shard_map.205 = (bf16[512,2048]{1,0:T(8,128)(2,1)}, f32[32,1,512]{2,1,0:T(1,128)}, bf16[4096,2048]{1,0:T(8,128)(2,1)}) custom-call(bf16[512,2048]{1,0:T(8,128)(2,1)} %get-tuple-element.68.q_ref, bf16[1536,1024]{1,0:T(8,128)(2,1)} %get-tuple-element.69.k_ref.v_ref, bf16[1536,1024]{1,0:T(8,128)(2,1)} %get-tuple-element.69.k_ref.v_ref, s32[1,512]{1,0:T(1,128)} %bitcast.78, ...), custom_call_target="tpu_custom_call" | custom-call | flops 21474836480 | bytes 7340032 | tf_op jit(solution)/shard_map/pallas_call | solution.py:163
  248.8 7.8 multiply_reduce_fusion.2
  256.6 1.9 copy-done
  258.6 1.7 multiply_convert_fusion.own_ref
  260.3 88.6 %shard_map.206 = (bf16[4096,2048]{1,0:T(8,128)(2,1)}, bf16[4096,1024]{1,0:T(8,128)(2,1)}, bf16[4096,1024]{1,0:T(8,128)(2,1)}, bf16[4096,1024]{1,0:T(8,128)(2,1)}, bf16[2,2048,1024]{2,1,0:T(8,128)(2,1)}) custom-call(bf16[512,2048]{1,0:T(8,128)(2,1)} %multiply_convert_fusion.own_ref, bf16[2048,1024]{1,0:T(8,128)(2,1)} %all-gather.4.cloned.1.call-done.wg_ref, ...), custom_call_target="tpu_custom_call" | custom-call | flops 1000000 | tf_op jit(solution)/shard_map/pallas_call | solution.py:841
  348.9 14.2 %convolution_convert_fusion.1 = bf16[2048,2048]{1,0:T(8,128)(2,1)} fusion(bf16[2048,1024]{1,0:T(8,128)(2,1)} %all-gather.8.cloned.1.call-done, bf16[2,2048,1024]{2,1,0:T(8,128)(2,1)} %get-tuple-element.75), kind=kOutput, calls=%fused_computation.18 | convolution fusion | flops 8594128896 | bytes 16777216 | tf_op jit(solution)/shard_map/dot_general | solution.py:36
  363.1 36.8 %convolution_convert_fusion.4 = bf16[2048,1024]{1,0:T(8,128)(2,1)} fusion(bf16[4096,2048]{1,0:T(8,128)(2,1)} %get-tuple-element.81, bf16[4096,1024]{1,0:T(8,128)(2,1)S(1)} %copy-done.20), kind=kOutput, calls=%fused_computation.47 | convolution fusion | flops 17181966336 | bytes 29360128 | tf_op jit(solution)/shard_map/dot_general | solution.py:40
  399.9 15.2 %add_convert_fusion = bf16[2048,2048]{1,0:T(8,128)(2,1)} fusion(bf16[2048,2048]{1,0:T(8,128)(2,1)} %collective-permute-done, bf16[2048,1024]{1,0:T(8,128)(2,1)} %all-gather.8.cloned.1.call-done, bf16[2,2048,1024]{2,1,0:T(8,128)(2,1)} %get-tuple-element.75), kind=kOutput, calls=%fused_computation.11 | convolution fusion | flops 8602517504 | bytes 25165824 | tf_op jit(solution)/shard_map/dot_general | solution.py:36
  415.1 0.0 reduce-scatter.7.cloned.1.call-start
  415.2 31.2 %fusion.7 = (bf16[4096,1024]{1,0:T(8,128)(2,1)}, bf16[4096,1024]{1,0:T(8,128)(2,1)S(1)}) fusion(bf16[4096,1024]{1,0:T(8,128)(2,1)} %get-tuple-element.83, bf16[4096,1024]{1,0:T(8,128)(2,1)} %get-tuple-element.82, bf16[4096,2048]{1,0:T(8,128)(2,1)} %get-tuple-element.81, bf16[2048,1024]{1,0:T(8,128)(2,1)} %all-gather.8.cloned.1.call-done), kind=kOutput, calls=%fused_computation.10 | convolution fusion | flops 17242783744 | bytes 54525952 | tf_op jit(solution)/shard_map/dot_general | solution.py:32
  446.4 3.3 copy-done.23
  449.6 21.4 %convolution_convert_fusion.3 = bf16[2048,1024]{1,0:T(8,128)(2,1)} fusion(bf16[4096,2048]{1,0:T(8,128)(2,1)} %get-tuple-element.84, bf16[4096,1024]{1,0:T(8,128)(2,1)S(1)} %get-tuple-element.124.dgate_ref), kind=kOutput, calls=%fused_computation.46 | convolution fusion | flops 17181966336 | bytes 29360128 | tf_op jit(solution)/shard_map/dot_general | solution.py:40
  471.1 0.0 reduce-scatter.9.cloned.1.call-start
  471.2 3.8 dynamic-slice_bitcast_fusion.2
  475.0 0.8 collective-permute-start.2
  475.8 0.1 collective-permute-start.1
  476.0 0.3 copy-done.22
  476.3 21.3 %convolution_convert_fusion.2 = bf16[2048,1024]{1,0:T(8,128)(2,1)} fusion(bf16[4096,2048]{1,0:T(8,128)(2,1)} %get-tuple-element.84, bf16[4096,1024]{1,0:T(8,128)(2,1)S(1)} %copy-done.22), kind=kOutput, calls=%fused_computation.45 | convolution fusion | flops 17181966336 | bytes 29360128 | tf_op jit(solution)/shard_map/dot_general | solution.py:40
  497.7 0.0 reduce-scatter.11.cloned.1.call-start
  497.7 2.8 collective-permute-done.2
  500.5 0.4 collective-permute-done.1
  500.9 3.1 fusion.32
  504.0 1.5 pad_maximum_fusion
  505.5 1.5 pad_maximum_fusion.1
  507.0 88.4 %shard_map.207 = f32[512,2048]{1,0:T(8,128)} custom-call(bf16[4096,1024]{1,0:T(8,128)(2,1)} %copy-done.23, bf16[4096,1024]{1,0:T(8,128)(2,1)} %get-tuple-element.87.dup_ref, bf16[2048,1024]{1,0:T(8,128)(2,1)} %all-gather.4.cloned.1.call-done.wg_ref, bf16[2048,1024]{1,0:T(8,128)(2,1)} %all-gather.6.cloned.1.call-done.wu_ref), custom_call_target="tpu_custom_call" | custom-call | flops 34359738368 | bytes 29360128 | tf_op jit(solution)/shard_map/pallas_call | solution.py:1040
  595.5 0.0 reduce-scatter.5.cloned.1.call-done.refs_0_
  595.5 4.7 multiply_reduce_fusion.1
  600.2 1.3 copy-done.6
  601.5 1.4 subtract_add_fusion
  603.0 10.6 %convolution_convert_fusion.5.do_ref = bf16[512,2048]{1,0:T(8,128)(2,1)} fusion(bf16[2048,2048]{1,0:T(8,128)(2,1)} %get-tuple-element.71, f32[512,2048]{1,0:T(8,128)S(1)} %subtract_add_fusion), kind=kOutput, calls=%fused_computation.49 | convolution fusion | flops 4297064448 | bytes 14680064 | tf_op jit(solution)/shard_map/dot_general | solution.py:32
  613.6 6.8 convolution_convert_fusion
  620.4 0.9 collective-permute-start.3
  621.3 1.1 collective-permute-start.4
  622.5 140.2 %shard_map.208 = (bf16[512,2048]{1,0:T(8,128)(2,1)}, bf16[512,1024]{1,0:T(8,128)(2,1)}, bf16[256,2048]{1,0:T(8,128)(2,1)}, bf16[256,2048]{1,0:T(8,128)(2,1)}) custom-call(bf16[512,2048]{1,0:T(8,128)(2,1)} %get-tuple-element.68.q_ref, bf16[512,2048]{1,0:T(8,128)(2,1)} %convolution_convert_fusion.5.do_ref, bf16[512,2048]{1,0:T(8,128)(2,1)} %get-tuple-element.70.o_ref, ...), custom_call_target="tpu_custom_call" | custom-call | flops 53687091200 | bytes 14680064 | tf_op jit(solution)/shard_map/pallas_call | solution.py:316
  762.7 6.9 fusion.39
  769.7 2.9 convert_element_type.146
  772.6 1.6 convert_element_type.148
  774.2 2.4 reduce-scatter.11.cloned.1.call-done.wo_ref
  776.6 12.1 %fusion.19 = (f32[512]{0:T(512)S(1)}, f32[2048]{0:T(1024)S(1)}, f32[512,2048]{1,0:T(8,128)}) fusion(bf16[1,512,2048]{2,1,0:T(8,128)(2,1)S(1)} %copy-done.4, f32[2048]{0:T(1024)S(1)} %copy-done.14, f32[512]{0:T(512)S(1)} %copy-done.19, f32[512,2048]{1,0:T(8,128)} %fusion.39, bf16[512,2048]{1,0:T(8,128)(2,1)} %get-tuple-element.101.dq_ref, ...), kind=kOutput, calls=%fused_computation.30 | convolution fusion | flops 4303353344 | bytes 20992000 | tf_op jit(solution)/shard_map/dot_general | solution.py:36
  788.7 0.6 pad_maximum_fusion.5.gain_ref
  789.3 106.3 %shard_map.209 = (f32[256,512]{1,0:T(8,128)}, f32[256,256]{1,0:T(8,128)}, f32[256,512]{1,0:T(8,128)}, f32[2,2048]{1,0:T(2,128)}, bf16[256,2048]{1,0:T(8,128)(2,1)}) custom-call(bf16[512,2048]{1,0:T(8,128)(2,1)} %fusion.10.x_ref, bf16[512,2048]{1,0:T(8,128)(2,1)} %get-tuple-element.101.dq_ref, bf16[512,1024]{1,0:T(8,128)(2,1)} %get-tuple-element.103.dkv_ref, ...), custom_call_target="tpu_custom_call" | custom-call | flops 120000004096 | bytes 6291456 | tf_op jit(solution)/shard_map/pallas_call | solution.py:1209
  895.6 1.4 fusion.38
  897.0 1.7 fusion.37
  898.7 2.8 convert_element_type.147
  901.5 6.4 fusion.31
  907.9 5.9 fusion.30
  913.8 0.8 copy.26
  914.6 0.8 copy.27
  (63 shorter events, 0.3 us)
Async XLA Ops:
  7.2 253.1 %all-gather.4.cloned.1.call-start = ((), (), s32[]{:S(2)}) async-start(), calls=%async_computation.4 | async-start | bytes 5242880 | tf_op jit(solution)/shard_map/all_gather | solution.py:1347
  58.6 1.6 copy-start.3
  58.6 2.1 copy-start.15
  58.6 2.4 copy-start.13
  58.6 201.7 %all-gather.6.cloned.1.call-start = ((), (), s32[]{:S(2)}) async-start(), calls=%async_computation.5 | async-start | bytes 5242880 | tf_op jit(solution)/shard_map/all_gather | solution.py:1347
  59.4 289.5 %all-gather.8.cloned.1.call-start = ((), (), s32[]{:S(2)}) async-start(), calls=%async_computation.6 | async-start | bytes 5242880 | tf_op jit(solution)/shard_map/all_gather | solution.py:1347
  60.1 535.4 %reduce-scatter.5.cloned.1.call-start = ((), (), s32[]{:S(2)}) async-start(), calls=%async_computation.7 | async-start | bytes 5242880 | tf_op jit(solution)/shard_map/reduce_scatter | solution.py:1352
  60.7 100.7 %copy-start.18 = (f32[512]{0:T(512)}, f32[512]{0:T(512)S(1)}, u32[]{:S(2)}) copy-start(f32[512]{0:T(512)S(1)} %add_rsqrt_fusion.1) | copy-start | bytes 6148
  248.8 9.8 %copy-start.11 = (f32[2048]{0:T(1024)S(1)}, f32[2048]{0:T(1024)}, u32[]{:S(2)}) copy-start(f32[2048]{0:T(1024)} %param.19) | copy-start | bytes 24580
  256.6 2.0 copy-start
  256.6 2.0 copy-start.16
  348.9 14.2 %copy-start.20 = (bf16[4096,1024]{1,0:T(8,128)(2,1)S(1)}, bf16[4096,1024]{1,0:T(8,128)(2,1)}, u32[]{:S(2)}) copy-start(bf16[4096,1024]{1,0:T(8,128)(2,1)} %get-tuple-element.78) | copy-start | bytes 25165828
  363.1 36.8 %collective-permute-start = (bf16[2048,2048]{1,0:T(8,128)(2,1)}, bf16[2048,2048]{1,0:T(8,128)(2,1)}, u32[]{:S(2)}, u32[]{:S(2)}) collective-permute-start(bf16[2048,2048]{1,0:T(8,128)(2,1)} %convolution_convert_fusion.1), channel_id=1, source_target_pairs={{0,4},{4,0},{8,12},{12,8},{16,20},{20,16},{24,28},{28,24},{1,5},{5... | collective-permute-start | bytes 25165832 | tf_op jit(solution)/shard_map/ppermute | solution.py:1294
  415.1 205.2 %reduce-scatter.7.cloned.1.call-start = ((), (), s32[]{:S(2)}) async-start(), calls=%async_computation.8 | async-start | bytes 5242880 | tf_op jit(solution)/shard_map/reduce_scatter | solution.py:1352
  446.4 3.3 copy-start.23
  471.1 298.6 %reduce-scatter.9.cloned.1.call-start = ((), (), s32[]{:S(2)}) async-start(), calls=%async_computation.9 | async-start | bytes 5242880 | tf_op jit(solution)/shard_map/reduce_scatter | solution.py:1352
  471.2 5.1 copy-start.22
  475.0 25.5 %collective-permute-start.2 = (bf16[256,2048]{1,0:T(8,128)(2,1)}, bf16[256,2048]{1,0:T(8,128)(2,1)}, u32[]{:S(2)}, u32[]{:S(2)}) collective-permute-start(bf16[256,2048]{1,0:T(8,128)(2,1)} %get-tuple-element.127), channel_id=1, source_target_pairs={{0,8},{4,12},{8,0},{12,4},{16,24},{20,28},{24,16},{28,20},{1,9},{5... | collective-permute-start | bytes 3145736 | tf_op jit(solution)/shard_map/ppermute | solution.py:1294
  475.8 25.1 %collective-permute-start.1 = (bf16[256,2048]{1,0:T(8,128)(2,1)S(1)}, bf16[256,2048]{1,0:T(8,128)(2,1)}, u32[]{:S(2)}, u32[]{:S(2)}) collective-permute-start(bf16[256,2048]{1,0:T(8,128)(2,1)S(1)} %get-tuple-element.126), channel_id=1, source_target_pairs={{0,16},{4,20},{8,24},{12,28},{16,0},{20,4},{24,8},{28,12},{1,17},{... | collective-permute-start | bytes 3145736 | tf_op jit(solution)/shard_map/ppermute | solution.py:1294
  497.7 278.9 %reduce-scatter.11.cloned.1.call-start = ((), (), s32[]{:S(2)}) async-start(), calls=%async_computation.10 | async-start | bytes 9437184 | tf_op jit(solution)/shard_map/reduce_scatter | solution.py:1305
  507.0 88.5 %copy-start.12 = (f32[2048]{0:T(1024)S(1)}, f32[2048]{0:T(1024)}, u32[]{:S(2)}) copy-start(f32[2048]{0:T(1024)} %param.19) | copy-start | bytes 24580
  507.0 88.5 %copy-start.17 = (f32[512]{0:T(512)S(1)}, f32[512]{0:T(512)}, u32[]{:S(2)}) copy-start(f32[512]{0:T(512)} %copy-done.16) | copy-start | bytes 6148
  507.0 93.2 %copy-start.7 = (bf16[1,512,2048]{2,1,0:T(8,128)(2,1)S(1)}, bf16[1,512,2048]{2,1,0:T(8,128)(2,1)}, u32[]{:S(2)}) copy-start(bf16[1,512,2048]{2,1,0:T(8,128)(2,1)} %param.23) | copy-start | bytes 6291460
  595.5 4.7 copy-start.1
  595.5 6.0 copy-start.6
  602.9 10.6 %copy-start.5 = (f32[512,2048]{1,0:T(8,128)}, f32[512,2048]{1,0:T(8,128)S(1)}, u32[]{:S(2)}) copy-start(f32[512,2048]{1,0:T(8,128)S(1)} %subtract_add_fusion) | copy-start | bytes 12582916
  603.0 10.6 %copy-start.21 = (bf16[512,2048]{1,0:T(8,128)(2,1)S(1)}, bf16[512,2048]{1,0:T(8,128)(2,1)}, u32[]{:S(2)}) copy-start(bf16[512,2048]{1,0:T(8,128)(2,1)} %get-tuple-element.70.o_ref) | copy-start | bytes 6291460
  620.4 168.9 %collective-permute-start.3 = (bf16[512,2048]{1,0:T(8,128)(2,1)}, bf16[512,2048]{1,0:T(8,128)(2,1)}, u32[]{:S(2)}, u32[]{:S(2)}) collective-permute-start(bf16[512,2048]{1,0:T(8,128)(2,1)} %pad_maximum_fusion), channel_id=1, source_target_pairs={{0,8},{4,12},{8,0},{12,4},{16,24},{20,28},{24,16},{28,20},{1,9},{5... | collective-permute-start | bytes 6291464 | tf_op jit(solution)/shard_map/ppermute | solution.py:1294
  621.3 168.0 %collective-permute-start.4 = (bf16[512,2048]{1,0:T(8,128)(2,1)}, bf16[512,2048]{1,0:T(8,128)(2,1)}, u32[]{:S(2)}, u32[]{:S(2)}) collective-permute-start(bf16[512,2048]{1,0:T(8,128)(2,1)} %pad_maximum_fusion.1), channel_id=1, source_target_pairs={{0,16},{4,20},{8,24},{12,28},{16,0},{20,4},{24,8},{28,12},{1,17},{... | collective-permute-start | bytes 6291464 | tf_op jit(solution)/shard_map/ppermute | solution.py:1294
  762.7 9.9 %copy-start.8 = (bf16[256,2048]{1,0:T(8,128)(2,1)S(1)}, bf16[256,2048]{1,0:T(8,128)(2,1)}, u32[]{:S(2)}) copy-start(bf16[256,2048]{1,0:T(8,128)(2,1)} %get-tuple-element.118) | copy-start | bytes 3145732
  769.7 6.9 copy-start.4
  769.7 6.9 copy-start.14
  769.7 6.9 copy-start.19
  901.5 6.4 copy-start.2
  907.9 5.9 copy-start.10
  907.9 6.7 copy-start.9
Sparse Core Ops, SparseCore 0:
  58.7 97.5 all-gather.3
  157.9 94.0 all-gather.5
  253.5 79.0 all-gather.7
  415.3 118.3 reduce-scatter.4
  535.9 77.2 reduce-scatter.6
  615.3 78.7 reduce-scatter.8
  698.0 78.5 reduce-scatter.10

commit v7 on v6

--- a/solution.py
+++ b/solution.py
@@ -94,7 +94,7 @@
 
 
 def attend_kernel(
-    reach, wide, q_ref, k_ref, v_ref, low_ref, own_ref, att_ref, lse_ref, all_ref,
+    reach, wide, q_ref, k_ref, v_ref, low_ref, own_ref, _, att_ref, lse_ref, all_ref,
     bias_ref, full, own_sem, send_sem, recv_sem, out_sem,
 ):
     head, tile, pair = pl.program_id(0), pl.program_id(1), pl.program_id(2)
@@ -102,24 +102,26 @@
     inner = pl.num_programs(1) * pl.num_programs(2)
     step = head * inner + tile * pl.num_programs(2) + pair
     ring = Ring(wide, full, own_ref.shape[0], send_sem, recv_sem)
+    right = pl.ds(own_ref.shape[1] - full.shape[1], full.shape[1])
 
     def outward(slot, *flips):
         where = ring.whole(*flips)
-        return pltpu.make_async_copy(full.at[where], all_ref.at[where], out_sem.at[slot])
+        return pltpu.make_async_copy(full.at[where], all_ref.at[where, right], out_sem.at[slot])
 
     near = [(0, 0, 0), (0, 0, 1), (0, 1, 0), (1, 0, 0)]
     rest = [(0, 1, 1), (1, 0, 1), (1, 1, 0), (1, 1, 1)]
 
     @pl.when(step == 0)
     def _():
-        local = pltpu.make_async_copy(own_ref, full.at[ring.mine()], own_sem)
+        local = pltpu.make_async_copy(own_ref.at[:, right], full.at[ring.mine()], own_sem)
         local.start()
         meet(ring.peers)
         local.wait()
         ring.start_own()
         fill_bias(bias_ref, low_ref, reach)
 
-    pl.when(step == 4 * inner)(ring.first_halves)
+    pl.when(step == 2 * inner)(ring.first_halves)
+    pl.when(step == 4 * inner)(ring.second_halves)
 
     keys = pl.ds(pl.multiple_of(tile * QTILE, QTILE), bias_ref.shape[1])
     queries = spread_pair(q_ref[...], half)
@@ -135,7 +137,6 @@
 
     @pl.when(step == pl.num_programs(0) * inner - 1)
     def _():
-        ring.second_halves()
         ring.from_sibling("own", 0, 1)
         for slot, flips in enumerate(near):
             outward(slot, *flips).start()
@@ -149,7 +150,7 @@
         ring.sent()
 
 
-def attend(q, kv, low, grad, dp_size):
+def attend(q, kv, low, grad, grads, dp_size):
     rows, width = q.shape
     keys = kv.shape[0]
     reach = keys - rows
@@ -158,7 +159,7 @@
     heads = kv.shape[1] // LANES
     per_head = pairs // heads
     span = reach + QTILE
-    whole = (GROUP * grad.shape[0], grad.shape[1])
+    right = (grads.shape[0], grads.shape[1] // 2)
     far = pl.BlockSpec(memory_space=pl.ANY)
     return pl.pallas_call(
         functools.partial(attend_kernel, reach, 2 * math.isqrt(dp_size // GROUP)),
@@ -169,6 +170,7 @@
             pl.BlockSpec((keys, LANES), lambda a, t, p: (0, 2 * (a // 2) + 1)),
             pl.BlockSpec((1, rows), lambda a, t, p: (0, 0)),
             far,
+            far,
         ],
         out_specs=[
             pl.BlockSpec((QTILE, LANES), lambda a, t, p: (t, a * per_head + p)),
@@ -178,16 +180,17 @@
         out_shape=[
             jax.ShapeDtypeStruct((rows, width), BF16),
             jax.ShapeDtypeStruct((pairs * tiles, 1, 2 * QTILE), F32),
-            jax.ShapeDtypeStruct(whole, BF16),
+            jax.ShapeDtypeStruct(grads.shape, BF16),
         ],
         scratch_shapes=[
             pltpu.VMEM((tiles, span, QTILE), F32),
-            pltpu.VMEM(whole, BF16),
+            pltpu.VMEM(right, BF16),
             pltpu.SemaphoreType.DMA,
             pltpu.SemaphoreType.DMA((Ring.COPIES,)),
             pltpu.SemaphoreType.DMA((Ring.COPIES,)),
             pltpu.SemaphoreType.DMA((8,)),
         ],
+        input_output_aliases={5: 2},
         compiler_params=pltpu.CompilerParams(
             collective_id=7, has_side_effects=True, vmem_limit_bytes=56 << 20
         ),
@@ -196,7 +199,7 @@
             bytes_accessed=4 * rows * width + 2 * keys * kv.shape[1],
             transcendentals=2 * rows * span * pairs,
         ),
-    )(q, kv, kv, low, grad)
+    )(q, kv, kv, low, grad, grads)
 
 
 def attend_back_kernel(
@@ -621,14 +624,18 @@
 
 
 def project_kernel(
-    wide, z_size, x_ref, cos_ref, sin_ref, wkv_ref, wq_ref, wo_ref,
-    q_ref, kv_ref, wkv_out, wq_out, wo_out,
-    wkv_all, wq_all, wo_all, keys, own_sem, send_sem, recv_sem, kv_send, kv_recv, out_sem,
+    wide, z_size, x_ref, cos_ref, sin_ref, wkv_ref, wq_ref, wo_ref, grad_ref,
+    q_ref, kv_ref, wkv_out, wq_out, wo_out, grad_out,
+    wkv_all, wq_all, wo_all, grad_all, keys, own_sem, send_sem, recv_sem, kv_send, kv_recv, out_sem,
 ):
     place = lax.axis_index("tensor")
     rows = x_ref.shape[0]
     count = keys.shape[0] // rows - 1
-    parts = ((wkv_ref, wkv_all, wkv_out), (wq_ref, wq_all, wq_out), (wo_ref, wo_all, wo_out))
+    left = pl.ds(0, grad_all.shape[1])
+    parts = (
+        (wkv_ref, wkv_all, wkv_out), (wq_ref, wq_all, wq_out), (wo_ref, wo_all, wo_out),
+        (grad_ref.at[:, left], grad_all, grad_out.at[:, left]),
+    )
     rings = [
         Ring(wide, full, part.shape[0], send_sem.at[at], recv_sem.at[at])
         for at, (part, full, _) in enumerate(parts)
@@ -701,12 +708,18 @@
 
     rings[2].first_halves()
     rings[2].second_halves()
-    for step in range(2, count + 2):
+    rings[3].start_own()
+    for step in range(2, count + 1):
         pass_keys(step)
-    keys_out = pltpu.make_async_copy(keys, kv_ref, out_sem.at[3])
-    keys_out.start()
     finish(rings[2])
     outward[2].start()
+    rings[3].first_halves()
+    rings[3].second_halves()
+    finish(rings[3])
+    outward[3].start()
+    pass_keys(count + 1)
+    keys_out = pltpu.make_async_copy(keys, kv_ref, out_sem.at[4])
+    keys_out.start()
     for step in range(1, count + 1):
         sends = (place + 1 < z_size) & (place >= step - 1)
         pl.when(sends)(lambda: hop(step).wait_send())
@@ -716,27 +729,29 @@
         copy.wait()
 
 
-def project(x, cosine, sine, wkv, wq, wo, reach, dp_size, z_size):
+def project(x, cosine, sine, wkv, wq, wo, grad, reach, dp_size, z_size):
     rows, width = x.shape
     far = pl.BlockSpec(memory_space=pl.ANY)
     near = pl.BlockSpec(memory_space=pltpu.VMEM)
     weights = (wkv, wq, wo)
     whole = [(GROUP * w.shape[0], w.shape[1]) for w in weights]
     keys = (reach + rows, wkv.shape[1])
+    grads = (GROUP * grad.shape[0], grad.shape[1])
+    left = (grads[0], grads[1] // 2)
     return pl.pallas_call(
         functools.partial(project_kernel, 2 * math.isqrt(dp_size // GROUP), z_size),
-        in_specs=[near] * 3 + [far] * 3,
-        out_specs=[near] + [far] * 4,
+        in_specs=[near] * 3 + [far] * 4,
+        out_specs=[near] + [far] * 5,
         out_shape=[jax.ShapeDtypeStruct((rows, wq.shape[1]), BF16)]
-        + [jax.ShapeDtypeStruct(shape, BF16) for shape in [keys] + whole],
-        scratch_shapes=[pltpu.VMEM(shape, BF16) for shape in whole + [keys]]
+        + [jax.ShapeDtypeStruct(shape, BF16) for shape in [keys] + whole + [grads]],
+        scratch_shapes=[pltpu.VMEM(shape, BF16) for shape in whole + [left, keys]]
         + [
-            pltpu.SemaphoreType.DMA((3,)),
-            pltpu.SemaphoreType.DMA((3, Ring.COPIES)),
-            pltpu.SemaphoreType.DMA((3, Ring.COPIES)),
+            pltpu.SemaphoreType.DMA((4,)),
+            pltpu.SemaphoreType.DMA((4, Ring.COPIES)),
+            pltpu.SemaphoreType.DMA((4, Ring.COPIES)),
             pltpu.SemaphoreType.DMA((reach // rows,)),
             pltpu.SemaphoreType.DMA((reach // rows,)),
-            pltpu.SemaphoreType.DMA((4,)),
+            pltpu.SemaphoreType.DMA((5,)),
         ],
         compiler_params=pltpu.CompilerParams(
             collective_id=3, has_side_effects=True, vmem_limit_bytes=56 << 20
@@ -745,7 +760,7 @@
             flops=2 * LONG, bytes_accessed=4 * width * sum(w.shape[1] for w in weights),
             transcendentals=0,
         ),
-    )(x, cosine, sine, wkv, wq, wo)
+    )(x, cosine, sine, wkv, wq, wo, grad)
 
 
 def gate_up_kernel(
@@ -1355,12 +1370,12 @@
 
     r1 = rms_scale(x)
     xn = (x * r1 * attn_gain).astype(BF16)
-    q, kv_all, wkv, wq, wo = project(
-        layout.from_cols(xn), cosine, sine, *spread[3:], reach, dp_size, z_size
+    q, kv_all, wkv, wq, wo, dy = project(
+        layout.from_cols(xn), cosine, sine, *spread[3:], cotangent[0], reach, dp_size, z_size
     )
     wd = gather_z(spread[2])
     wkv, wq, wo = layout.to_rows(wkv), layout.to_rows(wq), layout.to_rows(wo)
-    att, lse, dy = attend(q, kv_all, low, cotangent[0], dp_size)
+    att, lse, dy = attend(q, kv_all, low, cotangent[0], dy, dp_size)
     h = x + dot_nt(att, wo)
 
     r2 = rms_scale(h)
@@ -1374,8 +1389,8 @@
     total_wd = dot_tn(dy, hidden).astype(BF16)
     near_sum = dot_nt(by_core[0], wd) + layout.swap(away, 1).astype(F32)
     near_sum = near_sum.astype(BF16)
-    dy, total_wd, near_sum = lax.optimization_barrier((dy, total_wd, near_sum))
     part_wd = along_z(total_wd)
+    dy, near_sum = lax.optimization_barrier((dy, near_sum))
     near_sum = near_sum.reshape(GROUP // 2, rows, width)
     far_chunk = chunk(near_sum, 1 - row, 1 - col)
     from_x = layout.swap(far_chunk[rows // 2 :], 2)

time: 926 us -> 891 us (0.962)
  Pallas kernels: 656 us -> 627 us
  matrix products: 184 us -> 173 us
    pallas_call x1, Pallas kernels: 140 us -> 101 us  [attend_back(): pl.pallas_call(functools.partial(attend_back_kernel, reach, 2 * math.isqr...]
    pallas_call x1, Pallas kernels: 95.7 us -> 131 us  [project(): pl.pallas_call(functools.partial(project_kernel, 2 * math.isqrt(dp_size /...]
    pallas_call x1, Pallas kernels: 87.3 us -> 63.3 us  [attend(): pl.pallas_call(functools.partial(attend_kernel, reach, 2 * math.isqrt(dp_...]
    dot_general x4, matrix products: 86.3 us -> 73.5 us  [dot_tn(): lax.dot_general(left, right, (((0,), (0,)), ((), ())), preferred_element_...]
  transfers between devices with their start and end apart: 12 -> 12, of which waited for: 3 -> 3; matrix products, arithmetic and copies ran while one was open for 20% -> 21% of each run, Pallas kernels for 54% -> 53%
where the time goes in v7:
time: 891 us; the launch traced here: 882 us
  Pallas kernels  627 us (70%)
  matrix products  173 us (19%)
  other arithmetic  42.4 us (5%)
  between operations  15 us (2%)
  local copies, waits for them, and re-layouts  11.8 us (1%)
    pallas_call x1, Pallas kernels, project(): pl.pallas_call(functools.partial(project_kernel, 2 * math.isqrt(dp_size /...  131 us
    pallas_call x1, Pallas kernels, last_grads(): pl.pallas_call(functools.partial(tail_kernel, 2 * math.isqrt(dp_size // G...  106 us
    pallas_call x1, Pallas kernels, attend_back(): pl.pallas_call(functools.partial(attend_back_kernel, reach, 2 * math.isqr...  101 us
    pallas_call x1, Pallas kernels, hidden_back(): pl.pallas_call(functools.partial(hidden_back_kernel, 2 * math.isqrt(dp_si...  88.7 us
    pallas_call x1, Pallas kernels, gate_up(): pl.pallas_call(functools.partial(gate_up_kernel, 2 * math.isqrt(dp_size /...  87.8 us
    dot_general x4, matrix products, dot_tn(): lax.dot_general(left, right, (((0,), (0,)), ((), ())), preferred_element_...  73.5 us
    pallas_call x1, Pallas kernels, attend(): pl.pallas_call(functools.partial(attend_kernel, reach, 2 * math.isqrt(dp_...  63.3 us
    dot_general x5, matrix products, dot_nt(): lax.dot_general(left, right, (((1,), (1,)), ((), ())), preferred_element_...  54.6 us
  transfers between devices with their start and end apart: 12, of which 3 were waited for; matrix products, arithmetic and copies ran while one was open for 21% of the time, Pallas kernels for 53%

profile of v7, /device:TPU:0, one launch (start us, length us, event | category | flops | bytes accessed | tf_op | source)
XLA Modules:
  0.0 882.1 jit_solution(4772898779792836285)
XLA Ops:
  7.2 0.0 all-gather.4.cloned.1.call-start
  7.2 1.5 pad_maximum_fusion.4.refs_3_
  8.8 49.8 %shard_map.203 = (bf16[2048,256]{1,0:T(8,128)(2,1)}, bf16[2048,256]{1,0:T(8,128)(2,1)}, bf16[2048,256]{1,0:T(8,128)(2,1)}, bf16[256,1024]{1,0:T(8,128)(2,1)}, bf...) custom-call(bf16[256,2048]{1,0:T(8,128)(2,1)} %refs_0_.1, bf16[256,2048]{1,0:T(8,128)(2,1)} %refs_1_.1, ...), custom_call_target="tpu_custom_call" | custom-call | flops 60000002048 | tf_op jit(solution)/shard_map/pallas_call | solution.py:527
  58.6 0.0 all-gather.6.cloned.1.call-start
  58.7 0.7 all-gather.6.cloned.1.call-update
  59.4 0.0 all-gather.8.cloned.1.call-start
  59.4 0.7 all-gather.8.cloned.1.call-update
  60.1 0.0 reduce-scatter.5.cloned.1.call-start
  60.2 0.1 convert_reduce_fusion
  60.3 0.5 fusion.16
  60.8 0.1 select_reduce_fusion
  60.9 0.7 subtract_add_fusion.1
  61.6 1.0 fusion.36
  62.6 1.9 fusion.10.x_ref
  64.4 1.3 pad_maximum_fusion.2
  65.7 130.8 %shard_map.204 = (bf16[512,2048]{1,0:T(8,128)(2,1)}, bf16[1536,1024]{1,0:T(8,128)(2,1)}, bf16[2048,1024]{1,0:T(8,128)(2,1)}, bf16[2048,2048]{1,0:T(8,128)(2,1)},...) custom-call(bf16[512,2048]{1,0:T(8,128)(2,1)} %fusion.10.x_ref, f32[512,128]{1,0:T(8,128)} %get-tuple-element.143.cos_ref.cos_all, ...), custom_call_target="tpu_custom_call" | custom-call | flops 120000004096 | bytes 41943040 | tf_op jit(solution)/shard_map/pallas_call | solution.py:741
  196.5 63.3 %shard_map.205 = (bf16[512,2048]{1,0:T(8,128)(2,1)}, f32[32,1,512]{2,1,0:T(1,128)}, bf16[4096,2048]{1,0:T(8,128)(2,1)}) custom-call(bf16[512,2048]{1,0:T(8,128)(2,1)} %get-tuple-element.68.q_ref, bf16[1536,1024]{1,0:T(8,128)(2,1)} %get-tuple-element.69.k_ref.v_ref, ...), custom_call_target="tpu_custom_call", output_to_operand_aliasing={{2}: (5, {})} | custom-call | flops 21474836480 | bytes 7340032 | tf_op jit(solution)/shard_map/pallas_call | solution.py:164
  259.8 8.0 multiply_reduce_fusion.2
  267.8 1.9 copy-done
  269.8 1.7 multiply_convert_fusion.own_ref
  271.5 87.8 %shard_map.206 = (bf16[4096,2048]{1,0:T(8,128)(2,1)}, bf16[4096,1024]{1,0:T(8,128)(2,1)}, bf16[4096,1024]{1,0:T(8,128)(2,1)}, bf16[4096,1024]{1,0:T(8,128)(2,1)}, bf16[2,2048,1024]{2,1,0:T(8,128)(2,1)}) custom-call(bf16[512,2048]{1,0:T(8,128)(2,1)} %multiply_convert_fusion.own_ref, bf16[2048,1024]{1,0:T(8,128)(2,1)} %all-gather.4.cloned.1.call-done.wg_ref, ...), custom_call_target="tpu_custom_call" | custom-call | flops 1000000 | tf_op jit(solution)/shard_map/pallas_call | solution.py:856
  359.3 14.4 %convolution_convert_fusion.1 = bf16[2048,2048]{1,0:T(8,128)(2,1)} fusion(bf16[2048,1024]{1,0:T(8,128)(2,1)} %all-gather.8.cloned.1.call-done, bf16[2,2048,1024]{2,1,0:T(8,128)(2,1)} %get-tuple-element.76), kind=kOutput, calls=%fused_computation.18 | convolution fusion | flops 8594128896 | bytes 16777216 | tf_op jit(solution)/shard_map/dot_general | solution.py:36
  373.7 21.5 %convolution_convert_fusion.2 = bf16[2048,1024]{1,0:T(8,128)(2,1)} fusion(bf16[4096,2048]{1,0:T(8,128)(2,1)} %get-tuple-element.81, bf16[4096,1024]{1,0:T(8,128)(2,1)S(1)} %copy-done.19), kind=kOutput, calls=%fused_computation.45 | convolution fusion | flops 17181966336 | bytes 29360128 | tf_op jit(solution)/shard_map/dot_general | solution.py:40
  395.2 0.0 reduce-scatter.7.cloned.1.call-start
  395.3 15.8 %add_convert_fusion = bf16[2048,2048]{1,0:T(8,128)(2,1)} fusion(bf16[2048,2048]{1,0:T(8,128)(2,1)} %collective-permute-done, bf16[2048,1024]{1,0:T(8,128)(2,1)} %all-gather.8.cloned.1.call-done, bf16[2,2048,1024]{2,1,0:T(8,128)(2,1)} %get-tuple-element.76), kind=kOutput, calls=%fused_computation.11 | convolution fusion | flops 8602517504 | bytes 25165824 | tf_op jit(solution)/shard_map/dot_general | solution.py:36
  411.1 34.3 %fusion.7 = (bf16[4096,1024]{1,0:T(8,128)(2,1)}, bf16[4096,1024]{1,0:T(8,128)(2,1)}) fusion(bf16[4096,1024]{1,0:T(8,128)(2,1)} %get-tuple-element.83, bf16[4096,1024]{1,0:T(8,128)(2,1)} %get-tuple-element.82, bf16[4096,2048]{1,0:T(8,128)(2,1)} %get-tuple-element.81, bf16[2048,1024]{1,0:T(8,128)(2,1)S(1)} %copy-done.20), kind=kOutput, calls=%fused_computation.10 | convolution fusion | flops 17242783744 | bytes 54525952 | tf_op jit(solution)/shard_map/dot_general | solution.py:32
  445.5 24.0 %convolution_convert_fusion.4 = bf16[2048,1024]{1,0:T(8,128)(2,1)} fusion(bf16[4096,2048]{1,0:T(8,128)(2,1)} %get-tuple-element.84, bf16[4096,1024]{1,0:T(8,128)(2,1)} %get-tuple-element.124.dgate_ref), kind=kOutput, calls=%fused_computation.47 | convolution fusion | flops 17181966336 | bytes 29360128 | tf_op jit(solution)/shard_map/dot_general | solution.py:40
  469.5 0.0 reduce-scatter.9.cloned.1.call-start
  469.6 3.7 dynamic-slice_bitcast_fusion.2
  473.3 0.6 collective-permute-start.1
  474.0 0.9 collective-permute-start.2
  474.9 21.2 %convolution_convert_fusion.3 = bf16[2048,1024]{1,0:T(8,128)(2,1)} fusion(bf16[4096,2048]{1,0:T(8,128)(2,1)} %get-tuple-element.84, bf16[4096,1024]{1,0:T(8,128)(2,1)S(1)} %copy-done.24), kind=kOutput, calls=%fused_computation.46 | convolution fusion | flops 17181966336 | bytes 29360128 | tf_op jit(solution)/shard_map/dot_general | solution.py:40
  496.1 0.0 reduce-scatter.11.cloned.1.call-start
  496.2 3.1 collective-permute-done.1
  499.3 0.1 collective-permute-done.2
  499.4 3.1 fusion.32
  502.5 1.5 pad_maximum_fusion.1
  504.0 1.5 pad_maximum_fusion
  505.5 88.7 %shard_map.207 = f32[512,2048]{1,0:T(8,128)} custom-call(bf16[4096,1024]{1,0:T(8,128)(2,1)} %get-tuple-element.124.dgate_ref, bf16[4096,1024]{1,0:T(8,128)(2,1)} %get-tuple-element.87.dup_ref, bf16[2048,1024]{1,0:T(8,128)(2,1)} %all-gather.4.cloned.1.call-done.wg_ref, bf16[2048,1024]{1,0:T(8,128)(2,1)} %all-gather.6.cloned.1.call-done.wu_ref), custom_call_target="tpu_custom_call" | custom-call | flops 34359738368 | bytes 29360128 | tf_op jit(solution)/shard_map/pallas_call | solution.py:1055
  594.2 0.0 reduce-scatter.5.cloned.1.call-done.refs_0_
  594.3 4.7 multiply_reduce_fusion.1
  598.9 0.0 copy-done.1
  599.0 1.3 copy-done.6
  600.3 1.4 subtract_add_fusion
  601.7 10.6 %convolution_convert_fusion.5.do_ref = bf16[512,2048]{1,0:T(8,128)(2,1)} fusion(bf16[2048,2048]{1,0:T(8,128)(2,1)} %get-tuple-element.72, f32[512,2048]{1,0:T(8,128)S(1)} %subtract_add_fusion), kind=kOutput, calls=%fused_computation.49 | convolution fusion | flops 4297064448 | bytes 14680064 | tf_op jit(solution)/shard_map/dot_general | solution.py:32
  612.3 6.8 convolution_convert_fusion
  619.1 1.0 collective-permute-start.3
  620.2 1.1 collective-permute-start.4
  621.3 100.7 %shard_map.208 = (bf16[512,2048]{1,0:T(8,128)(2,1)}, bf16[512,1024]{1,0:T(8,128)(2,1)}, bf16[256,2048]{1,0:T(8,128)(2,1)}, bf16[256,2048]{1,0:T(8,128)(2,1)}) custom-call(bf16[512,2048]{1,0:T(8,128)(2,1)} %get-tuple-element.68.q_ref, bf16[512,2048]{1,0:T(8,128)(2,1)} %convolution_convert_fusion.5.do_ref, bf16[512,2048]{1,0:T(8,128)(2,1)} %get-tuple-element.71.o_ref, ...), custom_call_target="tpu_custom_call" | custom-call | flops 53687091200 | bytes 14680064 | tf_op jit(solution)/shard_map/pallas_call | solution.py:319
  722.0 0.0 reduce-scatter.9.cloned.1.call-done.refs_0_
  722.0 2.9 convert_element_type.146
  725.0 2.8 convert_element_type.148
  727.8 4.3 fusion.39
  732.1 3.9 reduce-scatter.11.cloned.1.call-done.wo_ref
  736.1 12.1 %fusion.19 = (f32[512]{0:T(512)S(1)}, f32[2048]{0:T(1024)S(1)}, f32[512,2048]{1,0:T(8,128)}) fusion(bf16[1,512,2048]{2,1,0:T(8,128)(2,1)S(1)} %copy-done.4, f32[2048]{0:T(1024)S(1)} %copy-done.13, f32[512]{0:T(512)S(1)} %copy-done.18, f32[512,2048]{1,0:T(8,128)} %fusion.39, bf16[512,2048]{1,0:T(8,128)(2,1)} %get-tuple-element.101.dq_ref, ...), kind=kOutput, calls=%fused_computation.30 | convolution fusion | flops 4303353344 | bytes 20992000 | tf_op jit(solution)/shard_map/dot_general | solution.py:36
  748.1 0.6 pad_maximum_fusion.5.gain_ref
  748.8 106.3 %shard_map.209 = (f32[256,512]{1,0:T(8,128)}, f32[256,256]{1,0:T(8,128)}, f32[256,512]{1,0:T(8,128)}, f32[2,2048]{1,0:T(2,128)}, bf16[256,2048]{1,0:T(8,128)(2,1)}) custom-call(bf16[512,2048]{1,0:T(8,128)(2,1)} %fusion.10.x_ref, bf16[512,2048]{1,0:T(8,128)(2,1)} %get-tuple-element.101.dq_ref, bf16[512,1024]{1,0:T(8,128)(2,1)} %get-tuple-element.103.dkv_ref, ...), custom_call_target="tpu_custom_call" | custom-call | flops 120000004096 | bytes 6291456 | tf_op jit(solution)/shard_map/pallas_call | solution.py:1224
  855.0 1.4 fusion.38
  856.4 1.7 fusion.37
  858.1 2.8 convert_element_type.147
  860.9 6.4 fusion.31
  867.3 5.9 fusion.30
  873.2 0.8 copy.28
  874.0 0.8 copy.29
  (65 shorter events, 0.3 us)
Async XLA Ops:
  7.2 264.3 %all-gather.4.cloned.1.call-start = ((), (), s32[]{:S(2)}) async-start(), calls=%async_computation.4 | async-start | bytes 5242880 | tf_op jit(solution)/shard_map/all_gather | solution.py:1362
  8.8 51.4 %copy-start.14 = (s32[1,2048]{1,0:T(1,128)S(1)}, s32[1,2048]{1,0:T(1,128)}, u32[]{:S(2)}) copy-start(s32[1,2048]{1,0:T(1,128)} %param.13) | copy-start | bytes 24580
  58.6 1.7 copy-start.3
  58.6 4.0 copy-start.12
  58.6 212.9 %all-gather.6.cloned.1.call-start = ((), (), s32[]{:S(2)}) async-start(), calls=%async_computation.5 | async-start | bytes 5242880 | tf_op jit(solution)/shard_map/all_gather | solution.py:1362
  59.4 299.9 %all-gather.8.cloned.1.call-start = ((), (), s32[]{:S(2)}) async-start(), calls=%async_computation.6 | async-start | bytes 5242880 | tf_op jit(solution)/shard_map/all_gather | solution.py:1362
  60.1 534.1 %reduce-scatter.5.cloned.1.call-start = ((), (), s32[]{:S(2)}) async-start(), calls=%async_computation.7 | async-start | bytes 5242880 | tf_op jit(solution)/shard_map/reduce_scatter | solution.py:1367
  60.8 135.7 %copy-start.17 = (f32[512]{0:T(512)}, f32[512]{0:T(512)S(1)}, u32[]{:S(2)}) copy-start(f32[512]{0:T(512)S(1)} %add_rsqrt_fusion.1) | copy-start | bytes 6148
  259.8 10.0 %copy-start.10 = (f32[2048]{0:T(1024)S(1)}, f32[2048]{0:T(1024)}, u32[]{:S(2)}) copy-start(f32[2048]{0:T(1024)} %param.19) | copy-start | bytes 24580
  267.8 2.0 copy-start
  267.8 1.9 copy-start.15
  359.3 14.4 %copy-start.19 = (bf16[4096,1024]{1,0:T(8,128)(2,1)S(1)}, bf16[4096,1024]{1,0:T(8,128)(2,1)}, u32[]{:S(2)}) copy-start(bf16[4096,1024]{1,0:T(8,128)(2,1)} %get-tuple-element.88) | copy-start | bytes 25165828
  373.7 21.6 %collective-permute-start = (bf16[2048,2048]{1,0:T(8,128)(2,1)}, bf16[2048,2048]{1,0:T(8,128)(2,1)}, u32[]{:S(2)}, u32[]{:S(2)}) collective-permute-start(bf16[2048,2048]{1,0:T(8,128)(2,1)} %convolution_convert_fusion.1), channel_id=1, source_target_pairs={{0,4},{4,0},{8,12},{12,8},{16,20},{20,16},{24,28},{28,24},{1,5},{5... | collective-permute-start | bytes 25165832 | tf_op jit(solution)/shard_map/ppermute | solution.py:1309
  395.2 223.9 %reduce-scatter.7.cloned.1.call-start = ((), (), s32[]{:S(2)}) async-start(), calls=%async_computation.8 | async-start | bytes 5242880 | tf_op jit(solution)/shard_map/reduce_scatter | solution.py:1367
  395.3 15.9 %copy-start.20 = (bf16[2048,1024]{1,0:T(8,128)(2,1)S(1)}, bf16[2048,1024]{1,0:T(8,128)(2,1)}, u32[]{:S(2)}) copy-start(bf16[2048,1024]{1,0:T(8,128)(2,1)} %all-gather.8.cloned.1.call-done) | copy-start | bytes 12582916
  469.5 252.5 %reduce-scatter.9.cloned.1.call-start = ((), (), s32[]{:S(2)}) async-start(), calls=%async_computation.9 | async-start | bytes 5242880 | tf_op jit(solution)/shard_map/reduce_scatter | solution.py:1367
  469.6 5.3 copy-start.24
  473.3 26.0 %collective-permute-start.1 = (bf16[256,2048]{1,0:T(8,128)(2,1)}, bf16[256,2048]{1,0:T(8,128)(2,1)}, u32[]{:S(2)}, u32[]{:S(2)}) collective-permute-start(bf16[256,2048]{1,0:T(8,128)(2,1)} %get-tuple-element.126), channel_id=1, source_target_pairs={{0,16},{4,20},{8,24},{12,28},{16,0},{20,4},{24,8},{28,12},{1,17},{... | collective-permute-start | bytes 3145736 | tf_op jit(solution)/shard_map/ppermute | solution.py:1309
  474.0 25.4 %collective-permute-start.2 = (bf16[256,2048]{1,0:T(8,128)(2,1)S(1)}, bf16[256,2048]{1,0:T(8,128)(2,1)}, u32[]{:S(2)}, u32[]{:S(2)}) collective-permute-start(bf16[256,2048]{1,0:T(8,128)(2,1)S(1)} %get-tuple-element.127), channel_id=1, source_target_pairs={{0,8},{4,12},{8,0},{12,4},{16,24},{20,28},{24,16},{28,20},{1,9},{5... | collective-permute-start | bytes 3145736 | tf_op jit(solution)/shard_map/ppermute | solution.py:1309
  496.1 239.9 %reduce-scatter.11.cloned.1.call-start = ((), (), s32[]{:S(2)}) async-start(), calls=%async_computation.10 | async-start | bytes 9437184 | tf_op jit(solution)/shard_map/reduce_scatter | solution.py:1320
  505.5 88.7 %copy-start.11 = (f32[2048]{0:T(1024)S(1)}, f32[2048]{0:T(1024)}, u32[]{:S(2)}) copy-start(f32[2048]{0:T(1024)} %param.19) | copy-start | bytes 24580
  505.5 88.7 %copy-start.16 = (f32[512]{0:T(512)S(1)}, f32[512]{0:T(512)}, u32[]{:S(2)}) copy-start(f32[512]{0:T(512)} %copy-done.15) | copy-start | bytes 6148
  505.5 93.4 %copy-start.7 = (bf16[1,512,2048]{2,1,0:T(8,128)(2,1)S(1)}, bf16[1,512,2048]{2,1,0:T(8,128)(2,1)}, u32[]{:S(2)}) copy-start(bf16[1,512,2048]{2,1,0:T(8,128)(2,1)} %param.23) | copy-start | bytes 6291460
  594.2 4.7 copy-start.1
  594.3 6.0 copy-start.6
  601.7 10.6 %copy-start.5 = (f32[512,2048]{1,0:T(8,128)}, f32[512,2048]{1,0:T(8,128)S(1)}, u32[]{:S(2)}) copy-start(f32[512,2048]{1,0:T(8,128)S(1)} %subtract_add_fusion) | copy-start | bytes 12582916
  601.7 10.6 %copy-start.23 = (bf16[512,2048]{1,0:T(8,128)(2,1)S(1)}, bf16[512,2048]{1,0:T(8,128)(2,1)}, u32[]{:S(2)}) copy-start(bf16[512,2048]{1,0:T(8,128)(2,1)} %get-tuple-element.71.o_ref) | copy-start | bytes 6291460
  619.1 129.6 %collective-permute-start.3 = (bf16[512,2048]{1,0:T(8,128)(2,1)}, bf16[512,2048]{1,0:T(8,128)(2,1)}, u32[]{:S(2)}, u32[]{:S(2)}) collective-permute-start(bf16[512,2048]{1,0:T(8,128)(2,1)} %pad_maximum_fusion), channel_id=1, source_target_pairs={{0,8},{4,12},{8,0},{12,4},{16,24},{20,28},{24,16},{28,20},{1,9},{5... | collective-permute-start | bytes 6291464 | tf_op jit(solution)/shard_map/ppermute | solution.py:1309
  620.2 128.6 %collective-permute-start.4 = (bf16[512,2048]{1,0:T(8,128)(2,1)}, bf16[512,2048]{1,0:T(8,128)(2,1)}, u32[]{:S(2)}, u32[]{:S(2)}) collective-permute-start(bf16[512,2048]{1,0:T(8,128)(2,1)} %pad_maximum_fusion.1), channel_id=1, source_target_pairs={{0,16},{4,20},{8,24},{12,28},{16,0},{20,4},{24,8},{28,12},{1,17},{... | collective-permute-start | bytes 6291464 | tf_op jit(solution)/shard_map/ppermute | solution.py:1309
  722.0 5.8 copy-start.22
  722.0 5.7 copy-start.21
  727.8 8.3 copy-start.4
  727.8 8.3 copy-start.13
  727.8 8.3 copy-start.18
  860.9 6.4 copy-start.2
  867.3 5.9 copy-start.9
  867.3 6.7 copy-start.8
Sparse Core Ops, SparseCore 0:
  58.7 97.5 all-gather.3
  157.8 94.0 all-gather.5
  253.5 78.9 all-gather.7
  395.3 79.1 reduce-scatter.4
  476.7 77.2 reduce-scatter.6
  556.2 77.2 reduce-scatter.8
  637.3 98.6 reduce-scatter.10

commit v8 on v7

--- a/solution.py
+++ b/solution.py
@@ -159,7 +159,7 @@
     heads = kv.shape[1] // LANES
     per_head = pairs // heads
     span = reach + QTILE
-    right = (grads.shape[0], grads.shape[1] // 2)
+    right = (grads.shape[0], grads.shape[1] * 5 // 8)
     far = pl.BlockSpec(memory_space=pl.ANY)
     return pl.pallas_call(
         functools.partial(attend_kernel, reach, 2 * math.isqrt(dp_size // GROUP)),
@@ -737,7 +737,7 @@
     whole = [(GROUP * w.shape[0], w.shape[1]) for w in weights]
     keys = (reach + rows, wkv.shape[1])
     grads = (GROUP * grad.shape[0], grad.shape[1])
-    left = (grads[0], grads[1] // 2)
+    left = (grads[0], grads[1] * 3 // 8)
     return pl.pallas_call(
         functools.partial(project_kernel, 2 * math.isqrt(dp_size // GROUP), z_size),
         in_specs=[near] * 3 + [far] * 4,
@@ -794,9 +794,8 @@
         half = (first + last) * (i % 2) + high * (1 - low)
         dx = middle * (1 - i % 2) + last
         dy = middle * (i % 2) + last
-        chip = 2 * ((ring.row + dy) % 2) + (ring.col + dx) % 2
         part = rows // 2
-        chip_rows = pl.ds(pl.multiple_of(chip * rows + half * part, part), part)
+        chip_rows = pl.ds(pl.multiple_of((2 * dy + dx) * rows + half * part, part), part)
         return ring.place(dy, dx, i // 2, half), i // 2, chip_rows
 
     @pl.loop(0, 16)
@@ -1074,19 +1073,35 @@
 
 
 def tail_kernel(
-    wide, z_size, mlp_count, x_ref, dq_ref, dkv_ref, wo_ref, gain_ref, *refs
+    wide, z_size, mlp_count, x_ref, dq_ref, dkv_ref, wo_ref, scale_ref, gain_ref,
+    raw_ref, dh_ref, wq_ref, wkv_ref, *refs
 ):
     mlp_ins, refs = refs[:mlp_count], refs[mlp_count:]
-    wq_out, wkv_out, wo_out, gain_out = refs[:4]
-    mlp_outs, scratch = refs[4 : 4 + mlp_count], refs[4 + mlp_count :]
+    wq_out, wkv_out, wo_out, gain_out, grad_out = refs[:5]
+    mlp_outs, scratch = refs[5 : 5 + mlp_count], refs[5 + mlp_count :]
     own_scratch = scratch[:12]
     sums, zrecv, gain_z, gain_p, z_send, z_recv, g_send, g_recv = scratch[12:20]
-    wo_recv, w_send, w_recv, m_own, m_send, m_recv = scratch[20:]
+    wo_recv, w_send, w_recv, m_own, m_send, m_recv = scratch[20:26]
+    wq_all, wkv_all, raw, dh, dxn, gain_sum, load_sem = scratch[26:]
     rings = [Reduce(wide, *own_scratch[6 * at : 6 * at + 6]) for at in range(2)]
     place = lax.axis_index("tensor")
     mine, found = others(wide)
     along = along_peers(place, z_size)
     around = [device for _, device in found]
+
+    tiles, tile_rows = raw.shape[0], raw.shape[1]
+    loads = [
+        pltpu.make_async_copy(wq_ref, wq_all, load_sem.at[0]),
+        pltpu.make_async_copy(wkv_ref, wkv_all, load_sem.at[1]),
+    ]
+    for tile in range(tiles):
+        here = pl.ds(tile * tile_rows, tile_rows)
+        loads += [
+            pltpu.make_async_copy(raw_ref.at[here], raw.at[tile], load_sem.at[2 + 2 * tile]),
+            pltpu.make_async_copy(dh_ref.at[here], dh.at[tile], load_sem.at[3 + 2 * tile]),
+        ]
+    for copy in loads:
+        copy.start()
     greet(along + around)
 
     mlp_copies = send_home(wide, mlp_ins, mlp_outs, m_own, m_send, m_recv)
@@ -1105,56 +1120,52 @@
     for copy in wo_copies:
         copy.start()
 
-    gain_z[place] = gain_ref[...]
-    gain_copies = [
-        pltpu.make_async_remote_copy(
-            src_ref=gain_ref, dst_ref=gain_z.at[place], send_sem=g_send.at[at],
-            recv_sem=g_recv.at[at], device_id=peer, device_id_type=MESH,
-        )
-        for at, peer in enumerate(along)
-    ]
-    for copy in gain_copies:
-        copy.start()
-
     rights = (dq_ref, dkv_ref)
     rows = sums.shape[0]
     outs = (wq_out, wkv_out)
+    starts = [0, rights[0].shape[1]]
     z_copies = []
-    for index, ring in enumerate(rings):
-        right = rights[index]
-        cols = right.shape[1]
+
+    def partial_sums(index):
+        ring, right = rings[index], rights[index]
 
         @pl.loop(0, 8)
         def _(step):
             chunk, target = ring.chunk(step)
             x = x_ref[:, pl.ds(pl.multiple_of(chunk * rows, rows), rows)].T
 
-            @pl.loop(0, cols // NTILE)
+            @pl.loop(0, right.shape[1] // NTILE)
             def _(at):
                 n = pl.ds(pl.multiple_of(at * NTILE, NTILE), NTILE)
                 target[:, n] = dot_nn(x, right[:, n]).astype(BF16)
 
             ring.after(step)
 
-        if index == 0:
-            for copy in mlp_copies:
-                copy.start()
-            for copy in gain_copies:
-                copy.wait_recv()
-            total = gain_z[0]
-            for at in range(1, z_size):
-                total = total + gain_z[at]
-            gain_p[mine] = total
-            for at, peer in enumerate(around):
-                copy = pltpu.make_async_remote_copy(
-                    src_ref=gain_p.at[mine], dst_ref=gain_p.at[mine],
-                    send_sem=g_send.at[z_size - 1 + at], recv_sem=g_recv.at[z_size - 1 + at],
-                    device_id=peer, device_id_type=MESH,
-                )
-                gain_copies.append(copy)
-                copy.start()
-
-    def send_along(index, ring, start):
+    gain_sum[...] = jnp.zeros_like(gain_sum)
+
+    def input_rows(tile):
+        part = pl.ds(tile * tile_rows, tile_rows)
+        dq, dkv = dq_ref[part, :], dkv_ref[part, :]
+
+        @pl.loop(0, dxn.shape[1] // NTILE)
+        def _(at):
+            n = pl.ds(pl.multiple_of(at * NTILE, NTILE), NTILE)
+            dxn[:, n] = dot_nt(dq, wq_all[n, :]) + dot_nt(dkv, wkv_all[n, :])
+
+        @pl.loop(0, tile_rows // STRIP)
+        def _(at):
+            here = pl.ds(pl.multiple_of(at * STRIP, STRIP), STRIP)
+            there = pl.ds(pl.multiple_of(tile * tile_rows + at * STRIP, STRIP), STRIP)
+            grad, value = dxn[here, :], raw[tile, here, :].astype(F32)
+            scale = scale_ref[there, :]
+            gained = grad * gain_ref[0:1, :]
+            inner = jnp.mean(gained * value, axis=1, keepdims=True)
+            gain_sum[...] += grad * value * scale
+            total = scale * gained - value * (scale * scale * scale * inner)
+            grad_out[there, :] = (dh[tile, here, :] + total).astype(BF16)
+
+    def send_along(index):
+        ring, start = rings[index], starts[index]
         cols = rights[index].shape[1]
         part = cols // z_size
 
@@ -1173,12 +1184,52 @@
             z_copies.append(copy)
             copy.start()
 
-    starts = [0, rights[0].shape[1]]
-    for index, ring in enumerate(rings):
-        ring.pass_on()
-        if index:
-            send_along(index - 1, rings[index - 1], starts[index - 1])
-    send_along(1, rings[1], starts[1])
+    partial_sums(0)
+    for copy in loads:
+        copy.wait()
+    input_rows(0)
+    rings[0].pass_on()
+    partial_sums(1)
+    for tile in range(1, tiles):
+        input_rows(tile)
+
+    gain_z[place, 0:1] = jnp.sum(gain_sum[...], axis=0, keepdims=True)
+    gain_z[place, 1:2] = gain_ref[1:2, :]
+    gain_copies = [
+        pltpu.make_async_remote_copy(
+            src_ref=gain_z.at[place], dst_ref=gain_z.at[place], send_sem=g_send.at[at],
+            recv_sem=g_recv.at[at], device_id=peer, device_id_type=MESH,
+        )
+        for at, peer in enumerate(along)
+    ]
+    for copy in gain_copies:
+        copy.start()
+    rings[1].pass_on()
+    for copy in mlp_copies:
+        copy.start()
+    send_along(0)
+
+    for copy in gain_copies:
+        copy.wait_recv()
+    total = gain_z[0]
+    for at in range(1, z_size):
+        total = total + gain_z[at]
+    gain_p[mine] = total
+    for at, peer in enumerate(around):
+        copy = pltpu.make_async_remote_copy(
+            src_ref=gain_p.at[mine], dst_ref=gain_p.at[mine],
+            send_sem=g_send.at[z_size - 1 + at], recv_sem=g_recv.at[z_size - 1 + at],
+            device_id=peer, device_id_type=MESH,
+        )
+        gain_copies.append(copy)
+        copy.start()
+    for copy in wo_copies:
+        copy.wait()
+    total = wo_ref[:, pl.ds(pl.multiple_of(place * wo_part, LANES), wo_part)].astype(F32)
+    for at in range(z_size - 1):
+        total += wo_recv[at].astype(F32)
+    wo_out[...] = total
+    send_along(1)
 
     for copy in gain_copies[z_size - 1 :]:
         copy.wait_recv()
@@ -1186,14 +1237,6 @@
     for at in range(1, GROUP):
         total = total + gain_p[at]
     gain_out[...] = total
-
-    for copy in wo_copies:
-        copy.wait()
-    total = wo_ref[:, pl.ds(pl.multiple_of(place * wo_part, LANES), wo_part)].astype(F32)
-    for at in range(z_size - 1):
-        total += wo_recv[at].astype(F32)
-    wo_out[...] = total
-
     for copy in z_copies:
         copy.wait_recv()
     for index in range(2):
@@ -1211,9 +1254,10 @@
         copy.wait()
 
 
-def last_grads(x, dq, dkv, wo_sum, gains, mlp, dp_size, z_size):
+def last_grads(x, dq, dkv, wo_sum, scale, gains, raw, dh, wq, wkv, mlp, dp_size, z_size):
     tokens, width = x.shape
     rows = width // GROUP
+    tiles = tokens // QTILE
     near = pl.BlockSpec(memory_space=pltpu.VMEM)
     far = pl.BlockSpec(memory_space=pl.ANY)
     sizes = [dq.shape[1], dkv.shape[1]]
@@ -1223,11 +1267,14 @@
     total = sum(sizes)
     return pl.pallas_call(
         functools.partial(tail_kernel, 2 * math.isqrt(dp_size // GROUP), z_size, len(mlp)),
-        in_specs=[near] * 5 + [far] * len(mlp),
-        out_specs=[near] * 4 + [far] * len(mlp),
+        in_specs=[near] * 6 + [far] * (4 + len(mlp)),
+        out_specs=[near] * 5 + [far] * len(mlp),
         out_shape=[jax.ShapeDtypeStruct((rows, cols // z_size), F32) for cols in sizes]
-        + [jax.ShapeDtypeStruct((rows, wo_sum.shape[1] // z_size), F32)]
-        + [jax.ShapeDtypeStruct(gains.shape, F32)]
+        + [
+            jax.ShapeDtypeStruct((rows, wo_sum.shape[1] // z_size), F32),
+            jax.ShapeDtypeStruct(gains.shape, F32),
+            jax.ShapeDtypeStruct((tokens, width), BF16),
+        ]
         + home_shapes(mlp),
         scratch_shapes=scratch
         + [
@@ -1243,14 +1290,21 @@
             pltpu.SemaphoreType.DMA((z_size - 1,)),
             pltpu.SemaphoreType.DMA((z_size - 1,)),
         ]
-        + home_scratch(mlp),
+        + home_scratch(mlp)
+        + [
+            pltpu.VMEM(wq.shape, BF16),
+            pltpu.VMEM(wkv.shape, BF16),
+            pltpu.VMEM((tiles, QTILE, width), BF16),
+            pltpu.VMEM((tiles, QTILE, width), F32),
+            pltpu.VMEM((QTILE, width), F32),
+            pltpu.VMEM((STRIP, width), F32),
+            pltpu.SemaphoreType.DMA((2 + 2 * tiles,)),
+        ],
         compiler_params=pltpu.CompilerParams(
-            collective_id=4, has_side_effects=True, vmem_limit_bytes=60 << 20
+            collective_id=4, has_side_effects=True, vmem_limit_bytes=62 << 20
         ),
-        cost_estimate=pl.CostEstimate(
-            flops=2 * LONG, bytes_accessed=4 * tokens * total, transcendentals=0
-        ),
-    )(x, dq, dkv, wo_sum, gains, *mlp)
+        cost_estimate=pl.CostEstimate(flops=SHORT, bytes_accessed=0, transcendentals=0),
+    )(x, dq, dkv, wo_sum, scale, gains, raw, dh, wq, wkv, *mlp)
 
 
 class Layout:
@@ -1380,42 +1434,40 @@
 
     r2 = rms_scale(h)
     hn, gate, up, hidden, by_core = gate_up((h * r2 * mlp_gain).astype(BF16), wg, wu, dp_size)
-    row, col, core = neighbours(2 * layout.cols)[0]
-    def chunk(array, y, x):
-        return lax.dynamic_index_in_dim(array, 2 * y + x, 0, False)
-
+    part = rows // 2
     away = dot_nt(by_core[1], wd).astype(BF16)
     dy, away = lax.optimization_barrier((dy, away))
     total_wd = dot_tn(dy, hidden).astype(BF16)
-    near_sum = dot_nt(by_core[0], wd) + layout.swap(away, 1).astype(F32)
-    near_sum = near_sum.astype(BF16)
     part_wd = along_z(total_wd)
-    dy, near_sum = lax.optimization_barrier((dy, near_sum))
-    near_sum = near_sum.reshape(GROUP // 2, rows, width)
-    far_chunk = chunk(near_sum, 1 - row, 1 - col)
-    from_x = layout.swap(far_chunk[rows // 2 :], 2)
-    from_y = layout.swap(far_chunk[: rows // 2], 4)
+    from_core = layout.swap(away, 1)
+
+    def out_rows(start, count, *more):
+        some = slice(start * part, (start + count) * part)
+        total = dot_nt(by_core[0, some], wd) + from_core[some].astype(F32)
+        for other in more:
+            total = total + other.astype(F32)
+        return total.astype(BF16)
+
+    far_y, far_x = out_rows(6, 1), out_rows(7, 1)
+    dy, far_x, far_y = lax.optimization_barrier((dy, far_x, far_y))
+    from_x, from_y = layout.swap(far_x, 2), layout.swap(far_y, 4)
     gate, up = gate.astype(F32), up.astype(F32)
     sigma = jax.nn.sigmoid(gate)
     dhid = dot_nn(dy, wd)
     dgate = (dhid * up * sigma * (1.0 + gate * (1.0 - sigma))).astype(BF16)
     dup = (dhid * gate * sigma).astype(BF16)
-    x_chunk = chunk(near_sum, row, 1 - col)
-    y_chunk = chunk(near_sum, 1 - row, col)
-    x_upper = (x_chunk[: rows // 2].astype(F32) + from_y.astype(F32)).astype(BF16)
-    y_lower = (y_chunk[rows // 2 :].astype(F32) + from_x.astype(F32)).astype(BF16)
-    x_chunk = jnp.concatenate([x_upper, x_chunk[rows // 2 :]], axis=0)
-    y_chunk = jnp.concatenate([y_chunk[: rows // 2], y_lower], axis=0)
+    dgate, dup, from_x, from_y = lax.optimization_barrier((dgate, dup, from_x, from_y))
+    pieces = (out_rows(2, 1, from_y), out_rows(3, 1), out_rows(4, 1), out_rows(5, 1, from_x))
+    dgate, dup, *pieces = lax.optimization_barrier((dgate, dup, *pieces))
     total_wg = dot_tn(hn, dgate).astype(BF16)
     dup, total_wg = lax.optimization_barrier((dup, total_wg))
     part_wg = along_z(total_wg)
     total_wu = dot_tn(hn, dup).astype(BF16)
     dup, total_wu = lax.optimization_barrier((dup, total_wu))
     part_wu = along_z(total_wu)
-    dup, x_chunk, y_chunk = lax.optimization_barrier((dup, x_chunk, y_chunk))
     dhn = hidden_back(dgate, dup, wg, wu, dp_size)
-    dhn, part_wd, x_chunk, y_chunk = lax.optimization_barrier((dhn, part_wd, x_chunk, y_chunk))
-    from_x, from_y = layout.swap(x_chunk, 2), layout.swap(y_chunk, 4)
+    dhn, part_wd, *pieces = lax.optimization_barrier((dhn, part_wd, *pieces))
+    pieces = [layout.swap(piece, flip) for piece, flip in zip(pieces, (2, 2, 4, 4))]
     gain_two, dh_norm = norm_back(h, r2, mlp_gain, dhn)
     dh = cotangent[0].astype(F32) + dh_norm
     dhb = dh.astype(BF16)
@@ -1428,16 +1480,15 @@
     )
     dq, part_wu = lax.optimization_barrier((dq, part_wu))
     dq, part_wo = lax.optimization_barrier((dq, part_wo))
-    dxn = dot_nt(dq, wq) + dot_nt(dkv, wkv)
-    gain_one, dx_norm = norm_back(x, r1, attn_gain, dxn)
-    input_grad = (dh + dx_norm).astype(BF16)
-    gains = layout.sum_outer(jnp.stack([gain_one, gain_two]))
-    gains, from_x, from_y = lax.optimization_barrier((gains, from_x, from_y))
-    output = h + chunk(near_sum, row, col).astype(F32)
-    output = output + from_x.astype(F32) + from_y.astype(F32)
-    wq_grad, wkv_grad, wo_grad, gains, wu_grad = last_grads(
-        layout.from_cols(xn), dq, dkv, part_wo, gains, (part_wu,), dp_size, z_size
+    wq_grad, wkv_grad, wo_grad, gains, input_grad, wu_grad = last_grads(
+        layout.from_cols(xn), dq, dkv, part_wo, r1, jnp.stack([attn_gain, gain_two]),
+        activations[0], dh, wq, wkv, (part_wu,), dp_size, z_size,
     )
+    gains = layout.sum_outer(gains)
+    gains, *pieces = lax.optimization_barrier((gains, *pieces))
+    output = h + out_rows(0, 2).astype(F32)
+    output = output + jnp.concatenate(pieces[:2]).astype(F32)
+    output = output + jnp.concatenate(pieces[2:]).astype(F32)
     wo_grad, wq_grad, wkv_grad, wd_grad, wg_grad, wu_grad = (
         layout.scatter_outer(grad).astype(F32)
         for grad in (wo_grad, wq_grad, wkv_grad, wd_grad, wg_grad, wu_grad)

time: 891 us -> 864 us (0.970)
  other arithmetic: 42.4 us -> 27.7 us
  Pallas kernels: 627 us -> 615 us
    pallas_call x1, Pallas kernels: 106 us -> 89.3 us  [last_grads(): pl.pallas_call(functools.partial(tail_kernel, 2 * math.isqrt(dp_size // G...]
    broadcast_in_dim x2 -> x0, other arithmetic: 12.3 us -> none  [the longest x1 6.42 us: per_device(): input_grad[None]]
    pallas_call x1, Pallas kernels: 131 us -> 121 us  [project(): pl.pallas_call(functools.partial(project_kernel, 2 * math.isqrt(dp_size /...]
    pallas_call x1, Pallas kernels: 101 us -> 110 us  [attend_back(): pl.pallas_call(functools.partial(attend_back_kernel, reach, 2 * math.isqr...]
    dot_general x5 -> x9, matrix products: 54.6 us -> 53.2 us  [dot_nt(): lax.dot_general(left, right, (((1,), (1,)), ((), ())), preferred_element_...]
  transfers between devices with their start and end apart: 12 -> 14, of which waited for: 3 -> 1; matrix products, arithmetic and copies ran while one was open for 21% -> 20% of each run, Pallas kernels for 53% -> 66%
where the time goes in v8:
time: 864 us; the launch traced here: 855 us
  Pallas kernels  615 us (71%)
  matrix products  173 us (20%)
  other arithmetic  27.7 us (3%)
  between operations  15 us (2%)
  local copies, waits for them, and re-layouts  11 us (1%)
    pallas_call x1, Pallas kernels, project(): pl.pallas_call(functools.partial(project_kernel, 2 * math.isqrt(dp_size /...  121 us
    pallas_call x1, Pallas kernels, attend_back(): pl.pallas_call(functools.partial(attend_back_kernel, reach, 2 * math.isqr...  110 us
    pallas_call x1, Pallas kernels, hidden_back(): pl.pallas_call(functools.partial(hidden_back_kernel, 2 * math.isqrt(dp_si...  89.8 us
    pallas_call x1, Pallas kernels, last_grads(): pl.pallas_call(functools.partial(tail_kernel, 2 * math.isqrt(dp_size // G...  89.3 us
    pallas_call x1, Pallas kernels, gate_up(): pl.pallas_call(functools.partial(gate_up_kernel, 2 * math.isqrt(dp_size /...  87.3 us
    dot_general x4, matrix products, dot_tn(): lax.dot_general(left, right, (((0,), (0,)), ((), ())), preferred_element_...  73.6 us
    pallas_call x1, Pallas kernels, attend(): pl.pallas_call(functools.partial(attend_kernel, reach, 2 * math.isqrt(dp_...  67.6 us
    dot_general x9, matrix products, dot_nt(): lax.dot_general(left, right, (((1,), (1,)), ((), ())), preferred_element_...  53.2 us
  transfers between devices with their start and end apart: 14, of which 1 were waited for; matrix products, arithmetic and copies ran while one was open for 20% of the time, Pallas kernels for 66%

profile of v8, /device:TPU:0, one launch (start us, length us, event | category | flops | bytes accessed | tf_op | source)
XLA Modules:
  0.0 855.1 jit_solution(10351295053719887672)
XLA Ops:
  7.2 0.0 all-gather.4.cloned.1.call-start
  7.2 1.5 pad_maximum_fusion.2.refs_3_
  8.8 49.8 %shard_map.203 = (bf16[2048,256]{1,0:T(8,128)(2,1)}, bf16[2048,256]{1,0:T(8,128)(2,1)}, bf16[2048,256]{1,0:T(8,128)(2,1)}, bf16[256,1024]{1,0:T(8,128)(2,1)}, bf...) custom-call(bf16[256,2048]{1,0:T(8,128)(2,1)} %refs_0_.1, bf16[256,2048]{1,0:T(8,128)(2,1)} %refs_1_.1, ...), custom_call_target="tpu_custom_call" | custom-call | flops 60000002048 | tf_op jit(solution)/shard_map/pallas_call | solution.py:527
  58.6 0.0 all-gather.6.cloned.1.call-start
  58.7 0.7 all-gather.6.cloned.1.call-update
  59.4 0.0 all-gather.8.cloned.1.call-start
  59.4 0.7 all-gather.8.cloned.1.call-update
  60.1 0.0 reduce-scatter.5.cloned.1.call-start
  60.2 0.1 convert_reduce_fusion
  60.3 0.1 select_reduce_fusion
  60.4 0.5 fusion.8
  60.9 0.7 subtract_add_fusion.1
  61.6 1.0 fusion.47
  62.6 1.9 fusion.10.x_ref
  64.5 1.3 pad_maximum_fusion
  65.7 121.2 %shard_map.204 = (bf16[512,2048]{1,0:T(8,128)(2,1)}, bf16[1536,1024]{1,0:T(8,128)(2,1)}, bf16[2048,1024]{1,0:T(8,128)(2,1)}, bf16[2048,2048]{1,0:T(8,128)(2,1)},...) custom-call(bf16[512,2048]{1,0:T(8,128)(2,1)} %fusion.10.x_ref, f32[512,128]{1,0:T(8,128)} %get-tuple-element.162.cos_ref.cos_all, ...), custom_call_target="tpu_custom_call" | custom-call | flops 120000004096 | bytes 41943040 | tf_op jit(solution)/shard_map/pallas_call | solution.py:741
  187.0 67.6 %shard_map.205 = (bf16[512,2048]{1,0:T(8,128)(2,1)}, f32[32,1,512]{2,1,0:T(1,128)}, bf16[4096,2048]{1,0:T(8,128)(2,1)}) custom-call(bf16[512,2048]{1,0:T(8,128)(2,1)} %get-tuple-element.81.q_ref, bf16[1536,1024]{1,0:T(8,128)(2,1)} %get-tuple-element.82.k_ref.v_ref, ...), custom_call_target="tpu_custom_call", output_to_operand_aliasing={{2}: (5, {})} | custom-call | flops 21474836480 | bytes 7340032 | tf_op jit(solution)/shard_map/pallas_call | solution.py:164
  254.5 7.8 multiply_reduce_fusion.2
  262.4 2.0 copy-done
  264.5 1.7 multiply_convert_fusion.own_ref
  266.2 87.3 %shard_map.206 = (bf16[4096,2048]{1,0:T(8,128)(2,1)}, bf16[4096,1024]{1,0:T(8,128)(2,1)}, bf16[4096,1024]{1,0:T(8,128)(2,1)}, bf16[4096,1024]{1,0:T(8,128)(2,1)}, bf16[2,2048,1024]{2,1,0:T(8,128)(2,1)}) custom-call(bf16[512,2048]{1,0:T(8,128)(2,1)} %multiply_convert_fusion.own_ref, bf16[2048,1024]{1,0:T(8,128)(2,1)} %all-gather.4.cloned.1.call-done.wg_ref, ...), custom_call_target="tpu_custom_call" | custom-call | flops 1000000 | tf_op jit(solution)/shard_map/pallas_call | solution.py:855
  353.5 0.0 all-gather.8.cloned.1.call-done
  353.5 14.4 %convolution_convert_fusion.1 = bf16[2048,2048]{1,0:T(8,128)(2,1)} fusion(bf16[2048,1024]{1,0:T(8,128)(2,1)} %all-gather.8.cloned.1.call-done, bf16[2,2048,1024]{2,1,0:T(8,128)(2,1)} %get-tuple-element.88), kind=kOutput, calls=%fused_computation.12 | convolution fusion | flops 8594128896 | bytes 16777216 | tf_op jit(solution)/shard_map/dot_general | solution.py:36
  367.9 21.5 %convolution_convert_fusion.2 = bf16[2048,1024]{1,0:T(8,128)(2,1)} fusion(bf16[4096,2048]{1,0:T(8,128)(2,1)} %get-tuple-element.93, bf16[4096,1024]{1,0:T(8,128)(2,1)S(1)} %copy-done.18), kind=kOutput, calls=%fused_computation.28 | convolution fusion | flops 17181966336 | bytes 29360128 | tf_op jit(solution)/shard_map/dot_general | solution.py:40
  389.4 0.0 reduce-scatter.7.cloned.1.call-start
  389.4 3.8 fusion.21
  393.2 2.4 fusion.31
  395.6 3.7 add_convert_fusion.6
  399.3 3.7 add_convert_fusion.7
  403.0 1.2 collective-permute-start.1
  404.3 0.1 collective-permute-start.2
  404.3 35.4 %fusion.7 = (bf16[4096,1024]{1,0:T(8,128)(2,1)}, bf16[4096,1024]{1,0:T(8,128)(2,1)}) fusion(bf16[4096,1024]{1,0:T(8,128)(2,1)} %get-tuple-element.95, bf16[4096,1024]{1,0:T(8,128)(2,1)} %get-tuple-element.94, bf16[4096,2048]{1,0:T(8,128)(2,1)} %get-tuple-element.93, bf16[2048,1024]{1,0:T(8,128)(2,1)S(1)} %copy-done.19), kind=kOutput, calls=%fused_computation.10 | convolution fusion | flops 17242783744 | bytes 54525952 | tf_op jit(solution)/shard_map/dot_general | solution.py:32
  439.8 3.7 add_convert_fusion.3
  443.5 3.9 add_convert_fusion.4
  447.3 3.8 add_convert_fusion.2
  451.2 21.5 %convolution_convert_fusion.4 = bf16[2048,1024]{1,0:T(8,128)(2,1)} fusion(bf16[4096,2048]{1,0:T(8,128)(2,1)} %get-tuple-element.104, bf16[4096,1024]{1,0:T(8,128)(2,1)S(1)} %bitcast.84), kind=kOutput, calls=%fused_computation.30 | convolution fusion | flops 17181966336 | bytes 29360128 | tf_op jit(solution)/shard_map/dot_general | solution.py:40
  472.7 0.0 reduce-scatter.9.cloned.1.call-start
  472.7 23.7 %convolution_convert_fusion.3 = bf16[2048,1024]{1,0:T(8,128)(2,1)} fusion(bf16[4096,2048]{1,0:T(8,128)(2,1)} %get-tuple-element.104, bf16[4096,1024]{1,0:T(8,128)(2,1)} %get-tuple-element.106.dup_ref), kind=kOutput, calls=%fused_computation.29 | convolution fusion | flops 17181966336 | bytes 29360128 | tf_op jit(solution)/shard_map/dot_general | solution.py:40
  496.5 0.0 reduce-scatter.11.cloned.1.call-start
  496.6 89.8 %shard_map.207 = f32[512,2048]{1,0:T(8,128)} custom-call(bf16[4096,1024]{1,0:T(8,128)(2,1)} %get-tuple-element.102.dgate_ref, bf16[4096,1024]{1,0:T(8,128)(2,1)} %get-tuple-element.106.dup_ref, bf16[2048,1024]{1,0:T(8,128)(2,1)} %all-gather.4.cloned.1.call-done.wg_ref, bf16[2048,1024]{1,0:T(8,128)(2,1)} %all-gather.6.cloned.1.call-done.wu_ref), custom_call_target="tpu_custom_call" | custom-call | flops 34359738368 | bytes 29360128 | tf_op jit(solution)/shard_map/pallas_call | solution.py:1054
  586.4 4.7 multiply_reduce_fusion
  591.1 1.3 copy-done.3
  592.4 1.4 subtract_add_fusion.dh_ref
  593.8 10.6 %convolution_convert_fusion.5.do_ref = bf16[512,2048]{1,0:T(8,128)(2,1)} fusion(bf16[2048,2048]{1,0:T(8,128)(2,1)} %get-tuple-element.85, f32[512,2048]{1,0:T(8,128)S(1)} %subtract_add_fusion.dh_ref), kind=kOutput, calls=%fused_computation.31 | convolution fusion | flops 4297064448 | bytes 14680064 | tf_op jit(solution)/shard_map/dot_general | solution.py:32
  604.4 6.9 convolution_convert_fusion
  611.4 0.7 copy-done.17
  612.0 0.9 copy.27.scale_ref
  612.9 0.7 collective-permute-start.3
  613.6 1.3 collective-permute-start.4
  614.9 0.7 collective-permute-start.5
  615.6 1.3 collective-permute-start.6
  617.0 0.6 pad_maximum_fusion.3.gain_ref
  617.6 109.9 %shard_map.208 = (bf16[512,2048]{1,0:T(8,128)(2,1)}, bf16[512,1024]{1,0:T(8,128)(2,1)}, bf16[256,2048]{1,0:T(8,128)(2,1)}, bf16[256,2048]{1,0:T(8,128)(2,1)}) custom-call(bf16[512,2048]{1,0:T(8,128)(2,1)} %get-tuple-element.81.q_ref, bf16[512,2048]{1,0:T(8,128)(2,1)} %convolution_convert_fusion.5.do_ref, bf16[512,2048]{1,0:T(8,128)(2,1)} %get-tuple-element.84.o_ref, ...), custom_call_target="tpu_custom_call" | custom-call | flops 53687091200 | bytes 14680064 | tf_op jit(solution)/shard_map/pallas_call | solution.py:319
  727.5 2.8 convert_element_type.158
  730.3 2.8 convert_element_type.160
  733.1 6.7 reduce-scatter.11.cloned.1.call-done.wo_ref
  739.8 89.3 %shard_map.209 = (f32[256,512]{1,0:T(8,128)}, f32[256,256]{1,0:T(8,128)}, f32[256,512]{1,0:T(8,128)}, f32[2,2048]{1,0:T(2,128)}, bf16[512,2048]{1,0:T(8,128)(2,1)}, /*index=5*/bf16[256,2048]{1,0:T(8,128)(2,1)}) custom-call(bf16[512,2048]{1,0:T(8,128)(2,1)} %fusion.10.x_ref, bf16[512,2048]{1,0:T(8,128)(2,1)} %get-tuple-element.122.dq_ref, ...), custom_call_target="tpu_custom_call" | custom-call | flops 1000000 | tf_op jit(solution)/shard_map/pallas_call | solution.py:1268
  829.1 1.4 fusion.49
  830.5 2.8 convert_element_type.159
  833.3 1.7 fusion.48
  835.0 9.9 %fusion.13 = bf16[1,512,2048]{2,1,0:T(8,128)(2,1)} fusion(f32[512,2048]{1,0:T(8,128)} %copy-done, bf16[2048,2048]{1,0:T(8,128)(2,1)} %collective-permute-done, bf16[256,2048]{1,0:T(8,128)(2,1)} %collective-permute-done.4, bf16[256,2048]{1,0:T(8,128)(2,1)} %collective-permute-done.3, bf16[256,2048]{1,0:T(8,128)(2,1)} %collective-permute-done.6, ...), kind=kOutput, calls=%fused_computation.32 | convolution fusion | flops 2164260864 | bytes 17825792 | tf_op jit(solution)/shard_map/dot_general | solution.py:36
  844.9 1.3 copy.32
  846.3 0.8 copy.33
  847.1 0.8 copy.34
  (66 shorter events, 0.3 us)
Async XLA Ops:
  7.2 259.0 %all-gather.4.cloned.1.call-start = ((), (), s32[]{:S(2)}) async-start(), calls=%async_computation.4 | async-start | bytes 5242880 | tf_op jit(solution)/shard_map/all_gather | solution.py:1416
  8.8 51.4 %copy-start.13 = (s32[1,2048]{1,0:T(1,128)S(1)}, s32[1,2048]{1,0:T(1,128)}, u32[]{:S(2)}) copy-start(s32[1,2048]{1,0:T(1,128)} %param.13) | copy-start | bytes 24580
  58.6 1.8 copy-start.2
  58.6 4.0 copy-start.11
  58.6 207.6 %all-gather.6.cloned.1.call-start = ((), (), s32[]{:S(2)}) async-start(), calls=%async_computation.5 | async-start | bytes 5242880 | tf_op jit(solution)/shard_map/all_gather | solution.py:1416
  59.4 294.1 %all-gather.8.cloned.1.call-start = ((), (), s32[]{:S(2)}) async-start(), calls=%async_computation.6 | async-start | bytes 5242880 | tf_op jit(solution)/shard_map/all_gather | solution.py:1416
  60.1 526.3 %reduce-scatter.5.cloned.1.call-start = ((), (), s32[]{:S(2)}) async-start(), calls=%async_computation.7 | async-start | bytes 5242880 | tf_op jit(solution)/shard_map/reduce_scatter | solution.py:1421
  60.9 126.1 %copy-start.16 = (f32[512]{0:T(512)}, f32[512]{0:T(512)S(1)}, u32[]{:S(2)}) copy-start(f32[512]{0:T(512)S(1)} %add_rsqrt_fusion.1) | copy-start | bytes 6148
  254.5 9.9 %copy-start.9 = (f32[2048]{0:T(1024)S(1)}, f32[2048]{0:T(1024)}, u32[]{:S(2)}) copy-start(f32[2048]{0:T(1024)} %param.19) | copy-start | bytes 24580
  262.4 2.1 copy-start
  262.4 2.1 copy-start.14
  353.5 14.4 %copy-start.18 = (bf16[4096,1024]{1,0:T(8,128)(2,1)S(1)}, bf16[4096,1024]{1,0:T(8,128)(2,1)}, u32[]{:S(2)}) copy-start(bf16[4096,1024]{1,0:T(8,128)(2,1)} %get-tuple-element.107) | copy-start | bytes 25165828
  367.9 27.8 %collective-permute-start = (bf16[2048,2048]{1,0:T(8,128)(2,1)}, bf16[2048,2048]{1,0:T(8,128)(2,1)}, u32[]{:S(2)}, u32[]{:S(2)}) collective-permute-start(bf16[2048,2048]{1,0:T(8,128)(2,1)} %convolution_convert_fusion.1), channel_id=1, source_target_pairs={{0,4},{4,0},{8,12},{12,8},{16,20},{20,16},{24,28},{28,24},{1,5},{5... | collective-permute-start | bytes 25165832 | tf_op jit(solution)/shard_map/ppermute | solution.py:1363
  389.4 221.9 %reduce-scatter.7.cloned.1.call-start = ((), (), s32[]{:S(2)}) async-start(), calls=%async_computation.8 | async-start | bytes 5242880 | tf_op jit(solution)/shard_map/reduce_scatter | solution.py:1421
  389.4 3.8 copy-start.19
  403.0 44.3 %collective-permute-start.1 = (bf16[256,2048]{1,0:T(8,128)(2,1)}, bf16[256,2048]{1,0:T(8,128)(2,1)S(1)}, u32[]{:S(2)}, u32[]{:S(2)}) collective-permute-start(bf16[256,2048]{1,0:T(8,128)(2,1)} %add_convert_fusion.7), channel_id=1, source_target_pairs={{0,8},{4,12},{8,0},{12,4},{16,24},{20,28},{24,16},{28,20},{1,9},{5... | collective-permute-start | bytes 3145736 | tf_op jit(solution)/shard_map/ppermute | solution.py:1363
  404.3 43.1 %collective-permute-start.2 = (bf16[256,2048]{1,0:T(8,128)(2,1)}, bf16[256,2048]{1,0:T(8,128)(2,1)S(1)}, u32[]{:S(2)}, u32[]{:S(2)}) collective-permute-start(bf16[256,2048]{1,0:T(8,128)(2,1)} %add_convert_fusion.6), channel_id=1, source_target_pairs={{0,16},{4,20},{8,24},{12,28},{16,0},{20,4},{24,8},{28,12},{1,17},{... | collective-permute-start | bytes 3145736 | tf_op jit(solution)/shard_map/ppermute | solution.py:1363
  443.5 7.7 slice-start
  447.3 3.8 slice-start.1
  472.7 254.9 %reduce-scatter.9.cloned.1.call-start = ((), (), s32[]{:S(2)}) async-start(), calls=%async_computation.9 | async-start | bytes 5242880 | tf_op jit(solution)/shard_map/reduce_scatter | solution.py:1421
  496.5 89.9 %copy-start.10 = (f32[2048]{0:T(1024)S(1)}, f32[2048]{0:T(1024)}, u32[]{:S(2)}) copy-start(f32[2048]{0:T(1024)} %param.19) | copy-start | bytes 24580
  496.5 89.9 %copy-start.15 = (f32[512]{0:T(512)S(1)}, f32[512]{0:T(512)}, u32[]{:S(2)}) copy-start(f32[512]{0:T(512)} %copy-done.14) | copy-start | bytes 6148
  496.5 243.3 %reduce-scatter.11.cloned.1.call-start = ((), (), s32[]{:S(2)}) async-start(), calls=%async_computation.10 | async-start | bytes 9437184 | tf_op jit(solution)/shard_map/reduce_scatter | solution.py:1374
  496.5 94.5 %copy-start.6 = (bf16[1,512,2048]{2,1,0:T(8,128)(2,1)S(1)}, bf16[1,512,2048]{2,1,0:T(8,128)(2,1)}, u32[]{:S(2)}) copy-start(bf16[1,512,2048]{2,1,0:T(8,128)(2,1)} %param.23) | copy-start | bytes 6291460
  586.4 4.7 copy-start.1
  586.4 6.0 copy-start.3
  593.8 10.6 %copy-start.4 = (f32[512,2048]{1,0:T(8,128)}, f32[512,2048]{1,0:T(8,128)S(1)}, u32[]{:S(2)}) copy-start(f32[512,2048]{1,0:T(8,128)S(1)} %subtract_add_fusion.dh_ref) | copy-start | bytes 12582916
  593.8 10.6 %copy-start.20 = (bf16[512,2048]{1,0:T(8,128)(2,1)S(1)}, bf16[512,2048]{1,0:T(8,128)(2,1)}, u32[]{:S(2)}) copy-start(bf16[512,2048]{1,0:T(8,128)(2,1)} %get-tuple-element.84.o_ref) | copy-start | bytes 6291460
  611.3 0.7 copy-start.17
  611.3 5.6 copy-start.12
  612.9 216.2 %collective-permute-start.3 = (bf16[256,2048]{1,0:T(8,128)(2,1)}, bf16[256,2048]{1,0:T(8,128)(2,1)}, u32[]{:S(2)}, u32[]{:S(2)}) collective-permute-start(bf16[256,2048]{1,0:T(8,128)(2,1)} %get-tuple-element.129), channel_id=1, source_target_pairs={{0,8},{4,12},{8,0},{12,4},{16,24},{20,28},{24,16},{28,20},{1,9},{5... | collective-permute-start | bytes 3145736 | tf_op jit(solution)/shard_map/ppermute | solution.py:1363
  613.6 215.5 %collective-permute-start.4 = (bf16[256,2048]{1,0:T(8,128)(2,1)}, bf16[256,2048]{1,0:T(8,128)(2,1)}, u32[]{:S(2)}, u32[]{:S(2)}) collective-permute-start(bf16[256,2048]{1,0:T(8,128)(2,1)} %add_convert_fusion.4), channel_id=1, source_target_pairs={{0,8},{4,12},{8,0},{12,4},{16,24},{20,28},{24,16},{28,20},{1,9},{5... | collective-permute-start | bytes 3145736 | tf_op jit(solution)/shard_map/ppermute | solution.py:1363
  614.9 214.2 %collective-permute-start.5 = (bf16[256,2048]{1,0:T(8,128)(2,1)}, bf16[256,2048]{1,0:T(8,128)(2,1)}, u32[]{:S(2)}, u32[]{:S(2)}) collective-permute-start(bf16[256,2048]{1,0:T(8,128)(2,1)} %add_convert_fusion.3), channel_id=1, source_target_pairs={{0,16},{4,20},{8,24},{12,28},{16,0},{20,4},{24,8},{28,12},{1,17},{... | collective-permute-start | bytes 3145736 | tf_op jit(solution)/shard_map/ppermute | solution.py:1363
  615.6 213.5 %collective-permute-start.6 = (bf16[256,2048]{1,0:T(8,128)(2,1)S(1)}, bf16[256,2048]{1,0:T(8,128)(2,1)}, u32[]{:S(2)}, u32[]{:S(2)}) collective-permute-start(bf16[256,2048]{1,0:T(8,128)(2,1)S(1)} %get-tuple-element.132), channel_id=1, source_target_pairs={{0,16},{4,20},{8,24},{12,28},{16,0},{20,4},{24,8},{28,12},{1,17},{... | collective-permute-start | bytes 3145736 | tf_op jit(solution)/shard_map/ppermute | solution.py:1363
  835.0 9.9 %copy-start.5 = (bf16[512,2048]{1,0:T(8,128)(2,1)S(1)}, bf16[512,2048]{1,0:T(8,128)(2,1)}, u32[]{:S(2)}) copy-start(bf16[512,2048]{1,0:T(8,128)(2,1)} %get-tuple-element.137) | copy-start | bytes 6291460
  844.9 1.3 copy-start.8
  844.9 2.1 copy-start.7
Sparse Core Ops, SparseCore 0:
  58.7 97.5 all-gather.3
  157.8 93.9 all-gather.5
  253.5 79.0 all-gather.7
  389.5 88.9 reduce-scatter.4
  480.7 81.0 reduce-scatter.6
  564.0 77.2 reduce-scatter.8
  645.1 94.6 reduce-scatter.10

commit v9 on v8

--- a/solution.py
+++ b/solution.py
@@ -447,10 +447,12 @@
 
 
 def spread_kernel(wide, z_size, mlp_count, *refs):
-    attn_count = (len(refs) - 5) // 2 - mlp_count
+    attn_count = (len(refs) - 7) // 2 - mlp_count
     count = mlp_count + attn_count
     ins, outs = refs[:count], refs[count : 2 * count]
-    own_sem, send_sem, recv_sem, z_send, z_recv = refs[2 * count :]
+    own_sem, send_sem, recv_sem, z_send, z_recv, ring_send, ring_recv = refs[2 * count :]
+    first = mlp_count
+    ring = Ring(wide, outs[first], ins[first].shape[0], ring_send, ring_recv)
     place = lax.axis_index("tensor")
     mine, found = others(wide)
     greet(along_peers(place, z_size) + [device for _, device in found])
@@ -474,7 +476,8 @@
 
     def block(at, origin):
         cols = ins[at].shape[1]
-        return outs[at].at[:, pl.ds(pl.multiple_of(origin * cols, LANES), cols)]
+        part = pl.ds(pl.multiple_of(origin * cols, LANES), cols)
+        return outs[at].at[ring.mine() if at == first else slice(None), part]
 
     def hop(at, way, step, receive=False):
         sign = 1 - 2 * way
@@ -501,16 +504,29 @@
             pl.when(sends(way, 1))(lambda: hop(at, way, 1).start())
     for copy in copies + local:
         copy.start()
+
+    def advance(at, step):
+        for way in range(2):
+            pl.when(receives(way, step))(lambda: hop(at, way, step, True).wait_recv())
+            if step + 1 < z_size:
+                pl.when(sends(way, step + 1))(lambda: hop(at, way, step + 1).start())
+
     for step in range(1, z_size):
-        for at in range(mlp_count, count):
-            for way in range(2):
-
-                @pl.when(receives(way, step))
-                def _():
-                    hop(at, way, step, True).wait_recv()
-
-                if step + 1 < z_size:
-                    pl.when(sends(way, step + 1))(lambda: hop(at, way, step + 1).start())
+        advance(first, step)
+    local.pop(first).wait()
+    ring.start_own()
+    stages = [ring.first_halves, ring.second_halves]
+    for step in range(1, z_size):
+        for at in range(first + 1, count):
+            advance(at, step)
+        if stages:
+            stages.pop(0)()
+    for stage in stages:
+        stage()
+    ring.far_halves()
+    for name in ("own", "x", "y", "d"):
+        ring.from_sibling(name, 0, 1)
+    ring.sent()
     for step in range(1, z_size):
         for at in range(mlp_count, count):
             for way in range(2):
@@ -523,7 +539,10 @@
     count = len(mlp) + len(attn)
     spec = pl.BlockSpec(memory_space=pl.ANY)
     out = [jax.ShapeDtypeStruct((GROUP * w.shape[0], w.shape[1] // GROUP), BF16) for w in mlp]
-    out += [jax.ShapeDtypeStruct((w.shape[0], z_size * w.shape[1]), BF16) for w in attn]
+    out += [
+        jax.ShapeDtypeStruct(((1 if at else GROUP) * w.shape[0], z_size * w.shape[1]), BF16)
+        for at, w in enumerate(attn)
+    ]
     return pl.pallas_call(
         functools.partial(spread_kernel, 2 * math.isqrt(dp_size // GROUP), z_size, len(mlp)),
         in_specs=[spec] * count,
@@ -535,6 +554,8 @@
             pltpu.SemaphoreType.DMA((len(mlp), GROUP - 1)),
             pltpu.SemaphoreType.DMA((len(attn), 2 * (z_size - 1))),
             pltpu.SemaphoreType.DMA((len(attn), 2 * (z_size - 1))),
+            pltpu.SemaphoreType.DMA((Ring.COPIES,)),
+            pltpu.SemaphoreType.DMA((Ring.COPIES,)),
         ],
         compiler_params=pltpu.CompilerParams(collective_id=2, has_side_effects=True),
         cost_estimate=pl.CostEstimate(flops=LONG, bytes_accessed=0, transcendentals=0),
@@ -625,7 +646,7 @@
 
 def project_kernel(
     wide, z_size, x_ref, cos_ref, sin_ref, wkv_ref, wq_ref, wo_ref, grad_ref,
-    q_ref, kv_ref, wkv_out, wq_out, wo_out, grad_out,
+    q_ref, kv_ref, wq_out, wo_out, grad_out,
     wkv_all, wq_all, wo_all, grad_all, keys, own_sem, send_sem, recv_sem, kv_send, kv_recv, out_sem,
 ):
     place = lax.axis_index("tensor")
@@ -633,7 +654,7 @@
     count = keys.shape[0] // rows - 1
     left = pl.ds(0, grad_all.shape[1])
     parts = (
-        (wkv_ref, wkv_all, wkv_out), (wq_ref, wq_all, wq_out), (wo_ref, wo_all, wo_out),
+        (wq_ref, wq_all, wq_out), (wo_ref, wo_all, wo_out),
         (grad_ref.at[:, left], grad_all, grad_out.at[:, left]),
     )
     rings = [
@@ -648,7 +669,8 @@
         pltpu.make_async_copy(full, out, out_sem.at[at])
         for at, (_, full, out) in enumerate(parts)
     ]
-    for copy in local:
+    load = pltpu.make_async_copy(wkv_ref, wkv_all, own_sem.at[len(parts)])
+    for copy in local + [load]:
         copy.start()
     keys[: count * rows, :] = jnp.zeros((count * rows, keys.shape[1]), BF16)
     greet([{"dp": peer} for peer in rings[0].peers] + along_peers(place, z_size))
@@ -679,11 +701,7 @@
             ring.from_sibling(name, 0, 1)
 
     rings[0].start_own()
-    rings[0].first_halves()
-    rings[0].second_halves()
-    rings[1].start_own()
-    finish(rings[0])
-    outward[0].start()
+    load.wait()
 
     @pl.loop(0, wkv_all.shape[1] // (2 * LANES))
     def _(at):
@@ -693,11 +711,11 @@
         keys[pl.ds(count * rows, rows), n] = both
 
     pass_keys(1)
-    rings[1].first_halves()
-    rings[1].second_halves()
-    rings[2].start_own()
-    finish(rings[1])
-    outward[1].start()
+    rings[0].first_halves()
+    rings[0].second_halves()
+    rings[1].start_own()
+    finish(rings[0])
+    outward[0].start()
 
     @pl.loop(0, wq_all.shape[1] // (2 * LANES))
     def _(at):
@@ -706,19 +724,19 @@
         both = [rotated(value[:, :LANES]), rotated(value[:, LANES:])]
         q_ref[:, n] = jnp.concatenate(both, axis=1)
 
+    for step in range(2, count + 1):
+        pass_keys(step)
+    rings[1].first_halves()
+    rings[1].second_halves()
+    rings[2].start_own()
+    finish(rings[1])
+    outward[1].start()
     rings[2].first_halves()
     rings[2].second_halves()
-    rings[3].start_own()
-    for step in range(2, count + 1):
-        pass_keys(step)
     finish(rings[2])
     outward[2].start()
-    rings[3].first_halves()
-    rings[3].second_halves()
-    finish(rings[3])
-    outward[3].start()
     pass_keys(count + 1)
-    keys_out = pltpu.make_async_copy(keys, kv_ref, out_sem.at[4])
+    keys_out = pltpu.make_async_copy(keys, kv_ref, out_sem.at[3])
     keys_out.start()
     for step in range(1, count + 1):
         sends = (place + 1 < z_size) & (place >= step - 1)
@@ -733,32 +751,30 @@
     rows, width = x.shape
     far = pl.BlockSpec(memory_space=pl.ANY)
     near = pl.BlockSpec(memory_space=pltpu.VMEM)
-    weights = (wkv, wq, wo)
-    whole = [(GROUP * w.shape[0], w.shape[1]) for w in weights]
+    whole = [(GROUP * w.shape[0], w.shape[1]) for w in (wq, wo)]
     keys = (reach + rows, wkv.shape[1])
     grads = (GROUP * grad.shape[0], grad.shape[1])
     left = (grads[0], grads[1] * 3 // 8)
     return pl.pallas_call(
         functools.partial(project_kernel, 2 * math.isqrt(dp_size // GROUP), z_size),
         in_specs=[near] * 3 + [far] * 4,
-        out_specs=[near] + [far] * 5,
+        out_specs=[near] + [far] * 4,
         out_shape=[jax.ShapeDtypeStruct((rows, wq.shape[1]), BF16)]
         + [jax.ShapeDtypeStruct(shape, BF16) for shape in [keys] + whole + [grads]],
-        scratch_shapes=[pltpu.VMEM(shape, BF16) for shape in whole + [left, keys]]
+        scratch_shapes=[pltpu.VMEM(shape, BF16) for shape in [wkv.shape] + whole + [left, keys]]
         + [
             pltpu.SemaphoreType.DMA((4,)),
-            pltpu.SemaphoreType.DMA((4, Ring.COPIES)),
-            pltpu.SemaphoreType.DMA((4, Ring.COPIES)),
+            pltpu.SemaphoreType.DMA((3, Ring.COPIES)),
+            pltpu.SemaphoreType.DMA((3, Ring.COPIES)),
             pltpu.SemaphoreType.DMA((reach // rows,)),
             pltpu.SemaphoreType.DMA((reach // rows,)),
-            pltpu.SemaphoreType.DMA((5,)),
+            pltpu.SemaphoreType.DMA((4,)),
         ],
         compiler_params=pltpu.CompilerParams(
             collective_id=3, has_side_effects=True, vmem_limit_bytes=56 << 20
         ),
         cost_estimate=pl.CostEstimate(
-            flops=2 * LONG, bytes_accessed=4 * width * sum(w.shape[1] for w in weights),
-            transcendentals=0,
+            flops=2 * LONG, bytes_accessed=0, transcendentals=0
         ),
     )(x, cosine, sine, wkv, wq, wo, grad)
 
@@ -1424,11 +1440,11 @@
 
     r1 = rms_scale(x)
     xn = (x * r1 * attn_gain).astype(BF16)
-    q, kv_all, wkv, wq, wo, dy = project(
+    q, kv_all, wq, wo, dy = project(
         layout.from_cols(xn), cosine, sine, *spread[3:], cotangent[0], reach, dp_size, z_size
     )
     wd = gather_z(spread[2])
-    wkv, wq, wo = layout.to_rows(wkv), layout.to_rows(wq), layout.to_rows(wo)
+    wkv, wq, wo = (layout.to_rows(w) for w in (spread[3], wq, wo))
     att, lse, dy = attend(q, kv_all, low, cotangent[0], dy, dp_size)
     h = x + dot_nt(att, wo)
 
@@ -1448,26 +1464,32 @@
             total = total + other.astype(F32)
         return total.astype(BF16)
 
-    far_y, far_x = out_rows(6, 1), out_rows(7, 1)
-    dy, far_x, far_y = lax.optimization_barrier((dy, far_x, far_y))
+    far_y, far_x, x_lower, y_upper = (out_rows(at, 1) for at in (6, 7, 3, 4))
+    dy, far_x, far_y, x_lower, y_upper = lax.optimization_barrier(
+        (dy, far_x, far_y, x_lower, y_upper)
+    )
     from_x, from_y = layout.swap(far_x, 2), layout.swap(far_y, 4)
+    x_lower, y_upper = layout.swap(x_lower, 2), layout.swap(y_upper, 4)
     gate, up = gate.astype(F32), up.astype(F32)
     sigma = jax.nn.sigmoid(gate)
     dhid = dot_nn(dy, wd)
     dgate = (dhid * up * sigma * (1.0 + gate * (1.0 - sigma))).astype(BF16)
     dup = (dhid * gate * sigma).astype(BF16)
-    dgate, dup, from_x, from_y = lax.optimization_barrier((dgate, dup, from_x, from_y))
-    pieces = (out_rows(2, 1, from_y), out_rows(3, 1), out_rows(4, 1), out_rows(5, 1, from_x))
-    dgate, dup, *pieces = lax.optimization_barrier((dgate, dup, *pieces))
+    dgate, dup, from_x, from_y, x_lower, y_upper = lax.optimization_barrier(
+        (dgate, dup, from_x, from_y, x_lower, y_upper)
+    )
+    x_upper, y_lower = out_rows(2, 1, from_y), out_rows(5, 1, from_x)
+    dgate, dup, x_upper, y_lower = lax.optimization_barrier((dgate, dup, x_upper, y_lower))
+    x_upper, y_lower = layout.swap(x_upper, 2), layout.swap(y_lower, 4)
     total_wg = dot_tn(hn, dgate).astype(BF16)
     dup, total_wg = lax.optimization_barrier((dup, total_wg))
     part_wg = along_z(total_wg)
     total_wu = dot_tn(hn, dup).astype(BF16)
     dup, total_wu = lax.optimization_barrier((dup, total_wu))
     part_wu = along_z(total_wu)
+    dup, x_upper, y_lower = lax.optimization_barrier((dup, x_upper, y_lower))
     dhn = hidden_back(dgate, dup, wg, wu, dp_size)
-    dhn, part_wd, *pieces = lax.optimization_barrier((dhn, part_wd, *pieces))
-    pieces = [layout.swap(piece, flip) for piece, flip in zip(pieces, (2, 2, 4, 4))]
+    dhn, part_wd = lax.optimization_barrier((dhn, part_wd))
     gain_two, dh_norm = norm_back(h, r2, mlp_gain, dhn)
     dh = cotangent[0].astype(F32) + dh_norm
     dhb = dh.astype(BF16)
@@ -1485,10 +1507,9 @@
         activations[0], dh, wq, wkv, (part_wu,), dp_size, z_size,
     )
     gains = layout.sum_outer(gains)
-    gains, *pieces = lax.optimization_barrier((gains, *pieces))
     output = h + out_rows(0, 2).astype(F32)
-    output = output + jnp.concatenate(pieces[:2]).astype(F32)
-    output = output + jnp.concatenate(pieces[2:]).astype(F32)
+    output = output + jnp.concatenate([x_upper, x_lower]).astype(F32)
+    output = output + jnp.concatenate([y_upper, y_lower]).astype(F32)
     wo_grad, wq_grad, wkv_grad, wd_grad, wg_grad, wu_grad = (
         layout.scatter_outer(grad).astype(F32)
         for grad in (wo_grad, wq_grad, wkv_grad, wd_grad, wg_grad, wu_grad)

time: 864 us -> 858 us (level)
  Pallas kernels: 615 us -> 602 us
  waiting for transfers between devices: 8.24 us -> 19.1 us
    pallas_call x1, Pallas kernels: 121 us -> 107 us  [project(): pl.pallas_call(functools.partial(project_kernel, 2 * math.isqrt(dp_size /...]
    pallas_call x1, Pallas kernels: 49.8 us -> 62.1 us  [spread_weights(): pl.pallas_call(functools.partial(spread_kernel, 2 * math.isqrt(dp_size //...]
    ppermute x7, waiting for transfers between devices: 0.02 us -> 10.4 us  [swap(): return lax.ppermute(array, 'dp', pairs)]
  transfers between devices with their start and end apart: 14 -> 14, of which waited for: 1 -> 3; matrix products, arithmetic and copies ran while one was open for 20% -> 21% of each run, Pallas kernels for 66% -> 53%
where the time goes in v9:
time: 858 us; the launch traced here: 854 us
  Pallas kernels  602 us (70%)
  matrix products  172 us (20%)
  other arithmetic  26.8 us (3%)
  waiting for transfers between devices  19.1 us (2%)
  between operations  15 us (2%)
  local copies, waits for them, and re-layouts  12.1 us (1%)
    pallas_call x1, Pallas kernels, project(): pl.pallas_call(functools.partial(project_kernel, 2 * math.isqrt(dp_size /...  107 us
    pallas_call x1, Pallas kernels, attend_back(): pl.pallas_call(functools.partial(attend_back_kernel, reach, 2 * math.isqr...  102 us
    pallas_call x1, Pallas kernels, gate_up(): pl.pallas_call(functools.partial(gate_up_kernel, 2 * math.isqrt(dp_size /...  89.4 us
    pallas_call x1, Pallas kernels, hidden_back(): pl.pallas_call(functools.partial(hidden_back_kernel, 2 * math.isqrt(dp_si...  87.9 us
    pallas_call x1, Pallas kernels, last_grads(): pl.pallas_call(functools.partial(tail_kernel, 2 * math.isqrt(dp_size // G...  87.1 us
    dot_general x4, matrix products, dot_tn(): lax.dot_general(left, right, (((0,), (0,)), ((), ())), preferred_element_...  73.6 us
    pallas_call x1, Pallas kernels, attend(): pl.pallas_call(functools.partial(attend_kernel, reach, 2 * math.isqrt(dp_...  67 us
    pallas_call x1, Pallas kernels, spread_weights(): pl.pallas_call(functools.partial(spread_kernel, 2 * math.isqrt(dp_size //...  62.1 us
  transfers between devices with their start and end apart: 14, of which 3 were waited for; matrix products, arithmetic and copies ran while one was open for 21% of the time, Pallas kernels for 53%

profile of v9, /device:TPU:0, one launch (start us, length us, event | category | flops | bytes accessed | tf_op | source)
XLA Modules:
  0.0 853.6 jit_solution(16513229333412738857)
XLA Ops:
  7.2 1.5 pad_maximum_fusion.2.refs_3_
  8.8 62.1 %shard_map.203 = (bf16[2048,256]{1,0:T(8,128)(2,1)}, bf16[2048,256]{1,0:T(8,128)(2,1)}, bf16[2048,256]{1,0:T(8,128)(2,1)}, bf16[2048,1024]{1,0:T(8,128)(2,1)}, b...) custom-call(bf16[256,2048]{1,0:T(8,128)(2,1)} %refs_0_.1, bf16[256,2048]{1,0:T(8,128)(2,1)} %refs_1_.1, ...), custom_call_target="tpu_custom_call" | custom-call | flops 60000002048 | tf_op jit(solution)/shard_map/pallas_call | solution.py:546
  71.0 0.7 all-gather.6.cloned.1.call-update
  71.7 0.7 all-gather.8.cloned.1.call-update
  72.5 0.1 convert_reduce_fusion
  72.6 0.1 select_reduce_fusion
  72.8 0.5 fusion.8
  73.3 0.7 subtract_add_fusion.1
  73.9 1.0 fusion.47
  74.9 1.9 fusion.10.x_ref
  76.8 1.3 pad_maximum_fusion
  78.0 106.8 %shard_map.204 = (bf16[512,2048]{1,0:T(8,128)(2,1)}, bf16[1536,1024]{1,0:T(8,128)(2,1)}, bf16[2048,2048]{1,0:T(8,128)(2,1)}, bf16[2048,2048]{1,0:T(8,128)(2,1)}, bf16[4096,2048]{1,0:T(8,128)(2,1)}) custom-call(bf16[512,2048]{1,0:T(8,128)(2,1)} %fusion.10.x_ref, f32[512,128]{1,0:T(8,128)} %get-tuple-element.152.cos_ref.cos_all, ...), custom_call_target="tpu_custom_call" | custom-call | flops 120000004096 | tf_op jit(solution)/shard_map/pallas_call | solution.py:758
  184.9 67.0 %shard_map.205 = (bf16[512,2048]{1,0:T(8,128)(2,1)}, f32[32,1,512]{2,1,0:T(1,128)}, bf16[4096,2048]{1,0:T(8,128)(2,1)}) custom-call(bf16[512,2048]{1,0:T(8,128)(2,1)} %get-tuple-element.76.q_ref, bf16[1536,1024]{1,0:T(8,128)(2,1)} %get-tuple-element.77.k_ref.v_ref, ...), custom_call_target="tpu_custom_call", output_to_operand_aliasing={{2}: (5, {})} | custom-call | flops 21474836480 | bytes 7340032 | tf_op jit(solution)/shard_map/pallas_call | solution.py:164
  251.9 7.9 multiply_reduce_fusion.2
  259.8 1.9 copy-done
  261.8 1.7 multiply_convert_fusion.own_ref
  263.5 7.2 all-gather.6.cloned.1.call-done.wu_ref
  270.7 89.4 %shard_map.206 = (bf16[4096,2048]{1,0:T(8,128)(2,1)}, bf16[4096,1024]{1,0:T(8,128)(2,1)}, bf16[4096,1024]{1,0:T(8,128)(2,1)}, bf16[4096,1024]{1,0:T(8,128)(2,1)}, bf16[2,2048,1024]{2,1,0:T(8,128)(2,1)}) custom-call(bf16[512,2048]{1,0:T(8,128)(2,1)} %multiply_convert_fusion.own_ref, bf16[2048,1024]{1,0:T(8,128)(2,1)} %all-gather.4.cloned.1.call-done.wg_ref, ...), custom_call_target="tpu_custom_call" | custom-call | flops 1000000 | tf_op jit(solution)/shard_map/pallas_call | solution.py:871
  360.2 14.6 %convolution_convert_fusion.1 = bf16[2048,2048]{1,0:T(8,128)(2,1)} fusion(bf16[2048,1024]{1,0:T(8,128)(2,1)} %all-gather.8.cloned.1.call-done, bf16[2,2048,1024]{2,1,0:T(8,128)(2,1)} %get-tuple-element.83), kind=kOutput, calls=%fused_computation.12 | convolution fusion | flops 8594128896 | bytes 16777216 | tf_op jit(solution)/shard_map/dot_general | solution.py:36
  374.8 0.1 collective-permute-start
  374.9 21.5 %convolution_convert_fusion.2 = bf16[2048,1024]{1,0:T(8,128)(2,1)} fusion(bf16[4096,2048]{1,0:T(8,128)(2,1)} %get-tuple-element.88, bf16[4096,1024]{1,0:T(8,128)(2,1)S(1)} %copy-done.18), kind=kOutput, calls=%fused_computation.28 | convolution fusion | flops 17181966336 | bytes 29360128 | tf_op jit(solution)/shard_map/dot_general | solution.py:40
  396.3 0.0 reduce-scatter.7.cloned.1.call-start
  396.4 3.8 fusion.21
  400.2 2.4 fusion.23
  402.6 3.7 add_convert_fusion.4
  406.3 3.8 add_convert_fusion.5
  410.1 3.7 add_convert_fusion.6
  413.8 3.7 add_convert_fusion.7
  417.6 0.8 collective-permute-start.1
  418.4 0.1 collective-permute-start.2
  418.5 2.0 collective-permute-start.3
  420.5 1.1 collective-permute-start.4
  421.6 34.5 %fusion.7 = (bf16[4096,1024]{1,0:T(8,128)(2,1)}, bf16[4096,1024]{1,0:T(8,128)(2,1)}) fusion(bf16[4096,1024]{1,0:T(8,128)(2,1)} %get-tuple-element.90, bf16[4096,1024]{1,0:T(8,128)(2,1)} %get-tuple-element.89, bf16[4096,2048]{1,0:T(8,128)(2,1)} %get-tuple-element.88, bf16[2048,1024]{1,0:T(8,128)(2,1)S(1)} %copy-done.19), kind=kOutput, calls=%fused_computation.10 | convolution fusion | flops 17242783744 | bytes 54525952 | tf_op jit(solution)/shard_map/dot_general | solution.py:32
  456.1 9.7 %collective-permute-done.3 = bf16[256,2048]{1,0:T(8,128)(2,1)} collective-permute-done((bf16[256,2048]{1,0:T(8,128)(2,1)}, bf16[256,2048]{1,0:T(8,128)(2,1)}, u32[]{:S(2)}, u32[]{:S(2)}) %collective-permute-start.3) | collective-permute-done | bytes 1048608 | tf_op jit(solution)/shard_map/ppermute | solution.py:1379
  465.9 0.6 collective-permute-done.4
  466.5 2.8 add_convert_fusion.2
  469.3 1.2 copy-done.21
  470.5 21.4 %convolution_convert_fusion.4 = bf16[2048,1024]{1,0:T(8,128)(2,1)} fusion(bf16[4096,2048]{1,0:T(8,128)(2,1)} %get-tuple-element.100, bf16[4096,1024]{1,0:T(8,128)(2,1)S(1)} %copy-done.21), kind=kOutput, calls=%fused_computation.30 | convolution fusion | flops 17181966336 | bytes 29360128 | tf_op jit(solution)/shard_map/dot_general | solution.py:40
  491.9 0.0 reduce-scatter.9.cloned.1.call-start
  492.0 1.2 collective-permute-start.5
  493.2 1.0 collective-permute-start.6
  494.1 23.9 %convolution_convert_fusion.3 = bf16[2048,1024]{1,0:T(8,128)(2,1)} fusion(bf16[4096,2048]{1,0:T(8,128)(2,1)} %get-tuple-element.100, bf16[4096,1024]{1,0:T(8,128)(2,1)} %get-tuple-element.110.dup_ref), kind=kOutput, calls=%fused_computation.29 | convolution fusion | flops 17181966336 | bytes 29360128 | tf_op jit(solution)/shard_map/dot_general | solution.py:40
  518.1 0.0 reduce-scatter.11.cloned.1.call-start
  518.1 87.9 %shard_map.207 = f32[512,2048]{1,0:T(8,128)} custom-call(bf16[4096,1024]{1,0:T(8,128)(2,1)} %get-tuple-element.101.dgate_ref, bf16[4096,1024]{1,0:T(8,128)(2,1)} %get-tuple-element.110.dup_ref, bf16[2048,1024]{1,0:T(8,128)(2,1)} %all-gather.4.cloned.1.call-done.wg_ref, bf16[2048,1024]{1,0:T(8,128)(2,1)} %all-gather.6.cloned.1.call-done.wu_ref), custom_call_target="tpu_custom_call" | custom-call | flops 34359738368 | bytes 29360128 | tf_op jit(solution)/shard_map/pallas_call | solution.py:1070
  606.1 4.7 multiply_reduce_fusion
  610.8 0.0 copy-done.1
  610.8 1.3 copy-done.3
  612.1 1.4 subtract_add_fusion.dh_ref
  613.5 10.6 %convolution_convert_fusion.5.do_ref = bf16[512,2048]{1,0:T(8,128)(2,1)} fusion(bf16[2048,2048]{1,0:T(8,128)(2,1)} %get-tuple-element.80, f32[512,2048]{1,0:T(8,128)S(1)} %subtract_add_fusion.dh_ref), kind=kOutput, calls=%fused_computation.31 | convolution fusion | flops 4297064448 | bytes 14680064 | tf_op jit(solution)/shard_map/dot_general | solution.py:32
  624.2 6.8 convolution_convert_fusion
  631.0 0.7 copy-done.17
  631.7 0.9 copy.27.scale_ref
  632.5 0.6 pad_maximum_fusion.3.gain_ref
  633.2 9.6 %fusion.13 = bf16[1,512,2048]{2,1,0:T(8,128)(2,1)} fusion(f32[512,2048]{1,0:T(8,128)} %copy-done, bf16[2048,2048]{1,0:T(8,128)(2,1)} %collective-permute-done, bf16[256,2048]{1,0:T(8,128)(2,1)} %collective-permute-done.3, bf16[256,2048]{1,0:T(8,128)(2,1)S(1)} %collective-permute-done.5, bf16[256,2048]{1,0:T(8,128)(2,1)} %collective-permute-done.6, ...), kind=kOutput, calls=%fused_computation.32 | convolution fusion | flops 2164260864 | bytes 17825792 | tf_op jit(solution)/shard_map/dot_general | solution.py:36
  642.7 101.9 %shard_map.208 = (bf16[512,2048]{1,0:T(8,128)(2,1)}, bf16[512,1024]{1,0:T(8,128)(2,1)}, bf16[256,2048]{1,0:T(8,128)(2,1)}, bf16[256,2048]{1,0:T(8,128)(2,1)}) custom-call(bf16[512,2048]{1,0:T(8,128)(2,1)} %get-tuple-element.76.q_ref, bf16[512,2048]{1,0:T(8,128)(2,1)} %convolution_convert_fusion.5.do_ref, bf16[512,2048]{1,0:T(8,128)(2,1)} %get-tuple-element.79.o_ref, ...), custom_call_target="tpu_custom_call" | custom-call | flops 53687091200 | bytes 14680064 | tf_op jit(solution)/shard_map/pallas_call | solution.py:319
  744.7 2.8 convert_element_type.158
  747.4 2.8 convert_element_type.160
  750.2 87.1 %shard_map.209 = (f32[256,512]{1,0:T(8,128)}, f32[256,256]{1,0:T(8,128)}, f32[256,512]{1,0:T(8,128)}, f32[2,2048]{1,0:T(2,128)}, bf16[512,2048]{1,0:T(8,128)(2,1)}, /*index=5*/bf16[256,2048]{1,0:T(8,128)(2,1)}) custom-call(bf16[512,2048]{1,0:T(8,128)(2,1)} %fusion.10.x_ref, bf16[512,2048]{1,0:T(8,128)(2,1)} %get-tuple-element.122.dq_ref, ...), custom_call_target="tpu_custom_call" | custom-call | flops 1000000 | tf_op jit(solution)/shard_map/pallas_call | solution.py:1284
  837.4 2.9 convert_element_type.159
  840.3 1.7 fusion.48
  842.0 1.4 fusion.49
  843.4 1.3 copy.32
  844.7 0.8 copy.33
  845.5 0.8 copy.34
  (63 shorter events, 0.4 us)
Async XLA Ops:
  7.2 256.3 %all-gather.4.cloned.1.call-start = ((), (), s32[]{:S(2)}) async-start(), calls=%async_computation.4 | async-start | bytes 5242880 | tf_op jit(solution)/shard_map/all_gather | solution.py:1432
  8.8 63.7 %copy-start.13 = (s32[1,2048]{1,0:T(1,128)S(1)}, s32[1,2048]{1,0:T(1,128)}, u32[]{:S(2)}) copy-start(s32[1,2048]{1,0:T(1,128)} %param.13) | copy-start | bytes 24580
  70.9 1.8 copy-start.2
  70.9 4.0 copy-start.11
  70.9 199.8 %all-gather.6.cloned.1.call-start = ((), (), s32[]{:S(2)}) async-start(), calls=%async_computation.5 | async-start | bytes 5242880 | tf_op jit(solution)/shard_map/all_gather | solution.py:1432
  71.7 288.5 %all-gather.8.cloned.1.call-start = ((), (), s32[]{:S(2)}) async-start(), calls=%async_computation.6 | async-start | bytes 5242880 | tf_op jit(solution)/shard_map/all_gather | solution.py:1432
  72.4 533.6 %reduce-scatter.5.cloned.1.call-start = ((), (), s32[]{:S(2)}) async-start(), calls=%async_computation.7 | async-start | bytes 5242880 | tf_op jit(solution)/shard_map/reduce_scatter | solution.py:1437
  73.2 111.6 %copy-start.16 = (f32[512]{0:T(512)}, f32[512]{0:T(512)S(1)}, u32[]{:S(2)}) copy-start(f32[512]{0:T(512)S(1)} %add_rsqrt_fusion.1) | copy-start | bytes 6148
  251.9 9.9 %copy-start.9 = (f32[2048]{0:T(1024)S(1)}, f32[2048]{0:T(1024)}, u32[]{:S(2)}) copy-start(f32[2048]{0:T(1024)} %param.19) | copy-start | bytes 24580
  259.8 2.0 copy-start
  259.8 1.9 copy-start.14
  360.2 14.7 %copy-start.18 = (bf16[4096,1024]{1,0:T(8,128)(2,1)S(1)}, bf16[4096,1024]{1,0:T(8,128)(2,1)}, u32[]{:S(2)}) copy-start(bf16[4096,1024]{1,0:T(8,128)(2,1)} %get-tuple-element.111) | copy-start | bytes 25165828
  374.8 27.8 %collective-permute-start = (bf16[2048,2048]{1,0:T(8,128)(2,1)}, bf16[2048,2048]{1,0:T(8,128)(2,1)}, u32[]{:S(2)}, u32[]{:S(2)}) collective-permute-start(bf16[2048,2048]{1,0:T(8,128)(2,1)} %convolution_convert_fusion.1), channel_id=1, source_target_pairs={{0,4},{4,0},{8,12},{12,8},{16,20},{20,16},{24,28},{28,24},{1,5},{5... | collective-permute-start | bytes 25165832 | tf_op jit(solution)/shard_map/ppermute | solution.py:1379
  396.3 234.7 %reduce-scatter.7.cloned.1.call-start = ((), (), s32[]{:S(2)}) async-start(), calls=%async_computation.8 | async-start | bytes 5242880 | tf_op jit(solution)/shard_map/reduce_scatter | solution.py:1437
  396.4 3.8 copy-start.19
  417.6 38.6 %collective-permute-start.1 = (bf16[256,2048]{1,0:T(8,128)(2,1)}, bf16[256,2048]{1,0:T(8,128)(2,1)S(1)}, u32[]{:S(2)}, u32[]{:S(2)}) collective-permute-start(bf16[256,2048]{1,0:T(8,128)(2,1)} %add_convert_fusion.7), channel_id=1, source_target_pairs={{0,8},{4,12},{8,0},{12,4},{16,24},{20,28},{24,16},{28,20},{1,9},{5... | collective-permute-start | bytes 3145736 | tf_op jit(solution)/shard_map/ppermute | solution.py:1379
  418.4 37.8 %collective-permute-start.2 = (bf16[256,2048]{1,0:T(8,128)(2,1)}, bf16[256,2048]{1,0:T(8,128)(2,1)S(1)}, u32[]{:S(2)}, u32[]{:S(2)}) collective-permute-start(bf16[256,2048]{1,0:T(8,128)(2,1)} %add_convert_fusion.6), channel_id=1, source_target_pairs={{0,16},{4,20},{8,24},{12,28},{16,0},{20,4},{24,8},{28,12},{1,17},{... | collective-permute-start | bytes 3145736 | tf_op jit(solution)/shard_map/ppermute | solution.py:1379
  418.5 47.4 %collective-permute-start.3 = (bf16[256,2048]{1,0:T(8,128)(2,1)}, bf16[256,2048]{1,0:T(8,128)(2,1)}, u32[]{:S(2)}, u32[]{:S(2)}) collective-permute-start(bf16[256,2048]{1,0:T(8,128)(2,1)} %add_convert_fusion.5), channel_id=1, source_target_pairs={{0,8},{4,12},{8,0},{12,4},{16,24},{20,28},{24,16},{28,20},{1,9},{5... | collective-permute-start | bytes 3145736 | tf_op jit(solution)/shard_map/ppermute | solution.py:1379
  420.5 46.0 %collective-permute-start.4 = (bf16[256,2048]{1,0:T(8,128)(2,1)}, bf16[256,2048]{1,0:T(8,128)(2,1)}, u32[]{:S(2)}, u32[]{:S(2)}) collective-permute-start(bf16[256,2048]{1,0:T(8,128)(2,1)} %add_convert_fusion.4), channel_id=1, source_target_pairs={{0,16},{4,20},{8,24},{12,28},{16,0},{20,4},{24,8},{28,12},{1,17},{... | collective-permute-start | bytes 3145736 | tf_op jit(solution)/shard_map/ppermute | solution.py:1379
  466.5 4.0 copy-start.21
  491.9 252.7 %reduce-scatter.9.cloned.1.call-start = ((), (), s32[]{:S(2)}) async-start(), calls=%async_computation.9 | async-start | bytes 5242880 | tf_op jit(solution)/shard_map/reduce_scatter | solution.py:1437
  492.0 26.2 %collective-permute-start.5 = (bf16[256,2048]{1,0:T(8,128)(2,1)S(1)}, bf16[256,2048]{1,0:T(8,128)(2,1)S(1)}, u32[]{:S(2)}, u32[]{:S(2)}) collective-permute-start(bf16[256,2048]{1,0:T(8,128)(2,1)S(1)} %get-tuple-element.104), channel_id=1, source_target_pairs={{0,8},{4,12},{8,0},{12,4},{16,24},{20,28},{24,16},{28,20},{1,9},{5... | collective-permute-start | bytes 3145736 | tf_op jit(solution)/shard_map/ppermute | solution.py:1379
  493.2 25.0 %collective-permute-start.6 = (bf16[256,2048]{1,0:T(8,128)(2,1)S(1)}, bf16[256,2048]{1,0:T(8,128)(2,1)}, u32[]{:S(2)}, u32[]{:S(2)}) collective-permute-start(bf16[256,2048]{1,0:T(8,128)(2,1)S(1)} %get-tuple-element.105), channel_id=1, source_target_pairs={{0,16},{4,20},{8,24},{12,28},{16,0},{20,4},{24,8},{28,12},{1,17},{... | collective-permute-start | bytes 3145736 | tf_op jit(solution)/shard_map/ppermute | solution.py:1379
  518.0 88.0 %copy-start.10 = (f32[2048]{0:T(1024)S(1)}, f32[2048]{0:T(1024)}, u32[]{:S(2)}) copy-start(f32[2048]{0:T(1024)} %param.19) | copy-start | bytes 24580
  518.1 88.0 %copy-start.15 = (f32[512]{0:T(512)S(1)}, f32[512]{0:T(512)}, u32[]{:S(2)}) copy-start(f32[512]{0:T(512)} %copy-done.14) | copy-start | bytes 6148
  518.1 232.2 %reduce-scatter.11.cloned.1.call-start = ((), (), s32[]{:S(2)}) async-start(), calls=%async_computation.10 | async-start | bytes 9437184 | tf_op jit(solution)/shard_map/reduce_scatter | solution.py:1390
  518.1 92.6 %copy-start.6 = (bf16[1,512,2048]{2,1,0:T(8,128)(2,1)S(1)}, bf16[1,512,2048]{2,1,0:T(8,128)(2,1)}, u32[]{:S(2)}) copy-start(bf16[1,512,2048]{2,1,0:T(8,128)(2,1)} %param.23) | copy-start | bytes 6291460
  606.1 4.7 copy-start.1
  606.1 6.0 copy-start.3
  613.5 10.6 %copy-start.4 = (f32[512,2048]{1,0:T(8,128)}, f32[512,2048]{1,0:T(8,128)S(1)}, u32[]{:S(2)}) copy-start(f32[512,2048]{1,0:T(8,128)S(1)} %subtract_add_fusion.dh_ref) | copy-start | bytes 12582916
  613.5 10.6 %copy-start.20 = (bf16[512,2048]{1,0:T(8,128)(2,1)S(1)}, bf16[512,2048]{1,0:T(8,128)(2,1)}, u32[]{:S(2)}) copy-start(bf16[512,2048]{1,0:T(8,128)(2,1)} %get-tuple-element.79.o_ref) | copy-start | bytes 6291460
  631.0 0.7 copy-start.17
  631.0 1.5 copy-start.12
  837.4 6.1 copy-start.5
  837.4 7.4 copy-start.8
  837.4 8.2 copy-start.7
Sparse Core Ops, SparseCore 0:
  71.1 98.2 all-gather.3
  170.9 99.7 all-gather.5
  272.3 78.7 all-gather.7
  396.5 80.3 reduce-scatter.4
  492.0 79.9 reduce-scatter.6
  574.2 77.2 reduce-scatter.8
  655.4 71.8 reduce-scatter.10

commit v10 on v9

--- a/solution.py
+++ b/solution.py
@@ -781,16 +781,24 @@
 
 def gate_up_kernel(
     wide, own_ref, wg_ref, wu_ref, all_ref, gate_ref, up_ref, hid_ref, core_ref,
-    full, stage, own_sem, send_sem, recv_sem, out_sem, all_sem,
+    full, stage, wg_all, wu_all, own_sem, load_sem, send_sem, recv_sem, out_sem, all_sem,
 ):
     rows = own_ref.shape[0]
     cols = gate_ref.shape[1]
     ring = Ring(wide, full, rows, send_sem, recv_sem)
     local = pltpu.make_async_copy(own_ref, full.at[ring.mine()], own_sem)
     local.start()
+    loads = [
+        pltpu.make_async_copy(wg_ref, wg_all, load_sem.at[0]),
+        pltpu.make_async_copy(wu_ref, wu_all, load_sem.at[1]),
+    ]
+    for copy in loads:
+        copy.start()
     meet(ring.peers)
     local.wait()
     ring.start_own()
+    for copy in loads:
+        copy.wait()
 
     def out_copies(slot, places):
         where, core, chip = places
@@ -847,8 +855,8 @@
         @pl.loop(0, cols // NTILE)
         def _(at):
             n = pl.ds(pl.multiple_of(at * NTILE, NTILE), NTILE)
-            gate = dot_nn(x, wg_ref[:, n])
-            up = dot_nn(x, wu_ref[:, n])
+            gate = dot_nn(x, wg_all[:, n])
+            up = dot_nn(x, wu_all[:, n])
             stage[slot, 0, :, n] = gate.astype(BF16)
             stage[slot, 1, :, n] = up.astype(BF16)
             stage[slot, 2, :, n] = (gate * up / (1.0 + jnp.exp(-gate))).astype(BF16)
@@ -867,10 +875,9 @@
     cols = wg.shape[1]
     tokens = GROUP * rows
     far = pl.BlockSpec(memory_space=pl.ANY)
-    near = pl.BlockSpec(memory_space=pltpu.VMEM)
     return pl.pallas_call(
         functools.partial(gate_up_kernel, 2 * math.isqrt(dp_size // GROUP)),
-        in_specs=[far, near, near],
+        in_specs=[far] * 3,
         out_specs=[far] * 5,
         out_shape=[jax.ShapeDtypeStruct((tokens, width), BF16)]
         + [jax.ShapeDtypeStruct((tokens, cols), BF16)] * 3
@@ -878,7 +885,10 @@
         scratch_shapes=[
             pltpu.VMEM((tokens, width), BF16),
             pltpu.VMEM((2, 3, rows // 2, cols), BF16),
+            pltpu.VMEM(wg.shape, BF16),
+            pltpu.VMEM(wu.shape, BF16),
             pltpu.SemaphoreType.DMA,
+            pltpu.SemaphoreType.DMA((2,)),
             pltpu.SemaphoreType.DMA((Ring.COPIES,)),
             pltpu.SemaphoreType.DMA((Ring.COPIES,)),
             pltpu.SemaphoreType.DMA((2, 4)),
@@ -1013,10 +1023,12 @@
 
 
 def hidden_back_kernel(
-    wide, dgate_ref, dup_ref, wg_ref, wu_ref, out_ref, loaded, load_sem, *scratch
+    wide, gain_ref, h_ref, grad_ref, dgate_ref, dup_ref, wg_ref, wu_ref,
+    dh_ref, low_ref, gain_out,
+    loaded, wg_all, wu_all, h_all, grad_all, load_sem, own_sem, *scratch,
 ):
     ring = Reduce(wide, *scratch)
-    rows = out_ref.shape[0]
+    rows = dh_ref.shape[0]
 
     def loads(step):
         chunk, _ = ring.chunk(step)
@@ -1028,9 +1040,15 @@
             for at, ref in enumerate((dgate_ref, dup_ref))
         ]
 
-    for copy in loads(0):
+    pairs = ((wg_ref, wg_all), (wu_ref, wu_all), (h_ref, h_all), (grad_ref, grad_all))
+    whole = [
+        pltpu.make_async_copy(src, dst, own_sem.at[at]) for at, (src, dst) in enumerate(pairs)
+    ]
+    for copy in loads(0) + whole:
         copy.start()
     meet(ring.peers)
+    for copy in whole[:2]:
+        copy.wait()
 
     @pl.loop(0, 8)
     def _(step):
@@ -1044,61 +1062,77 @@
         _, target = ring.chunk(step)
         dgate, dup = loaded[step % 2, 0], loaded[step % 2, 1]
 
-        @pl.loop(0, out_ref.shape[1] // NTILE)
+        @pl.loop(0, dh_ref.shape[1] // NTILE)
         def _(at):
             n = pl.ds(pl.multiple_of(at * NTILE, NTILE), NTILE)
-            value = dot_nt(dgate, wg_ref[n, :]) + dot_nt(dup, wu_ref[n, :])
+            value = dot_nt(dgate, wg_all[n, :]) + dot_nt(dup, wu_all[n, :])
             target[:, n] = value.astype(BF16)
 
         ring.after(step)
 
     ring.pass_on()
+    for copy in whole[2:]:
+        copy.wait()
+    gain_out[...] = jnp.zeros_like(gain_out)
 
     def store(here, value):
-        out_ref[here, :] = value
+        h = h_all[here, :]
+        scale = rms_scale(h)
+        gained = value * gain_ref[...]
+        inner = jnp.mean(gained * h, axis=1, keepdims=True)
+        gain_out[...] += value * h * scale
+        total = grad_all[here, :].astype(F32) + scale * gained
+        total -= h * (scale * scale * scale * inner)
+        dh_ref[here, :] = total
+        low_ref[here, :] = total.astype(BF16)
 
     ring.finish(store)
     ring.sent()
 
 
-def hidden_back(dgate, dup, wg, wu, dp_size):
+def hidden_back(gain, h, grad, dgate, dup, wg, wu, dp_size):
     tokens, cols = dgate.shape
-    width = wg.shape[0]
-    rows = tokens // GROUP
+    rows, width = h.shape
     far = pl.BlockSpec(memory_space=pl.ANY)
     near = pl.BlockSpec(memory_space=pltpu.VMEM)
     return pl.pallas_call(
         functools.partial(hidden_back_kernel, 2 * math.isqrt(dp_size // GROUP)),
-        in_specs=[far, far, near, near],
-        out_specs=near,
-        out_shape=jax.ShapeDtypeStruct((rows, width), F32),
+        in_specs=[near] + [far] * 6,
+        out_specs=[near] * 3,
+        out_shape=[
+            jax.ShapeDtypeStruct((rows, width), F32),
+            jax.ShapeDtypeStruct((rows, width), BF16),
+            jax.ShapeDtypeStruct((STRIP, width), F32),
+        ],
         scratch_shapes=[
             pltpu.VMEM((2, 2, rows, cols), BF16),
+            pltpu.VMEM(wg.shape, BF16),
+            pltpu.VMEM(wu.shape, BF16),
+            pltpu.VMEM(h.shape, F32),
+            pltpu.VMEM(grad.shape, BF16),
             pltpu.SemaphoreType.DMA((2, 2)),
+            pltpu.SemaphoreType.DMA((4,)),
         ]
         + Reduce.scratch(rows, width),
         compiler_params=pltpu.CompilerParams(
-            collective_id=6, has_side_effects=True, vmem_limit_bytes=60 << 20
+            collective_id=6, has_side_effects=True, vmem_limit_bytes=62 << 20
         ),
         cost_estimate=pl.CostEstimate(
-            flops=4 * tokens * width * cols,
-            bytes_accessed=4 * tokens * cols + 4 * width * cols + 4 * rows * width,
-            transcendentals=0,
+            flops=2 * LONG, bytes_accessed=4 * rows * width, transcendentals=0
         ),
-    )(dgate, dup, wg, wu)
+    )(gain, h, grad, dgate, dup, wg, wu)
 
 
 def tail_kernel(
-    wide, z_size, mlp_count, x_ref, dq_ref, dkv_ref, wo_ref, scale_ref, gain_ref,
+    wide, z_size, x_ref, dq_ref, dkv_ref, wo_ref, gain_ref,
     raw_ref, dh_ref, wq_ref, wkv_ref, *refs
 ):
-    mlp_ins, refs = refs[:mlp_count], refs[mlp_count:]
     wq_out, wkv_out, wo_out, gain_out, grad_out = refs[:5]
-    mlp_outs, scratch = refs[5 : 5 + mlp_count], refs[5 + mlp_count :]
+    scratch = refs[5:]
     own_scratch = scratch[:12]
     sums, zrecv, gain_z, gain_p, z_send, z_recv, g_send, g_recv = scratch[12:20]
-    wo_recv, w_send, w_recv, m_own, m_send, m_recv = scratch[20:26]
-    wq_all, wkv_all, raw, dh, dxn, gain_sum, load_sem = scratch[26:]
+    wo_recv, w_send, w_recv = scratch[20:23]
+    wq_all, wkv_all, raw, dh, dxn, gain_sum, load_sem = scratch[23:]
     rings = [Reduce(wide, *own_scratch[6 * at : 6 * at + 6]) for at in range(2)]
     place = lax.axis_index("tensor")
     mine, found = others(wide)
@@ -1120,7 +1154,6 @@
         copy.start()
     greet(along + around)
 
-    mlp_copies = send_home(wide, mlp_ins, mlp_outs, m_own, m_send, m_recv)
     wo_part = wo_out.shape[1]
     wo_copies = [
         pltpu.make_async_remote_copy(
@@ -1173,7 +1206,7 @@
             here = pl.ds(pl.multiple_of(at * STRIP, STRIP), STRIP)
             there = pl.ds(pl.multiple_of(tile * tile_rows + at * STRIP, STRIP), STRIP)
             grad, value = dxn[here, :], raw[tile, here, :].astype(F32)
-            scale = scale_ref[there, :]
+            scale = rms_scale(value)
             gained = grad * gain_ref[0:1, :]
             inner = jnp.mean(gained * value, axis=1, keepdims=True)
             gain_sum[...] += grad * value * scale
@@ -1221,8 +1254,6 @@
     for copy in gain_copies:
         copy.start()
     rings[1].pass_on()
-    for copy in mlp_copies:
-        copy.start()
     send_along(0)
 
     for copy in gain_copies:
@@ -1266,11 +1297,9 @@
         copy.wait_send()
     for ring in rings:
         ring.sent()
-    for copy in mlp_copies:
-        copy.wait()
-
-
-def last_grads(x, dq, dkv, wo_sum, scale, gains, raw, dh, wq, wkv, mlp, dp_size, z_size):
+
+
+def last_grads(x, dq, dkv, wo_sum, gains, raw, dh, wq, wkv, dp_size, z_size):
     tokens, width = x.shape
     rows = width // GROUP
     tiles = tokens // QTILE
@@ -1282,16 +1311,15 @@
         scratch += Reduce.scratch(rows, cols)
     total = sum(sizes)
     return pl.pallas_call(
-        functools.partial(tail_kernel, 2 * math.isqrt(dp_size // GROUP), z_size, len(mlp)),
-        in_specs=[near] * 6 + [far] * (4 + len(mlp)),
-        out_specs=[near] * 5 + [far] * len(mlp),
+        functools.partial(tail_kernel, 2 * math.isqrt(dp_size // GROUP), z_size),
+        in_specs=[near] * 5 + [far] * 4,
+        out_specs=[near] * 5,
         out_shape=[jax.ShapeDtypeStruct((rows, cols // z_size), F32) for cols in sizes]
         + [
             jax.ShapeDtypeStruct((rows, wo_sum.shape[1] // z_size), F32),
             jax.ShapeDtypeStruct(gains.shape, F32),
             jax.ShapeDtypeStruct((tokens, width), BF16),
-        ]
-        + home_shapes(mlp),
+        ],
         scratch_shapes=scratch
         + [
             pltpu.VMEM((rows, total), BF16),
@@ -1305,9 +1333,6 @@
             pltpu.VMEM((z_size - 1, rows, wo_sum.shape[1] // z_size), BF16),
             pltpu.SemaphoreType.DMA((z_size - 1,)),
             pltpu.SemaphoreType.DMA((z_size - 1,)),
-        ]
-        + home_scratch(mlp)
-        + [
             pltpu.VMEM(wq.shape, BF16),
             pltpu.VMEM(wkv.shape, BF16),
             pltpu.VMEM((tiles, QTILE, width), BF16),
@@ -1320,7 +1345,7 @@
             collective_id=4, has_side_effects=True, vmem_limit_bytes=62 << 20
         ),
         cost_estimate=pl.CostEstimate(flops=SHORT, bytes_accessed=0, transcendentals=0),
-    )(x, dq, dkv, wo_sum, scale, gains, raw, dh, wq, wkv, *mlp)
+    )(x, dq, dkv, wo_sum, gains, raw, dh, wq, wkv)
 
 
 class Layout:
@@ -1394,13 +1419,6 @@
 
 def rms_scale(values):
     return lax.rsqrt(jnp.mean(values * values, axis=-1, keepdims=True) + NORM_EPS)
-
-
-def norm_back(values, scaling, gain, grad):
-    gained = grad * gain
-    gain_part = jnp.sum(grad * values * scaling, axis=0)
-    inner = jnp.mean(gained * values, axis=-1, keepdims=True)
-    return gain_part, scaling * gained - values * scaling * scaling * scaling * inner
 
 
 def per_device(
@@ -1475,36 +1493,34 @@
     dhid = dot_nn(dy, wd)
     dgate = (dhid * up * sigma * (1.0 + gate * (1.0 - sigma))).astype(BF16)
     dup = (dhid * gate * sigma).astype(BF16)
-    dgate, dup, from_x, from_y, x_lower, y_upper = lax.optimization_barrier(
-        (dgate, dup, from_x, from_y, x_lower, y_upper)
-    )
+    dgate, dup, from_x, from_y = lax.optimization_barrier((dgate, dup, from_x, from_y))
     x_upper, y_lower = out_rows(2, 1, from_y), out_rows(5, 1, from_x)
     dgate, dup, x_upper, y_lower = lax.optimization_barrier((dgate, dup, x_upper, y_lower))
     x_upper, y_lower = layout.swap(x_upper, 2), layout.swap(y_lower, 4)
     total_wg = dot_tn(hn, dgate).astype(BF16)
-    dup, total_wg = lax.optimization_barrier((dup, total_wg))
     part_wg = along_z(total_wg)
+    dup, total_wg, x_lower, y_upper = lax.optimization_barrier((dup, total_wg, x_lower, y_upper))
     total_wu = dot_tn(hn, dup).astype(BF16)
     dup, total_wu = lax.optimization_barrier((dup, total_wu))
     part_wu = along_z(total_wu)
     dup, x_upper, y_lower = lax.optimization_barrier((dup, x_upper, y_lower))
-    dhn = hidden_back(dgate, dup, wg, wu, dp_size)
-    dhn, part_wd = lax.optimization_barrier((dhn, part_wd))
-    gain_two, dh_norm = norm_back(h, r2, mlp_gain, dhn)
-    dh = cotangent[0].astype(F32) + dh_norm
-    dhb = dh.astype(BF16)
+    dh, dhb, gain_two = hidden_back(
+        mlp_gain[None], h, cotangent[0], dgate, dup, wg, wu, dp_size
+    )
+    gain_two = jnp.sum(gain_two, axis=0)
+    dhb, part_wd = lax.optimization_barrier((dhb, part_wd))
     datt = dot_nn(dhb, wo).astype(BF16)
     total_wo = layout.from_rows(dot_tn(dhb, att).astype(BF16))
     datt, part_wg, total_wo = lax.optimization_barrier((datt, part_wg, total_wo))
+    datt, part_wu = lax.optimization_barrier((datt, part_wu))
     part_wo = layout.scatter(total_wo)
-    dq, dkv, wd_grad, wg_grad = attend_back(
-        q, datt, att, kv_all, lse, low, cosine, sine, (part_wd, part_wg), dp_size, z_size
+    dq, dkv, wd_grad, wg_grad, wu_grad = attend_back(
+        q, datt, att, kv_all, lse, low, cosine, sine, (part_wd, part_wg, part_wu), dp_size, z_size
     )
-    dq, part_wu = lax.optimization_barrier((dq, part_wu))
     dq, part_wo = lax.optimization_barrier((dq, part_wo))
-    wq_grad, wkv_grad, wo_grad, gains, input_grad, wu_grad = last_grads(
-        layout.from_cols(xn), dq, dkv, part_wo, r1, jnp.stack([attn_gain, gain_two]),
-        activations[0], dh, wq, wkv, (part_wu,), dp_size, z_size,
+    wq_grad, wkv_grad, wo_grad, gains, input_grad = last_grads(
+        layout.from_cols(xn), dq, dkv, part_wo, jnp.stack([attn_gain, gain_two]),
+        activations[0], dh, wq, wkv, dp_size, z_size,
     )
     gains = layout.sum_outer(gains)
     output = h + out_rows(0, 2).astype(F32)

time: 858 us -> 866 us (level)
  waiting for transfers between devices: 19.1 us -> 32.7 us
    ppermute x7, waiting for transfers between devices: 10.4 us -> 23.7 us  [swap(): return lax.ppermute(array, 'dp', pairs)]
  transfers between devices with their start and end apart: 14 -> 14, of which waited for: 3 -> 3; matrix products, arithmetic and copies ran while one was open for 21% -> 20% of each run, Pallas kernels for 53% -> 53%
where the time goes in v10:
time: 866 us; the launch traced here: 862 us
  Pallas kernels  605 us (70%)
  matrix products  170 us (20%)
  waiting for transfers between devices  32.7 us (4%)
  other arithmetic  19.4 us (2%)
  between operations  14.7 us (2%)
  local copies, waits for them, and re-layouts  12.1 us (1%)
    pallas_call x1, Pallas kernels, project(): pl.pallas_call(functools.partial(project_kernel, 2 * math.isqrt(dp_size /...  107 us
    pallas_call x1, Pallas kernels, attend_back(): pl.pallas_call(functools.partial(attend_back_kernel, reach, 2 * math.isqr...  102 us
    pallas_call x1, Pallas kernels, hidden_back(): pl.pallas_call(functools.partial(hidden_back_kernel, 2 * math.isqrt(dp_si...  93 us
    pallas_call x1, Pallas kernels, gate_up(): pl.pallas_call(functools.partial(gate_up_kernel, 2 * math.isqrt(dp_size /...  88.5 us
    pallas_call x1, Pallas kernels, last_grads(): pl.pallas_call(functools.partial(tail_kernel, 2 * math.isqrt(dp_size // G...  86.5 us
    dot_general x4, matrix products, dot_tn(): lax.dot_general(left, right, (((0,), (0,)), ((), ())), preferred_element_...  73.5 us
    pallas_call x1, Pallas kernels, attend(): pl.pallas_call(functools.partial(attend_kernel, reach, 2 * math.isqrt(dp_...  66.9 us
    pallas_call x1, Pallas kernels, spread_weights(): pl.pallas_call(functools.partial(spread_kernel, 2 * math.isqrt(dp_size //...  62.1 us
  transfers between devices with their start and end apart: 14, of which 3 were waited for; matrix products, arithmetic and copies ran while one was open for 20% of the time, Pallas kernels for 53%

profile of v10, /device:TPU:0, one launch (start us, length us, event | category | flops | bytes accessed | tf_op | source)
XLA Modules:
  0.0 861.6 jit_solution(13480320056139625229)
XLA Ops:
  7.2 0.0 all-gather.4.cloned.1.call-start
  7.2 1.5 pad_maximum_fusion.2.refs_3_
  8.8 62.1 %shard_map.203 = (bf16[2048,256]{1,0:T(8,128)(2,1)}, bf16[2048,256]{1,0:T(8,128)(2,1)}, bf16[2048,256]{1,0:T(8,128)(2,1)}, bf16[2048,1024]{1,0:T(8,128)(2,1)}, b...) custom-call(bf16[256,2048]{1,0:T(8,128)(2,1)} %refs_0_.1, bf16[256,2048]{1,0:T(8,128)(2,1)} %refs_1_.1, ...), custom_call_target="tpu_custom_call" | custom-call | flops 60000002048 | tf_op jit(solution)/shard_map/pallas_call | solution.py:546
  70.9 0.0 all-gather.6.cloned.1.call-start
  71.0 0.7 all-gather.6.cloned.1.call-update
  71.7 0.0 all-gather.8.cloned.1.call-start
  71.7 0.7 all-gather.8.cloned.1.call-update
  72.4 0.0 reduce-scatter.5.cloned.1.call-start
  72.5 0.1 convert_reduce_fusion
  72.6 0.1 select_reduce_fusion
  72.8 0.5 fusion.8
  73.2 0.7 subtract_add_fusion
  73.9 1.0 fusion.45
  74.9 1.9 fusion.10.x_ref
  76.8 1.3 pad_maximum_fusion
  78.0 106.9 %shard_map.204 = (bf16[512,2048]{1,0:T(8,128)(2,1)}, bf16[1536,1024]{1,0:T(8,128)(2,1)}, bf16[2048,2048]{1,0:T(8,128)(2,1)}, bf16[2048,2048]{1,0:T(8,128)(2,1)}, bf16[4096,2048]{1,0:T(8,128)(2,1)}) custom-call(bf16[512,2048]{1,0:T(8,128)(2,1)} %fusion.10.x_ref, f32[512,128]{1,0:T(8,128)} %get-tuple-element.154.cos_ref.cos_all, ...), custom_call_target="tpu_custom_call" | custom-call | flops 120000004096 | tf_op jit(solution)/shard_map/pallas_call | solution.py:758
  184.9 66.9 %shard_map.205 = (bf16[512,2048]{1,0:T(8,128)(2,1)}, f32[32,1,512]{2,1,0:T(1,128)}, bf16[4096,2048]{1,0:T(8,128)(2,1)}) custom-call(bf16[512,2048]{1,0:T(8,128)(2,1)} %get-tuple-element.78.q_ref, bf16[1536,1024]{1,0:T(8,128)(2,1)} %get-tuple-element.79.k_ref.v_ref, ...), custom_call_target="tpu_custom_call", output_to_operand_aliasing={{2}: (5, {})} | custom-call | flops 21474836480 | bytes 7340032 | tf_op jit(solution)/shard_map/pallas_call | solution.py:164
  251.8 7.9 multiply_reduce_fusion
  259.7 1.9 copy-done.1
  261.6 1.7 multiply_convert_fusion.own_ref
  263.3 7.4 all-gather.6.cloned.1.call-done.wu_ref
  270.8 88.5 %shard_map.206 = (bf16[4096,2048]{1,0:T(8,128)(2,1)}, bf16[4096,1024]{1,0:T(8,128)(2,1)}, bf16[4096,1024]{1,0:T(8,128)(2,1)}, bf16[4096,1024]{1,0:T(8,128)(2,1)}, bf16[2,2048,1024]{2,1,0:T(8,128)(2,1)}) custom-call(bf16[512,2048]{1,0:T(8,128)(2,1)} %multiply_convert_fusion.own_ref, bf16[2048,1024]{1,0:T(8,128)(2,1)} %all-gather.4.cloned.1.call-done.wg_ref, ...), custom_call_target="tpu_custom_call" | custom-call | flops 1000000 | tf_op jit(solution)/shard_map/pallas_call | solution.py:878
  359.3 14.3 %convolution_convert_fusion.1 = bf16[2048,2048]{1,0:T(8,128)(2,1)} fusion(bf16[2048,1024]{1,0:T(8,128)(2,1)} %all-gather.8.cloned.1.call-done, bf16[2,2048,1024]{2,1,0:T(8,128)(2,1)} %get-tuple-element.85), kind=kOutput, calls=%fused_computation.12 | convolution fusion | flops 8594128896 | bytes 16777216 | tf_op jit(solution)/shard_map/dot_general | solution.py:36
  373.7 0.1 collective-permute-start
  373.8 21.5 %convolution_convert_fusion.2 = bf16[2048,1024]{1,0:T(8,128)(2,1)} fusion(bf16[4096,2048]{1,0:T(8,128)(2,1)} %get-tuple-element.90, bf16[4096,1024]{1,0:T(8,128)(2,1)S(1)} %copy-done.10), kind=kOutput, calls=%fused_computation.25 | convolution fusion | flops 17181966336 | bytes 29360128 | tf_op jit(solution)/shard_map/dot_general | solution.py:40
  395.2 0.0 reduce-scatter.7.cloned.1.call-start
  395.3 3.8 fusion.19
  399.1 2.4 fusion.21
  401.5 3.7 add_convert_fusion.4
  405.2 3.7 add_convert_fusion.5
  408.9 3.7 add_convert_fusion.6
  412.6 3.7 add_convert_fusion.7
  416.4 0.9 collective-permute-start.1
  417.3 0.1 collective-permute-start.2
  417.4 34.7 %fusion.7 = (bf16[4096,1024]{1,0:T(8,128)(2,1)}, bf16[4096,1024]{1,0:T(8,128)(2,1)}) fusion(bf16[4096,1024]{1,0:T(8,128)(2,1)} %get-tuple-element.92, bf16[4096,1024]{1,0:T(8,128)(2,1)} %get-tuple-element.91, bf16[4096,2048]{1,0:T(8,128)(2,1)} %get-tuple-element.90, bf16[2048,1024]{1,0:T(8,128)(2,1)S(1)} %copy-done.11), kind=kOutput, calls=%fused_computation.10 | convolution fusion | flops 17242783744 | bytes 54525952 | tf_op jit(solution)/shard_map/dot_general | solution.py:32
  452.1 2.8 add_convert_fusion.2
  454.9 1.2 copy-done.19
  456.1 21.3 %convolution_convert_fusion.4 = bf16[2048,1024]{1,0:T(8,128)(2,1)} fusion(bf16[4096,2048]{1,0:T(8,128)(2,1)} %get-tuple-element.100, bf16[4096,1024]{1,0:T(8,128)(2,1)S(1)} %copy-done.19), kind=kOutput, calls=%fused_computation.27 | convolution fusion | flops 17181966336 | bytes 29360128 | tf_op jit(solution)/shard_map/dot_general | solution.py:40
  477.4 0.0 reduce-scatter.9.cloned.1.call-start
  477.5 2.1 collective-permute-start.3
  479.6 1.0 collective-permute-start.4
  480.6 22.4 %collective-permute-done.3 = bf16[256,2048]{1,0:T(8,128)(2,1)S(1)} collective-permute-done((bf16[256,2048]{1,0:T(8,128)(2,1)}, bf16[256,2048]{1,0:T(8,128)(2,1)S(1)}, u32[]{:S(2)}, u32[]{:S(2)}) %collective-permute-start.3) | collective-permute-done | bytes 1048608 | tf_op jit(solution)/shard_map/ppermute | solution.py:1404
  503.0 1.3 collective-permute-done.4
  504.3 1.4 collective-permute-start.5
  505.6 1.0 collective-permute-start.6
  506.7 24.0 %convolution_convert_fusion.3 = bf16[2048,1024]{1,0:T(8,128)(2,1)} fusion(bf16[4096,2048]{1,0:T(8,128)(2,1)} %get-tuple-element.100, bf16[4096,1024]{1,0:T(8,128)(2,1)} %get-tuple-element.112.dup_ref), kind=kOutput, calls=%fused_computation.26 | convolution fusion | flops 17181966336 | bytes 29360128 | tf_op jit(solution)/shard_map/dot_general | solution.py:40
  530.7 0.0 reduce-scatter.11.cloned.1.call-start
  530.7 93.0 %shard_map.207 = (f32[512,2048]{1,0:T(8,128)}, bf16[512,2048]{1,0:T(8,128)(2,1)}, f32[16,2048]{1,0:T(8,128)}) custom-call(f32[1,2048]{1,0:T(1,128)} %bitcast.77, f32[512,2048]{1,0:T(8,128)} %copy-done.1, bf16[512,2048]{1,0:T(8,128)(2,1)} %bitcast.84, bf16[4096,1024]{1,0:T(8,128)(2,1)} %get-tuple-element.101.dgate_ref, ...), custom_call_target="tpu_custom_call" | custom-call | flops 120000004096 | bytes 4194304 | tf_op jit(solution)/shard_map/pallas_call | solution.py:1098
  623.8 10.1 %convolution_convert_fusion.5.do_ref = bf16[512,2048]{1,0:T(8,128)(2,1)} fusion(bf16[512,2048]{1,0:T(8,128)(2,1)} %get-tuple-element.115, bf16[2048,2048]{1,0:T(8,128)(2,1)} %get-tuple-element.82), kind=kOutput, calls=%fused_computation.28 | convolution fusion | flops 4296015872 | bytes 12582912 | tf_op jit(solution)/shard_map/dot_general | solution.py:32
  633.8 6.8 convolution_convert_fusion
  640.7 0.8 copy-done.5
  641.6 0.6 pad_maximum_fusion.3.gain_ref
  642.2 0.1 copy-done.15
  642.3 8.8 %fusion.13 = bf16[1,512,2048]{2,1,0:T(8,128)(2,1)} fusion(f32[512,2048]{1,0:T(8,128)} %copy-done.1, bf16[2048,2048]{1,0:T(8,128)(2,1)} %collective-permute-done, bf16[256,2048]{1,0:T(8,128)(2,1)S(1)} %copy-done.13, bf16[256,2048]{1,0:T(8,128)(2,1)S(1)} %collective-permute-done.5, bf16[256,2048]{1,0:T(8,128)(2,1)} %collective-permute-done.6, ...), kind=kOutput, calls=%fused_computation.29 | convolution fusion | flops 2164260864 | bytes 17825792 | tf_op jit(solution)/shard_map/dot_general | solution.py:36
  651.1 101.7 %shard_map.208 = (bf16[512,2048]{1,0:T(8,128)(2,1)}, bf16[512,1024]{1,0:T(8,128)(2,1)}, bf16[256,2048]{1,0:T(8,128)(2,1)}, bf16[256,2048]{1,0:T(8,128)(2,1)}, bf16[256,2048]{1,0:T(8,128)(2,1)}) custom-call(bf16[512,2048]{1,0:T(8,128)(2,1)} %get-tuple-element.78.q_ref, bf16[512,2048]{1,0:T(8,128)(2,1)} %convolution_convert_fusion.5.do_ref, ...), custom_call_target="tpu_custom_call" | custom-call | flops 53687091200 | bytes 14680064 | tf_op jit(solution)/shard_map/pallas_call | solution.py:319
  752.9 2.9 convert_element_type.150
  755.8 2.8 convert_element_type.151
  758.5 1.6 convert_element_type.152
  760.1 86.5 %shard_map.209 = (f32[256,512]{1,0:T(8,128)}, f32[256,256]{1,0:T(8,128)}, f32[256,512]{1,0:T(8,128)}, f32[2,2048]{1,0:T(2,128)}, bf16[512,2048]{1,0:T(8,128)(2,1)}) custom-call(bf16[512,2048]{1,0:T(8,128)(2,1)} %fusion.10.x_ref, bf16[512,2048]{1,0:T(8,128)(2,1)} %get-tuple-element.125.dq_ref, bf16[512,1024]{1,0:T(8,128)(2,1)} %get-tuple-element.126.dkv_ref, ...), custom_call_target="tpu_custom_call" | custom-call | flops 1000000 | tf_op jit(solution)/shard_map/pallas_call | solution.py:1313
  846.6 1.8 fusion.46
  848.4 1.4 fusion.47
  849.8 3.2 copy.29
  852.9 0.8 copy.30
  853.7 0.8 copy.31
  (56 shorter events, 0.3 us)
Async XLA Ops:
  7.2 256.2 %all-gather.4.cloned.1.call-start = ((), (), s32[]{:S(2)}) async-start(), calls=%async_computation.4 | async-start | bytes 5242880 | tf_op jit(solution)/shard_map/all_gather | solution.py:1450
  8.8 63.7 %copy-start.8 = (s32[1,2048]{1,0:T(1,128)S(1)}, s32[1,2048]{1,0:T(1,128)}, u32[]{:S(2)}) copy-start(s32[1,2048]{1,0:T(1,128)} %param.13) | copy-start | bytes 24580
  70.9 1.8 copy-start
  70.9 4.0 copy-start.6
  70.9 199.8 %all-gather.6.cloned.1.call-start = ((), (), s32[]{:S(2)}) async-start(), calls=%async_computation.5 | async-start | bytes 5242880 | tf_op jit(solution)/shard_map/all_gather | solution.py:1450
  71.7 287.6 %all-gather.8.cloned.1.call-start = ((), (), s32[]{:S(2)}) async-start(), calls=%async_computation.6 | async-start | bytes 5242880 | tf_op jit(solution)/shard_map/all_gather | solution.py:1450
  72.4 551.3 %reduce-scatter.5.cloned.1.call-start = ((), (), s32[]{:S(2)}) async-start(), calls=%async_computation.7 | async-start | bytes 5242880 | tf_op jit(solution)/shard_map/reduce_scatter | solution.py:1455
  251.8 9.9 %copy-start.9 = (f32[2048]{0:T(1024)S(1)}, f32[2048]{0:T(1024)}, u32[]{:S(2)}) copy-start(f32[2048]{0:T(1024)} %param.19) | copy-start | bytes 24580
  259.7 2.0 copy-start.1
  359.3 14.4 %copy-start.10 = (bf16[4096,1024]{1,0:T(8,128)(2,1)S(1)}, bf16[4096,1024]{1,0:T(8,128)(2,1)}, u32[]{:S(2)}) copy-start(bf16[4096,1024]{1,0:T(8,128)(2,1)} %get-tuple-element.114) | copy-start | bytes 25165828
  373.7 27.8 %collective-permute-start = (bf16[2048,2048]{1,0:T(8,128)(2,1)}, bf16[2048,2048]{1,0:T(8,128)(2,1)}, u32[]{:S(2)}, u32[]{:S(2)}) collective-permute-start(bf16[2048,2048]{1,0:T(8,128)(2,1)} %convolution_convert_fusion.1), channel_id=1, source_target_pairs={{0,4},{4,0},{8,12},{12,8},{16,20},{20,16},{24,28},{28,24},{1,5},{5... | collective-permute-start | bytes 25165832 | tf_op jit(solution)/shard_map/ppermute | solution.py:1404
  395.2 245.4 %reduce-scatter.7.cloned.1.call-start = ((), (), s32[]{:S(2)}) async-start(), calls=%async_computation.8 | async-start | bytes 5242880 | tf_op jit(solution)/shard_map/reduce_scatter | solution.py:1455
  395.3 3.8 copy-start.11
  416.4 35.8 %collective-permute-start.1 = (bf16[256,2048]{1,0:T(8,128)(2,1)}, bf16[256,2048]{1,0:T(8,128)(2,1)S(1)}, u32[]{:S(2)}, u32[]{:S(2)}) collective-permute-start(bf16[256,2048]{1,0:T(8,128)(2,1)} %add_convert_fusion.7), channel_id=1, source_target_pairs={{0,8},{4,12},{8,0},{12,4},{16,24},{20,28},{24,16},{28,20},{1,9},{5... | collective-permute-start | bytes 3145736 | tf_op jit(solution)/shard_map/ppermute | solution.py:1404
  417.3 34.8 %collective-permute-start.2 = (bf16[256,2048]{1,0:T(8,128)(2,1)}, bf16[256,2048]{1,0:T(8,128)(2,1)S(1)}, u32[]{:S(2)}, u32[]{:S(2)}) collective-permute-start(bf16[256,2048]{1,0:T(8,128)(2,1)} %add_convert_fusion.6), channel_id=1, source_target_pairs={{0,16},{4,20},{8,24},{12,28},{16,0},{20,4},{24,8},{28,12},{1,17},{... | collective-permute-start | bytes 3145736 | tf_op jit(solution)/shard_map/ppermute | solution.py:1404
  452.1 4.0 copy-start.19
  477.4 2.2 copy-start.16
  477.4 173.7 %reduce-scatter.9.cloned.1.call-start = ((), (), s32[]{:S(2)}) async-start(), calls=%async_computation.9 | async-start | bytes 5242880 | tf_op jit(solution)/shard_map/reduce_scatter | solution.py:1455
  477.5 25.6 %collective-permute-start.3 = (bf16[256,2048]{1,0:T(8,128)(2,1)}, bf16[256,2048]{1,0:T(8,128)(2,1)S(1)}, u32[]{:S(2)}, u32[]{:S(2)}) collective-permute-start(bf16[256,2048]{1,0:T(8,128)(2,1)} %add_convert_fusion.5), channel_id=1, source_target_pairs={{0,8},{4,12},{8,0},{12,4},{16,24},{20,28},{24,16},{28,20},{1,9},{5... | collective-permute-start | bytes 3145736 | tf_op jit(solution)/shard_map/ppermute | solution.py:1404
  479.6 24.7 %collective-permute-start.4 = (bf16[256,2048]{1,0:T(8,128)(2,1)S(1)}, bf16[256,2048]{1,0:T(8,128)(2,1)S(1)}, u32[]{:S(2)}, u32[]{:S(2)}) collective-permute-start(bf16[256,2048]{1,0:T(8,128)(2,1)S(1)} %copy-done.16), channel_id=1, source_target_pairs={{0,16},{4,20},{8,24},{12,28},{16,0},{20,4},{24,8},{28,12},{1,17},{... | collective-permute-start | bytes 3145736 | tf_op jit(solution)/shard_map/ppermute | solution.py:1404
  503.0 2.6 copy-start.12
  504.3 1.4 copy-start.14
  504.3 26.4 %collective-permute-start.5 = (bf16[256,2048]{1,0:T(8,128)(2,1)S(1)}, bf16[256,2048]{1,0:T(8,128)(2,1)S(1)}, u32[]{:S(2)}, u32[]{:S(2)}) collective-permute-start(bf16[256,2048]{1,0:T(8,128)(2,1)S(1)} %get-tuple-element.106), channel_id=1, source_target_pairs={{0,8},{4,12},{8,0},{12,4},{16,24},{20,28},{24,16},{28,20},{1,9},{5... | collective-permute-start | bytes 3145736 | tf_op jit(solution)/shard_map/ppermute | solution.py:1404
  505.6 25.1 %collective-permute-start.6 = (bf16[256,2048]{1,0:T(8,128)(2,1)S(1)}, bf16[256,2048]{1,0:T(8,128)(2,1)}, u32[]{:S(2)}, u32[]{:S(2)}) collective-permute-start(bf16[256,2048]{1,0:T(8,128)(2,1)S(1)} %get-tuple-element.107), channel_id=1, source_target_pairs={{0,16},{4,20},{8,24},{12,28},{16,0},{20,4},{24,8},{28,12},{1,17},{... | collective-permute-start | bytes 3145736 | tf_op jit(solution)/shard_map/ppermute | solution.py:1404
  530.7 229.4 %reduce-scatter.11.cloned.1.call-start = ((), (), s32[]{:S(2)}) async-start(), calls=%async_computation.10 | async-start | bytes 9437184 | tf_op jit(solution)/shard_map/reduce_scatter | solution.py:1415
  623.8 10.1 %copy-start.17 = (bf16[512,2048]{1,0:T(8,128)(2,1)S(1)}, bf16[512,2048]{1,0:T(8,128)(2,1)}, u32[]{:S(2)}) copy-start(bf16[512,2048]{1,0:T(8,128)(2,1)} %get-tuple-element.81.o_ref) | copy-start | bytes 6291460
  623.8 10.1 %copy-start.18 = (bf16[512,2048]{1,0:T(8,128)(2,1)S(1)}, bf16[512,2048]{1,0:T(8,128)(2,1)}, u32[]{:S(2)}) copy-start(bf16[512,2048]{1,0:T(8,128)(2,1)} %get-tuple-element.115) | copy-start | bytes 6291460
  640.6 0.9 copy-start.5
  640.6 0.9 copy-start.7
  640.6 1.6 copy-start.13
  640.6 1.6 copy-start.15
  752.9 5.7 copy-start.2
  846.6 6.4 copy-start.4
  846.6 7.1 copy-start.3
Sparse Core Ops, SparseCore 0:
  71.1 98.2 all-gather.3
  170.9 99.7 all-gather.5
  272.3 78.7 all-gather.7
  395.4 79.8 reduce-scatter.4
  477.5 81.2 reduce-scatter.6
  561.0 77.2 reduce-scatter.8
  642.1 95.6 reduce-scatter.10

commit v11 on v10

--- a/solution.py
+++ b/solution.py
@@ -1129,11 +1129,13 @@
 ):
     wq_out, wkv_out, wo_out, gain_out, grad_out = refs[:5]
     scratch = refs[5:]
-    own_scratch = scratch[:12]
-    sums, zrecv, gain_z, gain_p, z_send, z_recv, g_send, g_recv = scratch[12:20]
-    wo_recv, w_send, w_recv = scratch[20:23]
-    wq_all, wkv_all, raw, dh, dxn, gain_sum, load_sem = scratch[23:]
-    rings = [Reduce(wide, *own_scratch[6 * at : 6 * at + 6]) for at in range(2)]
+    sub = wkv_out.shape[1]
+    halves = wq_out.shape[1] // sub
+    count = halves + 1
+    rings = [Reduce(wide, *scratch[6 * at : 6 * at + 6]) for at in range(count)]
+    sums, zrecv, gain_z, gain_p, z_send, z_recv, g_send, g_recv = scratch[6 * count : 6 * count + 8]
+    wo_recv, w_send, w_recv = scratch[6 * count + 8 : 6 * count + 11]
+    wq_all, wkv_all, raw, dh, dxn, gain_sum, load_sem = scratch[6 * count + 11 :]
     place = lax.axis_index("tensor")
     mine, found = others(wide)
     along = along_peers(place, z_size)
@@ -1169,24 +1171,24 @@
     for copy in wo_copies:
         copy.start()
 
-    rights = (dq_ref, dkv_ref)
-    rows = sums.shape[0]
-    outs = (wq_out, wkv_out)
-    starts = [0, rights[0].shape[1]]
+    pieces = [(dq_ref, wq_out, at * sub) for at in range(halves)] + [(dkv_ref, wkv_out, 0)]
+    rows = sums.shape[1]
     z_copies = []
 
     def partial_sums(index):
-        ring, right = rings[index], rights[index]
+        ring = rings[index]
+        right, out, offset = pieces[index]
 
         @pl.loop(0, 8)
         def _(step):
             chunk, target = ring.chunk(step)
             x = x_ref[:, pl.ds(pl.multiple_of(chunk * rows, rows), rows)].T
 
-            @pl.loop(0, right.shape[1] // NTILE)
+            @pl.loop(0, z_size)
             def _(at):
-                n = pl.ds(pl.multiple_of(at * NTILE, NTILE), NTILE)
-                target[:, n] = dot_nn(x, right[:, n]).astype(BF16)
+                n = pl.ds(pl.multiple_of(at * sub, LANES), sub)
+                source = pl.ds(pl.multiple_of(at * out.shape[1] + offset, LANES), sub)
+                target[:, n] = dot_nn(x, right[:, source]).astype(BF16)
 
             ring.after(step)
 
@@ -1214,19 +1216,15 @@
             grad_out[there, :] = (dh[tile, here, :] + total).astype(BF16)
 
     def send_along(index):
-        ring, start = rings[index], starts[index]
-        cols = rights[index].shape[1]
-        part = cols // z_size
-
         def store(here, value):
-            sums[here, pl.ds(start, cols)] = value.astype(BF16)
-
-        ring.finish(store)
+            sums[index, here, :] = value.astype(BF16)
+
+        rings[index].finish(store)
         for at, peer in enumerate(along):
             other = (place + at + 1) % z_size
             copy = pltpu.make_async_remote_copy(
-                src_ref=sums.at[:, pl.ds(pl.multiple_of(start + other * part, LANES), part)],
-                dst_ref=zrecv.at[at, :, pl.ds(start // z_size, part)],
+                src_ref=sums.at[index, :, pl.ds(pl.multiple_of(other * sub, LANES), sub)],
+                dst_ref=zrecv.at[index, at],
                 send_sem=z_send.at[index, at], recv_sem=z_recv.at[index, at],
                 device_id=peer, device_id_type=MESH,
             )
@@ -1238,8 +1236,14 @@
         copy.wait()
     input_rows(0)
     rings[0].pass_on()
-    partial_sums(1)
-    for tile in range(1, tiles):
+    for index in range(1, count):
+        partial_sums(index)
+        if index < tiles:
+            input_rows(index)
+        if index + 1 < count:
+            rings[index].pass_on()
+            send_along(index - 1)
+    for tile in range(count, tiles):
         input_rows(tile)
 
     gain_z[place, 0:1] = jnp.sum(gain_sum[...], axis=0, keepdims=True)
@@ -1253,8 +1257,8 @@
     ]
     for copy in gain_copies:
         copy.start()
-    rings[1].pass_on()
-    send_along(0)
+    rings[count - 1].pass_on()
+    send_along(count - 2)
 
     for copy in gain_copies:
         copy.wait_recv()
@@ -1276,7 +1280,7 @@
     for at in range(z_size - 1):
         total += wo_recv[at].astype(F32)
     wo_out[...] = total
-    send_along(1)
+    send_along(count - 1)
 
     for copy in gain_copies[z_size - 1 :]:
         copy.wait_recv()
@@ -1286,13 +1290,11 @@
     gain_out[...] = total
     for copy in z_copies:
         copy.wait_recv()
-    for index in range(2):
-        part = rights[index].shape[1] // z_size
-        own = pl.ds(pl.multiple_of(starts[index] + place * part, LANES), part)
-        value = sums[:, own].astype(F32)
+    for index, (_, out, offset) in enumerate(pieces):
+        value = sums[index, :, pl.ds(pl.multiple_of(place * sub, LANES), sub)].astype(F32)
         for at in range(z_size - 1):
-            value += zrecv[at, :, pl.ds(starts[index] // z_size, part)].astype(F32)
-        outs[index][...] = value
+            value += zrecv[index, at].astype(F32)
+        out[:, offset : offset + sub] = value
     for copy in z_copies + gain_copies:
         copy.wait_send()
     for ring in rings:
@@ -1306,15 +1308,16 @@
     near = pl.BlockSpec(memory_space=pltpu.VMEM)
     far = pl.BlockSpec(memory_space=pl.ANY)
     sizes = [dq.shape[1], dkv.shape[1]]
+    cols = dkv.shape[1]
+    count = sum(sizes) // cols
     scratch = []
-    for cols in sizes:
+    for _ in range(count):
         scratch += Reduce.scratch(rows, cols)
-    total = sum(sizes)
     return pl.pallas_call(
         functools.partial(tail_kernel, 2 * math.isqrt(dp_size // GROUP), z_size),
         in_specs=[near] * 5 + [far] * 4,
         out_specs=[near] * 5,
-        out_shape=[jax.ShapeDtypeStruct((rows, cols // z_size), F32) for cols in sizes]
+        out_shape=[jax.ShapeDtypeStruct((rows, size // z_size), F32) for size in sizes]
         + [
             jax.ShapeDtypeStruct((rows, wo_sum.shape[1] // z_size), F32),
             jax.ShapeDtypeStruct(gains.shape, F32),
@@ -1322,12 +1325,12 @@
         ],
         scratch_shapes=scratch
         + [
-            pltpu.VMEM((rows, total), BF16),
-            pltpu.VMEM((z_size - 1, rows, total // z_size), BF16),
+            pltpu.VMEM((count, rows, cols), BF16),
+            pltpu.VMEM((count, z_size - 1, rows, cols // z_size), BF16),
             pltpu.VMEM((z_size, *gains.shape), F32),
             pltpu.VMEM((GROUP, *gains.shape), F32),
-            pltpu.SemaphoreType.DMA((2, z_size - 1)),
-            pltpu.SemaphoreType.DMA((2, z_size - 1)),
+            pltpu.SemaphoreType.DMA((count, z_size - 1)),
+            pltpu.SemaphoreType.DMA((count, z_size - 1)),
             pltpu.SemaphoreType.DMA((z_size - 1 + GROUP - 1,)),
             pltpu.SemaphoreType.DMA((z_size - 1 + GROUP - 1,)),
             pltpu.VMEM((z_size - 1, rows, wo_sum.shape[1] // z_size), BF16),
@@ -1498,8 +1501,8 @@
     dgate, dup, x_upper, y_lower = lax.optimization_barrier((dgate, dup, x_upper, y_lower))
     x_upper, y_lower = layout.swap(x_upper, 2), layout.swap(y_lower, 4)
     total_wg = dot_tn(hn, dgate).astype(BF16)
+    dup, total_wg, x_lower, y_upper = lax.optimization_barrier((dup, total_wg, x_lower, y_upper))
     part_wg = along_z(total_wg)
-    dup, total_wg, x_lower, y_upper = lax.optimization_barrier((dup, total_wg, x_lower, y_upper))
     total_wu = dot_tn(hn, dup).astype(BF16)
     dup, total_wu = lax.optimization_barrier((dup, total_wu))
     part_wu = along_z(total_wu)

time: 866 us -> 845 us (0.976)
  waiting for transfers between devices: 32.7 us -> 21.8 us
  Pallas kernels: 605 us -> 596 us
    ppermute x7, waiting for transfers between devices: 23.7 us -> 0.02 us  [swap(): return lax.ppermute(array, 'dp', pairs)]
    reduce_scatter x3, waiting for transfers between devices: 0.04 us -> 13 us  [along_z(): lax.psum_scatter(layout.from_rows(total), 'tensor', scatter_dimension=1,...]
  transfers between devices with their start and end apart: 14 -> 14, of which waited for: 3 -> 2; matrix products, arithmetic and copies ran while one was open for 20% -> 21% of each run, Pallas kernels for 53% -> 54%
where the time goes in v11:
time: 845 us; the launch traced here: 840 us
  Pallas kernels  596 us (71%)
  matrix products  171 us (20%)
  waiting for transfers between devices  21.8 us (3%)
  other arithmetic  19.4 us (2%)
  between operations  14.9 us (2%)
  local copies, waits for them, and re-layouts  12.1 us (1%)
    pallas_call x1, Pallas kernels, project(): pl.pallas_call(functools.partial(project_kernel, 2 * math.isqrt(dp_size /...  107 us
    pallas_call x1, Pallas kernels, attend_back(): pl.pallas_call(functools.partial(attend_back_kernel, reach, 2 * math.isqr...  99 us
    pallas_call x1, Pallas kernels, hidden_back(): pl.pallas_call(functools.partial(hidden_back_kernel, 2 * math.isqrt(dp_si...  93.8 us
    pallas_call x1, Pallas kernels, gate_up(): pl.pallas_call(functools.partial(gate_up_kernel, 2 * math.isqrt(dp_size /...  88.5 us
    pallas_call x1, Pallas kernels, last_grads(): pl.pallas_call(functools.partial(tail_kernel, 2 * math.isqrt(dp_size // G...  78.4 us
    dot_general x4, matrix products, dot_tn(): lax.dot_general(left, right, (((0,), (0,)), ((), ())), preferred_element_...  73.5 us
    pallas_call x1, Pallas kernels, attend(): pl.pallas_call(functools.partial(attend_kernel, reach, 2 * math.isqrt(dp_...  66.9 us
    pallas_call x1, Pallas kernels, spread_weights(): pl.pallas_call(functools.partial(spread_kernel, 2 * math.isqrt(dp_size //...  62.1 us
  transfers between devices with their start and end apart: 14, of which 2 were waited for; matrix products, arithmetic and copies ran while one was open for 21% of the time, Pallas kernels for 54%

profile of v11, /device:TPU:0, one launch (start us, length us, event | category | flops | bytes accessed | tf_op | source)
XLA Modules:
  0.0 840.4 jit_solution(8740209687834460603)
XLA Ops:
  7.2 0.0 all-gather.4.cloned.1.call-start
  7.2 1.5 pad_maximum_fusion.2.refs_3_
  8.8 62.1 %shard_map.203 = (bf16[2048,256]{1,0:T(8,128)(2,1)}, bf16[2048,256]{1,0:T(8,128)(2,1)}, bf16[2048,256]{1,0:T(8,128)(2,1)}, bf16[2048,1024]{1,0:T(8,128)(2,1)}, b...) custom-call(bf16[256,2048]{1,0:T(8,128)(2,1)} %refs_0_.1, bf16[256,2048]{1,0:T(8,128)(2,1)} %refs_1_.1, ...), custom_call_target="tpu_custom_call" | custom-call | flops 60000002048 | tf_op jit(solution)/shard_map/pallas_call | solution.py:546
  70.9 0.0 all-gather.6.cloned.1.call-start
  71.0 0.7 all-gather.6.cloned.1.call-update
  71.7 0.0 all-gather.8.cloned.1.call-start
  71.7 0.7 all-gather.8.cloned.1.call-update
  72.4 0.0 reduce-scatter.5.cloned.1.call-start
  72.5 0.1 convert_reduce_fusion
  72.6 0.1 select_reduce_fusion
  72.8 0.5 fusion.8
  73.2 0.7 subtract_add_fusion
  73.9 1.0 fusion.45
  74.9 1.9 fusion.10.x_ref
  76.8 1.3 pad_maximum_fusion
  78.0 106.9 %shard_map.204 = (bf16[512,2048]{1,0:T(8,128)(2,1)}, bf16[1536,1024]{1,0:T(8,128)(2,1)}, bf16[2048,2048]{1,0:T(8,128)(2,1)}, bf16[2048,2048]{1,0:T(8,128)(2,1)}, bf16[4096,2048]{1,0:T(8,128)(2,1)}) custom-call(bf16[512,2048]{1,0:T(8,128)(2,1)} %fusion.10.x_ref, f32[512,128]{1,0:T(8,128)} %get-tuple-element.156.cos_ref.cos_all, ...), custom_call_target="tpu_custom_call" | custom-call | flops 120000004096 | tf_op jit(solution)/shard_map/pallas_call | solution.py:758
  184.9 66.9 %shard_map.205 = (bf16[512,2048]{1,0:T(8,128)(2,1)}, f32[32,1,512]{2,1,0:T(1,128)}, bf16[4096,2048]{1,0:T(8,128)(2,1)}) custom-call(bf16[512,2048]{1,0:T(8,128)(2,1)} %get-tuple-element.79.q_ref, bf16[1536,1024]{1,0:T(8,128)(2,1)} %get-tuple-element.80.k_ref.v_ref, ...), custom_call_target="tpu_custom_call", output_to_operand_aliasing={{2}: (5, {})} | custom-call | flops 21474836480 | bytes 7340032 | tf_op jit(solution)/shard_map/pallas_call | solution.py:164
  251.9 7.9 multiply_reduce_fusion
  259.8 2.0 copy-done.1
  261.7 1.7 multiply_convert_fusion.own_ref
  263.5 7.3 all-gather.6.cloned.1.call-done.wu_ref
  270.7 88.5 %shard_map.206 = (bf16[4096,2048]{1,0:T(8,128)(2,1)}, bf16[4096,1024]{1,0:T(8,128)(2,1)}, bf16[4096,1024]{1,0:T(8,128)(2,1)}, bf16[4096,1024]{1,0:T(8,128)(2,1)}, bf16[2,2048,1024]{2,1,0:T(8,128)(2,1)}) custom-call(bf16[512,2048]{1,0:T(8,128)(2,1)} %multiply_convert_fusion.own_ref, bf16[2048,1024]{1,0:T(8,128)(2,1)} %all-gather.4.cloned.1.call-done.wg_ref, ...), custom_call_target="tpu_custom_call" | custom-call | flops 1000000 | tf_op jit(solution)/shard_map/pallas_call | solution.py:878
  359.2 0.0 all-gather.8.cloned.1.call-done
  359.3 14.5 %convolution_convert_fusion.1 = bf16[2048,2048]{1,0:T(8,128)(2,1)} fusion(bf16[2048,1024]{1,0:T(8,128)(2,1)} %all-gather.8.cloned.1.call-done, bf16[2,2048,1024]{2,1,0:T(8,128)(2,1)} %get-tuple-element.86), kind=kOutput, calls=%fused_computation.12 | convolution fusion | flops 8594128896 | bytes 16777216 | tf_op jit(solution)/shard_map/dot_general | solution.py:36
  373.8 0.1 collective-permute-start
  373.9 21.5 %convolution_convert_fusion.2 = bf16[2048,1024]{1,0:T(8,128)(2,1)} fusion(bf16[4096,2048]{1,0:T(8,128)(2,1)} %get-tuple-element.91, bf16[4096,1024]{1,0:T(8,128)(2,1)S(1)} %copy-done.10), kind=kOutput, calls=%fused_computation.25 | convolution fusion | flops 17181966336 | bytes 29360128 | tf_op jit(solution)/shard_map/dot_general | solution.py:40
  395.4 0.0 reduce-scatter.7.cloned.1.call-start
  395.5 3.8 fusion.19
  399.3 2.4 fusion.21
  401.7 3.7 add_convert_fusion.4
  405.4 3.8 add_convert_fusion.5
  409.1 3.7 add_convert_fusion.6
  412.8 3.7 add_convert_fusion.7
  416.5 0.9 collective-permute-start.1
  417.4 0.1 collective-permute-start.2
  417.6 2.0 collective-permute-start.3
  419.6 1.0 collective-permute-start.4
  420.6 34.5 %fusion.7 = (bf16[4096,1024]{1,0:T(8,128)(2,1)}, bf16[4096,1024]{1,0:T(8,128)(2,1)}) fusion(bf16[4096,1024]{1,0:T(8,128)(2,1)} %get-tuple-element.93, bf16[4096,1024]{1,0:T(8,128)(2,1)} %get-tuple-element.92, bf16[4096,2048]{1,0:T(8,128)(2,1)} %get-tuple-element.91, bf16[2048,1024]{1,0:T(8,128)(2,1)S(1)} %copy-done.11), kind=kOutput, calls=%fused_computation.10 | convolution fusion | flops 17242783744 | bytes 54525952 | tf_op jit(solution)/shard_map/dot_general | solution.py:32
  455.2 2.8 add_convert_fusion.2
  457.9 1.2 copy-done.14
  459.2 21.2 %convolution_convert_fusion.4 = bf16[2048,1024]{1,0:T(8,128)(2,1)} fusion(bf16[4096,2048]{1,0:T(8,128)(2,1)} %get-tuple-element.101, bf16[4096,1024]{1,0:T(8,128)(2,1)S(1)} %copy-done.14), kind=kOutput, calls=%fused_computation.27 | convolution fusion | flops 17181966336 | bytes 29360128 | tf_op jit(solution)/shard_map/dot_general | solution.py:40
  480.4 0.0 reduce-scatter.9.cloned.1.call-start
  480.5 1.0 collective-permute-start.5
  481.5 0.2 collective-permute-start.6
  481.7 24.0 %convolution_convert_fusion.3 = bf16[2048,1024]{1,0:T(8,128)(2,1)} fusion(bf16[4096,2048]{1,0:T(8,128)(2,1)} %get-tuple-element.101, bf16[4096,1024]{1,0:T(8,128)(2,1)} %get-tuple-element.113.dup_ref), kind=kOutput, calls=%fused_computation.26 | convolution fusion | flops 17181966336 | bytes 29360128 | tf_op jit(solution)/shard_map/dot_general | solution.py:40
  505.7 0.0 reduce-scatter.11.cloned.1.call-start
  505.8 93.8 %shard_map.207 = (f32[512,2048]{1,0:T(8,128)}, bf16[512,2048]{1,0:T(8,128)(2,1)}, f32[16,2048]{1,0:T(8,128)}) custom-call(f32[1,2048]{1,0:T(1,128)} %bitcast.77, f32[512,2048]{1,0:T(8,128)} %copy-done.1, bf16[512,2048]{1,0:T(8,128)(2,1)} %bitcast.84, bf16[4096,1024]{1,0:T(8,128)(2,1)} %get-tuple-element.102.dgate_ref, ...), custom_call_target="tpu_custom_call" | custom-call | flops 120000004096 | bytes 4194304 | tf_op jit(solution)/shard_map/pallas_call | solution.py:1098
  599.6 0.0 reduce-scatter.5.cloned.1.call-done.refs_0_
  599.7 10.0 %convolution_convert_fusion.5.do_ref = bf16[512,2048]{1,0:T(8,128)(2,1)} fusion(bf16[512,2048]{1,0:T(8,128)(2,1)} %get-tuple-element.116, bf16[2048,2048]{1,0:T(8,128)(2,1)} %get-tuple-element.83), kind=kOutput, calls=%fused_computation.28 | convolution fusion | flops 4296015872 | bytes 12582912 | tf_op jit(solution)/shard_map/dot_general | solution.py:32
  609.7 6.8 convolution_convert_fusion
  616.5 0.9 copy-done.5
  617.4 0.6 pad_maximum_fusion.3.gain_ref
  618.0 9.5 %fusion.13 = bf16[1,512,2048]{2,1,0:T(8,128)(2,1)} fusion(f32[512,2048]{1,0:T(8,128)} %copy-done.1, bf16[2048,2048]{1,0:T(8,128)(2,1)} %collective-permute-done, bf16[256,2048]{1,0:T(8,128)(2,1)} %collective-permute-done.3, bf16[256,2048]{1,0:T(8,128)(2,1)S(1)} %collective-permute-done.5, bf16[256,2048]{1,0:T(8,128)(2,1)} %collective-permute-done.6, ...), kind=kOutput, calls=%fused_computation.29 | convolution fusion | flops 2164260864 | bytes 17825792 | tf_op jit(solution)/shard_map/dot_general | solution.py:36
  627.5 13.0 %reduce-scatter.9.cloned.1.call-done.refs_2_ = bf16[2048,256]{1,0:T(8,128)(2,1)} async-done(((bf16[2048,1024]{1,0:T(8,128)(2,1)}), bf16[2048,256]{1,0:T(8,128)(2,1)}) %reduce-scatter.9.cloned.1.call-update) | async-done | bytes 1048592 | tf_op jit(solution)/shard_map/reduce_scatter | solution.py:1458
  640.5 99.0 %shard_map.208 = (bf16[512,2048]{1,0:T(8,128)(2,1)}, bf16[512,1024]{1,0:T(8,128)(2,1)}, bf16[256,2048]{1,0:T(8,128)(2,1)}, bf16[256,2048]{1,0:T(8,128)(2,1)}, bf16[256,2048]{1,0:T(8,128)(2,1)}) custom-call(bf16[512,2048]{1,0:T(8,128)(2,1)} %get-tuple-element.79.q_ref, bf16[512,2048]{1,0:T(8,128)(2,1)} %convolution_convert_fusion.5.do_ref, ...), custom_call_target="tpu_custom_call" | custom-call | flops 53687091200 | bytes 14680064 | tf_op jit(solution)/shard_map/pallas_call | solution.py:319
  739.5 2.9 convert_element_type.150
  742.4 2.8 convert_element_type.151
  745.2 1.6 convert_element_type.152
  746.7 78.4 %shard_map.209 = (f32[256,512]{1,0:T(8,128)}, f32[256,256]{1,0:T(8,128)}, f32[256,512]{1,0:T(8,128)}, f32[2,2048]{1,0:T(2,128)}, bf16[512,2048]{1,0:T(8,128)(2,1)}) custom-call(bf16[512,2048]{1,0:T(8,128)(2,1)} %fusion.10.x_ref, bf16[512,2048]{1,0:T(8,128)(2,1)} %get-tuple-element.127.dq_ref, bf16[512,1024]{1,0:T(8,128)(2,1)} %get-tuple-element.128.dkv_ref, ...), custom_call_target="tpu_custom_call" | custom-call | flops 1000000 | tf_op jit(solution)/shard_map/pallas_call | solution.py:1316
  825.2 1.8 fusion.46
  827.0 1.4 fusion.47
  828.4 3.2 copy.29
  831.5 0.8 copy.30
  832.3 0.8 copy.31
  (46 shorter events, 0.2 us)
Async XLA Ops:
  7.2 256.3 %all-gather.4.cloned.1.call-start = ((), (), s32[]{:S(2)}) async-start(), calls=%async_computation.4 | async-start | bytes 5242880 | tf_op jit(solution)/shard_map/all_gather | solution.py:1453
  8.8 63.7 %copy-start.8 = (s32[1,2048]{1,0:T(1,128)S(1)}, s32[1,2048]{1,0:T(1,128)}, u32[]{:S(2)}) copy-start(s32[1,2048]{1,0:T(1,128)} %param.13) | copy-start | bytes 24580
  70.9 1.8 copy-start
  70.9 4.0 copy-start.6
  70.9 199.8 %all-gather.6.cloned.1.call-start = ((), (), s32[]{:S(2)}) async-start(), calls=%async_computation.5 | async-start | bytes 5242880 | tf_op jit(solution)/shard_map/all_gather | solution.py:1453
  71.7 287.6 %all-gather.8.cloned.1.call-start = ((), (), s32[]{:S(2)}) async-start(), calls=%async_computation.6 | async-start | bytes 5242880 | tf_op jit(solution)/shard_map/all_gather | solution.py:1453
  72.4 527.2 %reduce-scatter.5.cloned.1.call-start = ((), (), s32[]{:S(2)}) async-start(), calls=%async_computation.7 | async-start | bytes 5242880 | tf_op jit(solution)/shard_map/reduce_scatter | solution.py:1458
  251.8 9.9 %copy-start.9 = (f32[2048]{0:T(1024)S(1)}, f32[2048]{0:T(1024)}, u32[]{:S(2)}) copy-start(f32[2048]{0:T(1024)} %param.19) | copy-start | bytes 24580
  259.7 2.0 copy-start.1
  359.3 14.6 %copy-start.10 = (bf16[4096,1024]{1,0:T(8,128)(2,1)S(1)}, bf16[4096,1024]{1,0:T(8,128)(2,1)}, u32[]{:S(2)}) copy-start(bf16[4096,1024]{1,0:T(8,128)(2,1)} %get-tuple-element.115) | copy-start | bytes 25165828
  373.8 27.8 %collective-permute-start = (bf16[2048,2048]{1,0:T(8,128)(2,1)}, bf16[2048,2048]{1,0:T(8,128)(2,1)}, u32[]{:S(2)}, u32[]{:S(2)}) collective-permute-start(bf16[2048,2048]{1,0:T(8,128)(2,1)} %convolution_convert_fusion.1), channel_id=1, source_target_pairs={{0,4},{4,0},{8,12},{12,8},{16,20},{20,16},{24,28},{28,24},{1,5},{5... | collective-permute-start | bytes 25165832 | tf_op jit(solution)/shard_map/ppermute | solution.py:1407
  395.4 221.0 %reduce-scatter.7.cloned.1.call-start = ((), (), s32[]{:S(2)}) async-start(), calls=%async_computation.8 | async-start | bytes 5242880 | tf_op jit(solution)/shard_map/reduce_scatter | solution.py:1458
  395.5 3.8 copy-start.11
  416.5 38.6 %collective-permute-start.1 = (bf16[256,2048]{1,0:T(8,128)(2,1)}, bf16[256,2048]{1,0:T(8,128)(2,1)S(1)}, u32[]{:S(2)}, u32[]{:S(2)}) collective-permute-start(bf16[256,2048]{1,0:T(8,128)(2,1)} %add_convert_fusion.7), channel_id=1, source_target_pairs={{0,8},{4,12},{8,0},{12,4},{16,24},{20,28},{24,16},{28,20},{1,9},{5... | collective-permute-start | bytes 3145736 | tf_op jit(solution)/shard_map/ppermute | solution.py:1407
  417.4 37.7 %collective-permute-start.2 = (bf16[256,2048]{1,0:T(8,128)(2,1)}, bf16[256,2048]{1,0:T(8,128)(2,1)S(1)}, u32[]{:S(2)}, u32[]{:S(2)}) collective-permute-start(bf16[256,2048]{1,0:T(8,128)(2,1)} %add_convert_fusion.6), channel_id=1, source_target_pairs={{0,16},{4,20},{8,24},{12,28},{16,0},{20,4},{24,8},{28,12},{1,17},{... | collective-permute-start | bytes 3145736 | tf_op jit(solution)/shard_map/ppermute | solution.py:1407
  417.6 62.9 %collective-permute-start.3 = (bf16[256,2048]{1,0:T(8,128)(2,1)}, bf16[256,2048]{1,0:T(8,128)(2,1)}, u32[]{:S(2)}, u32[]{:S(2)}) collective-permute-start(bf16[256,2048]{1,0:T(8,128)(2,1)} %add_convert_fusion.5), channel_id=1, source_target_pairs={{0,8},{4,12},{8,0},{12,4},{16,24},{20,28},{24,16},{28,20},{1,9},{5... | collective-permute-start | bytes 3145736 | tf_op jit(solution)/shard_map/ppermute | solution.py:1407
  419.6 60.8 %collective-permute-start.4 = (bf16[256,2048]{1,0:T(8,128)(2,1)}, bf16[256,2048]{1,0:T(8,128)(2,1)}, u32[]{:S(2)}, u32[]{:S(2)}) collective-permute-start(bf16[256,2048]{1,0:T(8,128)(2,1)} %add_convert_fusion.4), channel_id=1, source_target_pairs={{0,16},{4,20},{8,24},{12,28},{16,0},{20,4},{24,8},{28,12},{1,17},{... | collective-permute-start | bytes 3145736 | tf_op jit(solution)/shard_map/ppermute | solution.py:1407
  455.1 4.0 copy-start.14
  480.4 160.0 %reduce-scatter.9.cloned.1.call-start = ((), (), s32[]{:S(2)}) async-start(), calls=%async_computation.9 | async-start | bytes 5242880 | tf_op jit(solution)/shard_map/reduce_scatter | solution.py:1458
  480.5 25.3 %collective-permute-start.5 = (bf16[256,2048]{1,0:T(8,128)(2,1)S(1)}, bf16[256,2048]{1,0:T(8,128)(2,1)S(1)}, u32[]{:S(2)}, u32[]{:S(2)}) collective-permute-start(bf16[256,2048]{1,0:T(8,128)(2,1)S(1)} %get-tuple-element.107), channel_id=1, source_target_pairs={{0,8},{4,12},{8,0},{12,4},{16,24},{20,28},{24,16},{28,20},{1,9},{5... | collective-permute-start | bytes 3145736 | tf_op jit(solution)/shard_map/ppermute | solution.py:1407
  481.5 24.3 %collective-permute-start.6 = (bf16[256,2048]{1,0:T(8,128)(2,1)S(1)}, bf16[256,2048]{1,0:T(8,128)(2,1)}, u32[]{:S(2)}, u32[]{:S(2)}) collective-permute-start(bf16[256,2048]{1,0:T(8,128)(2,1)S(1)} %get-tuple-element.108), channel_id=1, source_target_pairs={{0,16},{4,20},{8,24},{12,28},{16,0},{20,4},{24,8},{28,12},{1,17},{... | collective-permute-start | bytes 3145736 | tf_op jit(solution)/shard_map/ppermute | solution.py:1407
  505.7 241.0 %reduce-scatter.11.cloned.1.call-start = ((), (), s32[]{:S(2)}) async-start(), calls=%async_computation.10 | async-start | bytes 9437184 | tf_op jit(solution)/shard_map/reduce_scatter | solution.py:1418
  599.7 10.0 %copy-start.12 = (bf16[512,2048]{1,0:T(8,128)(2,1)S(1)}, bf16[512,2048]{1,0:T(8,128)(2,1)}, u32[]{:S(2)}) copy-start(bf16[512,2048]{1,0:T(8,128)(2,1)} %get-tuple-element.82.o_ref) | copy-start | bytes 6291460
  599.7 10.0 %copy-start.13 = (bf16[512,2048]{1,0:T(8,128)(2,1)S(1)}, bf16[512,2048]{1,0:T(8,128)(2,1)}, u32[]{:S(2)}) copy-start(bf16[512,2048]{1,0:T(8,128)(2,1)} %get-tuple-element.116) | copy-start | bytes 6291460
  616.5 0.9 copy-start.5
  616.5 0.9 copy-start.7
  739.5 5.7 copy-start.2
  825.2 6.4 copy-start.4
  825.2 7.1 copy-start.3
Sparse Core Ops, SparseCore 0:
  71.1 98.2 all-gather.3
  170.9 99.7 all-gather.5
  272.3 78.7 all-gather.7
  395.5 80.0 reduce-scatter.4
  480.6 80.3 reduce-scatter.6
  563.2 77.2 reduce-scatter.8
  644.3 79.5 reduce-scatter.10

commit v12 on v11

--- a/solution.py
+++ b/solution.py
@@ -446,11 +446,11 @@
 SIB, XN, YN = 0, 1, 2
 
 
-def spread_kernel(wide, z_size, mlp_count, *refs):
-    attn_count = (len(refs) - 7) // 2 - mlp_count
+def spread_kernel(wide, z_size, mlp_count, x_ref, gain_ref, *refs):
+    attn_count = (len(refs) - 8) // 2 - mlp_count
     count = mlp_count + attn_count
-    ins, outs = refs[:count], refs[count : 2 * count]
-    own_sem, send_sem, recv_sem, z_send, z_recv, ring_send, ring_recv = refs[2 * count :]
+    ins, xn_ref, outs = refs[:count], refs[count], refs[count + 1 : 2 * count + 1]
+    own_sem, send_sem, recv_sem, z_send, z_recv, ring_send, ring_recv = refs[2 * count + 1 :]
     first = mlp_count
     ring = Ring(wide, outs[first], ins[first].shape[0], ring_send, ring_recv)
     place = lax.axis_index("tensor")
@@ -504,6 +504,12 @@
             pl.when(sends(way, 1))(lambda: hop(at, way, 1).start())
     for copy in copies + local:
         copy.start()
+
+    @pl.loop(0, x_ref.shape[0] // STRIP)
+    def _(at):
+        here = pl.ds(pl.multiple_of(at * STRIP, STRIP), STRIP)
+        value = x_ref[here, :].astype(F32)
+        xn_ref[here, :] = (value * rms_scale(value) * gain_ref[...]).astype(BF16)
 
     def advance(at, step):
         for way in range(2):
@@ -535,18 +541,20 @@
         copy.wait()
 
 
-def spread_weights(mlp, attn, dp_size, z_size):
+def spread_weights(x, gain, mlp, attn, dp_size, z_size):
     count = len(mlp) + len(attn)
     spec = pl.BlockSpec(memory_space=pl.ANY)
-    out = [jax.ShapeDtypeStruct((GROUP * w.shape[0], w.shape[1] // GROUP), BF16) for w in mlp]
+    near = pl.BlockSpec(memory_space=pltpu.VMEM)
+    out = [jax.ShapeDtypeStruct(x.shape, BF16)]
+    out += [jax.ShapeDtypeStruct((GROUP * w.shape[0], w.shape[1] // GROUP), BF16) for w in mlp]
     out += [
         jax.ShapeDtypeStruct(((1 if at else GROUP) * w.shape[0], z_size * w.shape[1]), BF16)
         for at, w in enumerate(attn)
     ]
     return pl.pallas_call(
         functools.partial(spread_kernel, 2 * math.isqrt(dp_size // GROUP), z_size, len(mlp)),
-        in_specs=[spec] * count,
-        out_specs=[spec] * count,
+        in_specs=[near] * 2 + [spec] * count,
+        out_specs=[near] + [spec] * count,
         out_shape=out,
         scratch_shapes=[
             pltpu.SemaphoreType.DMA((count,)),
@@ -559,7 +567,7 @@
         ],
         compiler_params=pltpu.CompilerParams(collective_id=2, has_side_effects=True),
         cost_estimate=pl.CostEstimate(flops=LONG, bytes_accessed=0, transcendentals=0),
-    )(*mlp, *attn)
+    )(x, gain, *mlp, *attn)
 
 
 class Ring:
@@ -1124,18 +1132,20 @@
 
 
 def tail_kernel(
-    wide, z_size, x_ref, dq_ref, dkv_ref, wo_ref, gain_ref,
+    wide, z_size, mlp_count, x_ref, dq_ref, dkv_ref, wo_ref, gain_ref,
     raw_ref, dh_ref, wq_ref, wkv_ref, *refs
 ):
+    mlp_ins, refs = refs[:mlp_count], refs[mlp_count:]
     wq_out, wkv_out, wo_out, gain_out, grad_out = refs[:5]
-    scratch = refs[5:]
+    mlp_outs, scratch = refs[5 : 5 + mlp_count], refs[5 + mlp_count :]
     sub = wkv_out.shape[1]
     halves = wq_out.shape[1] // sub
     count = halves + 1
     rings = [Reduce(wide, *scratch[6 * at : 6 * at + 6]) for at in range(count)]
     sums, zrecv, gain_z, gain_p, z_send, z_recv, g_send, g_recv = scratch[6 * count : 6 * count + 8]
     wo_recv, w_send, w_recv = scratch[6 * count + 8 : 6 * count + 11]
-    wq_all, wkv_all, raw, dh, dxn, gain_sum, load_sem = scratch[6 * count + 11 :]
+    wq_all, wkv_all, raw, dh, dxn, gain_sum, load_sem = scratch[6 * count + 11 : 6 * count + 18]
+    mlp_copies = send_home(wide, mlp_ins, mlp_outs, *scratch[6 * count + 18 :])
     place = lax.axis_index("tensor")
     mine, found = others(wide)
     along = along_peers(place, z_size)
@@ -1258,6 +1268,8 @@
     for copy in gain_copies:
         copy.start()
     rings[count - 1].pass_on()
+    for copy in mlp_copies:
+        copy.start()
     send_along(count - 2)
 
     for copy in gain_copies:
@@ -1299,9 +1311,11 @@
         copy.wait_send()
     for ring in rings:
         ring.sent()
-
-
-def last_grads(x, dq, dkv, wo_sum, gains, raw, dh, wq, wkv, dp_size, z_size):
+    for copy in mlp_copies:
+        copy.wait()
+
+
+def last_grads(x, dq, dkv, wo_sum, gains, raw, dh, wq, wkv, mlp, dp_size, z_size):
     tokens, width = x.shape
     rows = width // GROUP
     tiles = tokens // QTILE
@@ -1314,15 +1328,16 @@
     for _ in range(count):
         scratch += Reduce.scratch(rows, cols)
     return pl.pallas_call(
-        functools.partial(tail_kernel, 2 * math.isqrt(dp_size // GROUP), z_size),
-        in_specs=[near] * 5 + [far] * 4,
-        out_specs=[near] * 5,
+        functools.partial(tail_kernel, 2 * math.isqrt(dp_size // GROUP), z_size, len(mlp)),
+        in_specs=[near] * 5 + [far] * (4 + len(mlp)),
+        out_specs=[near] * 5 + [far] * len(mlp),
         out_shape=[jax.ShapeDtypeStruct((rows, size // z_size), F32) for size in sizes]
         + [
             jax.ShapeDtypeStruct((rows, wo_sum.shape[1] // z_size), F32),
             jax.ShapeDtypeStruct(gains.shape, F32),
             jax.ShapeDtypeStruct((tokens, width), BF16),
-        ],
+        ]
+        + home_shapes(mlp),
         scratch_shapes=scratch
         + [
             pltpu.VMEM((count, rows, cols), BF16),
@@ -1343,12 +1358,13 @@
             pltpu.VMEM((QTILE, width), F32),
             pltpu.VMEM((STRIP, width), F32),
             pltpu.SemaphoreType.DMA((2 + 2 * tiles,)),
-        ],
+        ]
+        + home_scratch(mlp),
         compiler_params=pltpu.CompilerParams(
             collective_id=4, has_side_effects=True, vmem_limit_bytes=62 << 20
         ),
         cost_estimate=pl.CostEstimate(flops=SHORT, bytes_accessed=0, transcendentals=0),
-    )(x, dq, dkv, wo_sum, gains, raw, dh, wq, wkv)
+    )(x, dq, dkv, wo_sum, gains, raw, dh, wq, wkv, *mlp)
 
 
 class Layout:
@@ -1448,7 +1464,9 @@
         layout.gather_outer(w)
         for w in (w_gate, w_up, w_down, jnp.concatenate([w_key, w_value], axis=1), w_query, w_out)
     ]
-    spread = spread_weights(shards[:3], shards[3:], dp_size, z_size)
+    xn, *spread = spread_weights(
+        activations[0], attn_gain[None], shards[:3], shards[3:], dp_size, z_size
+    )
     def gather_z(array):
         return layout.to_rows(lax.all_gather(array, "tensor", axis=1, tiled=True))
 
@@ -1459,8 +1477,6 @@
             layout.from_rows(total), "tensor", scatter_dimension=1, tiled=True
         )
 
-    r1 = rms_scale(x)
-    xn = (x * r1 * attn_gain).astype(BF16)
     q, kv_all, wq, wo, dy = project(
         layout.from_cols(xn), cosine, sine, *spread[3:], cotangent[0], reach, dp_size, z_size
     )
@@ -1515,15 +1531,15 @@
     datt = dot_nn(dhb, wo).astype(BF16)
     total_wo = layout.from_rows(dot_tn(dhb, att).astype(BF16))
     datt, part_wg, total_wo = lax.optimization_barrier((datt, part_wg, total_wo))
-    datt, part_wu = lax.optimization_barrier((datt, part_wu))
     part_wo = layout.scatter(total_wo)
-    dq, dkv, wd_grad, wg_grad, wu_grad = attend_back(
-        q, datt, att, kv_all, lse, low, cosine, sine, (part_wd, part_wg, part_wu), dp_size, z_size
+    dq, dkv, wd_grad, wg_grad = attend_back(
+        q, datt, att, kv_all, lse, low, cosine, sine, (part_wd, part_wg), dp_size, z_size
     )
+    dq, part_wu = lax.optimization_barrier((dq, part_wu))
     dq, part_wo = lax.optimization_barrier((dq, part_wo))
-    wq_grad, wkv_grad, wo_grad, gains, input_grad = last_grads(
+    wq_grad, wkv_grad, wo_grad, gains, input_grad, wu_grad = last_grads(
         layout.from_cols(xn), dq, dkv, part_wo, jnp.stack([attn_gain, gain_two]),
-        activations[0], dh, wq, wkv, dp_size, z_size,
+        activations[0], dh, wq, wkv, (part_wu,), dp_size, z_size,
     )
     gains = layout.sum_outer(gains)
     output = h + out_rows(0, 2).astype(F32)

time: 845 us -> 838 us (level)
    reduce_scatter x3, waiting for transfers between devices: 13 us -> 0.04 us  [along_z(): lax.psum_scatter(layout.from_rows(total), 'tensor', scatter_dimension=1,...]
  transfers between devices with their start and end apart: 14 -> 14, of which waited for: 2 -> 1; matrix products, arithmetic and copies ran while one was open for 21% -> 20% of each run, Pallas kernels for 54% -> 55%
where the time goes in v12:
time: 838 us; the launch traced here: 834 us
  Pallas kernels  601 us (72%)
  matrix products  171 us (20%)
  other arithmetic  18.4 us (2%)
  between operations  14.7 us (2%)
  waiting for transfers between devices  13.6 us (2%)
  local copies, waits for them, and re-layouts  10.1 us (1%)
    pallas_call x1, Pallas kernels, project(): pl.pallas_call(functools.partial(project_kernel, 2 * math.isqrt(dp_size /...  107 us
    pallas_call x1, Pallas kernels, attend_back(): pl.pallas_call(functools.partial(attend_back_kernel, reach, 2 * math.isqr...  100 us
    pallas_call x1, Pallas kernels, hidden_back(): pl.pallas_call(functools.partial(hidden_back_kernel, 2 * math.isqrt(dp_si...  93.5 us
    pallas_call x1, Pallas kernels, gate_up(): pl.pallas_call(functools.partial(gate_up_kernel, 2 * math.isqrt(dp_size /...  88.5 us
    pallas_call x1, Pallas kernels, last_grads(): pl.pallas_call(functools.partial(tail_kernel, 2 * math.isqrt(dp_size // G...  80.2 us
    dot_general x4, matrix products, dot_tn(): lax.dot_general(left, right, (((0,), (0,)), ((), ())), preferred_element_...  73.4 us
    pallas_call x1, Pallas kernels, attend(): pl.pallas_call(functools.partial(attend_kernel, reach, 2 * math.isqrt(dp_...  67 us
    pallas_call x1, Pallas kernels, spread_weights(): pl.pallas_call(functools.partial(spread_kernel, 2 * math.isqrt(dp_size //...  65.1 us
  transfers between devices with their start and end apart: 14, of which 1 were waited for; matrix products, arithmetic and copies ran while one was open for 20% of the time, Pallas kernels for 55%

profile of v12, /device:TPU:0, one launch (start us, length us, event | category | flops | bytes accessed | tf_op | source)
XLA Modules:
  0.0 834.2 jit_solution(17344987000923431575)
XLA Ops:
  7.2 0.0 all-gather.4.cloned.1.call-start
  7.2 1.5 pad_maximum_fusion.2.refs_3_
  8.8 65.1 %shard_map.203 = (bf16[512,2048]{1,0:T(8,128)(2,1)}, bf16[2048,256]{1,0:T(8,128)(2,1)}, bf16[2048,256]{1,0:T(8,128)(2,1)}, bf16[2048,256]{1,0:T(8,128)(2,1)}, bf...) custom-call(bf16[512,2048]{1,0:T(8,128)(2,1)} %bitcast.70, f32[1,2048]{1,0:T(1,128)} %bitcast.76, ...), custom_call_target="tpu_custom_call" | custom-call | flops 60000002048 | tf_op jit(solution)/shard_map/pallas_call | solution.py:554
  73.8 0.0 all-gather.4.cloned.1.call-update
  73.9 0.0 all-gather.6.cloned.1.call-start
  73.9 0.7 all-gather.6.cloned.1.call-update
  74.6 0.0 all-gather.8.cloned.1.call-start
  74.7 0.7 all-gather.8.cloned.1.call-update
  75.4 0.0 reduce-scatter.5.cloned.1.call-start
  75.4 0.1 convert_reduce_fusion
  75.6 0.1 select_reduce_fusion
  75.7 0.7 subtract_add_fusion
  76.3 1.0 fusion.42
  77.3 1.3 pad_maximum_fusion
  78.6 106.6 %shard_map.204 = (bf16[512,2048]{1,0:T(8,128)(2,1)}, bf16[1536,1024]{1,0:T(8,128)(2,1)}, bf16[2048,2048]{1,0:T(8,128)(2,1)}, bf16[2048,2048]{1,0:T(8,128)(2,1)}, bf16[4096,2048]{1,0:T(8,128)(2,1)}) custom-call(bf16[512,2048]{1,0:T(8,128)(2,1)} %get-tuple-element.77.x_ref, f32[512,128]{1,0:T(8,128)} %get-tuple-element.158.cos_ref.cos_all, ...), custom_call_target="tpu_custom_call" | custom-call | flops 120000004096 | tf_op jit(solution)/shard_map/pallas_call | solution.py:766
  185.2 67.0 %shard_map.205 = (bf16[512,2048]{1,0:T(8,128)(2,1)}, f32[32,1,512]{2,1,0:T(1,128)}, bf16[4096,2048]{1,0:T(8,128)(2,1)}) custom-call(bf16[512,2048]{1,0:T(8,128)(2,1)} %get-tuple-element.81.q_ref, bf16[1536,1024]{1,0:T(8,128)(2,1)} %get-tuple-element.82.k_ref.v_ref, ...), custom_call_target="tpu_custom_call", output_to_operand_aliasing={{2}: (5, {})} | custom-call | flops 21474836480 | bytes 7340032 | tf_op jit(solution)/shard_map/pallas_call | solution.py:164
  252.3 7.8 multiply_reduce_fusion
  260.1 1.9 copy-done
  262.1 1.7 multiply_convert_fusion.own_ref
  263.8 12.0 %all-gather.6.cloned.1.call-done.wu_ref = bf16[2048,1024]{1,0:T(8,128)(2,1)} async-done(((bf16[2048,256]{1,0:T(8,128)(2,1)}), bf16[2048,1024]{1,0:T(8,128)(2,1)}) %all-gather.6.cloned.1.call-update) | async-done | bytes 4194320 | tf_op jit(solution)/shard_map/all_gather | solution.py:1471
  275.8 88.5 %shard_map.206 = (bf16[4096,2048]{1,0:T(8,128)(2,1)}, bf16[4096,1024]{1,0:T(8,128)(2,1)}, bf16[4096,1024]{1,0:T(8,128)(2,1)}, bf16[4096,1024]{1,0:T(8,128)(2,1)}, bf16[2,2048,1024]{2,1,0:T(8,128)(2,1)}) custom-call(bf16[512,2048]{1,0:T(8,128)(2,1)} %multiply_convert_fusion.own_ref, bf16[2048,1024]{1,0:T(8,128)(2,1)} %all-gather.4.cloned.1.call-done.wg_ref, ...), custom_call_target="tpu_custom_call" | custom-call | flops 1000000 | tf_op jit(solution)/shard_map/pallas_call | solution.py:886
  364.3 0.0 all-gather.8.cloned.1.call-done
  364.3 14.4 %convolution_convert_fusion.1 = bf16[2048,2048]{1,0:T(8,128)(2,1)} fusion(bf16[2048,1024]{1,0:T(8,128)(2,1)} %all-gather.8.cloned.1.call-done, bf16[2,2048,1024]{2,1,0:T(8,128)(2,1)} %get-tuple-element.88), kind=kOutput, calls=%fused_computation.12 | convolution fusion | flops 8594128896 | bytes 16777216 | tf_op jit(solution)/shard_map/dot_general | solution.py:36
  378.7 0.1 collective-permute-start
  378.8 21.5 %convolution_convert_fusion.2 = bf16[2048,1024]{1,0:T(8,128)(2,1)} fusion(bf16[4096,2048]{1,0:T(8,128)(2,1)} %get-tuple-element.93, bf16[4096,1024]{1,0:T(8,128)(2,1)S(1)} %copy-done.9), kind=kOutput, calls=%fused_computation.20 | convolution fusion | flops 17181966336 | bytes 29360128 | tf_op jit(solution)/shard_map/dot_general | solution.py:40
  400.3 0.0 reduce-scatter.7.cloned.1.call-start
  400.4 3.8 fusion.16
  404.2 2.4 fusion.18
  406.6 4.1 add_convert_fusion.4
  410.6 3.7 add_convert_fusion.5
  414.3 3.7 add_convert_fusion.6
  418.0 3.7 add_convert_fusion.7
  421.7 0.2 collective-permute-start.1
  421.9 0.6 collective-permute-start.2
  422.5 1.6 collective-permute-start.3
  424.1 1.7 collective-permute-start.4
  425.8 34.7 %fusion.7 = (bf16[4096,1024]{1,0:T(8,128)(2,1)}, bf16[4096,1024]{1,0:T(8,128)(2,1)}) fusion(bf16[4096,1024]{1,0:T(8,128)(2,1)} %get-tuple-element.95, bf16[4096,1024]{1,0:T(8,128)(2,1)} %get-tuple-element.94, bf16[4096,2048]{1,0:T(8,128)(2,1)} %get-tuple-element.93, bf16[2048,1024]{1,0:T(8,128)(2,1)S(1)} %copy-done.10), kind=kOutput, calls=%fused_computation.10 | convolution fusion | flops 17242783744 | bytes 54525952 | tf_op jit(solution)/shard_map/dot_general | solution.py:32
  460.6 2.8 add_convert_fusion.2
  463.4 1.2 copy-done.13
  464.6 21.3 %convolution_convert_fusion.4 = bf16[2048,1024]{1,0:T(8,128)(2,1)} fusion(bf16[4096,2048]{1,0:T(8,128)(2,1)} %get-tuple-element.103, bf16[4096,1024]{1,0:T(8,128)(2,1)S(1)} %copy-done.13), kind=kOutput, calls=%fused_computation.22 | convolution fusion | flops 17181966336 | bytes 29360128 | tf_op jit(solution)/shard_map/dot_general | solution.py:40
  485.9 0.0 reduce-scatter.7.cloned.1.call-update
  485.9 0.0 reduce-scatter.9.cloned.1.call-start
  486.0 0.3 collective-permute-start.5
  486.3 0.5 collective-permute-start.6
  486.8 23.9 %convolution_convert_fusion.3 = bf16[2048,1024]{1,0:T(8,128)(2,1)} fusion(bf16[4096,2048]{1,0:T(8,128)(2,1)} %get-tuple-element.103, bf16[4096,1024]{1,0:T(8,128)(2,1)} %get-tuple-element.115.dup_ref), kind=kOutput, calls=%fused_computation.21 | convolution fusion | flops 17181966336 | bytes 29360128 | tf_op jit(solution)/shard_map/dot_general | solution.py:40
  510.8 0.0 reduce-scatter.11.cloned.1.call-start
  510.8 93.5 %shard_map.207 = (f32[512,2048]{1,0:T(8,128)}, bf16[512,2048]{1,0:T(8,128)(2,1)}, f32[16,2048]{1,0:T(8,128)}) custom-call(f32[1,2048]{1,0:T(1,128)} %bitcast.75, f32[512,2048]{1,0:T(8,128)} %copy-done, bf16[512,2048]{1,0:T(8,128)(2,1)} %bitcast.84, bf16[4096,1024]{1,0:T(8,128)(2,1)} %get-tuple-element.104.dgate_ref, ...), custom_call_target="tpu_custom_call" | custom-call | flops 120000004096 | bytes 4194304 | tf_op jit(solution)/shard_map/pallas_call | solution.py:1106
  604.4 0.0 reduce-scatter.5.cloned.1.call-done.refs_0_
  604.4 10.1 %convolution_convert_fusion.5.do_ref = bf16[512,2048]{1,0:T(8,128)(2,1)} fusion(bf16[512,2048]{1,0:T(8,128)(2,1)} %get-tuple-element.118, bf16[2048,2048]{1,0:T(8,128)(2,1)} %get-tuple-element.85), kind=kOutput, calls=%fused_computation.23 | convolution fusion | flops 4296015872 | bytes 12582912 | tf_op jit(solution)/shard_map/dot_general | solution.py:32
  614.5 6.8 convolution_convert_fusion
  621.3 0.9 copy-done.5
  622.2 0.6 pad_maximum_fusion.3.gain_ref
  622.8 9.5 %fusion.10 = bf16[1,512,2048]{2,1,0:T(8,128)(2,1)} fusion(f32[512,2048]{1,0:T(8,128)} %copy-done, bf16[2048,2048]{1,0:T(8,128)(2,1)} %collective-permute-done, bf16[256,2048]{1,0:T(8,128)(2,1)} %collective-permute-done.3, bf16[256,2048]{1,0:T(8,128)(2,1)S(1)} %collective-permute-done.5, bf16[256,2048]{1,0:T(8,128)(2,1)} %collective-permute-done.6, ...), kind=kOutput, calls=%fused_computation.24 | convolution fusion | flops 2164260864 | bytes 17825792 | tf_op jit(solution)/shard_map/dot_general | solution.py:36
  632.4 100.0 %shard_map.208 = (bf16[512,2048]{1,0:T(8,128)(2,1)}, bf16[512,1024]{1,0:T(8,128)(2,1)}, bf16[256,2048]{1,0:T(8,128)(2,1)}, bf16[256,2048]{1,0:T(8,128)(2,1)}) custom-call(bf16[512,2048]{1,0:T(8,128)(2,1)} %get-tuple-element.81.q_ref, bf16[512,2048]{1,0:T(8,128)(2,1)} %convolution_convert_fusion.5.do_ref, bf16[512,2048]{1,0:T(8,128)(2,1)} %get-tuple-element.84.o_ref, ...), custom_call_target="tpu_custom_call" | custom-call | flops 53687091200 | bytes 14680064 | tf_op jit(solution)/shard_map/pallas_call | solution.py:319
  732.3 0.0 reduce-scatter.9.cloned.1.call-done.refs_0_
  732.4 2.8 convert_element_type.146
  735.2 2.8 convert_element_type.148
  738.0 80.2 %shard_map.209 = (f32[256,512]{1,0:T(8,128)}, f32[256,256]{1,0:T(8,128)}, f32[256,512]{1,0:T(8,128)}, f32[2,2048]{1,0:T(2,128)}, bf16[512,2048]{1,0:T(8,128)(2,1)}, /*index=5*/bf16[256,2048]{1,0:T(8,128)(2,1)}) custom-call(bf16[512,2048]{1,0:T(8,128)(2,1)} %get-tuple-element.77.x_ref, bf16[512,2048]{1,0:T(8,128)(2,1)} %get-tuple-element.128.dq_ref, ...), custom_call_target="tpu_custom_call" | custom-call | flops 1000000 | tf_op jit(solution)/shard_map/pallas_call | solution.py:1330
  818.2 2.9 convert_element_type.147
  821.1 1.7 fusion.43
  822.8 1.4 fusion.44
  824.2 1.3 copy.29
  825.5 0.8 copy.30
  826.3 0.8 copy.31
  (41 shorter events, 0.2 us)
Async XLA Ops:
  7.2 256.6 %all-gather.4.cloned.1.call-start = ((), (), s32[]{:S(2)}) async-start(), calls=%async_computation.4 | async-start | bytes 5242880 | tf_op jit(solution)/shard_map/all_gather | solution.py:1471
  8.8 66.7 %copy-start.6 = (s32[1,2048]{1,0:T(1,128)S(1)}, s32[1,2048]{1,0:T(1,128)}, u32[]{:S(2)}) copy-start(s32[1,2048]{1,0:T(1,128)} %param.13) | copy-start | bytes 24580
  73.9 201.9 %all-gather.6.cloned.1.call-start = ((), (), s32[]{:S(2)}) async-start(), calls=%async_computation.5 | async-start | bytes 5242880 | tf_op jit(solution)/shard_map/all_gather | solution.py:1471
  74.6 289.7 %all-gather.8.cloned.1.call-start = ((), (), s32[]{:S(2)}) async-start(), calls=%async_computation.6 | async-start | bytes 5242880 | tf_op jit(solution)/shard_map/all_gather | solution.py:1471
  75.4 529.0 %reduce-scatter.5.cloned.1.call-start = ((), (), s32[]{:S(2)}) async-start(), calls=%async_computation.7 | async-start | bytes 5242880 | tf_op jit(solution)/shard_map/reduce_scatter | solution.py:1476
  185.2 67.0 %copy-start.2 = (bf16[1,512,2048]{2,1,0:T(8,128)(2,1)S(1)}, bf16[1,512,2048]{2,1,0:T(8,128)(2,1)}, u32[]{:S(2)}) copy-start(bf16[1,512,2048]{2,1,0:T(8,128)(2,1)} %param.12) | copy-start | bytes 6291460
  252.2 9.8 %copy-start.7 = (f32[2048]{0:T(1024)S(1)}, f32[2048]{0:T(1024)}, u32[]{:S(2)}) copy-start(f32[2048]{0:T(1024)} %param.19) | copy-start | bytes 24580
  260.1 2.0 copy-start
  364.3 14.5 %copy-start.9 = (bf16[4096,1024]{1,0:T(8,128)(2,1)S(1)}, bf16[4096,1024]{1,0:T(8,128)(2,1)}, u32[]{:S(2)}) copy-start(bf16[4096,1024]{1,0:T(8,128)(2,1)} %get-tuple-element.117) | copy-start | bytes 25165828
  378.7 27.8 %collective-permute-start = (bf16[2048,2048]{1,0:T(8,128)(2,1)}, bf16[2048,2048]{1,0:T(8,128)(2,1)}, u32[]{:S(2)}, u32[]{:S(2)}) collective-permute-start(bf16[2048,2048]{1,0:T(8,128)(2,1)} %convolution_convert_fusion.1), channel_id=1, source_target_pairs={{0,4},{4,0},{8,12},{12,8},{16,20},{20,16},{24,28},{28,24},{1,5},{5... | collective-permute-start | bytes 25165832 | tf_op jit(solution)/shard_map/ppermute | solution.py:1423
  400.3 221.0 %reduce-scatter.7.cloned.1.call-start = ((), (), s32[]{:S(2)}) async-start(), calls=%async_computation.8 | async-start | bytes 5242880 | tf_op jit(solution)/shard_map/reduce_scatter | solution.py:1476
  400.4 3.8 copy-start.10
  421.7 38.8 %collective-permute-start.1 = (bf16[256,2048]{1,0:T(8,128)(2,1)}, bf16[256,2048]{1,0:T(8,128)(2,1)S(1)}, u32[]{:S(2)}, u32[]{:S(2)}) collective-permute-start(bf16[256,2048]{1,0:T(8,128)(2,1)} %add_convert_fusion.7), channel_id=1, source_target_pairs={{0,8},{4,12},{8,0},{12,4},{16,24},{20,28},{24,16},{28,20},{1,9},{5... | collective-permute-start | bytes 3145736 | tf_op jit(solution)/shard_map/ppermute | solution.py:1423
  421.9 38.6 %collective-permute-start.2 = (bf16[256,2048]{1,0:T(8,128)(2,1)}, bf16[256,2048]{1,0:T(8,128)(2,1)S(1)}, u32[]{:S(2)}, u32[]{:S(2)}) collective-permute-start(bf16[256,2048]{1,0:T(8,128)(2,1)} %add_convert_fusion.6), channel_id=1, source_target_pairs={{0,16},{4,20},{8,24},{12,28},{16,0},{20,4},{24,8},{28,12},{1,17},{... | collective-permute-start | bytes 3145736 | tf_op jit(solution)/shard_map/ppermute | solution.py:1423
  422.5 63.4 %collective-permute-start.3 = (bf16[256,2048]{1,0:T(8,128)(2,1)}, bf16[256,2048]{1,0:T(8,128)(2,1)}, u32[]{:S(2)}, u32[]{:S(2)}) collective-permute-start(bf16[256,2048]{1,0:T(8,128)(2,1)} %add_convert_fusion.5), channel_id=1, source_target_pairs={{0,8},{4,12},{8,0},{12,4},{16,24},{20,28},{24,16},{28,20},{1,9},{5... | collective-permute-start | bytes 3145736 | tf_op jit(solution)/shard_map/ppermute | solution.py:1423
  424.1 61.8 %collective-permute-start.4 = (bf16[256,2048]{1,0:T(8,128)(2,1)}, bf16[256,2048]{1,0:T(8,128)(2,1)}, u32[]{:S(2)}, u32[]{:S(2)}) collective-permute-start(bf16[256,2048]{1,0:T(8,128)(2,1)} %add_convert_fusion.4), channel_id=1, source_target_pairs={{0,16},{4,20},{8,24},{12,28},{16,0},{20,4},{24,8},{28,12},{1,17},{... | collective-permute-start | bytes 3145736 | tf_op jit(solution)/shard_map/ppermute | solution.py:1423
  460.5 4.1 copy-start.13
  485.9 246.4 %reduce-scatter.9.cloned.1.call-start = ((), (), s32[]{:S(2)}) async-start(), calls=%async_computation.9 | async-start | bytes 5242880 | tf_op jit(solution)/shard_map/reduce_scatter | solution.py:1476
  486.0 24.8 %collective-permute-start.5 = (bf16[256,2048]{1,0:T(8,128)(2,1)S(1)}, bf16[256,2048]{1,0:T(8,128)(2,1)S(1)}, u32[]{:S(2)}, u32[]{:S(2)}) collective-permute-start(bf16[256,2048]{1,0:T(8,128)(2,1)S(1)} %get-tuple-element.109), channel_id=1, source_target_pairs={{0,8},{4,12},{8,0},{12,4},{16,24},{20,28},{24,16},{28,20},{1,9},{5... | collective-permute-start | bytes 3145736 | tf_op jit(solution)/shard_map/ppermute | solution.py:1423
  486.3 24.6 %collective-permute-start.6 = (bf16[256,2048]{1,0:T(8,128)(2,1)S(1)}, bf16[256,2048]{1,0:T(8,128)(2,1)}, u32[]{:S(2)}, u32[]{:S(2)}) collective-permute-start(bf16[256,2048]{1,0:T(8,128)(2,1)S(1)} %get-tuple-element.110), channel_id=1, source_target_pairs={{0,16},{4,20},{8,24},{12,28},{16,0},{20,4},{24,8},{28,12},{1,17},{... | collective-permute-start | bytes 3145736 | tf_op jit(solution)/shard_map/ppermute | solution.py:1423
  510.8 227.2 %reduce-scatter.11.cloned.1.call-start = ((), (), s32[]{:S(2)}) async-start(), calls=%async_computation.10 | async-start | bytes 9437184 | tf_op jit(solution)/shard_map/reduce_scatter | solution.py:1434
  604.4 10.1 %copy-start.11 = (bf16[512,2048]{1,0:T(8,128)(2,1)S(1)}, bf16[512,2048]{1,0:T(8,128)(2,1)}, u32[]{:S(2)}) copy-start(bf16[512,2048]{1,0:T(8,128)(2,1)} %get-tuple-element.84.o_ref) | copy-start | bytes 6291460
  604.4 10.1 %copy-start.12 = (bf16[512,2048]{1,0:T(8,128)(2,1)S(1)}, bf16[512,2048]{1,0:T(8,128)(2,1)}, u32[]{:S(2)}) copy-start(bf16[512,2048]{1,0:T(8,128)(2,1)} %get-tuple-element.118) | copy-start | bytes 6291460
  621.3 0.9 copy-start.5
  621.3 0.9 copy-start.8
  818.1 6.1 copy-start.1
  818.2 7.4 copy-start.4
  818.2 8.2 copy-start.3
Sparse Core Ops, SparseCore 0:
  74.0 98.2 all-gather.3
  173.9 101.9 all-gather.5
  277.4 78.7 all-gather.7
  400.4 77.9 reduce-scatter.4
  486.0 77.9 reduce-scatter.6
  566.2 77.2 reduce-scatter.8
  647.4 71.7 reduce-scatter.10

commit v13 on v12

--- a/solution.py
+++ b/solution.py
@@ -159,7 +159,7 @@
     heads = kv.shape[1] // LANES
     per_head = pairs // heads
     span = reach + QTILE
-    right = (grads.shape[0], grads.shape[1] * 5 // 8)
+    right = (grads.shape[0], grads.shape[1] // 2)
     far = pl.BlockSpec(memory_space=pl.ANY)
     return pl.pallas_call(
         functools.partial(attend_kernel, reach, 2 * math.isqrt(dp_size // GROUP)),
@@ -447,10 +447,12 @@
 
 
 def spread_kernel(wide, z_size, mlp_count, x_ref, gain_ref, *refs):
-    attn_count = (len(refs) - 8) // 2 - mlp_count
+    attn_count = (len(refs) - 10) // 2 - mlp_count
     count = mlp_count + attn_count
     ins, xn_ref, outs = refs[:count], refs[count], refs[count + 1 : 2 * count + 1]
-    own_sem, send_sem, recv_sem, z_send, z_recv, ring_send, ring_recv = refs[2 * count + 1 :]
+    x_all, x_sem, own_sem, send_sem, recv_sem, z_send, z_recv, ring_send, ring_recv = refs[
+        2 * count + 1 :
+    ]
     first = mlp_count
     ring = Ring(wide, outs[first], ins[first].shape[0], ring_send, ring_recv)
     place = lax.axis_index("tensor")
@@ -504,11 +506,14 @@
             pl.when(sends(way, 1))(lambda: hop(at, way, 1).start())
     for copy in copies + local:
         copy.start()
-
-    @pl.loop(0, x_ref.shape[0] // STRIP)
+    load = pltpu.make_async_copy(x_ref, x_all, x_sem)
+    load.start()
+    load.wait()
+
+    @pl.loop(0, x_all.shape[0] // STRIP)
     def _(at):
         here = pl.ds(pl.multiple_of(at * STRIP, STRIP), STRIP)
-        value = x_ref[here, :].astype(F32)
+        value = x_all[here, :].astype(F32)
         xn_ref[here, :] = (value * rms_scale(value) * gain_ref[...]).astype(BF16)
 
     def advance(at, step):
@@ -553,10 +558,12 @@
     ]
     return pl.pallas_call(
         functools.partial(spread_kernel, 2 * math.isqrt(dp_size // GROUP), z_size, len(mlp)),
-        in_specs=[near] * 2 + [spec] * count,
+        in_specs=[spec, near] + [spec] * count,
         out_specs=[near] + [spec] * count,
         out_shape=out,
         scratch_shapes=[
+            pltpu.VMEM(x.shape, BF16),
+            pltpu.SemaphoreType.DMA,
             pltpu.SemaphoreType.DMA((count,)),
             pltpu.SemaphoreType.DMA((len(mlp), GROUP - 1)),
             pltpu.SemaphoreType.DMA((len(mlp), GROUP - 1)),
@@ -762,7 +769,7 @@
     whole = [(GROUP * w.shape[0], w.shape[1]) for w in (wq, wo)]
     keys = (reach + rows, wkv.shape[1])
     grads = (GROUP * grad.shape[0], grad.shape[1])
-    left = (grads[0], grads[1] * 3 // 8)
+    left = (grads[0], grads[1] // 2)
     return pl.pallas_call(
         functools.partial(project_kernel, 2 * math.isqrt(dp_size // GROUP), z_size),
         in_specs=[near] * 3 + [far] * 4,
@@ -1032,11 +1039,11 @@
 
 def hidden_back_kernel(
     wide, gain_ref, h_ref, grad_ref, dgate_ref, dup_ref, wg_ref, wu_ref,
-    dh_ref, low_ref, gain_out,
+    low_ref, gain_out,
     loaded, wg_all, wu_all, h_all, grad_all, load_sem, own_sem, *scratch,
 ):
     ring = Reduce(wide, *scratch)
-    rows = dh_ref.shape[0]
+    rows = low_ref.shape[0]
 
     def loads(step):
         chunk, _ = ring.chunk(step)
@@ -1070,7 +1077,7 @@
         _, target = ring.chunk(step)
         dgate, dup = loaded[step % 2, 0], loaded[step % 2, 1]
 
-        @pl.loop(0, dh_ref.shape[1] // NTILE)
+        @pl.loop(0, low_ref.shape[1] // NTILE)
         def _(at):
             n = pl.ds(pl.multiple_of(at * NTILE, NTILE), NTILE)
             value = dot_nt(dgate, wg_all[n, :]) + dot_nt(dup, wu_all[n, :])
@@ -1091,7 +1098,6 @@
         gain_out[...] += value * h * scale
         total = grad_all[here, :].astype(F32) + scale * gained
         total -= h * (scale * scale * scale * inner)
-        dh_ref[here, :] = total
         low_ref[here, :] = total.astype(BF16)
 
     ring.finish(store)
@@ -1106,9 +1112,8 @@
     return pl.pallas_call(
         functools.partial(hidden_back_kernel, 2 * math.isqrt(dp_size // GROUP)),
         in_specs=[near] + [far] * 6,
-        out_specs=[near] * 3,
+        out_specs=[near] * 2,
         out_shape=[
-            jax.ShapeDtypeStruct((rows, width), F32),
             jax.ShapeDtypeStruct((rows, width), BF16),
             jax.ShapeDtypeStruct((STRIP, width), F32),
         ],
@@ -1223,7 +1228,7 @@
             inner = jnp.mean(gained * value, axis=1, keepdims=True)
             gain_sum[...] += grad * value * scale
             total = scale * gained - value * (scale * scale * scale * inner)
-            grad_out[there, :] = (dh[tile, here, :] + total).astype(BF16)
+            grad_out[there, :] = (dh[tile, here, :].astype(F32) + total).astype(BF16)
 
     def send_along(index):
         def store(here, value):
@@ -1354,7 +1359,7 @@
             pltpu.VMEM(wq.shape, BF16),
             pltpu.VMEM(wkv.shape, BF16),
             pltpu.VMEM((tiles, QTILE, width), BF16),
-            pltpu.VMEM((tiles, QTILE, width), F32),
+            pltpu.VMEM((tiles, QTILE, width), BF16),
             pltpu.VMEM((QTILE, width), F32),
             pltpu.VMEM((STRIP, width), F32),
             pltpu.SemaphoreType.DMA((2 + 2 * tiles,)),
@@ -1494,12 +1499,14 @@
     part_wd = along_z(total_wd)
     from_core = layout.swap(away, 1)
 
-    def out_rows(start, count, *more):
-        some = slice(start * part, (start + count) * part)
-        total = dot_nt(by_core[0, some], wd) + from_core[some].astype(F32)
-        for other in more:
-            total = total + other.astype(F32)
-        return total.astype(BF16)
+    near = (dot_nt(by_core[0], wd) + from_core.astype(F32)).astype(BF16)
+    dy, near = lax.optimization_barrier((dy, near))
+
+    def out_rows(start, count):
+        return near[start * part : (start + count) * part]
+
+    def joined(some, other):
+        return (some.astype(F32) + other.astype(F32)).astype(BF16)
 
     far_y, far_x, x_lower, y_upper = (out_rows(at, 1) for at in (6, 7, 3, 4))
     dy, far_x, far_y, x_lower, y_upper = lax.optimization_barrier(
@@ -1513,7 +1520,7 @@
     dgate = (dhid * up * sigma * (1.0 + gate * (1.0 - sigma))).astype(BF16)
     dup = (dhid * gate * sigma).astype(BF16)
     dgate, dup, from_x, from_y = lax.optimization_barrier((dgate, dup, from_x, from_y))
-    x_upper, y_lower = out_rows(2, 1, from_y), out_rows(5, 1, from_x)
+    x_upper, y_lower = joined(out_rows(2, 1), from_y), joined(out_rows(5, 1), from_x)
     dgate, dup, x_upper, y_lower = lax.optimization_barrier((dgate, dup, x_upper, y_lower))
     x_upper, y_lower = layout.swap(x_upper, 2), layout.swap(y_lower, 4)
     total_wg = dot_tn(hn, dgate).astype(BF16)
@@ -1523,7 +1530,7 @@
     dup, total_wu = lax.optimization_barrier((dup, total_wu))
     part_wu = along_z(total_wu)
     dup, x_upper, y_lower = lax.optimization_barrier((dup, x_upper, y_lower))
-    dh, dhb, gain_two = hidden_back(
+    dhb, gain_two = hidden_back(
         mlp_gain[None], h, cotangent[0], dgate, dup, wg, wu, dp_size
     )
     gain_two = jnp.sum(gain_two, axis=0)
@@ -1539,7 +1546,7 @@
     dq, part_wo = lax.optimization_barrier((dq, part_wo))
     wq_grad, wkv_grad, wo_grad, gains, input_grad, wu_grad = last_grads(
         layout.from_cols(xn), dq, dkv, part_wo, jnp.stack([attn_gain, gain_two]),
-        activations[0], dh, wq, wkv, (part_wu,), dp_size, z_size,
+        activations[0], dhb, wq, wkv, (part_wu,), dp_size, z_size,
     )
     gains = layout.sum_outer(gains)
     output = h + out_rows(0, 2).astype(F32)

time: 838 us -> 821 us (0.980)
  matrix products: 171 us -> 154 us
    dot_general x9 -> x3, matrix products: 53.1 us -> 35.4 us  [dot_nt(): lax.dot_general(left, right, (((1,), (1,)), ((), ())), preferred_element_...]
    pallas_call x1, Pallas kernels: 107 us -> 116 us  [project(): pl.pallas_call(functools.partial(project_kernel, 2 * math.isqrt(dp_size /...]
  transfers between devices with their start and end apart: 14 -> 14, of which waited for: 1 -> 3; matrix products, arithmetic and copies ran while one was open for 20% -> 20% of each run, Pallas kernels for 55% -> 56%
where the time goes in v13:
time: 821 us; the launch traced here: 817 us
  Pallas kernels  600 us (73%)
  matrix products  154 us (19%)
  other arithmetic  24.3 us (3%)
  between operations  14.7 us (2%)
  local copies, waits for them, and re-layouts  11.2 us (1%)
    pallas_call x1, Pallas kernels, project(): pl.pallas_call(functools.partial(project_kernel, 2 * math.isqrt(dp_size /...  116 us
    pallas_call x1, Pallas kernels, attend_back(): pl.pallas_call(functools.partial(attend_back_kernel, reach, 2 * math.isqr...  95.8 us
    pallas_call x1, Pallas kernels, hidden_back(): pl.pallas_call(functools.partial(hidden_back_kernel, 2 * math.isqrt(dp_si...  92.1 us
    pallas_call x1, Pallas kernels, gate_up(): pl.pallas_call(functools.partial(gate_up_kernel, 2 * math.isqrt(dp_size /...  88.4 us
    pallas_call x1, Pallas kernels, last_grads(): pl.pallas_call(functools.partial(tail_kernel, 2 * math.isqrt(dp_size // G...  80.2 us
    dot_general x4, matrix products, dot_tn(): lax.dot_general(left, right, (((0,), (0,)), ((), ())), preferred_element_...  75.7 us
    pallas_call x1, Pallas kernels, spread_weights(): pl.pallas_call(functools.partial(spread_kernel, 2 * math.isqrt(dp_size //...  64.2 us
    pallas_call x1, Pallas kernels, attend(): pl.pallas_call(functools.partial(attend_kernel, reach, 2 * math.isqrt(dp_...  63.4 us
  transfers between devices with their start and end apart: 14, of which 3 were waited for; matrix products, arithmetic and copies ran while one was open for 20% of the time, Pallas kernels for 56%

profile of v13, /device:TPU:0, one launch (start us, length us, event | category | flops | bytes accessed | tf_op | source)
XLA Modules:
  0.0 816.8 jit_solution(305021278417886091)
XLA Ops:
  7.2 0.0 all-gather.4.cloned.1.call-start
  7.2 1.5 pad_maximum_fusion.2.refs_3_
  8.8 64.2 %shard_map.203 = (bf16[512,2048]{1,0:T(8,128)(2,1)}, bf16[2048,256]{1,0:T(8,128)(2,1)}, bf16[2048,256]{1,0:T(8,128)(2,1)}, bf16[2048,256]{1,0:T(8,128)(2,1)}, bf...) custom-call(bf16[512,2048]{1,0:T(8,128)(2,1)} %bitcast.37, f32[1,2048]{1,0:T(1,128)} %bitcast.44, ...), custom_call_target="tpu_custom_call" | custom-call | flops 60000002048 | tf_op jit(solution)/shard_map/pallas_call | solution.py:559
  73.0 0.0 all-gather.4.cloned.1.call-update
  73.0 0.0 all-gather.6.cloned.1.call-start
  73.0 0.7 all-gather.6.cloned.1.call-update
  73.7 0.0 all-gather.8.cloned.1.call-start
  73.8 0.7 all-gather.8.cloned.1.call-update
  74.5 0.0 reduce-scatter.5.cloned.1.call-start
  74.6 0.1 convert_reduce_fusion
  74.7 0.1 select_reduce_fusion
  74.8 0.7 subtract_add_fusion
  75.4 1.0 fusion.16
  76.4 1.3 pad_maximum_fusion
  77.7 115.6 %shard_map.204 = (bf16[512,2048]{1,0:T(8,128)(2,1)}, bf16[1536,1024]{1,0:T(8,128)(2,1)}, bf16[2048,2048]{1,0:T(8,128)(2,1)}, bf16[2048,2048]{1,0:T(8,128)(2,1)}, bf16[4096,2048]{1,0:T(8,128)(2,1)}) custom-call(bf16[512,2048]{1,0:T(8,128)(2,1)} %get-tuple-element.78.x_ref, f32[512,128]{1,0:T(8,128)} %get-tuple-element.164.cos_ref.cos_all, ...), custom_call_target="tpu_custom_call" | custom-call | flops 120000004096 | tf_op jit(solution)/shard_map/pallas_call | solution.py:773
  193.4 63.4 %shard_map.205 = (bf16[512,2048]{1,0:T(8,128)(2,1)}, f32[32,1,512]{2,1,0:T(1,128)}, bf16[4096,2048]{1,0:T(8,128)(2,1)}) custom-call(bf16[512,2048]{1,0:T(8,128)(2,1)} %get-tuple-element.82.q_ref, bf16[1536,1024]{1,0:T(8,128)(2,1)} %get-tuple-element.83.k_ref.v_ref, ...), custom_call_target="tpu_custom_call", output_to_operand_aliasing={{2}: (5, {})} | custom-call | flops 21474836480 | bytes 7340032 | tf_op jit(solution)/shard_map/pallas_call | solution.py:164
  256.8 7.9 multiply_reduce_fusion
  264.7 2.0 copy-done
  266.7 1.7 multiply_convert_fusion.own_ref
  268.4 6.1 all-gather.6.cloned.1.call-done.wu_ref
  274.5 88.4 %shard_map.206 = (bf16[4096,2048]{1,0:T(8,128)(2,1)}, bf16[4096,1024]{1,0:T(8,128)(2,1)}, bf16[4096,1024]{1,0:T(8,128)(2,1)}, bf16[4096,1024]{1,0:T(8,128)(2,1)}, bf16[2,2048,1024]{2,1,0:T(8,128)(2,1)}) custom-call(bf16[512,2048]{1,0:T(8,128)(2,1)} %multiply_convert_fusion.own_ref, bf16[2048,1024]{1,0:T(8,128)(2,1)} %all-gather.4.cloned.1.call-done.wg_ref, ...), custom_call_target="tpu_custom_call" | custom-call | flops 1000000 | tf_op jit(solution)/shard_map/pallas_call | solution.py:893
  362.9 0.0 all-gather.8.cloned.1.call-done
  363.0 14.3 %convolution_convert_fusion.1 = bf16[2048,2048]{1,0:T(8,128)(2,1)} fusion(bf16[2048,1024]{1,0:T(8,128)(2,1)} %all-gather.8.cloned.1.call-done, bf16[2,2048,1024]{2,1,0:T(8,128)(2,1)} %get-tuple-element.90), kind=kOutput, calls=%fused_computation.13 | convolution fusion | flops 8594128896 | bytes 16777216 | tf_op jit(solution)/shard_map/dot_general | solution.py:36
  377.3 0.1 collective-permute-start
  377.4 21.5 %convolution_convert_fusion.2 = bf16[2048,1024]{1,0:T(8,128)(2,1)} fusion(bf16[4096,2048]{1,0:T(8,128)(2,1)} %get-tuple-element.96, bf16[4096,1024]{1,0:T(8,128)(2,1)S(1)} %copy-done.15), kind=kOutput, calls=%fused_computation.23 | convolution fusion | flops 17181966336 | bytes 29360128 | tf_op jit(solution)/shard_map/dot_general | solution.py:40
  398.9 0.0 reduce-scatter.7.cloned.1.call-start
  399.0 13.2 %add_convert_fusion = bf16[2048,2048]{1,0:T(8,128)(2,1)S(1)} fusion(bf16[2048,2048]{1,0:T(8,128)(2,1)} %collective-permute-done, bf16[2048,1024]{1,0:T(8,128)(2,1)} %all-gather.8.cloned.1.call-done, bf16[2,2048,1024]{2,1,0:T(8,128)(2,1)} %get-tuple-element.90), kind=kOutput, calls=%fused_computation.11 | convolution fusion | flops 8602517504 | bytes 25165824 | tf_op jit(solution)/shard_map/dot_general | solution.py:36
  412.2 2.2 fusion.17
  414.4 0.6 collective-permute-start.1
  414.9 0.3 collective-permute-start.2
  415.3 1.9 collective-permute-start.3
  417.2 1.3 collective-permute-start.4
  418.4 32.3 %fusion.7 = (bf16[4096,1024]{1,0:T(8,128)(2,1)}, bf16[4096,1024]{1,0:T(8,128)(2,1)}) fusion(bf16[4096,1024]{1,0:T(8,128)(2,1)} %get-tuple-element.98, bf16[4096,1024]{1,0:T(8,128)(2,1)} %get-tuple-element.97, bf16[4096,2048]{1,0:T(8,128)(2,1)} %get-tuple-element.96, bf16[2048,1024]{1,0:T(8,128)(2,1)} %all-gather.8.cloned.1.call-done), kind=kOutput, calls=%fused_computation.10 | convolution fusion | flops 17242783744 | bytes 54525952 | tf_op jit(solution)/shard_map/dot_general | solution.py:32
  450.8 3.6 add_convert_fusion.2
  454.4 23.8 %convolution_convert_fusion.4 = bf16[2048,1024]{1,0:T(8,128)(2,1)} fusion(bf16[4096,2048]{1,0:T(8,128)(2,1)} %get-tuple-element.106, bf16[4096,1024]{1,0:T(8,128)(2,1)} %get-tuple-element.107.dgate_ref), kind=kOutput, calls=%fused_computation.25 | convolution fusion | flops 17181966336 | bytes 29360128 | tf_op jit(solution)/shard_map/dot_general | solution.py:40
  478.2 0.0 reduce-scatter.9.cloned.1.call-start
  478.3 0.6 collective-permute-start.5
  478.9 0.3 collective-permute-start.6
  479.2 23.7 %convolution_convert_fusion.3 = bf16[2048,1024]{1,0:T(8,128)(2,1)} fusion(bf16[4096,2048]{1,0:T(8,128)(2,1)} %get-tuple-element.106, bf16[4096,1024]{1,0:T(8,128)(2,1)} %get-tuple-element.118.dup_ref), kind=kOutput, calls=%fused_computation.24 | convolution fusion | flops 17181966336 | bytes 29360128 | tf_op jit(solution)/shard_map/dot_general | solution.py:40
  502.9 0.0 reduce-scatter.9.cloned.1.call-update
  503.0 0.0 reduce-scatter.11.cloned.1.call-start
  503.0 0.1 collective-permute-done.5
  503.1 0.2 collective-permute-done.6
  503.4 92.1 %shard_map.207 = (bf16[512,2048]{1,0:T(8,128)(2,1)}, f32[16,2048]{1,0:T(8,128)}) custom-call(f32[1,2048]{1,0:T(1,128)} %bitcast.43, f32[512,2048]{1,0:T(8,128)} %copy-done, bf16[512,2048]{1,0:T(8,128)(2,1)} %bitcast.52, bf16[4096,1024]{1,0:T(8,128)(2,1)} %get-tuple-element.107.dgate_ref, bf16[4096,1024]{1,0:T(8,128)(2,1)} %get-tuple-element.118.dup_ref, ...), custom_call_target="tpu_custom_call" | custom-call | flops 120000004096 | bytes 4194304 | tf_op jit(solution)/shard_map/pallas_call | solution.py:1112
  595.5 0.0 reduce-scatter.5.cloned.1.call-done.refs_0_
  595.5 10.1 %convolution_convert_fusion.5.do_ref = bf16[512,2048]{1,0:T(8,128)(2,1)} fusion(bf16[512,2048]{1,0:T(8,128)(2,1)} %get-tuple-element.121.dh_ref, bf16[2048,2048]{1,0:T(8,128)(2,1)} %get-tuple-element.86), kind=kOutput, calls=%fused_computation.26 | convolution fusion | flops 4296015872 | bytes 12582912 | tf_op jit(solution)/shard_map/dot_general | solution.py:32
  605.6 6.8 convolution_convert_fusion
  612.4 0.0 reduce-scatter.7.cloned.1.call-done.refs_1_
  612.4 0.0 reduce-scatter.11.cloned.1.call-update
  612.4 0.8 copy-done.11
  613.3 0.6 pad_maximum_fusion.3.gain_ref
  613.9 0.1 copy-done.8
  614.0 5.2 fusion.15
  619.2 95.8 %shard_map.208 = (bf16[512,2048]{1,0:T(8,128)(2,1)}, bf16[512,1024]{1,0:T(8,128)(2,1)}, bf16[256,2048]{1,0:T(8,128)(2,1)}, bf16[256,2048]{1,0:T(8,128)(2,1)}) custom-call(bf16[512,2048]{1,0:T(8,128)(2,1)} %get-tuple-element.82.q_ref, bf16[512,2048]{1,0:T(8,128)(2,1)} %convolution_convert_fusion.5.do_ref, bf16[512,2048]{1,0:T(8,128)(2,1)} %get-tuple-element.85.o_ref, ...), custom_call_target="tpu_custom_call" | custom-call | flops 53687091200 | bytes 14680064 | tf_op jit(solution)/shard_map/pallas_call | solution.py:319
  715.0 0.0 reduce-scatter.9.cloned.1.call-done.refs_0_
  715.0 2.8 convert_element_type.114
  717.8 2.8 convert_element_type.116
  720.6 80.2 %shard_map.209 = (f32[256,512]{1,0:T(8,128)}, f32[256,256]{1,0:T(8,128)}, f32[256,512]{1,0:T(8,128)}, f32[2,2048]{1,0:T(2,128)}, bf16[512,2048]{1,0:T(8,128)(2,1)}, /*index=5*/bf16[256,2048]{1,0:T(8,128)(2,1)}) custom-call(bf16[512,2048]{1,0:T(8,128)(2,1)} %get-tuple-element.78.x_ref, bf16[512,2048]{1,0:T(8,128)(2,1)} %get-tuple-element.131.dq_ref, ...), custom_call_target="tpu_custom_call" | custom-call | flops 1000000 | tf_op jit(solution)/shard_map/pallas_call | solution.py:1335
  800.8 1.5 fusion.19
  802.3 1.7 fusion.18
  804.0 2.8 convert_element_type.115
  806.8 1.3 copy.29
  808.2 0.8 copy.30
  809.0 0.8 copy.31
  (43 shorter events, 0.2 us)
Async XLA Ops:
  7.2 261.2 %all-gather.4.cloned.1.call-start = ((), (), s32[]{:S(2)}) async-start(), calls=%async_computation.4 | async-start | bytes 5242880 | tf_op jit(solution)/shard_map/all_gather | solution.py:1476
  8.8 65.8 %copy-start.12 = (s32[1,2048]{1,0:T(1,128)S(1)}, s32[1,2048]{1,0:T(1,128)}, u32[]{:S(2)}) copy-start(s32[1,2048]{1,0:T(1,128)} %param.13) | copy-start | bytes 24580
  73.0 201.5 %all-gather.6.cloned.1.call-start = ((), (), s32[]{:S(2)}) async-start(), calls=%async_computation.5 | async-start | bytes 5242880 | tf_op jit(solution)/shard_map/all_gather | solution.py:1476
  73.7 289.2 %all-gather.8.cloned.1.call-start = ((), (), s32[]{:S(2)}) async-start(), calls=%async_computation.6 | async-start | bytes 5242880 | tf_op jit(solution)/shard_map/all_gather | solution.py:1476
  74.5 521.0 %reduce-scatter.5.cloned.1.call-start = ((), (), s32[]{:S(2)}) async-start(), calls=%async_computation.7 | async-start | bytes 5242880 | tf_op jit(solution)/shard_map/reduce_scatter | solution.py:1481
  193.4 63.4 %copy-start.2 = (bf16[1,512,2048]{2,1,0:T(8,128)(2,1)S(1)}, bf16[1,512,2048]{2,1,0:T(8,128)(2,1)}, u32[]{:S(2)}) copy-start(bf16[1,512,2048]{2,1,0:T(8,128)(2,1)} %param.12) | copy-start | bytes 6291460
  256.8 9.9 %copy-start.13 = (f32[2048]{0:T(1024)S(1)}, f32[2048]{0:T(1024)}, u32[]{:S(2)}) copy-start(f32[2048]{0:T(1024)} %param.19) | copy-start | bytes 24580
  264.7 2.0 copy-start
  363.0 14.4 %copy-start.15 = (bf16[4096,1024]{1,0:T(8,128)(2,1)S(1)}, bf16[4096,1024]{1,0:T(8,128)(2,1)}, u32[]{:S(2)}) copy-start(bf16[4096,1024]{1,0:T(8,128)(2,1)} %get-tuple-element.120) | copy-start | bytes 25165828
  377.3 21.6 %collective-permute-start = (bf16[2048,2048]{1,0:T(8,128)(2,1)}, bf16[2048,2048]{1,0:T(8,128)(2,1)}, u32[]{:S(2)}, u32[]{:S(2)}) collective-permute-start(bf16[2048,2048]{1,0:T(8,128)(2,1)} %convolution_convert_fusion.1), channel_id=1, source_target_pairs={{0,4},{4,0},{8,12},{12,8},{16,20},{20,16},{24,28},{28,24},{1,5},{5... | collective-permute-start | bytes 25165832 | tf_op jit(solution)/shard_map/ppermute | solution.py:1428
  398.9 213.5 %reduce-scatter.7.cloned.1.call-start = ((), (), s32[]{:S(2)}) async-start(), calls=%async_computation.8 | async-start | bytes 5242880 | tf_op jit(solution)/shard_map/reduce_scatter | solution.py:1481
  412.2 38.6 %copy-start.1 = (bf16[2048,2048]{1,0:T(8,128)(2,1)}, bf16[2048,2048]{1,0:T(8,128)(2,1)S(1)}, u32[]{:S(2)}) copy-start(bf16[2048,2048]{1,0:T(8,128)(2,1)S(1)} %add_convert_fusion) | copy-start | bytes 25165828
  414.4 36.4 %collective-permute-start.1 = (bf16[256,2048]{1,0:T(8,128)(2,1)}, bf16[256,2048]{1,0:T(8,128)(2,1)}, u32[]{:S(2)}, u32[]{:S(2)}) collective-permute-start(bf16[256,2048]{1,0:T(8,128)(2,1)} %get-tuple-element.99), channel_id=1, source_target_pairs={{0,8},{4,12},{8,0},{12,4},{16,24},{20,28},{24,16},{28,20},{1,9},{5... | collective-permute-start | bytes 3145736 | tf_op jit(solution)/shard_map/ppermute | solution.py:1428
  414.9 35.8 %collective-permute-start.2 = (bf16[256,2048]{1,0:T(8,128)(2,1)}, bf16[256,2048]{1,0:T(8,128)(2,1)}, u32[]{:S(2)}, u32[]{:S(2)}) collective-permute-start(bf16[256,2048]{1,0:T(8,128)(2,1)} %get-tuple-element.100), channel_id=1, source_target_pairs={{0,16},{4,20},{8,24},{12,28},{16,0},{20,4},{24,8},{28,12},{1,17},{... | collective-permute-start | bytes 3145736 | tf_op jit(solution)/shard_map/ppermute | solution.py:1428
  415.3 62.9 %collective-permute-start.3 = (bf16[256,2048]{1,0:T(8,128)(2,1)}, bf16[256,2048]{1,0:T(8,128)(2,1)S(1)}, u32[]{:S(2)}, u32[]{:S(2)}) collective-permute-start(bf16[256,2048]{1,0:T(8,128)(2,1)} %get-tuple-element.108), channel_id=1, source_target_pairs={{0,8},{4,12},{8,0},{12,4},{16,24},{20,28},{24,16},{28,20},{1,9},{5... | collective-permute-start | bytes 3145736 | tf_op jit(solution)/shard_map/ppermute | solution.py:1428
  417.2 61.0 %collective-permute-start.4 = (bf16[256,2048]{1,0:T(8,128)(2,1)}, bf16[256,2048]{1,0:T(8,128)(2,1)S(1)}, u32[]{:S(2)}, u32[]{:S(2)}) collective-permute-start(bf16[256,2048]{1,0:T(8,128)(2,1)} %get-tuple-element.109), channel_id=1, source_target_pairs={{0,16},{4,20},{8,24},{12,28},{16,0},{20,4},{24,8},{28,12},{1,17},{... | collective-permute-start | bytes 3145736 | tf_op jit(solution)/shard_map/ppermute | solution.py:1428
  478.2 24.7 %copy-start.5 = (bf16[256,2048]{1,0:T(8,128)(2,1)}, bf16[256,2048]{1,0:T(8,128)(2,1)S(1)}, u32[]{:S(2)}) copy-start(bf16[256,2048]{1,0:T(8,128)(2,1)S(1)} %collective-permute-done.3) | copy-start | bytes 3145732
  478.2 24.7 %copy-start.7 = (bf16[256,2048]{1,0:T(8,128)(2,1)}, bf16[256,2048]{1,0:T(8,128)(2,1)S(1)}, u32[]{:S(2)}) copy-start(bf16[256,2048]{1,0:T(8,128)(2,1)S(1)} %collective-permute-done.4) | copy-start | bytes 3145732
  478.2 236.7 %reduce-scatter.9.cloned.1.call-start = ((), (), s32[]{:S(2)}) async-start(), calls=%async_computation.9 | async-start | bytes 5242880 | tf_op jit(solution)/shard_map/reduce_scatter | solution.py:1481
  478.3 24.9 %collective-permute-start.5 = (bf16[256,2048]{1,0:T(8,128)(2,1)}, bf16[256,2048]{1,0:T(8,128)(2,1)}, u32[]{:S(2)}, u32[]{:S(2)}) collective-permute-start(bf16[256,2048]{1,0:T(8,128)(2,1)} %get-tuple-element.112), channel_id=1, source_target_pairs={{0,8},{4,12},{8,0},{12,4},{16,24},{20,28},{24,16},{28,20},{1,9},{5... | collective-permute-start | bytes 3145736 | tf_op jit(solution)/shard_map/ppermute | solution.py:1428
  478.9 24.4 %collective-permute-start.6 = (bf16[256,2048]{1,0:T(8,128)(2,1)}, bf16[256,2048]{1,0:T(8,128)(2,1)}, u32[]{:S(2)}, u32[]{:S(2)}) collective-permute-start(bf16[256,2048]{1,0:T(8,128)(2,1)} %get-tuple-element.113), channel_id=1, source_target_pairs={{0,16},{4,20},{8,24},{12,28},{16,0},{20,4},{24,8},{28,12},{1,17},{... | collective-permute-start | bytes 3145736 | tf_op jit(solution)/shard_map/ppermute | solution.py:1428
  503.0 217.6 %reduce-scatter.11.cloned.1.call-start = ((), (), s32[]{:S(2)}) async-start(), calls=%async_computation.10 | async-start | bytes 9437184 | tf_op jit(solution)/shard_map/reduce_scatter | solution.py:1439
  595.5 10.1 %copy-start.3 = (bf16[512,2048]{1,0:T(8,128)(2,1)S(1)}, bf16[512,2048]{1,0:T(8,128)(2,1)}, u32[]{:S(2)}) copy-start(bf16[512,2048]{1,0:T(8,128)(2,1)} %get-tuple-element.121.dh_ref) | copy-start | bytes 6291460
  595.5 10.1 %copy-start.16 = (bf16[512,2048]{1,0:T(8,128)(2,1)S(1)}, bf16[512,2048]{1,0:T(8,128)(2,1)}, u32[]{:S(2)}) copy-start(bf16[512,2048]{1,0:T(8,128)(2,1)} %get-tuple-element.85.o_ref) | copy-start | bytes 6291460
  612.4 0.9 copy-start.11
  612.4 0.9 copy-start.14
  612.4 1.6 copy-start.6
  612.4 1.6 copy-start.8
  800.8 6.1 copy-start.4
  800.8 7.4 copy-start.10
  804.0 5.0 copy-start.9
Sparse Core Ops, SparseCore 0:
  73.1 98.2 all-gather.3
  173.0 101.4 all-gather.5
  276.1 78.7 all-gather.7
  399.0 76.5 reduce-scatter.4
  478.4 76.7 reduce-scatter.6
  557.3 77.2 reduce-scatter.8
  638.5 71.7 reduce-scatter.10

commit v14 on v13

--- a/solution.py
+++ b/solution.py
@@ -1372,6 +1372,33 @@
     )(x, dq, dkv, wo_sum, gains, raw, dh, wq, wkv, *mlp)
 
 
+def emit_kernel(*refs):
+    ins, outs = refs[:7], refs[7:]
+    for src, dst in zip(ins[:6], outs[:6]):
+        dst[...] = src[...].astype(dst.dtype)
+    outs[6][...] = ins[6][:, :LANES]
+    outs[7][...] = ins[6][:, LANES:]
+
+
+def emit(mlp, grad, wq, wo, wkv):
+    ins = (*mlp, grad, wq, wo, wkv)
+    apart = (wkv.shape[0], LANES)
+    outs = [(m.shape, F32) for m in mlp] + [(grad.shape, BF16), (wq.shape, F32), (wo.shape, F32)]
+    outs += [(apart, F32)] * 2
+    steps = 4
+
+    def spec(shape):
+        return pl.BlockSpec((shape[0] // steps, shape[1]), lambda at: (at, 0))
+
+    return pl.pallas_call(
+        emit_kernel,
+        grid=(steps,),
+        in_specs=[spec(array.shape) for array in ins],
+        out_specs=[spec(shape) for shape, _ in outs],
+        out_shape=[jax.ShapeDtypeStruct(*out) for out in outs],
+    )(*ins)
+
+
 class Layout:
     def __init__(self, dp_size):
         self.blocks = dp_size // GROUP
@@ -1553,17 +1580,19 @@
     output = output + jnp.concatenate([x_upper, x_lower]).astype(F32)
     output = output + jnp.concatenate([y_upper, y_lower]).astype(F32)
     wo_grad, wq_grad, wkv_grad, wd_grad, wg_grad, wu_grad = (
-        layout.scatter_outer(grad).astype(F32)
+        layout.scatter_outer(grad)
         for grad in (wo_grad, wq_grad, wkv_grad, wd_grad, wg_grad, wu_grad)
     )
-    key_cols = w_key.shape[1]
+    wd_grad, wg_grad, wu_grad, input_grad, wq_grad, wo_grad, wk_grad, wv_grad = emit(
+        (wd_grad, wg_grad, wu_grad), input_grad, wq_grad, wo_grad, wkv_grad
+    )
     return (
         output.astype(BF16)[None],
         input_grad[None],
         gains[0],
         wq_grad,
-        wkv_grad[:, :key_cols],
-        wkv_grad[:, key_cols:],
+        wk_grad,
+        wv_grad,
         wo_grad,
         gains[1],
         wg_grad,

time: 821 us -> 814 us (level)
  other arithmetic: 24.3 us -> 15.9 us
    convert_element_type x3 -> x0, other arithmetic: 8.42 us -> none  [per_device(): layout.scatter_outer(grad).astype(F32)]
  transfers between devices with their start and end apart: 14 -> 14, of which waited for: 3 -> 3; matrix products, arithmetic and copies ran while one was open for 20% -> 19% of each run, Pallas kernels for 56% -> 56%
where the time goes in v14:
time: 814 us; the launch traced here: 811 us
  Pallas kernels  607 us (75%)
  matrix products  154 us (19%)
  other arithmetic  15.9 us (2%)
  between operations  14.7 us (2%)
    pallas_call x1, Pallas kernels, project(): pl.pallas_call(functools.partial(project_kernel, 2 * math.isqrt(dp_size /...  116 us
    pallas_call x1, Pallas kernels, attend_back(): pl.pallas_call(functools.partial(attend_back_kernel, reach, 2 * math.isqr...  95.8 us
    pallas_call x1, Pallas kernels, hidden_back(): pl.pallas_call(functools.partial(hidden_back_kernel, 2 * math.isqrt(dp_si...  92.1 us
    pallas_call x1, Pallas kernels, gate_up(): pl.pallas_call(functools.partial(gate_up_kernel, 2 * math.isqrt(dp_size /...  88.4 us
    pallas_call x1, Pallas kernels, last_grads(): pl.pallas_call(functools.partial(tail_kernel, 2 * math.isqrt(dp_size // G...  80.4 us
    dot_general x4, matrix products, dot_tn(): lax.dot_general(left, right, (((0,), (0,)), ((), ())), preferred_element_...  75.7 us
    pallas_call x1, Pallas kernels, spread_weights(): pl.pallas_call(functools.partial(spread_kernel, 2 * math.isqrt(dp_size //...  64.2 us
    pallas_call x1, Pallas kernels, attend(): pl.pallas_call(functools.partial(attend_kernel, reach, 2 * math.isqrt(dp_...  63.5 us
  transfers between devices with their start and end apart: 14, of which 3 were waited for; matrix products, arithmetic and copies ran while one was open for 19% of the time, Pallas kernels for 56%

profile of v14, /device:TPU:0, one launch (start us, length us, event | category | flops | bytes accessed | tf_op | source)
XLA Modules:
  0.0 810.6 jit_solution(5537970622013372606)
XLA Ops:
  7.2 0.0 all-gather.4.cloned.1.call-start
  7.2 1.5 pad_maximum_fusion.2.refs_3_
  8.8 64.2 %shard_map.203 = (bf16[512,2048]{1,0:T(8,128)(2,1)}, bf16[2048,256]{1,0:T(8,128)(2,1)}, bf16[2048,256]{1,0:T(8,128)(2,1)}, bf16[2048,256]{1,0:T(8,128)(2,1)}, bf...) custom-call(bf16[512,2048]{1,0:T(8,128)(2,1)} %bitcast.37, f32[1,2048]{1,0:T(1,128)} %bitcast.43, ...), custom_call_target="tpu_custom_call" | custom-call | flops 60000002048 | tf_op jit(solution)/shard_map/pallas_call | solution.py:559
  73.0 0.0 all-gather.4.cloned.1.call-update
  73.0 0.0 all-gather.6.cloned.1.call-start
  73.0 0.7 all-gather.6.cloned.1.call-update
  73.7 0.0 all-gather.8.cloned.1.call-start
  73.8 0.7 all-gather.8.cloned.1.call-update
  74.5 0.0 reduce-scatter.5.cloned.1.call-start
  74.5 0.1 convert_reduce_fusion
  74.7 0.1 select_reduce_fusion
  74.8 0.7 subtract_add_fusion
  75.4 1.0 fusion.16
  76.4 1.3 pad_maximum_fusion
  77.7 115.6 %shard_map.204 = (bf16[512,2048]{1,0:T(8,128)(2,1)}, bf16[1536,1024]{1,0:T(8,128)(2,1)}, bf16[2048,2048]{1,0:T(8,128)(2,1)}, bf16[2048,2048]{1,0:T(8,128)(2,1)}, bf16[4096,2048]{1,0:T(8,128)(2,1)}) custom-call(bf16[512,2048]{1,0:T(8,128)(2,1)} %get-tuple-element.86.x_ref, f32[512,128]{1,0:T(8,128)} %get-tuple-element.178.cos_ref.cos_all, ...), custom_call_target="tpu_custom_call" | custom-call | flops 120000004096 | tf_op jit(solution)/shard_map/pallas_call | solution.py:773
  193.3 0.0 copy-start.2
  193.3 63.5 %shard_map.205 = (bf16[512,2048]{1,0:T(8,128)(2,1)}, f32[32,1,512]{2,1,0:T(1,128)}, bf16[4096,2048]{1,0:T(8,128)(2,1)}) custom-call(bf16[512,2048]{1,0:T(8,128)(2,1)} %get-tuple-element.90.q_ref, bf16[1536,1024]{1,0:T(8,128)(2,1)} %get-tuple-element.91.k_ref.v_ref, ...), custom_call_target="tpu_custom_call", output_to_operand_aliasing={{2}: (5, {})} | custom-call | flops 21474836480 | bytes 7340032 | tf_op jit(solution)/shard_map/pallas_call | solution.py:164
  256.8 0.0 copy-start.10
  256.8 7.9 multiply_reduce_fusion
  264.7 2.0 copy-done
  266.7 1.7 multiply_convert_fusion.own_ref
  268.4 6.1 all-gather.6.cloned.1.call-done.wu_ref
  274.5 88.4 %shard_map.206 = (bf16[4096,2048]{1,0:T(8,128)(2,1)}, bf16[4096,1024]{1,0:T(8,128)(2,1)}, bf16[4096,1024]{1,0:T(8,128)(2,1)}, bf16[4096,1024]{1,0:T(8,128)(2,1)}, bf16[2,2048,1024]{2,1,0:T(8,128)(2,1)}) custom-call(bf16[512,2048]{1,0:T(8,128)(2,1)} %multiply_convert_fusion.own_ref, bf16[2048,1024]{1,0:T(8,128)(2,1)} %all-gather.4.cloned.1.call-done.wg_ref, ...), custom_call_target="tpu_custom_call" | custom-call | flops 1000000 | tf_op jit(solution)/shard_map/pallas_call | solution.py:893
  362.9 0.0 all-gather.8.cloned.1.call-done
  363.0 14.3 %convolution_convert_fusion.1 = bf16[2048,2048]{1,0:T(8,128)(2,1)} fusion(bf16[2048,1024]{1,0:T(8,128)(2,1)} %all-gather.8.cloned.1.call-done, bf16[2,2048,1024]{2,1,0:T(8,128)(2,1)} %get-tuple-element.98), kind=kOutput, calls=%fused_computation.13 | convolution fusion | flops 8594128896 | bytes 16777216 | tf_op jit(solution)/shard_map/dot_general | solution.py:36
  377.3 0.1 collective-permute-start
  377.4 21.5 %convolution_convert_fusion.2 = bf16[2048,1024]{1,0:T(8,128)(2,1)} fusion(bf16[4096,2048]{1,0:T(8,128)(2,1)} %get-tuple-element.104, bf16[4096,1024]{1,0:T(8,128)(2,1)S(1)} %copy-done.12), kind=kOutput, calls=%fused_computation.23 | convolution fusion | flops 17181966336 | bytes 29360128 | tf_op jit(solution)/shard_map/dot_general | solution.py:40
  398.8 0.0 reduce-scatter.5.cloned.1.call-update
  398.9 0.0 reduce-scatter.7.cloned.1.call-start
  398.9 13.2 %add_convert_fusion = bf16[2048,2048]{1,0:T(8,128)(2,1)S(1)} fusion(bf16[2048,2048]{1,0:T(8,128)(2,1)} %collective-permute-done, bf16[2048,1024]{1,0:T(8,128)(2,1)} %all-gather.8.cloned.1.call-done, bf16[2,2048,1024]{2,1,0:T(8,128)(2,1)} %get-tuple-element.98), kind=kOutput, calls=%fused_computation.11 | convolution fusion | flops 8602517504 | bytes 25165824 | tf_op jit(solution)/shard_map/dot_general | solution.py:36
  412.2 2.1 fusion.17
  414.3 0.6 collective-permute-start.1
  414.9 0.3 collective-permute-start.2
  415.2 1.9 collective-permute-start.3
  417.1 1.3 collective-permute-start.4
  418.4 32.3 %fusion.7 = (bf16[4096,1024]{1,0:T(8,128)(2,1)}, bf16[4096,1024]{1,0:T(8,128)(2,1)}) fusion(bf16[4096,1024]{1,0:T(8,128)(2,1)} %get-tuple-element.106, bf16[4096,1024]{1,0:T(8,128)(2,1)} %get-tuple-element.105, bf16[4096,2048]{1,0:T(8,128)(2,1)} %get-tuple-element.104, bf16[2048,1024]{1,0:T(8,128)(2,1)} %all-gather.8.cloned.1.call-done), kind=kOutput, calls=%fused_computation.10 | convolution fusion | flops 17242783744 | bytes 54525952 | tf_op jit(solution)/shard_map/dot_general | solution.py:32
  450.7 3.7 add_convert_fusion.2
  454.4 23.7 %convolution_convert_fusion.4 = bf16[2048,1024]{1,0:T(8,128)(2,1)} fusion(bf16[4096,2048]{1,0:T(8,128)(2,1)} %get-tuple-element.114, bf16[4096,1024]{1,0:T(8,128)(2,1)} %get-tuple-element.115.dgate_ref), kind=kOutput, calls=%fused_computation.25 | convolution fusion | flops 17181966336 | bytes 29360128 | tf_op jit(solution)/shard_map/dot_general | solution.py:40
  478.2 0.0 copy-start.6
  478.2 0.0 reduce-scatter.7.cloned.1.call-update
  478.2 0.0 reduce-scatter.9.cloned.1.call-start
  478.2 0.6 collective-permute-start.5
  478.9 0.3 collective-permute-start.6
  479.2 23.7 %convolution_convert_fusion.3 = bf16[2048,1024]{1,0:T(8,128)(2,1)} fusion(bf16[4096,2048]{1,0:T(8,128)(2,1)} %get-tuple-element.114, bf16[4096,1024]{1,0:T(8,128)(2,1)} %get-tuple-element.126.dup_ref), kind=kOutput, calls=%fused_computation.24 | convolution fusion | flops 17181966336 | bytes 29360128 | tf_op jit(solution)/shard_map/dot_general | solution.py:40
  502.9 0.0 reduce-scatter.9.cloned.1.call-update
  502.9 0.0 reduce-scatter.11.cloned.1.call-start
  503.0 0.1 collective-permute-done.5
  503.1 0.3 collective-permute-done.6
  503.3 92.1 %shard_map.207 = (bf16[512,2048]{1,0:T(8,128)(2,1)}, f32[16,2048]{1,0:T(8,128)}) custom-call(f32[1,2048]{1,0:T(1,128)} %bitcast.42, f32[512,2048]{1,0:T(8,128)} %copy-done, bf16[512,2048]{1,0:T(8,128)(2,1)} %bitcast.51, bf16[4096,1024]{1,0:T(8,128)(2,1)} %get-tuple-element.115.dgate_ref, bf16[4096,1024]{1,0:T(8,128)(2,1)} %get-tuple-element.126.dup_ref, ...), custom_call_target="tpu_custom_call" | custom-call | flops 120000004096 | bytes 4194304 | tf_op jit(solution)/shard_map/pallas_call | solution.py:1112
  595.4 0.0 reduce-scatter.5.cloned.1.call-done.refs_0_
  595.5 10.1 %convolution_convert_fusion.5.do_ref = bf16[512,2048]{1,0:T(8,128)(2,1)} fusion(bf16[512,2048]{1,0:T(8,128)(2,1)} %get-tuple-element.129.dh_ref, bf16[2048,2048]{1,0:T(8,128)(2,1)} %get-tuple-element.94), kind=kOutput, calls=%fused_computation.26 | convolution fusion | flops 4296015872 | bytes 12582912 | tf_op jit(solution)/shard_map/dot_general | solution.py:32
  605.6 6.8 convolution_convert_fusion
  612.4 0.0 reduce-scatter.7.cloned.1.call-done.refs_1_
  612.4 0.0 reduce-scatter.11.cloned.1.call-update
  612.4 0.8 copy-done.8
  613.3 0.6 pad_maximum_fusion.3.gain_ref
  613.9 0.1 copy-done.7
  614.0 5.2 fusion.15
  619.2 95.8 %shard_map.208 = (bf16[512,2048]{1,0:T(8,128)(2,1)}, bf16[512,1024]{1,0:T(8,128)(2,1)}, bf16[256,2048]{1,0:T(8,128)(2,1)}, bf16[256,2048]{1,0:T(8,128)(2,1)}) custom-call(bf16[512,2048]{1,0:T(8,128)(2,1)} %get-tuple-element.90.q_ref, bf16[512,2048]{1,0:T(8,128)(2,1)} %convolution_convert_fusion.5.do_ref, bf16[512,2048]{1,0:T(8,128)(2,1)} %get-tuple-element.93.o_ref, ...), custom_call_target="tpu_custom_call" | custom-call | flops 53687091200 | bytes 14680064 | tf_op jit(solution)/shard_map/pallas_call | solution.py:319
  714.9 0.0 reduce-scatter.9.cloned.1.call-done.refs_0_
  715.0 0.0 reduce-scatter.11.cloned.1.call-done.wo_ref
  715.0 80.4 %shard_map.209 = (f32[256,512]{1,0:T(8,128)}, f32[256,256]{1,0:T(8,128)}, f32[256,512]{1,0:T(8,128)}, f32[2,2048]{1,0:T(2,128)}, bf16[512,2048]{1,0:T(8,128)(2,1)}, /*index=5*/bf16[256,2048]{1,0:T(8,128)(2,1)}) custom-call(bf16[512,2048]{1,0:T(8,128)(2,1)} %get-tuple-element.86.x_ref, bf16[512,2048]{1,0:T(8,128)(2,1)} %get-tuple-element.141.dq_ref, ...), custom_call_target="tpu_custom_call" | custom-call | flops 1000000 | tf_op jit(solution)/shard_map/pallas_call | solution.py:1335
  795.4 1.4 fusion.18
  796.8 6.7 shard_map.210
  (31 shorter events, 0.1 us)
Async XLA Ops:
  7.2 261.2 %all-gather.4.cloned.1.call-start = ((), (), s32[]{:S(2)}) async-start(), calls=%async_computation.4 | async-start | bytes 5242880 | tf_op jit(solution)/shard_map/all_gather | solution.py:1503
  8.8 65.8 %copy-start.9 = (s32[1,2048]{1,0:T(1,128)S(1)}, s32[1,2048]{1,0:T(1,128)}, u32[]{:S(2)}) copy-start(s32[1,2048]{1,0:T(1,128)} %param.13) | copy-start | bytes 24580
  73.0 201.5 %all-gather.6.cloned.1.call-start = ((), (), s32[]{:S(2)}) async-start(), calls=%async_computation.5 | async-start | bytes 5242880 | tf_op jit(solution)/shard_map/all_gather | solution.py:1503
  73.7 289.2 %all-gather.8.cloned.1.call-start = ((), (), s32[]{:S(2)}) async-start(), calls=%async_computation.6 | async-start | bytes 5242880 | tf_op jit(solution)/shard_map/all_gather | solution.py:1503
  74.5 521.0 %reduce-scatter.5.cloned.1.call-start = ((), (), s32[]{:S(2)}) async-start(), calls=%async_computation.7 | async-start | bytes 5242880 | tf_op jit(solution)/shard_map/reduce_scatter | solution.py:1508
  193.3 63.5 %copy-start.2 = (bf16[1,512,2048]{2,1,0:T(8,128)(2,1)S(1)}, bf16[1,512,2048]{2,1,0:T(8,128)(2,1)}, u32[]{:S(2)}) copy-start(bf16[1,512,2048]{2,1,0:T(8,128)(2,1)} %param.12) | copy-start | bytes 6291460
  256.8 9.9 %copy-start.10 = (f32[2048]{0:T(1024)S(1)}, f32[2048]{0:T(1024)}, u32[]{:S(2)}) copy-start(f32[2048]{0:T(1024)} %param.19) | copy-start | bytes 24580
  264.7 2.0 copy-start
  362.9 14.4 %copy-start.12 = (bf16[4096,1024]{1,0:T(8,128)(2,1)S(1)}, bf16[4096,1024]{1,0:T(8,128)(2,1)}, u32[]{:S(2)}) copy-start(bf16[4096,1024]{1,0:T(8,128)(2,1)} %get-tuple-element.128) | copy-start | bytes 25165828
  377.3 21.6 %collective-permute-start = (bf16[2048,2048]{1,0:T(8,128)(2,1)}, bf16[2048,2048]{1,0:T(8,128)(2,1)}, u32[]{:S(2)}, u32[]{:S(2)}) collective-permute-start(bf16[2048,2048]{1,0:T(8,128)(2,1)} %convolution_convert_fusion.1), channel_id=1, source_target_pairs={{0,4},{4,0},{8,12},{12,8},{16,20},{20,16},{24,28},{28,24},{1,5},{5... | collective-permute-start | bytes 25165832 | tf_op jit(solution)/shard_map/ppermute | solution.py:1455
  398.9 213.5 %reduce-scatter.7.cloned.1.call-start = ((), (), s32[]{:S(2)}) async-start(), calls=%async_computation.8 | async-start | bytes 5242880 | tf_op jit(solution)/shard_map/reduce_scatter | solution.py:1508
  412.2 38.6 %copy-start.1 = (bf16[2048,2048]{1,0:T(8,128)(2,1)}, bf16[2048,2048]{1,0:T(8,128)(2,1)S(1)}, u32[]{:S(2)}) copy-start(bf16[2048,2048]{1,0:T(8,128)(2,1)S(1)} %add_convert_fusion) | copy-start | bytes 25165828
  414.3 36.4 %collective-permute-start.1 = (bf16[256,2048]{1,0:T(8,128)(2,1)}, bf16[256,2048]{1,0:T(8,128)(2,1)}, u32[]{:S(2)}, u32[]{:S(2)}) collective-permute-start(bf16[256,2048]{1,0:T(8,128)(2,1)} %get-tuple-element.107), channel_id=1, source_target_pairs={{0,8},{4,12},{8,0},{12,4},{16,24},{20,28},{24,16},{28,20},{1,9},{5... | collective-permute-start | bytes 3145736 | tf_op jit(solution)/shard_map/ppermute | solution.py:1455
  414.9 35.8 %collective-permute-start.2 = (bf16[256,2048]{1,0:T(8,128)(2,1)}, bf16[256,2048]{1,0:T(8,128)(2,1)}, u32[]{:S(2)}, u32[]{:S(2)}) collective-permute-start(bf16[256,2048]{1,0:T(8,128)(2,1)} %get-tuple-element.108), channel_id=1, source_target_pairs={{0,16},{4,20},{8,24},{12,28},{16,0},{20,4},{24,8},{28,12},{1,17},{... | collective-permute-start | bytes 3145736 | tf_op jit(solution)/shard_map/ppermute | solution.py:1455
  415.2 62.9 %collective-permute-start.3 = (bf16[256,2048]{1,0:T(8,128)(2,1)}, bf16[256,2048]{1,0:T(8,128)(2,1)S(1)}, u32[]{:S(2)}, u32[]{:S(2)}) collective-permute-start(bf16[256,2048]{1,0:T(8,128)(2,1)} %get-tuple-element.116), channel_id=1, source_target_pairs={{0,8},{4,12},{8,0},{12,4},{16,24},{20,28},{24,16},{28,20},{1,9},{5... | collective-permute-start | bytes 3145736 | tf_op jit(solution)/shard_map/ppermute | solution.py:1455
  417.1 61.0 %collective-permute-start.4 = (bf16[256,2048]{1,0:T(8,128)(2,1)}, bf16[256,2048]{1,0:T(8,128)(2,1)S(1)}, u32[]{:S(2)}, u32[]{:S(2)}) collective-permute-start(bf16[256,2048]{1,0:T(8,128)(2,1)} %get-tuple-element.117), channel_id=1, source_target_pairs={{0,16},{4,20},{8,24},{12,28},{16,0},{20,4},{24,8},{28,12},{1,17},{... | collective-permute-start | bytes 3145736 | tf_op jit(solution)/shard_map/ppermute | solution.py:1455
  478.1 24.8 %copy-start.4 = (bf16[256,2048]{1,0:T(8,128)(2,1)}, bf16[256,2048]{1,0:T(8,128)(2,1)S(1)}, u32[]{:S(2)}) copy-start(bf16[256,2048]{1,0:T(8,128)(2,1)S(1)} %collective-permute-done.3) | copy-start | bytes 3145732
  478.2 24.8 %copy-start.6 = (bf16[256,2048]{1,0:T(8,128)(2,1)}, bf16[256,2048]{1,0:T(8,128)(2,1)S(1)}, u32[]{:S(2)}) copy-start(bf16[256,2048]{1,0:T(8,128)(2,1)S(1)} %collective-permute-done.4) | copy-start | bytes 3145732
  478.2 236.8 %reduce-scatter.9.cloned.1.call-start = ((), (), s32[]{:S(2)}) async-start(), calls=%async_computation.9 | async-start | bytes 5242880 | tf_op jit(solution)/shard_map/reduce_scatter | solution.py:1508
  478.2 24.8 %collective-permute-start.5 = (bf16[256,2048]{1,0:T(8,128)(2,1)}, bf16[256,2048]{1,0:T(8,128)(2,1)}, u32[]{:S(2)}, u32[]{:S(2)}) collective-permute-start(bf16[256,2048]{1,0:T(8,128)(2,1)} %get-tuple-element.120), channel_id=1, source_target_pairs={{0,8},{4,12},{8,0},{12,4},{16,24},{20,28},{24,16},{28,20},{1,9},{5... | collective-permute-start | bytes 3145736 | tf_op jit(solution)/shard_map/ppermute | solution.py:1455
  478.9 24.4 %collective-permute-start.6 = (bf16[256,2048]{1,0:T(8,128)(2,1)}, bf16[256,2048]{1,0:T(8,128)(2,1)}, u32[]{:S(2)}, u32[]{:S(2)}) collective-permute-start(bf16[256,2048]{1,0:T(8,128)(2,1)} %get-tuple-element.121), channel_id=1, source_target_pairs={{0,16},{4,20},{8,24},{12,28},{16,0},{20,4},{24,8},{28,12},{1,17},{... | collective-permute-start | bytes 3145736 | tf_op jit(solution)/shard_map/ppermute | solution.py:1455
  502.9 212.0 %reduce-scatter.11.cloned.1.call-start = ((), (), s32[]{:S(2)}) async-start(), calls=%async_computation.10 | async-start | bytes 9437184 | tf_op jit(solution)/shard_map/reduce_scatter | solution.py:1466
  595.5 10.1 %copy-start.3 = (bf16[512,2048]{1,0:T(8,128)(2,1)S(1)}, bf16[512,2048]{1,0:T(8,128)(2,1)}, u32[]{:S(2)}) copy-start(bf16[512,2048]{1,0:T(8,128)(2,1)} %get-tuple-element.129.dh_ref) | copy-start | bytes 6291460
  595.5 10.1 %copy-start.13 = (bf16[512,2048]{1,0:T(8,128)(2,1)S(1)}, bf16[512,2048]{1,0:T(8,128)(2,1)}, u32[]{:S(2)}) copy-start(bf16[512,2048]{1,0:T(8,128)(2,1)} %get-tuple-element.93.o_ref) | copy-start | bytes 6291460
  612.4 0.9 copy-start.8
  612.4 0.9 copy-start.11
  612.4 1.6 copy-start.5
  612.4 1.6 copy-start.7
Sparse Core Ops, SparseCore 0:
  73.1 98.2 all-gather.3
  173.0 101.4 all-gather.5
  276.1 78.7 all-gather.7
  399.0 76.6 reduce-scatter.4
  478.3 76.8 reduce-scatter.6
  557.4 77.2 reduce-scatter.8
  638.5 71.7 reduce-scatter.10

commit v15 on v14

--- a/solution.py
+++ b/solution.py
@@ -20,7 +20,7 @@
 LOG2E = 1.4426950408889634
 FAR = -1e30
 NTILE = 512
-STRIP = 16
+STRIP = 32
 LONG = 60_000_000_000
 SHORT = 1_000_000
 

time: 814 us -> 811 us (level)
  no operation moved by 1% of the time
where the time goes in v15:
time: 811 us; the launch traced here: 808 us
  Pallas kernels  604 us (74%)
  matrix products  153 us (19%)
  other arithmetic  15.9 us (2%)
  between operations  14.7 us (2%)
    pallas_call x1, Pallas kernels, project(): pl.pallas_call(functools.partial(project_kernel, 2 * math.isqrt(dp_size /...  116 us
    pallas_call x1, Pallas kernels, attend_back(): pl.pallas_call(functools.partial(attend_back_kernel, reach, 2 * math.isqr...  96.2 us
    pallas_call x1, Pallas kernels, hidden_back(): pl.pallas_call(functools.partial(hidden_back_kernel, 2 * math.isqrt(dp_si...  91.1 us
    pallas_call x1, Pallas kernels, gate_up(): pl.pallas_call(functools.partial(gate_up_kernel, 2 * math.isqrt(dp_size /...  88.4 us
    pallas_call x1, Pallas kernels, last_grads(): pl.pallas_call(functools.partial(tail_kernel, 2 * math.isqrt(dp_size // G...  78.6 us
    dot_general x4, matrix products, dot_tn(): lax.dot_general(left, right, (((0,), (0,)), ((), ())), preferred_element_...  75.7 us
    pallas_call x1, Pallas kernels, spread_weights(): pl.pallas_call(functools.partial(spread_kernel, 2 * math.isqrt(dp_size //...  64.2 us
    pallas_call x1, Pallas kernels, attend(): pl.pallas_call(functools.partial(attend_kernel, reach, 2 * math.isqrt(dp_...  63.5 us
  transfers between devices with their start and end apart: 14, of which 3 were waited for; matrix products, arithmetic and copies ran while one was open for 19% of the time, Pallas kernels for 56%

profile of v15, /device:TPU:0, one launch (start us, length us, event | category | flops | bytes accessed | tf_op | source)
XLA Modules:
  0.0 808.1 jit_solution(5707039113858599454)
XLA Ops:
  7.2 0.0 all-gather.4.cloned.1.call-start
  7.2 1.5 pad_maximum_fusion.2.refs_3_
  8.8 64.2 %shard_map.203 = (bf16[512,2048]{1,0:T(8,128)(2,1)}, bf16[2048,256]{1,0:T(8,128)(2,1)}, bf16[2048,256]{1,0:T(8,128)(2,1)}, bf16[2048,256]{1,0:T(8,128)(2,1)}, bf...) custom-call(bf16[512,2048]{1,0:T(8,128)(2,1)} %bitcast.37, f32[1,2048]{1,0:T(1,128)} %bitcast.43, ...), custom_call_target="tpu_custom_call" | custom-call | flops 60000002048 | tf_op jit(solution)/shard_map/pallas_call | solution.py:559
  73.0 0.0 all-gather.4.cloned.1.call-update
  73.0 0.0 all-gather.6.cloned.1.call-start
  73.0 0.7 all-gather.6.cloned.1.call-update
  73.7 0.0 all-gather.8.cloned.1.call-start
  73.8 0.7 all-gather.8.cloned.1.call-update
  74.5 0.0 reduce-scatter.5.cloned.1.call-start
  74.5 0.1 convert_reduce_fusion
  74.7 0.1 select_reduce_fusion
  74.8 0.7 subtract_add_fusion
  75.4 1.0 fusion.16
  76.4 1.3 pad_maximum_fusion
  77.7 115.6 %shard_map.204 = (bf16[512,2048]{1,0:T(8,128)(2,1)}, bf16[1536,1024]{1,0:T(8,128)(2,1)}, bf16[2048,2048]{1,0:T(8,128)(2,1)}, bf16[2048,2048]{1,0:T(8,128)(2,1)}, bf16[4096,2048]{1,0:T(8,128)(2,1)}) custom-call(bf16[512,2048]{1,0:T(8,128)(2,1)} %get-tuple-element.86.x_ref, f32[512,128]{1,0:T(8,128)} %get-tuple-element.178.cos_ref.cos_all, ...), custom_call_target="tpu_custom_call" | custom-call | flops 120000004096 | tf_op jit(solution)/shard_map/pallas_call | solution.py:773
  193.3 0.0 copy-start.2
  193.3 63.5 %shard_map.205 = (bf16[512,2048]{1,0:T(8,128)(2,1)}, f32[32,1,512]{2,1,0:T(1,128)}, bf16[4096,2048]{1,0:T(8,128)(2,1)}) custom-call(bf16[512,2048]{1,0:T(8,128)(2,1)} %get-tuple-element.90.q_ref, bf16[1536,1024]{1,0:T(8,128)(2,1)} %get-tuple-element.91.k_ref.v_ref, ...), custom_call_target="tpu_custom_call", output_to_operand_aliasing={{2}: (5, {})} | custom-call | flops 21474836480 | bytes 7340032 | tf_op jit(solution)/shard_map/pallas_call | solution.py:164
  256.8 0.0 copy-start.10
  256.8 7.9 multiply_reduce_fusion
  264.7 2.0 copy-done
  266.7 1.7 multiply_convert_fusion.own_ref
  268.4 6.1 all-gather.6.cloned.1.call-done.wu_ref
  274.5 88.4 %shard_map.206 = (bf16[4096,2048]{1,0:T(8,128)(2,1)}, bf16[4096,1024]{1,0:T(8,128)(2,1)}, bf16[4096,1024]{1,0:T(8,128)(2,1)}, bf16[4096,1024]{1,0:T(8,128)(2,1)}, bf16[2,2048,1024]{2,1,0:T(8,128)(2,1)}) custom-call(bf16[512,2048]{1,0:T(8,128)(2,1)} %multiply_convert_fusion.own_ref, bf16[2048,1024]{1,0:T(8,128)(2,1)} %all-gather.4.cloned.1.call-done.wg_ref, ...), custom_call_target="tpu_custom_call" | custom-call | flops 1000000 | tf_op jit(solution)/shard_map/pallas_call | solution.py:893
  362.9 0.0 all-gather.8.cloned.1.call-done
  363.0 14.3 %convolution_convert_fusion.1 = bf16[2048,2048]{1,0:T(8,128)(2,1)} fusion(bf16[2048,1024]{1,0:T(8,128)(2,1)} %all-gather.8.cloned.1.call-done, bf16[2,2048,1024]{2,1,0:T(8,128)(2,1)} %get-tuple-element.98), kind=kOutput, calls=%fused_computation.13 | convolution fusion | flops 8594128896 | bytes 16777216 | tf_op jit(solution)/shard_map/dot_general | solution.py:36
  377.3 0.1 collective-permute-start
  377.4 21.5 %convolution_convert_fusion.2 = bf16[2048,1024]{1,0:T(8,128)(2,1)} fusion(bf16[4096,2048]{1,0:T(8,128)(2,1)} %get-tuple-element.104, bf16[4096,1024]{1,0:T(8,128)(2,1)S(1)} %copy-done.12), kind=kOutput, calls=%fused_computation.23 | convolution fusion | flops 17181966336 | bytes 29360128 | tf_op jit(solution)/shard_map/dot_general | solution.py:40
  398.8 0.0 reduce-scatter.5.cloned.1.call-update
  398.9 0.0 reduce-scatter.7.cloned.1.call-start
  398.9 13.2 %add_convert_fusion = bf16[2048,2048]{1,0:T(8,128)(2,1)S(1)} fusion(bf16[2048,2048]{1,0:T(8,128)(2,1)} %collective-permute-done, bf16[2048,1024]{1,0:T(8,128)(2,1)} %all-gather.8.cloned.1.call-done, bf16[2,2048,1024]{2,1,0:T(8,128)(2,1)} %get-tuple-element.98), kind=kOutput, calls=%fused_computation.11 | convolution fusion | flops 8602517504 | bytes 25165824 | tf_op jit(solution)/shard_map/dot_general | solution.py:36
  412.2 2.1 fusion.17
  414.3 0.6 collective-permute-start.1
  414.9 0.3 collective-permute-start.2
  415.2 1.9 collective-permute-start.3
  417.1 1.3 collective-permute-start.4
  418.4 32.3 %fusion.7 = (bf16[4096,1024]{1,0:T(8,128)(2,1)}, bf16[4096,1024]{1,0:T(8,128)(2,1)}) fusion(bf16[4096,1024]{1,0:T(8,128)(2,1)} %get-tuple-element.106, bf16[4096,1024]{1,0:T(8,128)(2,1)} %get-tuple-element.105, bf16[4096,2048]{1,0:T(8,128)(2,1)} %get-tuple-element.104, bf16[2048,1024]{1,0:T(8,128)(2,1)} %all-gather.8.cloned.1.call-done), kind=kOutput, calls=%fused_computation.10 | convolution fusion | flops 17242783744 | bytes 54525952 | tf_op jit(solution)/shard_map/dot_general | solution.py:32
  450.7 3.7 add_convert_fusion.2
  454.4 23.7 %convolution_convert_fusion.4 = bf16[2048,1024]{1,0:T(8,128)(2,1)} fusion(bf16[4096,2048]{1,0:T(8,128)(2,1)} %get-tuple-element.114, bf16[4096,1024]{1,0:T(8,128)(2,1)} %get-tuple-element.115.dgate_ref), kind=kOutput, calls=%fused_computation.25 | convolution fusion | flops 17181966336 | bytes 29360128 | tf_op jit(solution)/shard_map/dot_general | solution.py:40
  478.2 0.0 copy-start.6
  478.2 0.0 reduce-scatter.7.cloned.1.call-update
  478.2 0.0 reduce-scatter.9.cloned.1.call-start
  478.2 0.6 collective-permute-start.5
  478.9 0.3 collective-permute-start.6
  479.2 23.7 %convolution_convert_fusion.3 = bf16[2048,1024]{1,0:T(8,128)(2,1)} fusion(bf16[4096,2048]{1,0:T(8,128)(2,1)} %get-tuple-element.114, bf16[4096,1024]{1,0:T(8,128)(2,1)} %get-tuple-element.126.dup_ref), kind=kOutput, calls=%fused_computation.24 | convolution fusion | flops 17181966336 | bytes 29360128 | tf_op jit(solution)/shard_map/dot_general | solution.py:40
  502.9 0.0 reduce-scatter.9.cloned.1.call-update
  502.9 0.0 reduce-scatter.11.cloned.1.call-start
  503.0 0.1 collective-permute-done.5
  503.1 0.3 collective-permute-done.6
  503.3 91.1 %shard_map.207 = (bf16[512,2048]{1,0:T(8,128)(2,1)}, f32[32,2048]{1,0:T(8,128)}) custom-call(f32[1,2048]{1,0:T(1,128)} %bitcast.42, f32[512,2048]{1,0:T(8,128)} %copy-done, bf16[512,2048]{1,0:T(8,128)(2,1)} %bitcast.51, bf16[4096,1024]{1,0:T(8,128)(2,1)} %get-tuple-element.115.dgate_ref, bf16[4096,1024]{1,0:T(8,128)(2,1)} %get-tuple-element.126.dup_ref, ...), custom_call_target="tpu_custom_call" | custom-call | flops 120000004096 | bytes 4194304 | tf_op jit(solution)/shard_map/pallas_call | solution.py:1112
  594.4 0.0 reduce-scatter.5.cloned.1.call-done.refs_0_
  594.5 10.0 %convolution_convert_fusion.5.do_ref = bf16[512,2048]{1,0:T(8,128)(2,1)} fusion(bf16[512,2048]{1,0:T(8,128)(2,1)} %get-tuple-element.129.dh_ref, bf16[2048,2048]{1,0:T(8,128)(2,1)} %get-tuple-element.94), kind=kOutput, calls=%fused_computation.26 | convolution fusion | flops 4296015872 | bytes 12582912 | tf_op jit(solution)/shard_map/dot_general | solution.py:32
  604.4 6.8 convolution_convert_fusion
  611.2 0.0 reduce-scatter.7.cloned.1.call-done.refs_1_
  611.3 0.0 reduce-scatter.11.cloned.1.call-update
  611.3 0.9 copy-done.8
  612.2 0.6 pad_maximum_fusion.3.gain_ref
  612.9 0.0 copy-done.7
  612.9 5.2 fusion.15
  618.0 96.2 %shard_map.208 = (bf16[512,2048]{1,0:T(8,128)(2,1)}, bf16[512,1024]{1,0:T(8,128)(2,1)}, bf16[256,2048]{1,0:T(8,128)(2,1)}, bf16[256,2048]{1,0:T(8,128)(2,1)}) custom-call(bf16[512,2048]{1,0:T(8,128)(2,1)} %get-tuple-element.90.q_ref, bf16[512,2048]{1,0:T(8,128)(2,1)} %convolution_convert_fusion.5.do_ref, bf16[512,2048]{1,0:T(8,128)(2,1)} %get-tuple-element.93.o_ref, ...), custom_call_target="tpu_custom_call" | custom-call | flops 53687091200 | bytes 14680064 | tf_op jit(solution)/shard_map/pallas_call | solution.py:319
  714.2 0.0 reduce-scatter.9.cloned.1.call-done.refs_0_
  714.3 0.0 reduce-scatter.11.cloned.1.call-done.wo_ref
  714.3 78.6 %shard_map.209 = (f32[256,512]{1,0:T(8,128)}, f32[256,256]{1,0:T(8,128)}, f32[256,512]{1,0:T(8,128)}, f32[2,2048]{1,0:T(2,128)}, bf16[512,2048]{1,0:T(8,128)(2,1)}, /*index=5*/bf16[256,2048]{1,0:T(8,128)(2,1)}) custom-call(bf16[512,2048]{1,0:T(8,128)(2,1)} %get-tuple-element.86.x_ref, bf16[512,2048]{1,0:T(8,128)(2,1)} %get-tuple-element.141.dq_ref, ...), custom_call_target="tpu_custom_call" | custom-call | flops 1000000 | tf_op jit(solution)/shard_map/pallas_call | solution.py:1335
  792.9 1.4 fusion.18
  794.3 6.7 shard_map.210
  (31 shorter events, 0.1 us)
Async XLA Ops:
  7.2 261.2 %all-gather.4.cloned.1.call-start = ((), (), s32[]{:S(2)}) async-start(), calls=%async_computation.4 | async-start | bytes 5242880 | tf_op jit(solution)/shard_map/all_gather | solution.py:1503
  8.8 65.8 %copy-start.9 = (s32[1,2048]{1,0:T(1,128)S(1)}, s32[1,2048]{1,0:T(1,128)}, u32[]{:S(2)}) copy-start(s32[1,2048]{1,0:T(1,128)} %param.13) | copy-start | bytes 24580
  73.0 201.5 %all-gather.6.cloned.1.call-start = ((), (), s32[]{:S(2)}) async-start(), calls=%async_computation.5 | async-start | bytes 5242880 | tf_op jit(solution)/shard_map/all_gather | solution.py:1503
  73.7 289.2 %all-gather.8.cloned.1.call-start = ((), (), s32[]{:S(2)}) async-start(), calls=%async_computation.6 | async-start | bytes 5242880 | tf_op jit(solution)/shard_map/all_gather | solution.py:1503
  74.5 520.0 %reduce-scatter.5.cloned.1.call-start = ((), (), s32[]{:S(2)}) async-start(), calls=%async_computation.7 | async-start | bytes 5242880 | tf_op jit(solution)/shard_map/reduce_scatter | solution.py:1508
  193.3 63.5 %copy-start.2 = (bf16[1,512,2048]{2,1,0:T(8,128)(2,1)S(1)}, bf16[1,512,2048]{2,1,0:T(8,128)(2,1)}, u32[]{:S(2)}) copy-start(bf16[1,512,2048]{2,1,0:T(8,128)(2,1)} %param.12) | copy-start | bytes 6291460
  256.8 9.9 %copy-start.10 = (f32[2048]{0:T(1024)S(1)}, f32[2048]{0:T(1024)}, u32[]{:S(2)}) copy-start(f32[2048]{0:T(1024)} %param.19) | copy-start | bytes 24580
  264.7 2.0 copy-start
  362.9 14.4 %copy-start.12 = (bf16[4096,1024]{1,0:T(8,128)(2,1)S(1)}, bf16[4096,1024]{1,0:T(8,128)(2,1)}, u32[]{:S(2)}) copy-start(bf16[4096,1024]{1,0:T(8,128)(2,1)} %get-tuple-element.128) | copy-start | bytes 25165828
  377.3 21.6 %collective-permute-start = (bf16[2048,2048]{1,0:T(8,128)(2,1)}, bf16[2048,2048]{1,0:T(8,128)(2,1)}, u32[]{:S(2)}, u32[]{:S(2)}) collective-permute-start(bf16[2048,2048]{1,0:T(8,128)(2,1)} %convolution_convert_fusion.1), channel_id=1, source_target_pairs={{0,4},{4,0},{8,12},{12,8},{16,20},{20,16},{24,28},{28,24},{1,5},{5... | collective-permute-start | bytes 25165832 | tf_op jit(solution)/shard_map/ppermute | solution.py:1455
  398.9 212.4 %reduce-scatter.7.cloned.1.call-start = ((), (), s32[]{:S(2)}) async-start(), calls=%async_computation.8 | async-start | bytes 5242880 | tf_op jit(solution)/shard_map/reduce_scatter | solution.py:1508
  412.2 38.6 %copy-start.1 = (bf16[2048,2048]{1,0:T(8,128)(2,1)}, bf16[2048,2048]{1,0:T(8,128)(2,1)S(1)}, u32[]{:S(2)}) copy-start(bf16[2048,2048]{1,0:T(8,128)(2,1)S(1)} %add_convert_fusion) | copy-start | bytes 25165828
  414.3 36.4 %collective-permute-start.1 = (bf16[256,2048]{1,0:T(8,128)(2,1)}, bf16[256,2048]{1,0:T(8,128)(2,1)}, u32[]{:S(2)}, u32[]{:S(2)}) collective-permute-start(bf16[256,2048]{1,0:T(8,128)(2,1)} %get-tuple-element.107), channel_id=1, source_target_pairs={{0,8},{4,12},{8,0},{12,4},{16,24},{20,28},{24,16},{28,20},{1,9},{5... | collective-permute-start | bytes 3145736 | tf_op jit(solution)/shard_map/ppermute | solution.py:1455
  414.9 35.8 %collective-permute-start.2 = (bf16[256,2048]{1,0:T(8,128)(2,1)}, bf16[256,2048]{1,0:T(8,128)(2,1)}, u32[]{:S(2)}, u32[]{:S(2)}) collective-permute-start(bf16[256,2048]{1,0:T(8,128)(2,1)} %get-tuple-element.108), channel_id=1, source_target_pairs={{0,16},{4,20},{8,24},{12,28},{16,0},{20,4},{24,8},{28,12},{1,17},{... | collective-permute-start | bytes 3145736 | tf_op jit(solution)/shard_map/ppermute | solution.py:1455
  415.2 62.9 %collective-permute-start.3 = (bf16[256,2048]{1,0:T(8,128)(2,1)}, bf16[256,2048]{1,0:T(8,128)(2,1)S(1)}, u32[]{:S(2)}, u32[]{:S(2)}) collective-permute-start(bf16[256,2048]{1,0:T(8,128)(2,1)} %get-tuple-element.116), channel_id=1, source_target_pairs={{0,8},{4,12},{8,0},{12,4},{16,24},{20,28},{24,16},{28,20},{1,9},{5... | collective-permute-start | bytes 3145736 | tf_op jit(solution)/shard_map/ppermute | solution.py:1455
  417.1 61.0 %collective-permute-start.4 = (bf16[256,2048]{1,0:T(8,128)(2,1)}, bf16[256,2048]{1,0:T(8,128)(2,1)S(1)}, u32[]{:S(2)}, u32[]{:S(2)}) collective-permute-start(bf16[256,2048]{1,0:T(8,128)(2,1)} %get-tuple-element.117), channel_id=1, source_target_pairs={{0,16},{4,20},{8,24},{12,28},{16,0},{20,4},{24,8},{28,12},{1,17},{... | collective-permute-start | bytes 3145736 | tf_op jit(solution)/shard_map/ppermute | solution.py:1455
  478.1 24.8 %copy-start.4 = (bf16[256,2048]{1,0:T(8,128)(2,1)}, bf16[256,2048]{1,0:T(8,128)(2,1)S(1)}, u32[]{:S(2)}) copy-start(bf16[256,2048]{1,0:T(8,128)(2,1)S(1)} %collective-permute-done.3) | copy-start | bytes 3145732
  478.2 24.8 %copy-start.6 = (bf16[256,2048]{1,0:T(8,128)(2,1)}, bf16[256,2048]{1,0:T(8,128)(2,1)S(1)}, u32[]{:S(2)}) copy-start(bf16[256,2048]{1,0:T(8,128)(2,1)S(1)} %collective-permute-done.4) | copy-start | bytes 3145732
  478.2 236.1 %reduce-scatter.9.cloned.1.call-start = ((), (), s32[]{:S(2)}) async-start(), calls=%async_computation.9 | async-start | bytes 5242880 | tf_op jit(solution)/shard_map/reduce_scatter | solution.py:1508
  478.2 24.8 %collective-permute-start.5 = (bf16[256,2048]{1,0:T(8,128)(2,1)}, bf16[256,2048]{1,0:T(8,128)(2,1)}, u32[]{:S(2)}, u32[]{:S(2)}) collective-permute-start(bf16[256,2048]{1,0:T(8,128)(2,1)} %get-tuple-element.120), channel_id=1, source_target_pairs={{0,8},{4,12},{8,0},{12,4},{16,24},{20,28},{24,16},{28,20},{1,9},{5... | collective-permute-start | bytes 3145736 | tf_op jit(solution)/shard_map/ppermute | solution.py:1455
  478.9 24.4 %collective-permute-start.6 = (bf16[256,2048]{1,0:T(8,128)(2,1)}, bf16[256,2048]{1,0:T(8,128)(2,1)}, u32[]{:S(2)}, u32[]{:S(2)}) collective-permute-start(bf16[256,2048]{1,0:T(8,128)(2,1)} %get-tuple-element.121), channel_id=1, source_target_pairs={{0,16},{4,20},{8,24},{12,28},{16,0},{20,4},{24,8},{28,12},{1,17},{... | collective-permute-start | bytes 3145736 | tf_op jit(solution)/shard_map/ppermute | solution.py:1455
  502.9 211.4 %reduce-scatter.11.cloned.1.call-start = ((), (), s32[]{:S(2)}) async-start(), calls=%async_computation.10 | async-start | bytes 9437184 | tf_op jit(solution)/shard_map/reduce_scatter | solution.py:1466
  594.4 10.0 %copy-start.3 = (bf16[512,2048]{1,0:T(8,128)(2,1)S(1)}, bf16[512,2048]{1,0:T(8,128)(2,1)}, u32[]{:S(2)}) copy-start(bf16[512,2048]{1,0:T(8,128)(2,1)} %get-tuple-element.129.dh_ref) | copy-start | bytes 6291460
  594.4 10.0 %copy-start.13 = (bf16[512,2048]{1,0:T(8,128)(2,1)S(1)}, bf16[512,2048]{1,0:T(8,128)(2,1)}, u32[]{:S(2)}) copy-start(bf16[512,2048]{1,0:T(8,128)(2,1)} %get-tuple-element.93.o_ref) | copy-start | bytes 6291460
  611.2 0.9 copy-start.8
  611.2 1.0 copy-start.11
  611.2 1.6 copy-start.5
  611.2 1.6 copy-start.7
Sparse Core Ops, SparseCore 0:
  73.1 98.2 all-gather.3
  173.0 101.4 all-gather.5
  276.1 78.7 all-gather.7
  399.0 76.6 reduce-scatter.4
  478.3 76.8 reduce-scatter.6
  557.4 77.2 reduce-scatter.8
  638.5 71.7 reduce-scatter.10
